TPU v7x, 256 devices: a whole 4x4x8 slice. The times are simulated.
256 devices in a mesh: seq: 16 (over z, core), grp: 16 (over x, y).
Axes of the slice: x: 4, y: 4, z: 8, core: 2. Of those that a mesh axis runs over, the one named last changes fastest.
Arguments:
- tokens: bfloat16 [131072, 1536], P(('seq', 'grp')), may hold values from -6 to 6
- w_query: bfloat16 [1536, 768], replicated, may hold values from -0.15625 to 0.15625
- w_key: bfloat16 [1536, 768], replicated, may hold values from -0.15625 to 0.15625
- w_value: bfloat16 [1536, 768], replicated, may hold values from -0.15625 to 0.15625
- w_output: bfloat16 [768, 1536], replicated, may hold values from -0.21875 to 0.21875
- level_weights: float32 [9, 6], replicated, may hold values from 0.05 to 0.5
Outputs:
- mixed: bfloat16 [131072, 1536], P(('seq', 'grp'))
All inputs are finite; a program needn't handle non-finite values.
Results may differ from a plain program's by a relative error of at most 0.013.
Values may be sent and summed in bfloat16 or wider, within the bound.
No kernel may reach another device: no remote copies, remote signals or barrier semaphores. Data moves between devices by JAX's collectives and lax.ppermute only.
A program may use at most 128 MiB of HBM per device.

v0:
```python
import jax
import jax.numpy as jnp
from jax import lax
from jax.sharding import PartitionSpec as P


def partner_2(value, axis, distance):
    mask = 2**distance
    pairs = [(source, source ^ mask) for source in range(lax.axis_size(axis))]
    return lax.ppermute(value, axis, pairs)


def unit_heads(matrix):
    return (matrix * lax.rsqrt(jnp.sum(matrix * matrix, -1, keepdims=True) + 1e-06)).astype(
        jnp.bfloat16
    )


def per_device(tokens, w_query, w_key, w_value, w_output, level_weights):
    rows = tokens.shape[0]
    heads = level_weights.shape[1]
    width = w_query.shape[1] // heads

    def project(weight):
        return jnp.dot(tokens, weight, preferred_element_type=jnp.float32).reshape(
            rows, heads, width
        )

    query = unit_heads(project(w_query))
    keys = unit_heads(project(w_key))
    values = project(w_value).astype(jnp.bfloat16)
    own_state = jnp.einsum("thd,the->hde", keys, values, preferred_element_type=jnp.float32)
    members = lax.axis_size("grp")
    groups = lax.axis_size("seq")
    member = lax.axis_index("grp")
    group = lax.axis_index("seq")
    member_bits = members.bit_length() - 1
    group_bits = groups.bit_length() - 1
    piece_len = heads * width * width // members
    pieces = own_state.reshape(1, members, piece_len)
    stack = (
        lax.all_to_all(pieces.astype(jnp.bfloat16), "grp", split_axis=1, concat_axis=0, tiled=True)
        .astype(pieces.dtype)
        .reshape(members, piece_len)
    )
    head_of = (member * piece_len + lax.iota(jnp.int32, piece_len)) // (width * width)
    picked = head_of[None, :] == lax.iota(jnp.int32, heads)[:, None]

    def spread(level):
        weight_row = level_weights[level + 1] * 2.0 ** (-0.5 * level)
        return jnp.sum(jnp.where(picked, weight_row[:, None], 0.0), 0)

    member_ids = lax.iota(jnp.int32, members)
    local_part = jnp.zeros((members, piece_len), jnp.float32)
    for level in range(member_bits):
        grouped = stack.reshape(members >> level, 1 << level, piece_len).sum(1)
        sibling = jnp.maximum((member_ids >> level) - 1, 0)
        present = (member_ids >> level & 1).astype(jnp.float32)
        local_part = local_part + present[:, None] * spread(level)[None, :] * grouped[sibling]
    block_total = jnp.sum(stack, 0)
    far_part = jnp.zeros((piece_len,), jnp.float32)
    for level in range(group_bits):
        partner = partner_2(block_total, "seq", level)
        present = (group >> level & 1).astype(jnp.float32)
        far_part = far_part + present * spread(member_bits + level) * partner
        block_total = block_total + partner
    outgoing = (local_part + far_part[None, :]).astype(jnp.bfloat16).reshape(members, 1, piece_len)
    returned = lax.all_to_all(outgoing, "grp", split_axis=0, concat_axis=1, tiled=True)
    combined = returned.reshape(heads, width, width)
    causal = lax.broadcasted_iota(jnp.int32, (rows, rows), 0) >= lax.broadcasted_iota(
        jnp.int32, (rows, rows), 1
    )
    scores = jnp.einsum("thd,shd->hts", query, keys, preferred_element_type=jnp.float32)
    weights = (jnp.where(causal[None], scores, 0.0) * level_weights[0][:, None, None]).astype(
        jnp.bfloat16
    )
    inside = jnp.einsum("hts,she->the", weights, values, preferred_element_type=jnp.float32)
    earlier = jnp.einsum("thd,hde->the", query, combined, preferred_element_type=jnp.float32)
    attended = (inside + earlier).astype(jnp.bfloat16).reshape(rows, heads * width)
    return jnp.dot(attended, w_output, preferred_element_type=jnp.float32).astype(jnp.bfloat16)


def solution(mesh):
    placed = (P(("seq", "grp"), None), P(), P(), P(), P(), P())
    return jax.shard_map(
        per_device, mesh=mesh, in_specs=placed, out_specs=P(("seq", "grp"), None), check_vma=False
    )
```

profile of v0, /device:TPU:32, one launch (start us, length us, event | category | flops | bytes accessed | tf_op | source)
XLA Modules:
  0.0 85.9 jit_solution(15517215109283051629)
XLA Ops:
  0.0 4.6 %convolution_convert_fusion.1 = bf16[512,768]{1,0:T(8,128)(2,1)} fusion(bf16[512,1536]{1,0:T(8,128)(2,1)} %param.6, bf16[1536,768]{1,0:T(8,128)(2,1)} %param.9), kind=kOutput, calls=%fused_computation.16 | convolution fusion | flops 1208352768 | bytes 4718592 | tf_op jit(solution)/shard_map/dot_general | solution.py:25
  4.6 1.4 %copy.28 = bf16[512,768]{0,1:T(8,128)(2,1)S(1)} copy(bf16[512,768]{1,0:T(8,128)(2,1)} %convolution_convert_fusion.1) | data formatting | bytes 1572864 | tf_op jit(solution)/shard_map/convert_element_type | solution.py:31
  6.0 3.8 %fusion.16 = f32[512,768]{0,1:T(8,128)S(1)} fusion(bf16[512,1536]{1,0:T(8,128)(2,1)} %param.6, bf16[1536,768]{1,0:T(8,128)(2,1)} %param.8), kind=kOutput, calls=%fused_computation.75 | convolution fusion | flops 1207959552 | bytes 5505024 | tf_op jit(solution)/shard_map/dot_general | solution.py:25
  9.8 0.2 multiply_reduce_fusion
  10.1 0.9 %copy-done.1 = f32[512,768]{0,1:T(8,128)} copy-done((f32[512,768]{0,1:T(8,128)}, f32[512,768]{0,1:T(8,128)S(1)}, u32[]{:S(2)}) %copy-start.1) | copy-done | bytes 1572888
  11.0 0.4 convolution_convert_fusion.2
  11.5 0.6 broadcast.472
  12.1 1.8 %reduce.20 = bf16[16,6144]{1,0:T(8,128)(2,1)S(1)} reduce(bf16[16,1,6144]{2,1,0:T(2,128)(2,1)S(1)} %bitcast.65, bf16[]{:T(256)} %broadcast.472), dimensions={1}, to_apply=%bitcast.42.reduce_sub_computation | reduce | bytes 393218
  13.9 0.8 reshape.480
  14.7 7.0 %all-to-all-start = ((bf16[16,2,3072]{2,1,0:T(2,128)(2,1)}), bf16[16,2,3072]{2,1,0:T(2,128)(2,1)S(1)}, u32[]{:S(2)}, u32[]{:S(2)}) async-start(bf16[16,2,3072]{2,1,0:T(2,128)(2,1)} %reshape.480), calls=%async_computation | async-start | bytes 393216 | tf_op jit(solution)/shard_map/all_to_all | solution.py:42
  21.7 0.8 iota_compare_fusion
  22.5 0.8 slice_reduce_fusion
  23.3 3.6 %fusion.15 = f32[512,768]{0,1:T(8,128)S(1)} fusion(bf16[512,1536]{1,0:T(8,128)(2,1)} %param.6, bf16[1536,768]{1,0:T(8,128)(2,1)} %param.7), kind=kOutput, calls=%fused_computation.74 | convolution fusion | flops 1207959552 | bytes 5505024 | tf_op jit(solution)/shard_map/dot_general | solution.py:25
  26.9 1.1 %copy-done.2 = f32[512,768]{0,1:T(8,128)} copy-done((f32[512,768]{0,1:T(8,128)}, f32[512,768]{0,1:T(8,128)S(1)}, u32[]{:S(2)}) %copy-start.2) | copy-done | bytes 1572888
  28.0 0.2 multiply_reduce_fusion.1
  28.2 0.6 add_rsqrt_fusion.1
  28.9 0.6 pad_clamp_fusion
  29.4 0.6 pad_clamp_fusion.1
  30.0 0.6 pad_clamp_fusion.2
  30.7 0.6 pad_clamp_fusion.3
  31.3 1.1 %select_reduce_fusion.7 = (f32[6144]{0:T(1024)}, f32[6144]{0:T(1024)}, f32[6144]{0:T(1024)}, f32[6144]{0:T(1024)}, f32[6144]{0:T(1024)}, /*index=5*/f32[6144]{0:T(1024)}, f32[6144]{0:T(1024)}, f32[6144]{0:T(1024)}) fusion(f32[6]{0:T(128)S(1)} %get-tuple-element.13, s32[6144]{0:T(1024)S(1)} %add_select_fusion, f32[6]{0:T(128)S(1)} %get-tuple-element.20, ...), kind=kLoop, calls=%fused_computation.38 | loop fusion | flops 577536 | bytes 221376 | tf_op jit(solution)/shard_map/reduce_sum | solution.py:51
  32.5 0.2 convert_reduce_fusion
  32.8 0.5 and_convert_fusion
  33.4 0.6 collective-permute-done
  34.0 0.6 copy-done.10
  34.7 0.5 and_convert_fusion.2
  35.3 3.2 %collective-permute-done.1 = f32[6144]{0:T(1024)S(1)} collective-permute-done((f32[6144]{0:T(1024)S(1)}, f32[6144]{0:T(1024)S(1)}, u32[]{:S(2)}, u32[]{:S(2)}) %collective-permute-start.1) | collective-permute-done | bytes 24608 | tf_op jit(solution)/shard_map/ppermute | solution.py:10
  38.4 3.4 %collective-permute-start.2 = (f32[6144]{0:T(1024)S(1)}, f32[6144]{0:T(1024)S(1)}, u32[]{:S(2)}, u32[]{:S(2)}) collective-permute-start(f32[6144]{0:T(1024)S(1)} %add.143), channel_id=1, source_target_pairs={{0,64},{16,80},{32,96},{48,112},{64,0},{80,16},{96,32},{112,48},{1... | collective-permute-start | bytes 73736 | tf_op jit(solution)/shard_map/ppermute | solution.py:10
  41.8 1.8 %collective-permute-done.2 = f32[6144]{0:T(1024)S(1)} collective-permute-done((f32[6144]{0:T(1024)S(1)}, f32[6144]{0:T(1024)S(1)}, u32[]{:S(2)}, u32[]{:S(2)}) %collective-permute-start.2) | collective-permute-done | bytes 24608 | tf_op jit(solution)/shard_map/ppermute | solution.py:10
  43.6 0.6 add.145
  44.2 5.9 %collective-permute-start.3 = (f32[6144]{0:T(1024)}, f32[6144]{0:T(1024)}, u32[]{:S(2)}, u32[]{:S(2)}) collective-permute-start(f32[6144]{0:T(1024)} %add.145), channel_id=1, source_target_pairs={{0,128},{16,144},{32,160},{48,176},{64,192},{80,208},{96,224},{112... | collective-permute-start | bytes 73736 | tf_op jit(solution)/shard_map/ppermute | solution.py:10
  50.4 1.0 %reshape.435 = f32[8,2,6144]{2,1,0:T(2,128)} reshape(bf16[1,16,6144]{2,1,0:T(8,128)(2,1)S(1)} %get-tuple-element.23) | data formatting | bytes 589824 | tf_op jit(solution)/shard_map/convert_element_type | solution.py:43
  51.4 0.3 reduce_sum.136
  51.7 1.5 %reduce_sum.134 = f32[8,6144]{1,0:T(8,128)S(1)} reduce(f32[8,2,6144]{2,1,0:T(2,128)} %reshape.435, f32[]{:T(128)} %constant.19.clone.1), dimensions={1}, to_apply=%region_4.5 | reduce | flops 49152 | bytes 589828 | tf_op jit(solution)/shard_map/reduce_sum | solution.py:56
  53.1 0.8 gather_fusion.3
  53.9 1.5 %gather_fusion.2 = f32[16,6144]{1,0:T(8,128)} fusion(f32[4,6144]{1,0:T(4,128)S(1)} %reduce_sum.136, s32[1024]{0:T(1024)} %pad_clamp_fusion.1), kind=kCustom, calls=%fused_computation.2 | custom fusion | bytes 786496 | tf_op jit(solution)/shard_map/gather | solution.py:59
  55.5 1.5 %gather_fusion.1 = f32[16,6144]{1,0:T(8,128)} fusion(f32[8,6144]{1,0:T(8,128)S(1)} %reduce_sum.134, s32[1024]{0:T(1024)} %pad_clamp_fusion.2), kind=kCustom, calls=%fused_computation.1 | custom fusion | bytes 786496 | tf_op jit(solution)/shard_map/gather | solution.py:59
  57.0 1.7 %gather_fusion = f32[16,6144]{1,0:T(8,128)} fusion(f32[16,6144]{1,0:T(8,128)S(1)} %convert_bitcast_fusion, s32[1024]{0:T(1024)} %pad_clamp_fusion.3), kind=kCustom, calls=%fused_computation | custom fusion | bytes 786496 | tf_op jit(solution)/shard_map/gather | solution.py:59
  58.8 0.8 multiply_add_fusion
  59.5 2.3 %fusion.8 = bf16[16,1,6144]{2,0,1:T(8,128)(2,1)} fusion(f32[16,6144]{1,0:T(8,128)S(1)} %gather_fusion.3, f32[16,6144]{1,0:T(8,128)} %gather_fusion.2, f32[16,6144]{1,0:T(8,128)} %gather_fusion.1, f32[16,6144]{1,0:T(8,128)} %gather_fusion, f32[6144]{0:T(1024)S(1)} %multiply_add_fusion, f32[6144]{0:T(1024)} %get-tuple-element.10, f32[16]{0:T(128)} %get-tuple-element.24, ...), kind=kLoop, calls=%fused_computation.22 | loop fusion | flops 1277952 | bytes 1892608 | tf_op jit(solution)/shard_map/convert_element_type | solution.py:67
  61.8 1.7 %reduce.21 = bf16[16,6144]{1,0:T(8,128)(2,1)S(1)} reduce(bf16[16,1,6144]{2,0,1:T(8,128)(2,1)} %fusion.8, bf16[]{:T(256)} %broadcast.472), dimensions={1}, to_apply=%copy.36.reduce_sub_computation | reduce | bytes 393218 | tf_op jit(solution)/shard_map/convert_element_type | solution.py:67
  63.5 0.8 reshape.482
  64.3 7.2 %all-to-all-start.1 = ((bf16[16,2,3072]{2,1,0:T(2,128)(2,1)}), bf16[16,2,3072]{2,1,0:T(2,128)(2,1)S(1)}, u32[]{:S(2)}, u32[]{:S(2)}) async-start(bf16[16,2,3072]{2,1,0:T(2,128)(2,1)} %reshape.482), calls=%async_computation.1 | async-start | bytes 393216 | tf_op jit(solution)/shard_map/all_to_all | solution.py:68
  71.5 5.3 %fusion = f32[6,128,512]{2,1,0:T(8,128)} fusion(bf16[512,6,128]{0,2,1:T(8,128)(2,1)S(1)} %bitcast.62, f32[6]{0:T(128)} %get-tuple-element.19, pred[512,512]{1,0:T(8,128)(4,1)} %iota_compare_fusion, f32[512,6,128]{0,2,1:T(8,128)} %bitcast.59, f32[512,6]{0,1:T(8,128)} %add_rsqrt_fusion.1, f32[512,6,128]{0,2,1:T(8,128)} %bitcast.57, f32[512,6]{0,1:T(8,128)S(1)} %add_rsqrt_fusion), kind=kOutput, calls=%fused_computation.5 | convolution fusion | flops 811597824 | bytes 5791768 | tf_op jit(solution)/shard_map/hts,she->the/dot_general | solution.py:77
  76.9 2.7 %all-to-all-done.1 = bf16[16,2,3072]{2,1,0:T(2,128)(2,1)S(1)} async-done(((bf16[16,2,3072]{2,1,0:T(2,128)(2,1)}), bf16[16,2,3072]{2,1,0:T(2,128)(2,1)S(1)}, u32[]{:S(2)}, u32[]{:S(2)}) %all-to-all-start.1) | async-done | bytes 196640 | tf_op jit(solution)/shard_map/all_to_all | solution.py:68
  79.8 1.1 %reduce.10 = bf16[16,6144]{1,0:T(8,128)(2,1)S(1)} reduce(bf16[16,1,6144]{2,1,0:T(2,128)(2,1)S(1)} %reshape.483, bf16[]{:T(256)} %constant.73), dimensions={1}, to_apply=%all_to_all.5.reduce_sub_computation | reduce | bytes 393218 | tf_op jit(solution)/shard_map/all_to_all | solution.py:68
  81.0 2.3 %add_convert_fusion = bf16[6,128,512]{2,1,0:T(8,128)(2,1)S(1)} fusion(f32[6,128,512]{2,1,0:T(8,128)} %fusion, bf16[6,128,128]{2,1,0:T(8,128)(2,1)S(1)} %reshape.433, f32[512,6,128]{0,2,1:T(8,128)} %bitcast.60, f32[512,6]{0,1:T(8,128)S(1)} %copy-done.16), kind=kOutput, calls=%fused_computation.11 | convolution fusion | flops 102236160 | bytes 4141056 | tf_op jit(solution)/shard_map/thd,hde->the/dot_general | solution.py:78
  83.3 2.6 %convolution_convert_fusion = bf16[512,1536]{1,0:T(8,128)(2,1)} fusion(bf16[512,768]{0,1:T(8,128)(2,1)S(1)} %bitcast.63, bf16[768,1536]{1,0:T(8,128)(2,1)S(1)} %copy-done), kind=kOutput, calls=%fused_computation.10 | convolution fusion | flops 1208745984 | bytes 4718592 | tf_op jit(solution)/shard_map/dot_general | solution.py:80
  (50 shorter events, 1.1 us)
Async XLA Ops:
  0.0 83.3 %copy-start = (bf16[768,1536]{1,0:T(8,128)(2,1)S(1)}, bf16[768,1536]{1,0:T(8,128)(2,1)}, u32[]{:S(2)}) copy-start(bf16[768,1536]{1,0:T(8,128)(2,1)} %param.10) | copy-start | bytes 7077892
  6.0 4.1 %copy-start.3 = (bf16[512,768]{0,1:T(8,128)(2,1)}, bf16[512,768]{0,1:T(8,128)(2,1)S(1)}, u32[]{:S(2)}) copy-start(bf16[512,768]{0,1:T(8,128)(2,1)S(1)} %copy.28) | copy-start | bytes 2359300
  9.8 1.2 %copy-start.1 = (f32[512,768]{0,1:T(8,128)}, f32[512,768]{0,1:T(8,128)S(1)}, u32[]{:S(2)}) copy-start(f32[512,768]{0,1:T(8,128)S(1)} %fusion.16) | copy-start | bytes 4718596
  11.4 11.1 %copy-start.5 = (f32[9,6]{0,1:T(8,128)S(1)}, f32[9,6]{0,1:T(8,128)}, u32[]{:S(2)}) copy-start(f32[9,6]{0,1:T(8,128)} %param.11) | copy-start | bytes 652
  14.7 17.7 %all-to-all-start = ((bf16[16,2,3072]{2,1,0:T(2,128)(2,1)}), bf16[16,2,3072]{2,1,0:T(2,128)(2,1)S(1)}, u32[]{:S(2)}, u32[]{:S(2)}) async-start(bf16[16,2,3072]{2,1,0:T(2,128)(2,1)} %reshape.480), calls=%async_computation | async-start | bytes 393216 | tf_op jit(solution)/shard_map/all_to_all | solution.py:42
  26.9 1.1 %copy-start.2 = (f32[512,768]{0,1:T(8,128)}, f32[512,768]{0,1:T(8,128)S(1)}, u32[]{:S(2)}) copy-start(f32[512,768]{0,1:T(8,128)S(1)} %fusion.15) | copy-start | bytes 4718596
  32.7 1.3 %collective-permute-start = (f32[6144]{0:T(1024)S(1)}, f32[6144]{0:T(1024)S(1)}, u32[]{:S(2)}, u32[]{:S(2)}) collective-permute-start(f32[6144]{0:T(1024)S(1)} %get-tuple-element.22), channel_id=1, source_target_pairs={{0,16},{16,0},{32,48},{48,32},{64,80},{80,64},{96,112},{112,96},{1... | collective-permute-start | bytes 73736 | tf_op jit(solution)/shard_map/ppermute | solution.py:10
  34.0 0.6 copy-start.10
  34.6 3.8 %collective-permute-start.1 = (f32[6144]{0:T(1024)S(1)}, f32[6144]{0:T(1024)S(1)}, u32[]{:S(2)}, u32[]{:S(2)}) collective-permute-start(f32[6144]{0:T(1024)S(1)} %add.141), channel_id=1, source_target_pairs={{0,32},{16,48},{32,0},{48,16},{64,96},{80,112},{96,64},{112,80},{1... | collective-permute-start | bytes 73736 | tf_op jit(solution)/shard_map/ppermute | solution.py:10
  38.4 3.4 %copy-start.12 = (f32[6144]{0:T(1024)}, f32[6144]{0:T(1024)S(1)}, u32[]{:S(2)}) copy-start(f32[6144]{0:T(1024)S(1)} %collective-permute-done.1) | copy-start | bytes 73732
  38.4 5.2 %collective-permute-start.2 = (f32[6144]{0:T(1024)S(1)}, f32[6144]{0:T(1024)S(1)}, u32[]{:S(2)}, u32[]{:S(2)}) collective-permute-start(f32[6144]{0:T(1024)S(1)} %add.143), channel_id=1, source_target_pairs={{0,64},{16,80},{32,96},{48,112},{64,0},{80,16},{96,32},{112,48},{1... | collective-permute-start | bytes 73736 | tf_op jit(solution)/shard_map/ppermute | solution.py:10
  43.6 6.6 %copy-start.14 = (f32[6144]{0:T(1024)}, f32[6144]{0:T(1024)S(1)}, u32[]{:S(2)}) copy-start(f32[6144]{0:T(1024)S(1)} %collective-permute-done.2) | copy-start | bytes 73732
  44.2 14.5 %collective-permute-start.3 = (f32[6144]{0:T(1024)}, f32[6144]{0:T(1024)}, u32[]{:S(2)}, u32[]{:S(2)}) collective-permute-start(f32[6144]{0:T(1024)} %add.145), channel_id=1, source_target_pairs={{0,128},{16,144},{32,160},{48,176},{64,192},{80,208},{96,224},{112... | collective-permute-start | bytes 73736 | tf_op jit(solution)/shard_map/ppermute | solution.py:10
  57.0 1.7 %copy-start.6 = (f32[6144]{0:T(1024)S(1)}, f32[6144]{0:T(1024)}, u32[]{:S(2)}) copy-start(f32[6144]{0:T(1024)} %get-tuple-element.6) | copy-start | bytes 73732
  57.0 1.7 %copy-start.7 = (f32[6144]{0:T(1024)S(1)}, f32[6144]{0:T(1024)}, u32[]{:S(2)}) copy-start(f32[6144]{0:T(1024)} %get-tuple-element.7) | copy-start | bytes 73732
  57.0 1.7 %copy-start.8 = (f32[6144]{0:T(1024)S(1)}, f32[6144]{0:T(1024)}, u32[]{:S(2)}) copy-start(f32[6144]{0:T(1024)} %get-tuple-element.8) | copy-start | bytes 73732
  57.0 1.7 %copy-start.9 = (f32[6144]{0:T(1024)S(1)}, f32[6144]{0:T(1024)}, u32[]{:S(2)}) copy-start(f32[6144]{0:T(1024)} %get-tuple-element.9) | copy-start | bytes 73732
  57.0 1.7 %copy-start.11 = (f32[6144]{0:T(1024)S(1)}, f32[6144]{0:T(1024)}, u32[]{:S(2)}) copy-start(f32[6144]{0:T(1024)} %copy-done.10) | copy-start | bytes 73732
  57.0 1.7 %copy-start.13 = (f32[6144]{0:T(1024)S(1)}, f32[6144]{0:T(1024)}, u32[]{:S(2)}) copy-start(f32[6144]{0:T(1024)} %copy-done.12) | copy-start | bytes 73732
  57.0 1.7 %copy-start.15 = (f32[6144]{0:T(1024)S(1)}, f32[6144]{0:T(1024)}, u32[]{:S(2)}) copy-start(f32[6144]{0:T(1024)} %copy-done.14) | copy-start | bytes 73732
  59.5 12.0 %copy-start.4 = (bf16[512,768]{0,1:T(8,128)(2,1)S(1)}, bf16[512,768]{0,1:T(8,128)(2,1)}, u32[]{:S(2)}) copy-start(bf16[512,768]{0,1:T(8,128)(2,1)} %copy-done.3) | copy-start | bytes 2359300
  64.3 15.3 %all-to-all-start.1 = ((bf16[16,2,3072]{2,1,0:T(2,128)(2,1)}), bf16[16,2,3072]{2,1,0:T(2,128)(2,1)S(1)}, u32[]{:S(2)}, u32[]{:S(2)}) async-start(bf16[16,2,3072]{2,1,0:T(2,128)(2,1)} %reshape.482), calls=%async_computation.1 | async-start | bytes 393216 | tf_op jit(solution)/shard_map/all_to_all | solution.py:68
  76.9 4.1 %copy-start.16 = (f32[512,6]{0,1:T(8,128)S(1)}, f32[512,6]{0,1:T(8,128)}, u32[]{:S(2)}) copy-start(f32[512,6]{0,1:T(8,128)} %add_rsqrt_fusion.1) | copy-start | bytes 36868
where the time goes:
time: 86.5 us; the launch traced here: 85.9 us
  starting transfers between devices  23.7 us (27%)
  matrix products  22.6 us (26%)
  other arithmetic  17.5 us (20%)
  local copies, waits for them, and re-layouts  13.4 us (15%)
  waiting for transfers between devices  8.3 us (10%)
    dot_general x3, matrix products, project(): jnp.dot(tokens, weight, preferred_element_type=jnp.float32)  12 us
    ppermute x4, starting transfers between devices, partner_2(): return lax.ppermute(value, axis, pairs)  9.48 us
    all_to_all x1, starting transfers between devices, per_device(): lax.all_to_all(outgoing, 'grp', split_axis=0, concat_axis=1, tiled=True)  7.22 us
    all_to_all x1, starting transfers between devices, per_device(): lax.all_to_all(pieces.astype(jnp.bfloat16), 'grp', split_axis=1, concat_a...  7.03 us
    ppermute x4, waiting for transfers between devices, partner_2(): return lax.ppermute(value, axis, pairs)  5.58 us
    gather x4, local copies, waits for them, and re-layouts, per_device(): grouped[sibling]  5.5 us
    dot_general x1, matrix products, per_device(): jnp.einsum('hts,she->the', weights, values, preferred_element_type=jnp.fl...  5.35 us
    unnamed x39, local copies, waits for them, and re-layouts  5.19 us
  transfers between devices with their start and end apart: 6, of which 4 were waited for; matrix products, arithmetic and copies ran while one was open for 28% of the time, Pallas kernels for 0%

commit v1 on v0

v1 whole, which is shorter than its diff:
```python
import functools

import jax
import jax.numpy as jnp
from jax import lax
from jax.experimental import pallas as pl
from jax.experimental.pallas import tpu as pltpu
from jax.sharding import PartitionSpec as P

BF16 = jnp.bfloat16
F32 = jnp.float32
VMEM = pl.BlockSpec(memory_space=pltpu.VMEM)
SMEM = pl.BlockSpec(memory_space=pltpu.SMEM)
ANY = pl.BlockSpec(memory_space=pl.ANY)
HBM = pl.BlockSpec(memory_space=pltpu.HBM)
QUARTERS = 4


def unit(matrix):
    return (matrix * lax.rsqrt(jnp.sum(matrix * matrix, -1, keepdims=True) + 1e-06)).astype(BF16)


def unit_pair(matrix, width):
    return jnp.concatenate([unit(matrix[:, :width]), unit(matrix[:, width:])], 1)


def dot(a, b):
    return jnp.dot(a, b, preferred_element_type=F32)


def state_kernel(
    width,
    tok_hbm,
    wk_hbm,
    wv_hbm,
    wq_hbm,
    k_ref,
    v_ref,
    tok,
    wq,
    own,
    one,
    two,
    three,
    wk,
    wv,
    slices,
    sems,
):
    depth = tok.shape[1]
    pair = 2 * width
    pairs = wk.shape[0]
    half = depth // 2
    part = width // QUARTERS
    parts = [
        pltpu.make_async_copy(
            tok_hbm.at[:, pl.ds(i * half, half)], tok.at[:, pl.ds(i * half, half)], sems.at[i]
        )
        for i in range(2)
    ]
    weights = []
    for j in range(pairs):
        for source, target in ((wk_hbm, wk), (wv_hbm, wv)):
            weights.append(
                pltpu.make_async_copy(
                    source.at[:, pl.ds(j * pair, pair)], target.at[j], sems.at[2 + len(weights)]
                )
            )
    last = pltpu.make_async_copy(wq_hbm, wq, sems.at[2 + 2 * pairs])
    parts[0].start()
    weights[0].start()
    parts[1].start()
    for copy in weights[1:]:
        copy.start()
    last.start()
    parts[0].wait()
    weights[0].wait()
    for j in range(pairs):
        if j == 0:
            k32 = dot(tok[:, :half], wk[j, :half])
            parts[1].wait()
            k32 = k32 + dot(tok[:, half:], wk[j, half:])
        else:
            weights[2 * j].wait()
            k32 = dot(tok[...], wk[j])
        keys = unit_pair(k32, width)
        k_ref[:, j * pair : (j + 1) * pair] = keys
        weights[2 * j + 1].wait()
        values = dot(tok[...], wv[j]).astype(BF16)
        v_ref[:, j * pair : (j + 1) * pair] = values
        both = lax.dot_general(keys, values, (((0,), (0,)), ((), ())), preferred_element_type=F32)
        for side in range(2):
            head = 2 * j + side
            state = both[side * width : (side + 1) * width, side * width : (side + 1) * width]
            for q in range(QUARTERS):
                slices[q, head * part : (head + 1) * part, :] = state[
                    q * part : (q + 1) * part
                ].astype(BF16)
    y = lax.axis_index("grp") % QUARTERS
    for distance, target in enumerate((own, one, two, three)):
        target[...] = slices[y ^ distance]
    last.wait()


def states_of(tokens, w_key, w_value, w_query, heads, width):
    rows, depth = tokens.shape
    inner = heads * width
    pairs = heads // 2
    piece = jax.ShapeDtypeStruct((inner // QUARTERS, width), BF16)
    side = jax.ShapeDtypeStruct((rows, inner), BF16)
    whole = [jax.ShapeDtypeStruct(a.shape, a.dtype) for a in (tokens, w_query)]
    return pl.pallas_call(
        functools.partial(state_kernel, width),
        out_shape=(side, side, *whole, piece, piece, piece, piece),
        in_specs=[HBM] * 4,
        out_specs=[VMEM] * 8,
        scratch_shapes=[
            pltpu.VMEM((pairs, depth, 2 * width), BF16),
            pltpu.VMEM((pairs, depth, 2 * width), BF16),
            pltpu.VMEM((QUARTERS, inner // QUARTERS, width), BF16),
            pltpu.SemaphoreType.DMA((3 + 2 * pairs,)),
        ],
        compiler_params=pltpu.CompilerParams(vmem_limit_bytes=20 << 20),
        name="states",
    )(*(pltpu.with_memory_space_constraint(a, pltpu.HBM) for a in (tokens, w_key, w_value, w_query)))


def query_kernel(width, tok, wq, q_ref):
    pair = 2 * width
    for j in range(wq.shape[1] // pair):
        columns = slice(j * pair, (j + 1) * pair)
        q_ref[:, columns] = unit_pair(dot(tok[...], wq[:, columns]), width)


def query_of(tok, wq, width):
    return pl.pallas_call(
        functools.partial(query_kernel, width),
        out_shape=jax.ShapeDtypeStruct((tok.shape[0], wq.shape[1]), BF16),
        in_specs=[VMEM, VMEM],
        out_specs=VMEM,
        compiler_params=pltpu.CompilerParams(vmem_limit_bytes=12 << 20),
        name="query",
    )(tok, wq)


def inside_kernel(width, first, q_ref, k_ref, v_ref, levels, after, inside_ref):
    rows, columns_here = inside_ref.shape
    block = rows // 2
    low = lax.broadcasted_iota(jnp.int32, (block, block), 0) >= lax.broadcasted_iota(
        jnp.int32, (block, block), 1
    )
    for local in range(columns_here // width):
        head = first + local
        columns = slice(head * width, (head + 1) * width)
        scale = levels[0, head]
        for i in range(2):
            here = slice(i * block, (i + 1) * block)
            q = q_ref[here, columns]

            def weigh(keys, masked):
                scores = lax.dot_general(
                    q, keys, (((1,), (1,)), ((), ())), preferred_element_type=F32
                )
                if masked:
                    scores = jnp.where(low, scores, 0.0)
                return (scores * scale).astype(BF16)

            out = dot(weigh(k_ref[here, columns], True), v_ref[here, columns])
            if i:
                out = out + dot(weigh(k_ref[:block, columns], False), v_ref[:block, columns])
            inside_ref[here, local * width : (local + 1) * width] = out


def inside_of(query, keys, values, level_weights, after, first, count, width):
    return pl.pallas_call(
        functools.partial(inside_kernel, width, first),
        out_shape=jax.ShapeDtypeStruct((query.shape[0], count * width), F32),
        in_specs=[VMEM, VMEM, VMEM, SMEM, ANY],
        out_specs=VMEM,
        compiler_params=pltpu.CompilerParams(vmem_limit_bytes=12 << 20),
        name="inside",
    )(query, keys, values, level_weights, after)


def gather_kernel(levels, *refs):
    near = refs[:4]
    x1, x2, x3, other, z1, z2, z3, local_ref, last_ref = refs[4:]
    member = lax.axis_index("grp")
    group = lax.axis_index("seq")
    y, x, core, z = member % 4, member // 4, group % 2, group // 2
    heads = levels.shape[1]
    part = last_ref.shape[0] // heads

    def bit(index, level):
        return ((index >> level) & 1).astype(F32)

    for head in range(heads):
        rows = slice(head * part, (head + 1) * part)

        def factor(level, present):
            return levels[level + 1, head] * (present * 2.0 ** (-0.5 * level))

        def read(ref):
            return ref[rows, :].astype(F32)

        far = (
            factor(2, bit(x, 0)) * read(x1)
            + factor(3, bit(x, 1)) * (read(x2) + read(x3))
            + factor(4, bit(core, 0)) * read(other)
            + factor(5, bit(z, 0)) * read(z1)
            + factor(6, bit(z, 1)) * (read(z2) + read(z3))
        )
        sides = [read(ref) for ref in near]
        for distance in range(4):
            target = y ^ distance
            local_ref[distance, rows, :] = (
                far
                + factor(0, bit(target, 0)) * sides[distance ^ 1]
                + factor(1, bit(target, 1)) * (sides[distance ^ 2] + sides[distance ^ 3])
            )
        last_ref[rows, :] = jnp.full(
            (part, last_ref.shape[1]), factor(7, bit(z, 2)), F32
        )


def gather_of(level_weights, near, others):
    shape = near[0].shape
    return pl.pallas_call(
        gather_kernel,
        out_shape=(
            jax.ShapeDtypeStruct((4, *shape), F32),
            jax.ShapeDtypeStruct(shape, F32),
        ),
        in_specs=[SMEM] + [VMEM] * 11,
        out_specs=[VMEM, VMEM],
        compiler_params=pltpu.CompilerParams(vmem_limit_bytes=4 << 20),
        name="gather",
    )(level_weights, *near, *others)


def mix_kernel(
    width, q_ref, low_ref, high_ref, own, one, two, three, wo, out_hbm, slices, attended, out, sems
):
    rows, inner = q_ref.shape
    part = width // QUARTERS
    pair = 2 * width
    y = lax.axis_index("grp") % QUARTERS
    for distance, source in enumerate((own, one, two, three)):
        slices[y ^ distance] = source[...]
    half = inner // 2
    zero = jnp.zeros((width, width), BF16)
    for j in range(inner // pair):
        halves = []
        insides = []
        for side in range(2):
            head = 2 * j + side
            state = jnp.concatenate(
                [slices[q, head * part : (head + 1) * part, :] for q in range(QUARTERS)], 0
            )
            halves.append(jnp.concatenate([zero, state] if side else [state, zero], 1))
            start = head * width
            insides.append(
                low_ref[:, start : start + width]
                if start < half
                else high_ref[:, start - half : start - half + width]
            )
        columns = slice(j * pair, (j + 1) * pair)
        earlier = dot(q_ref[:, columns], jnp.concatenate(halves, 0))
        attended[:, columns] = (jnp.concatenate(insides, 1) + earlier).astype(BF16)
    steps = sems.shape[0]
    block = out.shape[1] // steps
    copies = []
    for i in range(steps):
        columns = pl.ds(i * block, block)
        out[:, columns] = dot(attended[...], wo[:, columns]).astype(BF16)
        copy = pltpu.make_async_copy(out.at[:, columns], out_hbm.at[:, columns], sems.at[i])
        copy.start()
        copies.append(copy)
    for copy in copies:
        copy.wait()


def mixed_of(query, insides, pieces, w_output, width):
    rows, inner = query.shape
    wide = w_output.shape[1]
    return pl.pallas_call(
        functools.partial(mix_kernel, width),
        out_shape=jax.ShapeDtypeStruct((rows, wide), BF16),
        in_specs=[VMEM] * 8,
        out_specs=HBM,
        scratch_shapes=[
            pltpu.VMEM((QUARTERS, inner // QUARTERS, width), BF16),
            pltpu.VMEM((rows, inner), BF16),
            pltpu.VMEM((rows, wide), BF16),
            pltpu.SemaphoreType.DMA((6,)),
        ],
        compiler_params=pltpu.CompilerParams(vmem_limit_bytes=16 << 20),
        name="mix",
    )(query, *insides, *pieces, w_output)


def flip(value, axis, mask):
    pairs = [(source, source ^ mask) for source in range(lax.axis_size(axis))]
    return lax.ppermute(value, axis, pairs)


def flips(value, axis, masks):
    return [flip(value, axis, mask) for mask in masks]


def plus(total, others):
    for other in others:
        total = total + other.astype(F32)
    return total


def per_device(tokens, w_query, w_key, w_value, w_output, level_weights):
    heads = level_weights.shape[1]
    width = w_query.shape[1] // heads
    keys, values, tok, wq, *sent = states_of(tokens, w_key, w_value, w_query, heads, width)
    near = [sent[0]] + [None] * 3
    for distance in (3, 1, 2):
        near[distance] = flip(sent[distance], "grp", distance)
    query = query_of(tok, wq, width)
    *near, query = lax.optimization_barrier((*near, query))
    total = plus(near[0].astype(F32), near[1:])

    going = total.astype(BF16)
    x3, x1, x2 = flips(going, "grp", (12, 4, 8))
    low = inside_of(query, keys, values, level_weights, going, 0, heads // 2, width)
    x3, x1, x2, low = lax.optimization_barrier((x3, x1, x2, low))
    total = plus(total, (x1, x2, x3))
    (other,) = flips(total.astype(BF16), "seq", (1,))
    total = plus(total, (other,))
    going = total.astype(BF16)
    z1, z2, z3 = flips(going, "seq", (2, 4, 6))
    high = inside_of(query, keys, values, level_weights, going, heads // 2, heads // 2, width)
    z1, z2, z3, high = lax.optimization_barrier((z1, z2, z3, high))
    total = plus(total, (z1, z2, z3))
    (past,) = flips(total.astype(BF16), "seq", (12,))
    gathered, factor = gather_of(level_weights, near, (x1, x2, x3, other, z1, z2, z3))
    past, gathered, factor = lax.optimization_barrier((past, gathered, factor))
    back = [
        (gathered[distance] + factor * past.astype(F32)).astype(BF16) for distance in range(4)
    ]
    pieces = [back[0]] + [None] * 3
    for distance in (3, 1, 2):
        pieces[distance] = flip(back[distance], "grp", distance)
    return mixed_of(query, (low, high), pieces, w_output, width)


def solution(mesh):
    placed = (P(("seq", "grp"), None), P(), P(), P(), P(), P())
    return jax.shard_map(
        per_device, mesh=mesh, in_specs=placed, out_specs=P(("seq", "grp"), None), check_vma=False
    )
```

time: 86.5 us -> 55.9 us (0.65)
  the two profiles are of different devices: /device:TPU:32 before, /device:TPU:26 now
where the time goes in v1:
time: 55.9 us; the launch traced here: 55.8 us
  starting transfers between devices  22.8 us (41%)
  Pallas kernels  17.1 us (31%)
  waiting for transfers between devices  15.3 us (27%)
    ppermute x14, starting transfers between devices, flip(): return lax.ppermute(value, axis, pairs)  22.8 us
    ppermute x14, waiting for transfers between devices, flip(): return lax.ppermute(value, axis, pairs)  15.3 us
    pallas_call x1, Pallas kernels, states_of(): pl.pallas_call(functools.partial(state_kernel, width), out_shape=(side, s...  8.23 us
    pallas_call x2, Pallas kernels, inside_of(): pl.pallas_call(functools.partial(inside_kernel, width, first), out_shape=...  3.9 us
    pallas_call x1, Pallas kernels, mixed_of(): pl.pallas_call(functools.partial(mix_kernel, width), out_shape=jax.ShapeD...  2.51 us
    pallas_call x1, Pallas kernels, query_of(): pl.pallas_call(functools.partial(query_kernel, width), out_shape=jax.Shap...  1.6 us
  transfers between devices with their start and end apart: 14, of which 8 were waited for; matrix products, arithmetic and copies ran while one was open for 0% of the time, Pallas kernels for 11%

profile of v1, /device:TPU:26, one launch (start us, length us, event | category | flops | bytes accessed | tf_op | source)
XLA Modules:
  0.0 55.8 jit_solution(3392238662013195339)
XLA Ops:
  0.0 8.2 %states.1 = (bf16[512,768]{1,0:T(8,128)(2,1)S(1)}, bf16[512,768]{1,0:T(8,128)(2,1)S(1)}, bf16[512,1536]{1,0:T(8,128)(2,1)S(1)}, bf16[1536,768]{1,0:T(8,128)(2,1)...) custom-call(bf16[512,1536]{1,0:T(8,128)(2,1)} %tok_hbm.1, ...), custom_call_target="tpu_custom_call" | custom-call | tf_op jit(solution)/shard_map/states/pallas_call | solution.py:112
  8.2 0.8 %collective-permute-start = (bf16[192,128]{1,0:T(8,128)(2,1)S(1)}, bf16[192,128]{1,0:T(8,128)(2,1)S(1)}, u32[]{:S(2)}, u32[]{:S(2)}) collective-permute-start(bf16[192,128]{1,0:T(8,128)(2,1)S(1)} %get-tuple-element.32), channel_id=1, source_target_pairs={{0,1},{1,0},{2,3},{3,2},{4,5},{5,4},{6,7},{7,6},{8,9},{9,8},{10,11... | collective-permute-start | bytes 147464 | tf_op jit(solution)/shard_map/ppermute | solution.py:304
  9.1 0.9 %collective-permute-start.1 = (bf16[192,128]{1,0:T(8,128)(2,1)S(1)}, bf16[192,128]{1,0:T(8,128)(2,1)S(1)}, u32[]{:S(2)}, u32[]{:S(2)}) collective-permute-start(bf16[192,128]{1,0:T(8,128)(2,1)S(1)} %get-tuple-element.33), channel_id=1, source_target_pairs={{0,2},{1,3},{2,0},{3,1},{4,6},{5,7},{6,4},{7,5},{8,10},{9,11},{10,... | collective-permute-start | bytes 147464 | tf_op jit(solution)/shard_map/ppermute | solution.py:304
  10.0 3.0 %collective-permute-start.2 = (bf16[192,128]{1,0:T(8,128)(2,1)S(1)}, bf16[192,128]{1,0:T(8,128)(2,1)S(1)}, u32[]{:S(2)}, u32[]{:S(2)}) collective-permute-start(bf16[192,128]{1,0:T(8,128)(2,1)S(1)} %get-tuple-element.34), channel_id=1, source_target_pairs={{0,3},{1,2},{2,1},{3,0},{4,7},{5,6},{6,5},{7,4},{8,11},{9,10},{10,... | collective-permute-start | bytes 147464 | tf_op jit(solution)/shard_map/ppermute | solution.py:304
  13.0 0.0 copy-start.1
  13.0 1.6 %query.1.q_ref = bf16[512,768]{1,0:T(8,128)(2,1)S(1)} custom-call(bf16[512,1536]{1,0:T(8,128)(2,1)S(1)} %get-tuple-element.35.tok, bf16[1536,768]{1,0:T(8,128)(2,1)S(1)} %get-tuple-element.36.wq), custom_call_target="tpu_custom_call" | custom-call | tf_op jit(solution)/shard_map/query/pallas_call | solution.py:136
  14.6 0.0 collective-permute-done.refs_1_
  14.6 0.0 collective-permute-done.1.refs_2_
  14.7 0.6 %collective-permute-done.2.refs_3_ = bf16[192,128]{1,0:T(8,128)(2,1)S(1)} collective-permute-done((bf16[192,128]{1,0:T(8,128)(2,1)S(1)}, bf16[192,128]{1,0:T(8,128)(2,1)S(1)}, u32[]{:S(2)}, u32[]{:S(2)}) %collective-permute-start.2) | collective-permute-done | bytes 49184 | tf_op jit(solution)/shard_map/ppermute | solution.py:304
  15.3 1.6 %collective-permute-start.3 = (bf16[192,128]{1,0:T(8,128)(2,1)S(1)}, bf16[192,128]{1,0:T(8,128)(2,1)S(1)}, u32[]{:S(2)}, u32[]{:S(2)}) collective-permute-start(bf16[192,128]{1,0:T(8,128)(2,1)S(1)} %fusion.5.after), channel_id=1, source_target_pairs={{0,12},{1,13},{2,14},{3,15},{4,8},{5,9},{6,10},{7,11},{8,4},{9,5},... | collective-permute-start | bytes 147464 | tf_op jit(solution)/shard_map/ppermute | solution.py:304
  16.9 1.8 %collective-permute-start.4 = (bf16[192,128]{1,0:T(8,128)(2,1)S(1)}, bf16[192,128]{1,0:T(8,128)(2,1)S(1)}, u32[]{:S(2)}, u32[]{:S(2)}) collective-permute-start(bf16[192,128]{1,0:T(8,128)(2,1)S(1)} %fusion.5.after), channel_id=1, source_target_pairs={{0,4},{1,5},{2,6},{3,7},{4,0},{5,1},{6,2},{7,3},{8,12},{9,13},{10,... | collective-permute-start | bytes 147464 | tf_op jit(solution)/shard_map/ppermute | solution.py:304
  18.7 1.0 %collective-permute-start.5 = (bf16[192,128]{1,0:T(8,128)(2,1)S(1)}, bf16[192,128]{1,0:T(8,128)(2,1)S(1)}, u32[]{:S(2)}, u32[]{:S(2)}) collective-permute-start(bf16[192,128]{1,0:T(8,128)(2,1)S(1)} %fusion.5.after), channel_id=1, source_target_pairs={{0,8},{1,9},{2,10},{3,11},{4,12},{5,13},{6,14},{7,15},{8,0},{9,1},... | collective-permute-start | bytes 147464 | tf_op jit(solution)/shard_map/ppermute | solution.py:304
  19.8 0.0 copy-done.1
  19.8 0.1 copy.7.levels
  19.9 1.9 %inside.2.low_ref = f32[512,384]{1,0:T(8,128)S(1)} custom-call(bf16[512,768]{1,0:T(8,128)(2,1)S(1)} %query.1.q_ref, bf16[512,768]{1,0:T(8,128)(2,1)S(1)} %get-tuple-element.42.k_ref, bf16[512,768]{1,0:T(8,128)(2,1)S(1)} %get-tuple-element.43.v_ref, f32[9,6]{1,0:T(8,128)S(1)} %copy.7.levels, bf16[192,128]{1,0:T(8,128)(2,1)S(1)} %fusion.5.after), custom_call_target="tpu_custom_call" | custom-call | tf_op jit(solution)/shard_map/inside/pallas_call | solution.py:175
  21.8 0.0 collective-permute-done.3.refs_6_
  21.8 0.0 collective-permute-done.4.refs_4_
  21.8 2.5 %collective-permute-done.5.refs_5_ = bf16[192,128]{1,0:T(8,128)(2,1)S(1)} collective-permute-done((bf16[192,128]{1,0:T(8,128)(2,1)S(1)}, bf16[192,128]{1,0:T(8,128)(2,1)S(1)}, u32[]{:S(2)}, u32[]{:S(2)}) %collective-permute-start.5) | collective-permute-done | bytes 49184 | tf_op jit(solution)/shard_map/ppermute | solution.py:304
  24.3 0.1 fusion.6
  24.4 0.1 collective-permute-start.6
  24.5 1.2 %collective-permute-done.6.refs_7_ = bf16[192,128]{1,0:T(8,128)(2,1)S(1)} collective-permute-done((bf16[192,128]{1,0:T(8,128)(2,1)S(1)}, bf16[192,128]{1,0:T(8,128)(2,1)S(1)}, u32[]{:S(2)}, u32[]{:S(2)}) %collective-permute-start.6) | collective-permute-done | bytes 49184 | tf_op jit(solution)/shard_map/ppermute | solution.py:304
  25.7 0.0 copy-start
  25.7 2.0 %collective-permute-start.7 = (bf16[192,128]{1,0:T(8,128)(2,1)S(1)}, bf16[192,128]{1,0:T(8,128)(2,1)S(1)}, u32[]{:S(2)}, u32[]{:S(2)}) collective-permute-start(bf16[192,128]{1,0:T(8,128)(2,1)S(1)} %fusion.4.after), channel_id=1, source_target_pairs={{0,32},{16,48},{32,0},{48,16},{64,96},{80,112},{96,64},{112,80},{1... | collective-permute-start | bytes 147464 | tf_op jit(solution)/shard_map/ppermute | solution.py:304
  27.7 3.3 %collective-permute-start.8 = (bf16[192,128]{1,0:T(8,128)(2,1)S(1)}, bf16[192,128]{1,0:T(8,128)(2,1)S(1)}, u32[]{:S(2)}, u32[]{:S(2)}) collective-permute-start(bf16[192,128]{1,0:T(8,128)(2,1)S(1)} %fusion.4.after), channel_id=1, source_target_pairs={{0,64},{16,80},{32,96},{48,112},{64,0},{80,16},{96,32},{112,48},{1... | collective-permute-start | bytes 147464 | tf_op jit(solution)/shard_map/ppermute | solution.py:304
  31.0 0.0 collective-permute-start.9
  31.0 1.9 %inside.3.high_ref = f32[512,384]{1,0:T(8,128)S(1)} custom-call(bf16[512,768]{1,0:T(8,128)(2,1)S(1)} %query.1.q_ref, bf16[512,768]{1,0:T(8,128)(2,1)S(1)} %get-tuple-element.42.k_ref, bf16[512,768]{1,0:T(8,128)(2,1)S(1)} %get-tuple-element.43.v_ref, f32[9,6]{1,0:T(8,128)S(1)} %copy.7.levels, bf16[192,128]{1,0:T(8,128)(2,1)S(1)} %fusion.4.after), custom_call_target="tpu_custom_call" | custom-call | tf_op jit(solution)/shard_map/inside/pallas_call | solution.py:175
  33.0 0.0 collective-permute-done.7.refs_8_
  33.0 1.2 %collective-permute-done.8.refs_9_ = bf16[192,128]{1,0:T(8,128)(2,1)S(1)} collective-permute-done((bf16[192,128]{1,0:T(8,128)(2,1)S(1)}, bf16[192,128]{1,0:T(8,128)(2,1)S(1)}, u32[]{:S(2)}, u32[]{:S(2)}) %collective-permute-start.8) | collective-permute-done | bytes 49184 | tf_op jit(solution)/shard_map/ppermute | solution.py:304
  34.1 2.8 %collective-permute-done.9.refs_10_ = bf16[192,128]{1,0:T(8,128)(2,1)S(1)} collective-permute-done((bf16[192,128]{1,0:T(8,128)(2,1)S(1)}, bf16[192,128]{1,0:T(8,128)(2,1)S(1)}, u32[]{:S(2)}, u32[]{:S(2)}) %collective-permute-start.9) | collective-permute-done | bytes 49184 | tf_op jit(solution)/shard_map/ppermute | solution.py:304
  36.9 3.5 %collective-permute-start.10 = (bf16[192,128]{1,0:T(8,128)(2,1)S(1)}, bf16[192,128]{1,0:T(8,128)(2,1)S(1)}, u32[]{:S(2)}, u32[]{:S(2)}) collective-permute-start(bf16[192,128]{1,0:T(8,128)(2,1)S(1)} %add_convert_fusion), channel_id=1, source_target_pairs={{0,192},{16,208},{32,224},{48,240},{64,128},{80,144},{96,160},{112... | collective-permute-start | bytes 147464 | tf_op jit(solution)/shard_map/ppermute | solution.py:304
  40.4 0.8 %gather.1 = (f32[4,192,128]{2,1,0:T(8,128)S(1)}, f32[192,128]{1,0:T(8,128)S(1)}) custom-call(f32[9,6]{1,0:T(8,128)S(1)} %copy.7.levels, bf16[192,128]{1,0:T(8,128)(2,1)S(1)} %get-tuple-element.38.refs_0_, bf16[192,128]{1,0:T(8,128)(2,1)S(1)} %collective-permute-done.refs_1_, bf16[192,128]{1,0:T(8,128)(2,1)S(1)} %collective-permute-done.1.refs_2_, ...), custom_call_target="tpu_custom_call" | custom-call | tf_op jit(solution)/shard_map/gather/pallas_call | solution.py:228
  41.2 2.0 %collective-permute-done.10 = bf16[192,128]{1,0:T(8,128)(2,1)S(1)} collective-permute-done((bf16[192,128]{1,0:T(8,128)(2,1)S(1)}, bf16[192,128]{1,0:T(8,128)(2,1)S(1)}, u32[]{:S(2)}, u32[]{:S(2)}) %collective-permute-start.10) | collective-permute-done | bytes 49184 | tf_op jit(solution)/shard_map/ppermute | solution.py:304
  43.2 0.7 %collective-permute-start.11 = (bf16[192,128]{1,0:T(8,128)(2,1)S(1)}, bf16[192,128]{1,0:T(8,128)(2,1)S(1)}, u32[]{:S(2)}, u32[]{:S(2)}) collective-permute-start(bf16[192,128]{1,0:T(8,128)(2,1)S(1)} %get-tuple-element.61), channel_id=1, source_target_pairs={{0,1},{1,0},{2,3},{3,2},{4,5},{5,4},{6,7},{7,6},{8,9},{9,8},{10,11... | collective-permute-start | bytes 147464 | tf_op jit(solution)/shard_map/ppermute | solution.py:304
  44.0 3.8 %collective-permute-start.12 = (bf16[192,128]{1,0:T(8,128)(2,1)S(1)}, bf16[192,128]{1,0:T(8,128)(2,1)S(1)}, u32[]{:S(2)}, u32[]{:S(2)}) collective-permute-start(bf16[192,128]{1,0:T(8,128)(2,1)S(1)} %get-tuple-element.60), channel_id=1, source_target_pairs={{0,2},{1,3},{2,0},{3,1},{4,6},{5,7},{6,4},{7,5},{8,10},{9,11},{10,... | collective-permute-start | bytes 147464 | tf_op jit(solution)/shard_map/ppermute | solution.py:304
  47.8 0.2 collective-permute-start.13
  48.0 0.0 collective-permute-done.11.one
  48.0 2.4 %collective-permute-done.12.two = bf16[192,128]{1,0:T(8,128)(2,1)S(1)} collective-permute-done((bf16[192,128]{1,0:T(8,128)(2,1)S(1)}, bf16[192,128]{1,0:T(8,128)(2,1)S(1)}, u32[]{:S(2)}, u32[]{:S(2)}) %collective-permute-start.12) | collective-permute-done | bytes 49184 | tf_op jit(solution)/shard_map/ppermute | solution.py:304
  50.4 2.7 %collective-permute-done.13.three = bf16[192,128]{1,0:T(8,128)(2,1)S(1)} collective-permute-done((bf16[192,128]{1,0:T(8,128)(2,1)S(1)}, bf16[192,128]{1,0:T(8,128)(2,1)S(1)}, u32[]{:S(2)}, u32[]{:S(2)}) %collective-permute-start.13) | collective-permute-done | bytes 49184 | tf_op jit(solution)/shard_map/ppermute | solution.py:304
  53.1 0.0 copy-done
  53.1 2.5 %mix.1 = bf16[512,1536]{1,0:T(8,128)(2,1)} custom-call(bf16[512,768]{1,0:T(8,128)(2,1)S(1)} %query.1.q_ref, f32[512,384]{1,0:T(8,128)S(1)} %inside.2.low_ref, f32[512,384]{1,0:T(8,128)S(1)} %inside.3.high_ref, bf16[192,128]{1,0:T(8,128)(2,1)S(1)} %get-tuple-element.62.own, bf16[192,128]{1,0:T(8,128)(2,1)S(1)} %collective-permute-done.11.one, ...), custom_call_target="tpu_custom_call" | custom-call | tf_op jit(solution)/shard_map/mix/pallas_call | solution.py:286
  (4 shorter events, 0.1 us)
Async XLA Ops:
  8.2 6.4 %collective-permute-start = (bf16[192,128]{1,0:T(8,128)(2,1)S(1)}, bf16[192,128]{1,0:T(8,128)(2,1)S(1)}, u32[]{:S(2)}, u32[]{:S(2)}) collective-permute-start(bf16[192,128]{1,0:T(8,128)(2,1)S(1)} %get-tuple-element.32), channel_id=1, source_target_pairs={{0,1},{1,0},{2,3},{3,2},{4,5},{5,4},{6,7},{7,6},{8,9},{9,8},{10,11... | collective-permute-start | bytes 147464 | tf_op jit(solution)/shard_map/ppermute | solution.py:304
  9.1 5.6 %collective-permute-start.1 = (bf16[192,128]{1,0:T(8,128)(2,1)S(1)}, bf16[192,128]{1,0:T(8,128)(2,1)S(1)}, u32[]{:S(2)}, u32[]{:S(2)}) collective-permute-start(bf16[192,128]{1,0:T(8,128)(2,1)S(1)} %get-tuple-element.33), channel_id=1, source_target_pairs={{0,2},{1,3},{2,0},{3,1},{4,6},{5,7},{6,4},{7,5},{8,10},{9,11},{10,... | collective-permute-start | bytes 147464 | tf_op jit(solution)/shard_map/ppermute | solution.py:304
  10.0 5.3 %collective-permute-start.2 = (bf16[192,128]{1,0:T(8,128)(2,1)S(1)}, bf16[192,128]{1,0:T(8,128)(2,1)S(1)}, u32[]{:S(2)}, u32[]{:S(2)}) collective-permute-start(bf16[192,128]{1,0:T(8,128)(2,1)S(1)} %get-tuple-element.34), channel_id=1, source_target_pairs={{0,3},{1,2},{2,1},{3,0},{4,7},{5,6},{6,5},{7,4},{8,11},{9,10},{10,... | collective-permute-start | bytes 147464 | tf_op jit(solution)/shard_map/ppermute | solution.py:304
  13.0 6.7 %copy-start.1 = (f32[9,6]{0,1:T(8,128)S(1)}, f32[9,6]{0,1:T(8,128)}, u32[]{:S(2)}) copy-start(f32[9,6]{0,1:T(8,128)} %param.11) | copy-start | bytes 652
  15.3 6.5 %collective-permute-start.3 = (bf16[192,128]{1,0:T(8,128)(2,1)S(1)}, bf16[192,128]{1,0:T(8,128)(2,1)S(1)}, u32[]{:S(2)}, u32[]{:S(2)}) collective-permute-start(bf16[192,128]{1,0:T(8,128)(2,1)S(1)} %fusion.5.after), channel_id=1, source_target_pairs={{0,12},{1,13},{2,14},{3,15},{4,8},{5,9},{6,10},{7,11},{8,4},{9,5},... | collective-permute-start | bytes 147464 | tf_op jit(solution)/shard_map/ppermute | solution.py:304
  16.9 4.9 %collective-permute-start.4 = (bf16[192,128]{1,0:T(8,128)(2,1)S(1)}, bf16[192,128]{1,0:T(8,128)(2,1)S(1)}, u32[]{:S(2)}, u32[]{:S(2)}) collective-permute-start(bf16[192,128]{1,0:T(8,128)(2,1)S(1)} %fusion.5.after), channel_id=1, source_target_pairs={{0,4},{1,5},{2,6},{3,7},{4,0},{5,1},{6,2},{7,3},{8,12},{9,13},{10,... | collective-permute-start | bytes 147464 | tf_op jit(solution)/shard_map/ppermute | solution.py:304
  18.7 5.6 %collective-permute-start.5 = (bf16[192,128]{1,0:T(8,128)(2,1)S(1)}, bf16[192,128]{1,0:T(8,128)(2,1)S(1)}, u32[]{:S(2)}, u32[]{:S(2)}) collective-permute-start(bf16[192,128]{1,0:T(8,128)(2,1)S(1)} %fusion.5.after), channel_id=1, source_target_pairs={{0,8},{1,9},{2,10},{3,11},{4,12},{5,13},{6,14},{7,15},{8,0},{9,1},... | collective-permute-start | bytes 147464 | tf_op jit(solution)/shard_map/ppermute | solution.py:304
  24.4 1.3 %collective-permute-start.6 = (bf16[192,128]{1,0:T(8,128)(2,1)S(1)}, bf16[192,128]{1,0:T(8,128)(2,1)S(1)}, u32[]{:S(2)}, u32[]{:S(2)}) collective-permute-start(bf16[192,128]{1,0:T(8,128)(2,1)S(1)} %get-tuple-element.57), channel_id=1, source_target_pairs={{0,16},{16,0},{32,48},{48,32},{64,80},{80,64},{96,112},{112,96},{1... | collective-permute-start | bytes 147464 | tf_op jit(solution)/shard_map/ppermute | solution.py:304
  25.7 27.4 %copy-start = (bf16[768,1536]{1,0:T(8,128)(2,1)S(1)}, bf16[768,1536]{1,0:T(8,128)(2,1)}, u32[]{:S(2)}) copy-start(bf16[768,1536]{1,0:T(8,128)(2,1)} %wo.1) | copy-start | bytes 7077892
  25.7 7.2 %collective-permute-start.7 = (bf16[192,128]{1,0:T(8,128)(2,1)S(1)}, bf16[192,128]{1,0:T(8,128)(2,1)S(1)}, u32[]{:S(2)}, u32[]{:S(2)}) collective-permute-start(bf16[192,128]{1,0:T(8,128)(2,1)S(1)} %fusion.4.after), channel_id=1, source_target_pairs={{0,32},{16,48},{32,0},{48,16},{64,96},{80,112},{96,64},{112,80},{1... | collective-permute-start | bytes 147464 | tf_op jit(solution)/shard_map/ppermute | solution.py:304
  27.7 6.4 %collective-permute-start.8 = (bf16[192,128]{1,0:T(8,128)(2,1)S(1)}, bf16[192,128]{1,0:T(8,128)(2,1)S(1)}, u32[]{:S(2)}, u32[]{:S(2)}) collective-permute-start(bf16[192,128]{1,0:T(8,128)(2,1)S(1)} %fusion.4.after), channel_id=1, source_target_pairs={{0,64},{16,80},{32,96},{48,112},{64,0},{80,16},{96,32},{112,48},{1... | collective-permute-start | bytes 147464 | tf_op jit(solution)/shard_map/ppermute | solution.py:304
  31.0 5.9 %collective-permute-start.9 = (bf16[192,128]{1,0:T(8,128)(2,1)S(1)}, bf16[192,128]{1,0:T(8,128)(2,1)S(1)}, u32[]{:S(2)}, u32[]{:S(2)}) collective-permute-start(bf16[192,128]{1,0:T(8,128)(2,1)S(1)} %fusion.4.after), channel_id=1, source_target_pairs={{0,96},{16,112},{32,64},{48,80},{64,32},{80,48},{96,0},{112,16},{1... | collective-permute-start | bytes 147464 | tf_op jit(solution)/shard_map/ppermute | solution.py:304
  36.9 6.3 %collective-permute-start.10 = (bf16[192,128]{1,0:T(8,128)(2,1)S(1)}, bf16[192,128]{1,0:T(8,128)(2,1)S(1)}, u32[]{:S(2)}, u32[]{:S(2)}) collective-permute-start(bf16[192,128]{1,0:T(8,128)(2,1)S(1)} %add_convert_fusion), channel_id=1, source_target_pairs={{0,192},{16,208},{32,224},{48,240},{64,128},{80,144},{96,160},{112... | collective-permute-start | bytes 147464 | tf_op jit(solution)/shard_map/ppermute | solution.py:304
  43.2 4.8 %collective-permute-start.11 = (bf16[192,128]{1,0:T(8,128)(2,1)S(1)}, bf16[192,128]{1,0:T(8,128)(2,1)S(1)}, u32[]{:S(2)}, u32[]{:S(2)}) collective-permute-start(bf16[192,128]{1,0:T(8,128)(2,1)S(1)} %get-tuple-element.61), channel_id=1, source_target_pairs={{0,1},{1,0},{2,3},{3,2},{4,5},{5,4},{6,7},{7,6},{8,9},{9,8},{10,11... | collective-permute-start | bytes 147464 | tf_op jit(solution)/shard_map/ppermute | solution.py:304
  44.0 6.4 %collective-permute-start.12 = (bf16[192,128]{1,0:T(8,128)(2,1)S(1)}, bf16[192,128]{1,0:T(8,128)(2,1)S(1)}, u32[]{:S(2)}, u32[]{:S(2)}) collective-permute-start(bf16[192,128]{1,0:T(8,128)(2,1)S(1)} %get-tuple-element.60), channel_id=1, source_target_pairs={{0,2},{1,3},{2,0},{3,1},{4,6},{5,7},{6,4},{7,5},{8,10},{9,11},{10,... | collective-permute-start | bytes 147464 | tf_op jit(solution)/shard_map/ppermute | solution.py:304
  47.8 5.3 %collective-permute-start.13 = (bf16[192,128]{1,0:T(8,128)(2,1)S(1)}, bf16[192,128]{1,0:T(8,128)(2,1)S(1)}, u32[]{:S(2)}, u32[]{:S(2)}) collective-permute-start(bf16[192,128]{1,0:T(8,128)(2,1)S(1)} %get-tuple-element.59), channel_id=1, source_target_pairs={{0,3},{1,2},{2,1},{3,0},{4,7},{5,6},{6,5},{7,4},{8,11},{9,10},{10,... | collective-permute-start | bytes 147464 | tf_op jit(solution)/shard_map/ppermute | solution.py:304

commit v2 on v1

--- a/solution.py
+++ b/solution.py
@@ -319,23 +319,25 @@
     width = w_query.shape[1] // heads
     keys, values, tok, wq, *sent = states_of(tokens, w_key, w_value, w_query, heads, width)
     near = [sent[0]] + [None] * 3
-    for distance in (3, 1, 2):
+    for distance in (2, 1, 3):
         near[distance] = flip(sent[distance], "grp", distance)
     query = query_of(tok, wq, width)
-    *near, query = lax.optimization_barrier((*near, query))
+    near[2], near[1], near[3], near[0], query = lax.optimization_barrier(
+        (near[2], near[1], near[3], near[0], query)
+    )
     total = plus(near[0].astype(F32), near[1:])
 
     going = total.astype(BF16)
-    x3, x1, x2 = flips(going, "grp", (12, 4, 8))
+    x2, x1, x3 = flips(going, "grp", (8, 4, 12))
     low = inside_of(query, keys, values, level_weights, going, 0, heads // 2, width)
-    x3, x1, x2, low = lax.optimization_barrier((x3, x1, x2, low))
+    x2, x1, x3, low = lax.optimization_barrier((x2, x1, x3, low))
     total = plus(total, (x1, x2, x3))
     (other,) = flips(total.astype(BF16), "seq", (1,))
     total = plus(total, (other,))
     going = total.astype(BF16)
-    z1, z2, z3 = flips(going, "seq", (2, 4, 6))
+    z3, z2, z1 = flips(going, "seq", (6, 4, 2))
     high = inside_of(query, keys, values, level_weights, going, heads // 2, heads // 2, width)
-    z1, z2, z3, high = lax.optimization_barrier((z1, z2, z3, high))
+    z3, z2, z1, high = lax.optimization_barrier((z3, z2, z1, high))
     total = plus(total, (z1, z2, z3))
     (past,) = flips(total.astype(BF16), "seq", (12,))
     gathered, factor = gather_of(level_weights, near, (x1, x2, x3, other, z1, z2, z3))
@@ -344,8 +346,11 @@
         (gathered[distance] + factor * past.astype(F32)).astype(BF16) for distance in range(4)
     ]
     pieces = [back[0]] + [None] * 3
-    for distance in (3, 1, 2):
+    for distance in (2, 1, 3):
         pieces[distance] = flip(back[distance], "grp", distance)
+    pieces[2], pieces[1], pieces[3], pieces[0] = lax.optimization_barrier(
+        (pieces[2], pieces[1], pieces[3], pieces[0])
+    )
     return mixed_of(query, (low, high), pieces, w_output, width)
 
 

time: 55.9 us -> 53.5 us (0.957)
  the two profiles are of different devices: /device:TPU:26 before, /device:TPU:32 now
where the time goes in v2:
time: 53.5 us; the launch traced here: 53.2 us
  starting transfers between devices  22.3 us (42%)
  Pallas kernels  17.1 us (32%)
  waiting for transfers between devices  13.4 us (25%)
    ppermute x14, starting transfers between devices, flip(): return lax.ppermute(value, axis, pairs)  22.3 us
    ppermute x14, waiting for transfers between devices, flip(): return lax.ppermute(value, axis, pairs)  13.4 us
    pallas_call x1, Pallas kernels, states_of(): pl.pallas_call(functools.partial(state_kernel, width), out_shape=(side, s...  8.23 us
    pallas_call x2, Pallas kernels, inside_of(): pl.pallas_call(functools.partial(inside_kernel, width, first), out_shape=...  3.89 us
    pallas_call x1, Pallas kernels, mixed_of(): pl.pallas_call(functools.partial(mix_kernel, width), out_shape=jax.ShapeD...  2.52 us
    pallas_call x1, Pallas kernels, query_of(): pl.pallas_call(functools.partial(query_kernel, width), out_shape=jax.Shap...  1.6 us
  transfers between devices with their start and end apart: 14, of which 10 were waited for; matrix products, arithmetic and copies ran while one was open for 0% of the time, Pallas kernels for 12%

profile of v2, /device:TPU:32, one launch (start us, length us, event | category | flops | bytes accessed | tf_op | source)
XLA Modules:
  0.0 53.2 jit_solution(5028357003128071134)
XLA Ops:
  0.0 8.2 %states.1 = (bf16[512,768]{1,0:T(8,128)(2,1)S(1)}, bf16[512,768]{1,0:T(8,128)(2,1)S(1)}, bf16[512,1536]{1,0:T(8,128)(2,1)S(1)}, bf16[1536,768]{1,0:T(8,128)(2,1)...) custom-call(bf16[512,1536]{1,0:T(8,128)(2,1)} %tok_hbm.1, ...), custom_call_target="tpu_custom_call" | custom-call | tf_op jit(solution)/shard_map/states/pallas_call | solution.py:112
  8.2 3.3 %collective-permute-start = (bf16[192,128]{1,0:T(8,128)(2,1)S(1)}, bf16[192,128]{1,0:T(8,128)(2,1)S(1)}, u32[]{:S(2)}, u32[]{:S(2)}) collective-permute-start(bf16[192,128]{1,0:T(8,128)(2,1)S(1)} %get-tuple-element.35), channel_id=1, source_target_pairs={{0,2},{1,3},{2,0},{3,1},{4,6},{5,7},{6,4},{7,5},{8,10},{9,11},{10,... | collective-permute-start | bytes 147464 | tf_op jit(solution)/shard_map/ppermute | solution.py:304
  11.5 0.7 %collective-permute-start.1 = (bf16[192,128]{1,0:T(8,128)(2,1)S(1)}, bf16[192,128]{1,0:T(8,128)(2,1)S(1)}, u32[]{:S(2)}, u32[]{:S(2)}) collective-permute-start(bf16[192,128]{1,0:T(8,128)(2,1)S(1)} %get-tuple-element.36), channel_id=1, source_target_pairs={{0,1},{1,0},{2,3},{3,2},{4,5},{5,4},{6,7},{7,6},{8,9},{9,8},{10,11... | collective-permute-start | bytes 147464 | tf_op jit(solution)/shard_map/ppermute | solution.py:304
  12.2 0.4 collective-permute-start.2
  12.6 0.0 copy-start.1
  12.6 1.6 %query.1.q_ref = bf16[512,768]{1,0:T(8,128)(2,1)S(1)} custom-call(bf16[512,1536]{1,0:T(8,128)(2,1)S(1)} %get-tuple-element.39.tok, bf16[1536,768]{1,0:T(8,128)(2,1)S(1)} %get-tuple-element.40.wq), custom_call_target="tpu_custom_call" | custom-call | tf_op jit(solution)/shard_map/query/pallas_call | solution.py:136
  14.2 0.0 collective-permute-done.refs_2_
  14.2 1.4 %collective-permute-done.1.refs_1_ = bf16[192,128]{1,0:T(8,128)(2,1)S(1)} collective-permute-done((bf16[192,128]{1,0:T(8,128)(2,1)S(1)}, bf16[192,128]{1,0:T(8,128)(2,1)S(1)}, u32[]{:S(2)}, u32[]{:S(2)}) %collective-permute-start.1) | collective-permute-done | bytes 49184 | tf_op jit(solution)/shard_map/ppermute | solution.py:304
  15.6 1.9 %collective-permute-done.2.refs_3_ = bf16[192,128]{1,0:T(8,128)(2,1)S(1)} collective-permute-done((bf16[192,128]{1,0:T(8,128)(2,1)S(1)}, bf16[192,128]{1,0:T(8,128)(2,1)S(1)}, u32[]{:S(2)}, u32[]{:S(2)}) %collective-permute-start.2) | collective-permute-done | bytes 49184 | tf_op jit(solution)/shard_map/ppermute | solution.py:304
  17.5 3.1 %collective-permute-start.3 = (bf16[192,128]{1,0:T(8,128)(2,1)S(1)}, bf16[192,128]{1,0:T(8,128)(2,1)S(1)}, u32[]{:S(2)}, u32[]{:S(2)}) collective-permute-start(bf16[192,128]{1,0:T(8,128)(2,1)S(1)} %fusion.5.after), channel_id=1, source_target_pairs={{0,8},{1,9},{2,10},{3,11},{4,12},{5,13},{6,14},{7,15},{8,0},{9,1},... | collective-permute-start | bytes 147464 | tf_op jit(solution)/shard_map/ppermute | solution.py:304
  20.6 0.6 %collective-permute-start.4 = (bf16[192,128]{1,0:T(8,128)(2,1)S(1)}, bf16[192,128]{1,0:T(8,128)(2,1)S(1)}, u32[]{:S(2)}, u32[]{:S(2)}) collective-permute-start(bf16[192,128]{1,0:T(8,128)(2,1)S(1)} %fusion.5.after), channel_id=1, source_target_pairs={{0,4},{1,5},{2,6},{3,7},{4,0},{5,1},{6,2},{7,3},{8,12},{9,13},{10,... | collective-permute-start | bytes 147464 | tf_op jit(solution)/shard_map/ppermute | solution.py:304
  21.2 0.6 %collective-permute-start.5 = (bf16[192,128]{1,0:T(8,128)(2,1)S(1)}, bf16[192,128]{1,0:T(8,128)(2,1)S(1)}, u32[]{:S(2)}, u32[]{:S(2)}) collective-permute-start(bf16[192,128]{1,0:T(8,128)(2,1)S(1)} %fusion.5.after), channel_id=1, source_target_pairs={{0,12},{1,13},{2,14},{3,15},{4,8},{5,9},{6,10},{7,11},{8,4},{9,5},... | collective-permute-start | bytes 147464 | tf_op jit(solution)/shard_map/ppermute | solution.py:304
  21.8 0.0 copy-done.1
  21.8 0.1 copy.7.levels
  21.9 1.9 %inside.2.low_ref = f32[512,384]{1,0:T(8,128)S(1)} custom-call(bf16[512,768]{1,0:T(8,128)(2,1)S(1)} %query.1.q_ref, bf16[512,768]{1,0:T(8,128)(2,1)S(1)} %get-tuple-element.46.k_ref, bf16[512,768]{1,0:T(8,128)(2,1)S(1)} %get-tuple-element.47.v_ref, f32[9,6]{1,0:T(8,128)S(1)} %copy.7.levels, bf16[192,128]{1,0:T(8,128)(2,1)S(1)} %fusion.5.after), custom_call_target="tpu_custom_call" | custom-call | tf_op jit(solution)/shard_map/inside/pallas_call | solution.py:175
  23.8 0.0 collective-permute-done.3.refs_5_
  23.8 0.9 %collective-permute-done.4.refs_4_ = bf16[192,128]{1,0:T(8,128)(2,1)S(1)} collective-permute-done((bf16[192,128]{1,0:T(8,128)(2,1)S(1)}, bf16[192,128]{1,0:T(8,128)(2,1)S(1)}, u32[]{:S(2)}, u32[]{:S(2)}) %collective-permute-start.4) | collective-permute-done | bytes 49184 | tf_op jit(solution)/shard_map/ppermute | solution.py:304
  24.7 1.8 %collective-permute-done.5.refs_6_ = bf16[192,128]{1,0:T(8,128)(2,1)S(1)} collective-permute-done((bf16[192,128]{1,0:T(8,128)(2,1)S(1)}, bf16[192,128]{1,0:T(8,128)(2,1)S(1)}, u32[]{:S(2)}, u32[]{:S(2)}) %collective-permute-start.5) | collective-permute-done | bytes 49184 | tf_op jit(solution)/shard_map/ppermute | solution.py:304
  26.5 0.1 fusion.6
  26.6 0.1 collective-permute-start.6
  26.7 1.2 %collective-permute-done.6.refs_7_ = bf16[192,128]{1,0:T(8,128)(2,1)S(1)} collective-permute-done((bf16[192,128]{1,0:T(8,128)(2,1)S(1)}, bf16[192,128]{1,0:T(8,128)(2,1)S(1)}, u32[]{:S(2)}, u32[]{:S(2)}) %collective-permute-start.6) | collective-permute-done | bytes 49184 | tf_op jit(solution)/shard_map/ppermute | solution.py:304
  27.9 0.0 copy-start
  27.9 2.0 %collective-permute-start.7 = (bf16[192,128]{1,0:T(8,128)(2,1)S(1)}, bf16[192,128]{1,0:T(8,128)(2,1)S(1)}, u32[]{:S(2)}, u32[]{:S(2)}) collective-permute-start(bf16[192,128]{1,0:T(8,128)(2,1)S(1)} %fusion.4.after), channel_id=1, source_target_pairs={{0,96},{16,112},{32,64},{48,80},{64,32},{80,48},{96,0},{112,16},{1... | collective-permute-start | bytes 147464 | tf_op jit(solution)/shard_map/ppermute | solution.py:304
  29.9 1.5 %collective-permute-start.8 = (bf16[192,128]{1,0:T(8,128)(2,1)S(1)}, bf16[192,128]{1,0:T(8,128)(2,1)S(1)}, u32[]{:S(2)}, u32[]{:S(2)}) collective-permute-start(bf16[192,128]{1,0:T(8,128)(2,1)S(1)} %fusion.4.after), channel_id=1, source_target_pairs={{0,64},{16,80},{32,96},{48,112},{64,0},{80,16},{96,32},{112,48},{1... | collective-permute-start | bytes 147464 | tf_op jit(solution)/shard_map/ppermute | solution.py:304
  31.4 1.4 %collective-permute-start.9 = (bf16[192,128]{1,0:T(8,128)(2,1)S(1)}, bf16[192,128]{1,0:T(8,128)(2,1)S(1)}, u32[]{:S(2)}, u32[]{:S(2)}) collective-permute-start(bf16[192,128]{1,0:T(8,128)(2,1)S(1)} %fusion.4.after), channel_id=1, source_target_pairs={{0,32},{16,48},{32,0},{48,16},{64,96},{80,112},{96,64},{112,80},{1... | collective-permute-start | bytes 147464 | tf_op jit(solution)/shard_map/ppermute | solution.py:304
  32.8 1.9 %inside.3.high_ref = f32[512,384]{1,0:T(8,128)S(1)} custom-call(bf16[512,768]{1,0:T(8,128)(2,1)S(1)} %query.1.q_ref, bf16[512,768]{1,0:T(8,128)(2,1)S(1)} %get-tuple-element.46.k_ref, bf16[512,768]{1,0:T(8,128)(2,1)S(1)} %get-tuple-element.47.v_ref, f32[9,6]{1,0:T(8,128)S(1)} %copy.7.levels, bf16[192,128]{1,0:T(8,128)(2,1)S(1)} %fusion.4.after), custom_call_target="tpu_custom_call" | custom-call | tf_op jit(solution)/shard_map/inside/pallas_call | solution.py:175
  34.7 0.0 collective-permute-done.7.refs_10_
  34.7 0.2 collective-permute-done.8.refs_9_
  35.0 1.7 %collective-permute-done.9.refs_8_ = bf16[192,128]{1,0:T(8,128)(2,1)S(1)} collective-permute-done((bf16[192,128]{1,0:T(8,128)(2,1)S(1)}, bf16[192,128]{1,0:T(8,128)(2,1)S(1)}, u32[]{:S(2)}, u32[]{:S(2)}) %collective-permute-start.9) | collective-permute-done | bytes 49184 | tf_op jit(solution)/shard_map/ppermute | solution.py:304
  36.7 4.6 %collective-permute-start.10 = (bf16[192,128]{1,0:T(8,128)(2,1)S(1)}, bf16[192,128]{1,0:T(8,128)(2,1)S(1)}, u32[]{:S(2)}, u32[]{:S(2)}) collective-permute-start(bf16[192,128]{1,0:T(8,128)(2,1)S(1)} %add_convert_fusion), channel_id=1, source_target_pairs={{0,192},{16,208},{32,224},{48,240},{64,128},{80,144},{96,160},{112... | collective-permute-start | bytes 147464 | tf_op jit(solution)/shard_map/ppermute | solution.py:304
  41.3 0.8 %gather.1 = (f32[4,192,128]{2,1,0:T(8,128)S(1)}, f32[192,128]{1,0:T(8,128)S(1)}) custom-call(f32[9,6]{1,0:T(8,128)S(1)} %copy.7.levels, bf16[192,128]{1,0:T(8,128)(2,1)S(1)} %get-tuple-element.42.refs_0_, bf16[192,128]{1,0:T(8,128)(2,1)S(1)} %collective-permute-done.1.refs_1_, bf16[192,128]{1,0:T(8,128)(2,1)S(1)} %collective-permute-done.refs_2_, ...), custom_call_target="tpu_custom_call" | custom-call | tf_op jit(solution)/shard_map/gather/pallas_call | solution.py:228
  42.1 1.8 %collective-permute-done.10 = bf16[192,128]{1,0:T(8,128)(2,1)S(1)} collective-permute-done((bf16[192,128]{1,0:T(8,128)(2,1)S(1)}, bf16[192,128]{1,0:T(8,128)(2,1)S(1)}, u32[]{:S(2)}, u32[]{:S(2)}) %collective-permute-start.10) | collective-permute-done | bytes 49184 | tf_op jit(solution)/shard_map/ppermute | solution.py:304
  43.9 0.7 %collective-permute-start.11 = (bf16[192,128]{1,0:T(8,128)(2,1)S(1)}, bf16[192,128]{1,0:T(8,128)(2,1)S(1)}, u32[]{:S(2)}, u32[]{:S(2)}) collective-permute-start(bf16[192,128]{1,0:T(8,128)(2,1)S(1)} %get-tuple-element.70), channel_id=1, source_target_pairs={{0,2},{1,3},{2,0},{3,1},{4,6},{5,7},{6,4},{7,5},{8,10},{9,11},{10,... | collective-permute-start | bytes 147464 | tf_op jit(solution)/shard_map/ppermute | solution.py:304
  44.6 0.6 %collective-permute-start.12 = (bf16[192,128]{1,0:T(8,128)(2,1)S(1)}, bf16[192,128]{1,0:T(8,128)(2,1)S(1)}, u32[]{:S(2)}, u32[]{:S(2)}) collective-permute-start(bf16[192,128]{1,0:T(8,128)(2,1)S(1)} %get-tuple-element.69), channel_id=1, source_target_pairs={{0,1},{1,0},{2,3},{3,2},{4,5},{5,4},{6,7},{7,6},{8,9},{9,8},{10,11... | collective-permute-start | bytes 147464 | tf_op jit(solution)/shard_map/ppermute | solution.py:304
  45.3 2.8 %collective-permute-start.13 = (bf16[192,128]{1,0:T(8,128)(2,1)S(1)}, bf16[192,128]{1,0:T(8,128)(2,1)S(1)}, u32[]{:S(2)}, u32[]{:S(2)}) collective-permute-start(bf16[192,128]{1,0:T(8,128)(2,1)S(1)} %get-tuple-element.68), channel_id=1, source_target_pairs={{0,3},{1,2},{2,1},{3,0},{4,7},{5,6},{6,5},{7,4},{8,11},{9,10},{10,... | collective-permute-start | bytes 147464 | tf_op jit(solution)/shard_map/ppermute | solution.py:304
  48.1 1.5 %collective-permute-done.11.two = bf16[192,128]{1,0:T(8,128)(2,1)S(1)} collective-permute-done((bf16[192,128]{1,0:T(8,128)(2,1)S(1)}, bf16[192,128]{1,0:T(8,128)(2,1)S(1)}, u32[]{:S(2)}, u32[]{:S(2)}) %collective-permute-start.11) | collective-permute-done | bytes 49184 | tf_op jit(solution)/shard_map/ppermute | solution.py:304
  49.6 0.0 collective-permute-done.12.one
  49.6 1.0 %collective-permute-done.13.three = bf16[192,128]{1,0:T(8,128)(2,1)S(1)} collective-permute-done((bf16[192,128]{1,0:T(8,128)(2,1)S(1)}, bf16[192,128]{1,0:T(8,128)(2,1)S(1)}, u32[]{:S(2)}, u32[]{:S(2)}) %collective-permute-start.13) | collective-permute-done | bytes 49184 | tf_op jit(solution)/shard_map/ppermute | solution.py:304
  50.6 0.0 copy-done
  50.6 2.5 %mix.1 = bf16[512,1536]{1,0:T(8,128)(2,1)} custom-call(bf16[512,768]{1,0:T(8,128)(2,1)S(1)} %query.1.q_ref, f32[512,384]{1,0:T(8,128)S(1)} %inside.2.low_ref, f32[512,384]{1,0:T(8,128)S(1)} %inside.3.high_ref, bf16[192,128]{1,0:T(8,128)(2,1)S(1)} %get-tuple-element.61.own, bf16[192,128]{1,0:T(8,128)(2,1)S(1)} %collective-permute-done.12.one, ...), custom_call_target="tpu_custom_call" | custom-call | tf_op jit(solution)/shard_map/mix/pallas_call | solution.py:286
  (4 shorter events, 0.1 us)
Async XLA Ops:
  8.2 6.0 %collective-permute-start = (bf16[192,128]{1,0:T(8,128)(2,1)S(1)}, bf16[192,128]{1,0:T(8,128)(2,1)S(1)}, u32[]{:S(2)}, u32[]{:S(2)}) collective-permute-start(bf16[192,128]{1,0:T(8,128)(2,1)S(1)} %get-tuple-element.35), channel_id=1, source_target_pairs={{0,2},{1,3},{2,0},{3,1},{4,6},{5,7},{6,4},{7,5},{8,10},{9,11},{10,... | collective-permute-start | bytes 147464 | tf_op jit(solution)/shard_map/ppermute | solution.py:304
  11.5 4.1 %collective-permute-start.1 = (bf16[192,128]{1,0:T(8,128)(2,1)S(1)}, bf16[192,128]{1,0:T(8,128)(2,1)S(1)}, u32[]{:S(2)}, u32[]{:S(2)}) collective-permute-start(bf16[192,128]{1,0:T(8,128)(2,1)S(1)} %get-tuple-element.36), channel_id=1, source_target_pairs={{0,1},{1,0},{2,3},{3,2},{4,5},{5,4},{6,7},{7,6},{8,9},{9,8},{10,11... | collective-permute-start | bytes 147464 | tf_op jit(solution)/shard_map/ppermute | solution.py:304
  12.2 5.3 %collective-permute-start.2 = (bf16[192,128]{1,0:T(8,128)(2,1)S(1)}, bf16[192,128]{1,0:T(8,128)(2,1)S(1)}, u32[]{:S(2)}, u32[]{:S(2)}) collective-permute-start(bf16[192,128]{1,0:T(8,128)(2,1)S(1)} %get-tuple-element.37), channel_id=1, source_target_pairs={{0,3},{1,2},{2,1},{3,0},{4,7},{5,6},{6,5},{7,4},{8,11},{9,10},{10,... | collective-permute-start | bytes 147464 | tf_op jit(solution)/shard_map/ppermute | solution.py:304
  12.6 9.2 %copy-start.1 = (f32[9,6]{0,1:T(8,128)S(1)}, f32[9,6]{0,1:T(8,128)}, u32[]{:S(2)}) copy-start(f32[9,6]{0,1:T(8,128)} %param.11) | copy-start | bytes 652
  17.5 6.3 %collective-permute-start.3 = (bf16[192,128]{1,0:T(8,128)(2,1)S(1)}, bf16[192,128]{1,0:T(8,128)(2,1)S(1)}, u32[]{:S(2)}, u32[]{:S(2)}) collective-permute-start(bf16[192,128]{1,0:T(8,128)(2,1)S(1)} %fusion.5.after), channel_id=1, source_target_pairs={{0,8},{1,9},{2,10},{3,11},{4,12},{5,13},{6,14},{7,15},{8,0},{9,1},... | collective-permute-start | bytes 147464 | tf_op jit(solution)/shard_map/ppermute | solution.py:304
  20.6 4.1 %collective-permute-start.4 = (bf16[192,128]{1,0:T(8,128)(2,1)S(1)}, bf16[192,128]{1,0:T(8,128)(2,1)S(1)}, u32[]{:S(2)}, u32[]{:S(2)}) collective-permute-start(bf16[192,128]{1,0:T(8,128)(2,1)S(1)} %fusion.5.after), channel_id=1, source_target_pairs={{0,4},{1,5},{2,6},{3,7},{4,0},{5,1},{6,2},{7,3},{8,12},{9,13},{10,... | collective-permute-start | bytes 147464 | tf_op jit(solution)/shard_map/ppermute | solution.py:304
  21.2 5.3 %collective-permute-start.5 = (bf16[192,128]{1,0:T(8,128)(2,1)S(1)}, bf16[192,128]{1,0:T(8,128)(2,1)S(1)}, u32[]{:S(2)}, u32[]{:S(2)}) collective-permute-start(bf16[192,128]{1,0:T(8,128)(2,1)S(1)} %fusion.5.after), channel_id=1, source_target_pairs={{0,12},{1,13},{2,14},{3,15},{4,8},{5,9},{6,10},{7,11},{8,4},{9,5},... | collective-permute-start | bytes 147464 | tf_op jit(solution)/shard_map/ppermute | solution.py:304
  26.6 1.3 %collective-permute-start.6 = (bf16[192,128]{1,0:T(8,128)(2,1)S(1)}, bf16[192,128]{1,0:T(8,128)(2,1)S(1)}, u32[]{:S(2)}, u32[]{:S(2)}) collective-permute-start(bf16[192,128]{1,0:T(8,128)(2,1)S(1)} %get-tuple-element.65), channel_id=1, source_target_pairs={{0,16},{16,0},{32,48},{48,32},{64,80},{80,64},{96,112},{112,96},{1... | collective-permute-start | bytes 147464 | tf_op jit(solution)/shard_map/ppermute | solution.py:304
  27.9 22.6 %copy-start = (bf16[768,1536]{1,0:T(8,128)(2,1)S(1)}, bf16[768,1536]{1,0:T(8,128)(2,1)}, u32[]{:S(2)}) copy-start(bf16[768,1536]{1,0:T(8,128)(2,1)} %wo.1) | copy-start | bytes 7077892
  27.9 6.8 %collective-permute-start.7 = (bf16[192,128]{1,0:T(8,128)(2,1)S(1)}, bf16[192,128]{1,0:T(8,128)(2,1)S(1)}, u32[]{:S(2)}, u32[]{:S(2)}) collective-permute-start(bf16[192,128]{1,0:T(8,128)(2,1)S(1)} %fusion.4.after), channel_id=1, source_target_pairs={{0,96},{16,112},{32,64},{48,80},{64,32},{80,48},{96,0},{112,16},{1... | collective-permute-start | bytes 147464 | tf_op jit(solution)/shard_map/ppermute | solution.py:304
  29.9 5.0 %collective-permute-start.8 = (bf16[192,128]{1,0:T(8,128)(2,1)S(1)}, bf16[192,128]{1,0:T(8,128)(2,1)S(1)}, u32[]{:S(2)}, u32[]{:S(2)}) collective-permute-start(bf16[192,128]{1,0:T(8,128)(2,1)S(1)} %fusion.4.after), channel_id=1, source_target_pairs={{0,64},{16,80},{32,96},{48,112},{64,0},{80,16},{96,32},{112,48},{1... | collective-permute-start | bytes 147464 | tf_op jit(solution)/shard_map/ppermute | solution.py:304
  31.4 5.2 %collective-permute-start.9 = (bf16[192,128]{1,0:T(8,128)(2,1)S(1)}, bf16[192,128]{1,0:T(8,128)(2,1)S(1)}, u32[]{:S(2)}, u32[]{:S(2)}) collective-permute-start(bf16[192,128]{1,0:T(8,128)(2,1)S(1)} %fusion.4.after), channel_id=1, source_target_pairs={{0,32},{16,48},{32,0},{48,16},{64,96},{80,112},{96,64},{112,80},{1... | collective-permute-start | bytes 147464 | tf_op jit(solution)/shard_map/ppermute | solution.py:304
  36.7 7.2 %collective-permute-start.10 = (bf16[192,128]{1,0:T(8,128)(2,1)S(1)}, bf16[192,128]{1,0:T(8,128)(2,1)S(1)}, u32[]{:S(2)}, u32[]{:S(2)}) collective-permute-start(bf16[192,128]{1,0:T(8,128)(2,1)S(1)} %add_convert_fusion), channel_id=1, source_target_pairs={{0,192},{16,208},{32,224},{48,240},{64,128},{80,144},{96,160},{112... | collective-permute-start | bytes 147464 | tf_op jit(solution)/shard_map/ppermute | solution.py:304
  43.9 5.7 %collective-permute-start.11 = (bf16[192,128]{1,0:T(8,128)(2,1)S(1)}, bf16[192,128]{1,0:T(8,128)(2,1)S(1)}, u32[]{:S(2)}, u32[]{:S(2)}) collective-permute-start(bf16[192,128]{1,0:T(8,128)(2,1)S(1)} %get-tuple-element.70), channel_id=1, source_target_pairs={{0,2},{1,3},{2,0},{3,1},{4,6},{5,7},{6,4},{7,5},{8,10},{9,11},{10,... | collective-permute-start | bytes 147464 | tf_op jit(solution)/shard_map/ppermute | solution.py:304
  44.6 5.0 %collective-permute-start.12 = (bf16[192,128]{1,0:T(8,128)(2,1)S(1)}, bf16[192,128]{1,0:T(8,128)(2,1)S(1)}, u32[]{:S(2)}, u32[]{:S(2)}) collective-permute-start(bf16[192,128]{1,0:T(8,128)(2,1)S(1)} %get-tuple-element.69), channel_id=1, source_target_pairs={{0,1},{1,0},{2,3},{3,2},{4,5},{5,4},{6,7},{7,6},{8,9},{9,8},{10,11... | collective-permute-start | bytes 147464 | tf_op jit(solution)/shard_map/ppermute | solution.py:304
  45.3 5.3 %collective-permute-start.13 = (bf16[192,128]{1,0:T(8,128)(2,1)S(1)}, bf16[192,128]{1,0:T(8,128)(2,1)S(1)}, u32[]{:S(2)}, u32[]{:S(2)}) collective-permute-start(bf16[192,128]{1,0:T(8,128)(2,1)S(1)} %get-tuple-element.68), channel_id=1, source_target_pairs={{0,3},{1,2},{2,1},{3,0},{4,7},{5,6},{6,5},{7,4},{8,11},{9,10},{10,... | collective-permute-start | bytes 147464 | tf_op jit(solution)/shard_map/ppermute | solution.py:304

commit v3 on v2

--- a/solution.py
+++ b/solution.py
@@ -42,53 +42,50 @@
     one,
     two,
     three,
-    wk,
-    wv,
+    weights,
     slices,
+    sums,
     sems,
 ):
     depth = tok.shape[1]
     pair = 2 * width
-    pairs = wk.shape[0]
-    half = depth // 2
     part = width // QUARTERS
-    parts = [
-        pltpu.make_async_copy(
-            tok_hbm.at[:, pl.ds(i * half, half)], tok.at[:, pl.ds(i * half, half)], sems.at[i]
+    chunks = 3
+    chunk = depth // chunks
+    count = 0
+
+    def copy(source, target):
+        nonlocal count
+        count += 1
+        return pltpu.make_async_copy(source, target, sems.at[count - 1])
+
+    def columns(start, size):
+        return pl.ds(start * pair, size * pair)
+
+    first = []
+    for i in range(chunks):
+        rows = pl.ds(i * chunk, chunk)
+        first.append(copy(tok_hbm.at[:, rows], tok.at[:, rows]))
+        first.append(copy(wk_hbm.at[rows, columns(0, 2)], weights.at[0, rows]))
+    second = [
+        copy(wk_hbm.at[:, columns(2, 1)], weights.at[1, :, columns(0, 1)]),
+        copy(wv_hbm.at[:, columns(0, 1)], weights.at[1, :, columns(1, 1)]),
+    ]
+    third = copy(wv_hbm.at[:, columns(1, 2)], weights.at[2])
+    last = copy(wq_hbm, wq)
+    for item in (*first, *second, third, last):
+        item.start()
+
+    def finish_keys(j, product):
+        k_ref[:, j * pair : (j + 1) * pair] = unit_pair(product, width)
+
+    def finish_values(j, product):
+        here = slice(j * pair, (j + 1) * pair)
+        values = product.astype(BF16)
+        v_ref[:, here] = values
+        both = lax.dot_general(
+            k_ref[:, here], values, (((0,), (0,)), ((), ())), preferred_element_type=F32
         )
-        for i in range(2)
-    ]
-    weights = []
-    for j in range(pairs):
-        for source, target in ((wk_hbm, wk), (wv_hbm, wv)):
-            weights.append(
-                pltpu.make_async_copy(
-                    source.at[:, pl.ds(j * pair, pair)], target.at[j], sems.at[2 + len(weights)]
-                )
-            )
-    last = pltpu.make_async_copy(wq_hbm, wq, sems.at[2 + 2 * pairs])
-    parts[0].start()
-    weights[0].start()
-    parts[1].start()
-    for copy in weights[1:]:
-        copy.start()
-    last.start()
-    parts[0].wait()
-    weights[0].wait()
-    for j in range(pairs):
-        if j == 0:
-            k32 = dot(tok[:, :half], wk[j, :half])
-            parts[1].wait()
-            k32 = k32 + dot(tok[:, half:], wk[j, half:])
-        else:
-            weights[2 * j].wait()
-            k32 = dot(tok[...], wk[j])
-        keys = unit_pair(k32, width)
-        k_ref[:, j * pair : (j + 1) * pair] = keys
-        weights[2 * j + 1].wait()
-        values = dot(tok[...], wv[j]).astype(BF16)
-        v_ref[:, j * pair : (j + 1) * pair] = values
-        both = lax.dot_general(keys, values, (((0,), (0,)), ((), ())), preferred_element_type=F32)
         for side in range(2):
             head = 2 * j + side
             state = both[side * width : (side + 1) * width, side * width : (side + 1) * width]
@@ -96,6 +93,24 @@
                 slices[q, head * part : (head + 1) * part, :] = state[
                     q * part : (q + 1) * part
                 ].astype(BF16)
+
+    for i in range(chunks):
+        first[2 * i].wait()
+        first[2 * i + 1].wait()
+        rows = slice(i * chunk, (i + 1) * chunk)
+        product = dot(tok[:, rows], weights[0, rows])
+        sums[0] = product if i == 0 else sums[0] + product
+    for item in second:
+        item.wait()
+    sums[1] = dot(tok[...], weights[1])
+    finish_keys(0, sums[0, :, :pair])
+    finish_keys(1, sums[0, :, pair:])
+    third.wait()
+    sums[0] = dot(tok[...], weights[2])
+    finish_keys(2, sums[1, :, :pair])
+    finish_values(0, sums[1, :, pair:])
+    finish_values(1, sums[0, :, :pair])
+    finish_values(2, sums[0, :, pair:])
     y = lax.axis_index("grp") % QUARTERS
     for distance, target in enumerate((own, one, two, three)):
         target[...] = slices[y ^ distance]
@@ -105,24 +120,24 @@
 def states_of(tokens, w_key, w_value, w_query, heads, width):
     rows, depth = tokens.shape
     inner = heads * width
-    pairs = heads // 2
     piece = jax.ShapeDtypeStruct((inner // QUARTERS, width), BF16)
     side = jax.ShapeDtypeStruct((rows, inner), BF16)
     whole = [jax.ShapeDtypeStruct(a.shape, a.dtype) for a in (tokens, w_query)]
+    operands = (tokens, w_key, w_value, w_query)
     return pl.pallas_call(
         functools.partial(state_kernel, width),
         out_shape=(side, side, *whole, piece, piece, piece, piece),
         in_specs=[HBM] * 4,
         out_specs=[VMEM] * 8,
         scratch_shapes=[
-            pltpu.VMEM((pairs, depth, 2 * width), BF16),
-            pltpu.VMEM((pairs, depth, 2 * width), BF16),
+            pltpu.VMEM((3, depth, 4 * width), BF16),
             pltpu.VMEM((QUARTERS, inner // QUARTERS, width), BF16),
-            pltpu.SemaphoreType.DMA((3 + 2 * pairs,)),
+            pltpu.VMEM((2, rows, 4 * width), F32),
+            pltpu.SemaphoreType.DMA((10,)),
         ],
-        compiler_params=pltpu.CompilerParams(vmem_limit_bytes=20 << 20),
+        compiler_params=pltpu.CompilerParams(vmem_limit_bytes=24 << 20),
         name="states",
-    )(*(pltpu.with_memory_space_constraint(a, pltpu.HBM) for a in (tokens, w_key, w_value, w_query)))
+    )(*(pltpu.with_memory_space_constraint(operand, pltpu.HBM) for operand in operands))
 
 
 def query_kernel(width, tok, wq, q_ref):
@@ -335,11 +350,11 @@
     (other,) = flips(total.astype(BF16), "seq", (1,))
     total = plus(total, (other,))
     going = total.astype(BF16)
-    z3, z2, z1 = flips(going, "seq", (6, 4, 2))
+    z3, z2, z1 = flips(going, "seq", (7, 5, 3))
     high = inside_of(query, keys, values, level_weights, going, heads // 2, heads // 2, width)
     z3, z2, z1, high = lax.optimization_barrier((z3, z2, z1, high))
     total = plus(total, (z1, z2, z3))
-    (past,) = flips(total.astype(BF16), "seq", (12,))
+    (past,) = flips(total.astype(BF16), "seq", (13,))
     gathered, factor = gather_of(level_weights, near, (x1, x2, x3, other, z1, z2, z3))
     past, gathered, factor = lax.optimization_barrier((past, gathered, factor))
     back = [

time: 53.5 us -> 49.9 us (0.933)
  Pallas kernels: 17.1 us -> 13.6 us
    pallas_call x1, Pallas kernels: 8.23 us -> 4.72 us  [states_of(): pl.pallas_call(functools.partial(state_kernel, width), out_shape=(side, s...]
  transfers between devices with their start and end apart: 14 -> 14, of which waited for: 10 -> 9; matrix products, arithmetic and copies ran while one was open for 0% -> 0% of each run, Pallas kernels for 12% -> 13%
where the time goes in v3:
time: 49.9 us; the launch traced here: 49.8 us
  starting transfers between devices  22.1 us (44%)
  Pallas kernels  13.6 us (27%)
  waiting for transfers between devices  13.6 us (27%)
    ppermute x14, starting transfers between devices, flip(): return lax.ppermute(value, axis, pairs)  22.1 us
    ppermute x14, waiting for transfers between devices, flip(): return lax.ppermute(value, axis, pairs)  13.6 us
    pallas_call x1, Pallas kernels, states_of(): pl.pallas_call(functools.partial(state_kernel, width), out_shape=(side, s...  4.72 us
    pallas_call x2, Pallas kernels, inside_of(): pl.pallas_call(functools.partial(inside_kernel, width, first), out_shape=...  3.9 us
    pallas_call x1, Pallas kernels, mixed_of(): pl.pallas_call(functools.partial(mix_kernel, width), out_shape=jax.ShapeD...  2.52 us
    pallas_call x1, Pallas kernels, query_of(): pl.pallas_call(functools.partial(query_kernel, width), out_shape=jax.Shap...  1.6 us
  transfers between devices with their start and end apart: 14, of which 9 were waited for; matrix products, arithmetic and copies ran while one was open for 0% of the time, Pallas kernels for 13%

profile of v3, /device:TPU:32, one launch (start us, length us, event | category | flops | bytes accessed | tf_op | source)
XLA Modules:
  0.0 49.8 jit_solution(1367591285848363187)
XLA Ops:
  0.0 4.7 %states.1 = (bf16[512,768]{1,0:T(8,128)(2,1)S(1)}, bf16[512,768]{1,0:T(8,128)(2,1)S(1)}, bf16[512,1536]{1,0:T(8,128)(2,1)S(1)}, bf16[1536,768]{1,0:T(8,128)(2,1)...) custom-call(bf16[512,1536]{1,0:T(8,128)(2,1)} %tok_hbm.1, ...), custom_call_target="tpu_custom_call" | custom-call | tf_op jit(solution)/shard_map/states/pallas_call | solution.py:127
  4.7 3.3 %collective-permute-start = (bf16[192,128]{1,0:T(8,128)(2,1)S(1)}, bf16[192,128]{1,0:T(8,128)(2,1)S(1)}, u32[]{:S(2)}, u32[]{:S(2)}) collective-permute-start(bf16[192,128]{1,0:T(8,128)(2,1)S(1)} %get-tuple-element.35), channel_id=1, source_target_pairs={{0,2},{1,3},{2,0},{3,1},{4,6},{5,7},{6,4},{7,5},{8,10},{9,11},{10,... | collective-permute-start | bytes 147464 | tf_op jit(solution)/shard_map/ppermute | solution.py:319
  8.0 0.7 %collective-permute-start.1 = (bf16[192,128]{1,0:T(8,128)(2,1)S(1)}, bf16[192,128]{1,0:T(8,128)(2,1)S(1)}, u32[]{:S(2)}, u32[]{:S(2)}) collective-permute-start(bf16[192,128]{1,0:T(8,128)(2,1)S(1)} %get-tuple-element.36), channel_id=1, source_target_pairs={{0,1},{1,0},{2,3},{3,2},{4,5},{5,4},{6,7},{7,6},{8,9},{9,8},{10,11... | collective-permute-start | bytes 147464 | tf_op jit(solution)/shard_map/ppermute | solution.py:319
  8.7 0.4 collective-permute-start.2
  9.1 0.0 copy-start.1
  9.1 1.6 %query.1.q_ref = bf16[512,768]{1,0:T(8,128)(2,1)S(1)} custom-call(bf16[512,1536]{1,0:T(8,128)(2,1)S(1)} %get-tuple-element.39.tok, bf16[1536,768]{1,0:T(8,128)(2,1)S(1)} %get-tuple-element.40.wq), custom_call_target="tpu_custom_call" | custom-call | tf_op jit(solution)/shard_map/query/pallas_call | solution.py:151
  10.7 0.0 collective-permute-done.refs_2_
  10.7 1.4 %collective-permute-done.1.refs_1_ = bf16[192,128]{1,0:T(8,128)(2,1)S(1)} collective-permute-done((bf16[192,128]{1,0:T(8,128)(2,1)S(1)}, bf16[192,128]{1,0:T(8,128)(2,1)S(1)}, u32[]{:S(2)}, u32[]{:S(2)}) %collective-permute-start.1) | collective-permute-done | bytes 49184 | tf_op jit(solution)/shard_map/ppermute | solution.py:319
  12.1 1.9 %collective-permute-done.2.refs_3_ = bf16[192,128]{1,0:T(8,128)(2,1)S(1)} collective-permute-done((bf16[192,128]{1,0:T(8,128)(2,1)S(1)}, bf16[192,128]{1,0:T(8,128)(2,1)S(1)}, u32[]{:S(2)}, u32[]{:S(2)}) %collective-permute-start.2) | collective-permute-done | bytes 49184 | tf_op jit(solution)/shard_map/ppermute | solution.py:319
  14.0 3.1 %collective-permute-start.3 = (bf16[192,128]{1,0:T(8,128)(2,1)S(1)}, bf16[192,128]{1,0:T(8,128)(2,1)S(1)}, u32[]{:S(2)}, u32[]{:S(2)}) collective-permute-start(bf16[192,128]{1,0:T(8,128)(2,1)S(1)} %fusion.5.after), channel_id=1, source_target_pairs={{0,8},{1,9},{2,10},{3,11},{4,12},{5,13},{6,14},{7,15},{8,0},{9,1},... | collective-permute-start | bytes 147464 | tf_op jit(solution)/shard_map/ppermute | solution.py:319
  17.1 0.6 %collective-permute-start.4 = (bf16[192,128]{1,0:T(8,128)(2,1)S(1)}, bf16[192,128]{1,0:T(8,128)(2,1)S(1)}, u32[]{:S(2)}, u32[]{:S(2)}) collective-permute-start(bf16[192,128]{1,0:T(8,128)(2,1)S(1)} %fusion.5.after), channel_id=1, source_target_pairs={{0,4},{1,5},{2,6},{3,7},{4,0},{5,1},{6,2},{7,3},{8,12},{9,13},{10,... | collective-permute-start | bytes 147464 | tf_op jit(solution)/shard_map/ppermute | solution.py:319
  17.7 0.6 %collective-permute-start.5 = (bf16[192,128]{1,0:T(8,128)(2,1)S(1)}, bf16[192,128]{1,0:T(8,128)(2,1)S(1)}, u32[]{:S(2)}, u32[]{:S(2)}) collective-permute-start(bf16[192,128]{1,0:T(8,128)(2,1)S(1)} %fusion.5.after), channel_id=1, source_target_pairs={{0,12},{1,13},{2,14},{3,15},{4,8},{5,9},{6,10},{7,11},{8,4},{9,5},... | collective-permute-start | bytes 147464 | tf_op jit(solution)/shard_map/ppermute | solution.py:319
  18.3 0.0 copy-done.1
  18.3 0.1 copy.7.levels
  18.4 1.9 %inside.2.low_ref = f32[512,384]{1,0:T(8,128)S(1)} custom-call(bf16[512,768]{1,0:T(8,128)(2,1)S(1)} %query.1.q_ref, bf16[512,768]{1,0:T(8,128)(2,1)S(1)} %get-tuple-element.46.k_ref, bf16[512,768]{1,0:T(8,128)(2,1)S(1)} %get-tuple-element.47.v_ref, f32[9,6]{1,0:T(8,128)S(1)} %copy.7.levels, bf16[192,128]{1,0:T(8,128)(2,1)S(1)} %fusion.5.after), custom_call_target="tpu_custom_call" | custom-call | tf_op jit(solution)/shard_map/inside/pallas_call | solution.py:190
  20.3 0.0 collective-permute-done.3.refs_5_
  20.3 0.9 %collective-permute-done.4.refs_4_ = bf16[192,128]{1,0:T(8,128)(2,1)S(1)} collective-permute-done((bf16[192,128]{1,0:T(8,128)(2,1)S(1)}, bf16[192,128]{1,0:T(8,128)(2,1)S(1)}, u32[]{:S(2)}, u32[]{:S(2)}) %collective-permute-start.4) | collective-permute-done | bytes 49184 | tf_op jit(solution)/shard_map/ppermute | solution.py:319
  21.2 1.8 %collective-permute-done.5.refs_6_ = bf16[192,128]{1,0:T(8,128)(2,1)S(1)} collective-permute-done((bf16[192,128]{1,0:T(8,128)(2,1)S(1)}, bf16[192,128]{1,0:T(8,128)(2,1)S(1)}, u32[]{:S(2)}, u32[]{:S(2)}) %collective-permute-start.5) | collective-permute-done | bytes 49184 | tf_op jit(solution)/shard_map/ppermute | solution.py:319
  23.0 0.1 fusion.6
  23.1 0.1 collective-permute-start.6
  23.2 1.2 %collective-permute-done.6.refs_7_ = bf16[192,128]{1,0:T(8,128)(2,1)S(1)} collective-permute-done((bf16[192,128]{1,0:T(8,128)(2,1)S(1)}, bf16[192,128]{1,0:T(8,128)(2,1)S(1)}, u32[]{:S(2)}, u32[]{:S(2)}) %collective-permute-start.6) | collective-permute-done | bytes 49184 | tf_op jit(solution)/shard_map/ppermute | solution.py:319
  24.4 0.0 copy-start
  24.4 1.8 %collective-permute-start.7 = (bf16[192,128]{1,0:T(8,128)(2,1)S(1)}, bf16[192,128]{1,0:T(8,128)(2,1)S(1)}, u32[]{:S(2)}, u32[]{:S(2)}) collective-permute-start(bf16[192,128]{1,0:T(8,128)(2,1)S(1)} %fusion.4.after), channel_id=1, source_target_pairs={{0,112},{16,96},{32,80},{48,64},{64,48},{80,32},{96,16},{112,0},{1... | collective-permute-start | bytes 147464 | tf_op jit(solution)/shard_map/ppermute | solution.py:319
  26.2 1.4 %collective-permute-start.8 = (bf16[192,128]{1,0:T(8,128)(2,1)S(1)}, bf16[192,128]{1,0:T(8,128)(2,1)S(1)}, u32[]{:S(2)}, u32[]{:S(2)}) collective-permute-start(bf16[192,128]{1,0:T(8,128)(2,1)S(1)} %fusion.4.after), channel_id=1, source_target_pairs={{0,80},{16,64},{32,112},{48,96},{64,16},{80,0},{96,48},{112,32},{1... | collective-permute-start | bytes 147464 | tf_op jit(solution)/shard_map/ppermute | solution.py:319
  27.6 1.3 %collective-permute-start.9 = (bf16[192,128]{1,0:T(8,128)(2,1)S(1)}, bf16[192,128]{1,0:T(8,128)(2,1)S(1)}, u32[]{:S(2)}, u32[]{:S(2)}) collective-permute-start(bf16[192,128]{1,0:T(8,128)(2,1)S(1)} %fusion.4.after), channel_id=1, source_target_pairs={{0,48},{16,32},{32,16},{48,0},{64,112},{80,96},{96,80},{112,64},{1... | collective-permute-start | bytes 147464 | tf_op jit(solution)/shard_map/ppermute | solution.py:319
  29.0 1.9 %inside.3.high_ref = f32[512,384]{1,0:T(8,128)S(1)} custom-call(bf16[512,768]{1,0:T(8,128)(2,1)S(1)} %query.1.q_ref, bf16[512,768]{1,0:T(8,128)(2,1)S(1)} %get-tuple-element.46.k_ref, bf16[512,768]{1,0:T(8,128)(2,1)S(1)} %get-tuple-element.47.v_ref, f32[9,6]{1,0:T(8,128)S(1)} %copy.7.levels, bf16[192,128]{1,0:T(8,128)(2,1)S(1)} %fusion.4.after), custom_call_target="tpu_custom_call" | custom-call | tf_op jit(solution)/shard_map/inside/pallas_call | solution.py:190
  30.9 0.0 collective-permute-done.7.refs_10_
  30.9 0.0 collective-permute-done.8.refs_9_
  30.9 2.1 %collective-permute-done.9.refs_8_ = bf16[192,128]{1,0:T(8,128)(2,1)S(1)} collective-permute-done((bf16[192,128]{1,0:T(8,128)(2,1)S(1)}, bf16[192,128]{1,0:T(8,128)(2,1)S(1)}, u32[]{:S(2)}, u32[]{:S(2)}) %collective-permute-start.9) | collective-permute-done | bytes 49184 | tf_op jit(solution)/shard_map/ppermute | solution.py:319
  33.1 4.5 %collective-permute-start.10 = (bf16[192,128]{1,0:T(8,128)(2,1)S(1)}, bf16[192,128]{1,0:T(8,128)(2,1)S(1)}, u32[]{:S(2)}, u32[]{:S(2)}) collective-permute-start(bf16[192,128]{1,0:T(8,128)(2,1)S(1)} %add_convert_fusion), channel_id=1, source_target_pairs={{0,208},{16,192},{32,240},{48,224},{64,144},{80,128},{96,176},{112... | collective-permute-start | bytes 147464 | tf_op jit(solution)/shard_map/ppermute | solution.py:319
  37.7 0.8 %gather.1 = (f32[4,192,128]{2,1,0:T(8,128)S(1)}, f32[192,128]{1,0:T(8,128)S(1)}) custom-call(f32[9,6]{1,0:T(8,128)S(1)} %copy.7.levels, bf16[192,128]{1,0:T(8,128)(2,1)S(1)} %get-tuple-element.42.refs_0_, bf16[192,128]{1,0:T(8,128)(2,1)S(1)} %collective-permute-done.1.refs_1_, bf16[192,128]{1,0:T(8,128)(2,1)S(1)} %collective-permute-done.refs_2_, ...), custom_call_target="tpu_custom_call" | custom-call | tf_op jit(solution)/shard_map/gather/pallas_call | solution.py:243
  38.5 1.8 %collective-permute-done.10 = bf16[192,128]{1,0:T(8,128)(2,1)S(1)} collective-permute-done((bf16[192,128]{1,0:T(8,128)(2,1)S(1)}, bf16[192,128]{1,0:T(8,128)(2,1)S(1)}, u32[]{:S(2)}, u32[]{:S(2)}) %collective-permute-start.10) | collective-permute-done | bytes 49184 | tf_op jit(solution)/shard_map/ppermute | solution.py:319
  40.3 0.9 %collective-permute-start.11 = (bf16[192,128]{1,0:T(8,128)(2,1)S(1)}, bf16[192,128]{1,0:T(8,128)(2,1)S(1)}, u32[]{:S(2)}, u32[]{:S(2)}) collective-permute-start(bf16[192,128]{1,0:T(8,128)(2,1)S(1)} %get-tuple-element.70), channel_id=1, source_target_pairs={{0,2},{1,3},{2,0},{3,1},{4,6},{5,7},{6,4},{7,5},{8,10},{9,11},{10,... | collective-permute-start | bytes 147464 | tf_op jit(solution)/shard_map/ppermute | solution.py:319
  41.2 0.7 %collective-permute-start.12 = (bf16[192,128]{1,0:T(8,128)(2,1)S(1)}, bf16[192,128]{1,0:T(8,128)(2,1)S(1)}, u32[]{:S(2)}, u32[]{:S(2)}) collective-permute-start(bf16[192,128]{1,0:T(8,128)(2,1)S(1)} %get-tuple-element.69), channel_id=1, source_target_pairs={{0,1},{1,0},{2,3},{3,2},{4,5},{5,4},{6,7},{7,6},{8,9},{9,8},{10,11... | collective-permute-start | bytes 147464 | tf_op jit(solution)/shard_map/ppermute | solution.py:319
  41.9 2.8 %collective-permute-start.13 = (bf16[192,128]{1,0:T(8,128)(2,1)S(1)}, bf16[192,128]{1,0:T(8,128)(2,1)S(1)}, u32[]{:S(2)}, u32[]{:S(2)}) collective-permute-start(bf16[192,128]{1,0:T(8,128)(2,1)S(1)} %get-tuple-element.68), channel_id=1, source_target_pairs={{0,3},{1,2},{2,1},{3,0},{4,7},{5,6},{6,5},{7,4},{8,11},{9,10},{10,... | collective-permute-start | bytes 147464 | tf_op jit(solution)/shard_map/ppermute | solution.py:319
  44.7 1.7 %collective-permute-done.11.two = bf16[192,128]{1,0:T(8,128)(2,1)S(1)} collective-permute-done((bf16[192,128]{1,0:T(8,128)(2,1)S(1)}, bf16[192,128]{1,0:T(8,128)(2,1)S(1)}, u32[]{:S(2)}, u32[]{:S(2)}) %collective-permute-start.11) | collective-permute-done | bytes 49184 | tf_op jit(solution)/shard_map/ppermute | solution.py:319
  46.4 0.0 collective-permute-done.12.one
  46.4 0.8 %collective-permute-done.13.three = bf16[192,128]{1,0:T(8,128)(2,1)S(1)} collective-permute-done((bf16[192,128]{1,0:T(8,128)(2,1)S(1)}, bf16[192,128]{1,0:T(8,128)(2,1)S(1)}, u32[]{:S(2)}, u32[]{:S(2)}) %collective-permute-start.13) | collective-permute-done | bytes 49184 | tf_op jit(solution)/shard_map/ppermute | solution.py:319
  47.2 0.0 copy-done
  47.2 2.5 %mix.1 = bf16[512,1536]{1,0:T(8,128)(2,1)} custom-call(bf16[512,768]{1,0:T(8,128)(2,1)S(1)} %query.1.q_ref, f32[512,384]{1,0:T(8,128)S(1)} %inside.2.low_ref, f32[512,384]{1,0:T(8,128)S(1)} %inside.3.high_ref, bf16[192,128]{1,0:T(8,128)(2,1)S(1)} %get-tuple-element.61.own, bf16[192,128]{1,0:T(8,128)(2,1)S(1)} %collective-permute-done.12.one, ...), custom_call_target="tpu_custom_call" | custom-call | tf_op jit(solution)/shard_map/mix/pallas_call | solution.py:301
  (4 shorter events, 0.1 us)
Async XLA Ops:
  4.7 6.0 %collective-permute-start = (bf16[192,128]{1,0:T(8,128)(2,1)S(1)}, bf16[192,128]{1,0:T(8,128)(2,1)S(1)}, u32[]{:S(2)}, u32[]{:S(2)}) collective-permute-start(bf16[192,128]{1,0:T(8,128)(2,1)S(1)} %get-tuple-element.35), channel_id=1, source_target_pairs={{0,2},{1,3},{2,0},{3,1},{4,6},{5,7},{6,4},{7,5},{8,10},{9,11},{10,... | collective-permute-start | bytes 147464 | tf_op jit(solution)/shard_map/ppermute | solution.py:319
  8.0 4.1 %collective-permute-start.1 = (bf16[192,128]{1,0:T(8,128)(2,1)S(1)}, bf16[192,128]{1,0:T(8,128)(2,1)S(1)}, u32[]{:S(2)}, u32[]{:S(2)}) collective-permute-start(bf16[192,128]{1,0:T(8,128)(2,1)S(1)} %get-tuple-element.36), channel_id=1, source_target_pairs={{0,1},{1,0},{2,3},{3,2},{4,5},{5,4},{6,7},{7,6},{8,9},{9,8},{10,11... | collective-permute-start | bytes 147464 | tf_op jit(solution)/shard_map/ppermute | solution.py:319
  8.7 5.3 %collective-permute-start.2 = (bf16[192,128]{1,0:T(8,128)(2,1)S(1)}, bf16[192,128]{1,0:T(8,128)(2,1)S(1)}, u32[]{:S(2)}, u32[]{:S(2)}) collective-permute-start(bf16[192,128]{1,0:T(8,128)(2,1)S(1)} %get-tuple-element.37), channel_id=1, source_target_pairs={{0,3},{1,2},{2,1},{3,0},{4,7},{5,6},{6,5},{7,4},{8,11},{9,10},{10,... | collective-permute-start | bytes 147464 | tf_op jit(solution)/shard_map/ppermute | solution.py:319
  9.1 9.2 %copy-start.1 = (f32[9,6]{0,1:T(8,128)S(1)}, f32[9,6]{0,1:T(8,128)}, u32[]{:S(2)}) copy-start(f32[9,6]{0,1:T(8,128)} %param.11) | copy-start | bytes 652
  14.0 6.3 %collective-permute-start.3 = (bf16[192,128]{1,0:T(8,128)(2,1)S(1)}, bf16[192,128]{1,0:T(8,128)(2,1)S(1)}, u32[]{:S(2)}, u32[]{:S(2)}) collective-permute-start(bf16[192,128]{1,0:T(8,128)(2,1)S(1)} %fusion.5.after), channel_id=1, source_target_pairs={{0,8},{1,9},{2,10},{3,11},{4,12},{5,13},{6,14},{7,15},{8,0},{9,1},... | collective-permute-start | bytes 147464 | tf_op jit(solution)/shard_map/ppermute | solution.py:319
  17.1 4.1 %collective-permute-start.4 = (bf16[192,128]{1,0:T(8,128)(2,1)S(1)}, bf16[192,128]{1,0:T(8,128)(2,1)S(1)}, u32[]{:S(2)}, u32[]{:S(2)}) collective-permute-start(bf16[192,128]{1,0:T(8,128)(2,1)S(1)} %fusion.5.after), channel_id=1, source_target_pairs={{0,4},{1,5},{2,6},{3,7},{4,0},{5,1},{6,2},{7,3},{8,12},{9,13},{10,... | collective-permute-start | bytes 147464 | tf_op jit(solution)/shard_map/ppermute | solution.py:319
  17.7 5.3 %collective-permute-start.5 = (bf16[192,128]{1,0:T(8,128)(2,1)S(1)}, bf16[192,128]{1,0:T(8,128)(2,1)S(1)}, u32[]{:S(2)}, u32[]{:S(2)}) collective-permute-start(bf16[192,128]{1,0:T(8,128)(2,1)S(1)} %fusion.5.after), channel_id=1, source_target_pairs={{0,12},{1,13},{2,14},{3,15},{4,8},{5,9},{6,10},{7,11},{8,4},{9,5},... | collective-permute-start | bytes 147464 | tf_op jit(solution)/shard_map/ppermute | solution.py:319
  23.1 1.3 %collective-permute-start.6 = (bf16[192,128]{1,0:T(8,128)(2,1)S(1)}, bf16[192,128]{1,0:T(8,128)(2,1)S(1)}, u32[]{:S(2)}, u32[]{:S(2)}) collective-permute-start(bf16[192,128]{1,0:T(8,128)(2,1)S(1)} %get-tuple-element.65), channel_id=1, source_target_pairs={{0,16},{16,0},{32,48},{48,32},{64,80},{80,64},{96,112},{112,96},{1... | collective-permute-start | bytes 147464 | tf_op jit(solution)/shard_map/ppermute | solution.py:319
  24.4 22.8 %copy-start = (bf16[768,1536]{1,0:T(8,128)(2,1)S(1)}, bf16[768,1536]{1,0:T(8,128)(2,1)}, u32[]{:S(2)}) copy-start(bf16[768,1536]{1,0:T(8,128)(2,1)} %wo.1) | copy-start | bytes 7077892
  24.4 6.5 %collective-permute-start.7 = (bf16[192,128]{1,0:T(8,128)(2,1)S(1)}, bf16[192,128]{1,0:T(8,128)(2,1)S(1)}, u32[]{:S(2)}, u32[]{:S(2)}) collective-permute-start(bf16[192,128]{1,0:T(8,128)(2,1)S(1)} %fusion.4.after), channel_id=1, source_target_pairs={{0,112},{16,96},{32,80},{48,64},{64,48},{80,32},{96,16},{112,0},{1... | collective-permute-start | bytes 147464 | tf_op jit(solution)/shard_map/ppermute | solution.py:319
  26.2 4.7 %collective-permute-start.8 = (bf16[192,128]{1,0:T(8,128)(2,1)S(1)}, bf16[192,128]{1,0:T(8,128)(2,1)S(1)}, u32[]{:S(2)}, u32[]{:S(2)}) collective-permute-start(bf16[192,128]{1,0:T(8,128)(2,1)S(1)} %fusion.4.after), channel_id=1, source_target_pairs={{0,80},{16,64},{32,112},{48,96},{64,16},{80,0},{96,48},{112,32},{1... | collective-permute-start | bytes 147464 | tf_op jit(solution)/shard_map/ppermute | solution.py:319
  27.6 5.4 %collective-permute-start.9 = (bf16[192,128]{1,0:T(8,128)(2,1)S(1)}, bf16[192,128]{1,0:T(8,128)(2,1)S(1)}, u32[]{:S(2)}, u32[]{:S(2)}) collective-permute-start(bf16[192,128]{1,0:T(8,128)(2,1)S(1)} %fusion.4.after), channel_id=1, source_target_pairs={{0,48},{16,32},{32,16},{48,0},{64,112},{80,96},{96,80},{112,64},{1... | collective-permute-start | bytes 147464 | tf_op jit(solution)/shard_map/ppermute | solution.py:319
  33.1 7.2 %collective-permute-start.10 = (bf16[192,128]{1,0:T(8,128)(2,1)S(1)}, bf16[192,128]{1,0:T(8,128)(2,1)S(1)}, u32[]{:S(2)}, u32[]{:S(2)}) collective-permute-start(bf16[192,128]{1,0:T(8,128)(2,1)S(1)} %add_convert_fusion), channel_id=1, source_target_pairs={{0,208},{16,192},{32,240},{48,224},{64,144},{80,128},{96,176},{112... | collective-permute-start | bytes 147464 | tf_op jit(solution)/shard_map/ppermute | solution.py:319
  40.3 6.1 %collective-permute-start.11 = (bf16[192,128]{1,0:T(8,128)(2,1)S(1)}, bf16[192,128]{1,0:T(8,128)(2,1)S(1)}, u32[]{:S(2)}, u32[]{:S(2)}) collective-permute-start(bf16[192,128]{1,0:T(8,128)(2,1)S(1)} %get-tuple-element.70), channel_id=1, source_target_pairs={{0,2},{1,3},{2,0},{3,1},{4,6},{5,7},{6,4},{7,5},{8,10},{9,11},{10,... | collective-permute-start | bytes 147464 | tf_op jit(solution)/shard_map/ppermute | solution.py:319
  41.2 5.2 %collective-permute-start.12 = (bf16[192,128]{1,0:T(8,128)(2,1)S(1)}, bf16[192,128]{1,0:T(8,128)(2,1)S(1)}, u32[]{:S(2)}, u32[]{:S(2)}) collective-permute-start(bf16[192,128]{1,0:T(8,128)(2,1)S(1)} %get-tuple-element.69), channel_id=1, source_target_pairs={{0,1},{1,0},{2,3},{3,2},{4,5},{5,4},{6,7},{7,6},{8,9},{9,8},{10,11... | collective-permute-start | bytes 147464 | tf_op jit(solution)/shard_map/ppermute | solution.py:319
  41.9 5.3 %collective-permute-start.13 = (bf16[192,128]{1,0:T(8,128)(2,1)S(1)}, bf16[192,128]{1,0:T(8,128)(2,1)S(1)}, u32[]{:S(2)}, u32[]{:S(2)}) collective-permute-start(bf16[192,128]{1,0:T(8,128)(2,1)S(1)} %get-tuple-element.68), channel_id=1, source_target_pairs={{0,3},{1,2},{2,1},{3,0},{4,7},{5,6},{6,5},{7,4},{8,11},{9,10},{10,... | collective-permute-start | bytes 147464 | tf_op jit(solution)/shard_map/ppermute | solution.py:319

commit v4 on v3

--- a/solution.py
+++ b/solution.py
@@ -140,22 +140,44 @@
     )(*(pltpu.with_memory_space_constraint(operand, pltpu.HBM) for operand in operands))
 
 
-def query_kernel(width, tok, wq, q_ref):
+def position():
+    member = lax.axis_index("grp")
+    group = lax.axis_index("seq")
+    return member % 4, member // 4, group % 2, group // 2
+
+
+def bit(index, level):
+    return ((index >> level) & 1).astype(F32)
+
+
+def query_kernel(width, tok, wq, levels, q_ref, factors):
     pair = 2 * width
     for j in range(wq.shape[1] // pair):
         columns = slice(j * pair, (j + 1) * pair)
         q_ref[:, columns] = unit_pair(dot(tok[...], wq[:, columns]), width)
-
-
-def query_of(tok, wq, width):
+    x, z = position()[1], position()[3]
+    heads = levels.shape[1]
+    part = factors.shape[1] // heads
+    for head in range(heads):
+        rows = slice(head * part, (head + 1) * part)
+        for slot, (level, present) in enumerate(((2, bit(x, 0)), (3, bit(x, 1)), (7, bit(z, 2)))):
+            value = levels[level + 1, head] * (present * 2.0 ** (-0.5 * level))
+            factors[slot, rows, :] = jnp.full((part, factors.shape[2]), value, F32)
+
+
+def query_of(tok, wq, level_weights, width):
+    rows, inner = tok.shape[0], wq.shape[1]
     return pl.pallas_call(
         functools.partial(query_kernel, width),
-        out_shape=jax.ShapeDtypeStruct((tok.shape[0], wq.shape[1]), BF16),
-        in_specs=[VMEM, VMEM],
-        out_specs=VMEM,
+        out_shape=(
+            jax.ShapeDtypeStruct((rows, inner), BF16),
+            jax.ShapeDtypeStruct((3, inner // QUARTERS, width), F32),
+        ),
+        in_specs=[VMEM, VMEM, SMEM],
+        out_specs=[VMEM, VMEM],
         compiler_params=pltpu.CompilerParams(vmem_limit_bytes=12 << 20),
         name="query",
-    )(tok, wq)
+    )(tok, wq, level_weights)
 
 
 def inside_kernel(width, first, q_ref, k_ref, v_ref, levels, after, inside_ref):
@@ -199,16 +221,10 @@
 
 def gather_kernel(levels, *refs):
     near = refs[:4]
-    x1, x2, x3, other, z1, z2, z3, local_ref, last_ref = refs[4:]
-    member = lax.axis_index("grp")
-    group = lax.axis_index("seq")
-    y, x, core, z = member % 4, member // 4, group % 2, group // 2
+    crossed, mine, z1, z2, z3, local_ref = refs[4:]
+    y, _, core, z = position()
     heads = levels.shape[1]
-    part = last_ref.shape[0] // heads
-
-    def bit(index, level):
-        return ((index >> level) & 1).astype(F32)
-
+    part = mine.shape[0] // heads
     for head in range(heads):
         rows = slice(head * part, (head + 1) * part)
 
@@ -219,9 +235,8 @@
             return ref[rows, :].astype(F32)
 
         far = (
-            factor(2, bit(x, 0)) * read(x1)
-            + factor(3, bit(x, 1)) * (read(x2) + read(x3))
-            + factor(4, bit(core, 0)) * read(other)
+            read(crossed)
+            + factor(4, bit(core ^ 1, 0)) * read(mine)
             + factor(5, bit(z, 0)) * read(z1)
             + factor(6, bit(z, 1)) * (read(z2) + read(z3))
         )
@@ -233,21 +248,15 @@
                 + factor(0, bit(target, 0)) * sides[distance ^ 1]
                 + factor(1, bit(target, 1)) * (sides[distance ^ 2] + sides[distance ^ 3])
             )
-        last_ref[rows, :] = jnp.full(
-            (part, last_ref.shape[1]), factor(7, bit(z, 2)), F32
-        )
 
 
 def gather_of(level_weights, near, others):
     shape = near[0].shape
     return pl.pallas_call(
         gather_kernel,
-        out_shape=(
-            jax.ShapeDtypeStruct((4, *shape), F32),
-            jax.ShapeDtypeStruct(shape, F32),
-        ),
-        in_specs=[SMEM] + [VMEM] * 11,
-        out_specs=[VMEM, VMEM],
+        out_shape=jax.ShapeDtypeStruct((4, *shape), F32),
+        in_specs=[SMEM] + [VMEM] * 9,
+        out_specs=VMEM,
         compiler_params=pltpu.CompilerParams(vmem_limit_bytes=4 << 20),
         name="gather",
     )(level_weights, *near, *others)
@@ -314,13 +323,13 @@
     )(query, *insides, *pieces, w_output)
 
 
-def flip(value, axis, mask):
-    pairs = [(source, source ^ mask) for source in range(lax.axis_size(axis))]
-    return lax.ppermute(value, axis, pairs)
-
-
-def flips(value, axis, masks):
-    return [flip(value, axis, mask) for mask in masks]
+AXES = ("seq", "grp")
+CORE, Y, X, Z = 16, 1, 4, 32
+
+
+def flip(value, mask):
+    devices = lax.axis_size("seq") * lax.axis_size("grp")
+    return lax.ppermute(value, AXES, [(source, source ^ mask) for source in range(devices)])
 
 
 def plus(total, others):
@@ -332,41 +341,49 @@
 def per_device(tokens, w_query, w_key, w_value, w_output, level_weights):
     heads = level_weights.shape[1]
     width = w_query.shape[1] // heads
+    half = heads // 2
     keys, values, tok, wq, *sent = states_of(tokens, w_key, w_value, w_query, heads, width)
-    near = [sent[0]] + [None] * 3
-    for distance in (2, 1, 3):
-        near[distance] = flip(sent[distance], "grp", distance)
-    query = query_of(tok, wq, width)
-    near[2], near[1], near[3], near[0], query = lax.optimization_barrier(
-        (near[2], near[1], near[3], near[0], query)
+    n2, n1, n3, n0 = (
+        flip(sent[2], CORE | 2 * Y),
+        flip(sent[1], CORE | Y),
+        flip(sent[3], CORE | 3 * Y),
+        flip(sent[0], CORE),
     )
-    total = plus(near[0].astype(F32), near[1:])
-
+    query, factors = query_of(tok, wq, level_weights, width)
+    n2, n1, n3, n0, query, factors = lax.optimization_barrier((n2, n1, n3, n0, query, factors))
+    near = (n0, n1, n2, n3)
+    going = plus(n0.astype(F32), near[1:]).astype(BF16)
+
+    x2, x1, x3 = (flip(going, CORE | distance * X) for distance in (2, 1, 3))
+    own = flip(going, CORE)
+    low = inside_of(query, keys, values, level_weights, going, 0, half, width)
+    x2, x1, x3, own, low = lax.optimization_barrier((x2, x1, x3, own, low))
+    total = plus(own.astype(F32), (x1, x2, x3))
+    mine = total.astype(BF16)
+    crossing = (factors[0] * x1.astype(F32) + factors[1] * plus(x2.astype(F32), (x3,))).astype(BF16)
+
+    total = plus(total, (flip(mine, CORE),))
     going = total.astype(BF16)
-    x2, x1, x3 = flips(going, "grp", (8, 4, 12))
-    low = inside_of(query, keys, values, level_weights, going, 0, heads // 2, width)
-    x2, x1, x3, low = lax.optimization_barrier((x2, x1, x3, low))
-    total = plus(total, (x1, x2, x3))
-    (other,) = flips(total.astype(BF16), "seq", (1,))
-    total = plus(total, (other,))
-    going = total.astype(BF16)
-    z3, z2, z1 = flips(going, "seq", (7, 5, 3))
-    high = inside_of(query, keys, values, level_weights, going, heads // 2, heads // 2, width)
-    z3, z2, z1, high = lax.optimization_barrier((z3, z2, z1, high))
+    z3, z2, z1 = (flip(going, CORE | distance * Z) for distance in (3, 2, 1))
+    crossed = flip(crossing, CORE)
+    high = inside_of(query, keys, values, level_weights, going, half, half, width)
+    z3, z2, z1, crossed, high = lax.optimization_barrier((z3, z2, z1, crossed, high))
     total = plus(total, (z1, z2, z3))
-    (past,) = flips(total.astype(BF16), "seq", (13,))
-    gathered, factor = gather_of(level_weights, near, (x1, x2, x3, other, z1, z2, z3))
-    past, gathered, factor = lax.optimization_barrier((past, gathered, factor))
-    back = [
-        (gathered[distance] + factor * past.astype(F32)).astype(BF16) for distance in range(4)
-    ]
-    pieces = [back[0]] + [None] * 3
-    for distance in (2, 1, 3):
-        pieces[distance] = flip(back[distance], "grp", distance)
-    pieces[2], pieces[1], pieces[3], pieces[0] = lax.optimization_barrier(
-        (pieces[2], pieces[1], pieces[3], pieces[0])
+
+    past = flip(total.astype(BF16), CORE | 6 * Z)
+    gathered = gather_of(level_weights, near, (crossed, mine, z1, z2, z3))
+    past, gathered = lax.optimization_barrier((past, gathered))
+    last = factors[2] * past.astype(F32)
+    back = [(gathered[distance] + last).astype(BF16) for distance in range(4)]
+    p2, p1, p3, p0 = lax.optimization_barrier(
+        (
+            flip(back[2], CORE | 2 * Y),
+            flip(back[1], CORE | Y),
+            flip(back[3], CORE | 3 * Y),
+            flip(back[0], CORE),
+        )
     )
-    return mixed_of(query, (low, high), pieces, w_output, width)
+    return mixed_of(query, (low, high), (p0, p1, p2, p3), w_output, width)
 
 
 def solution(mesh):

time: 49.9 us -> 53.8 us (1.078)
  the two profiles are of different devices: /device:TPU:32 before, /device:TPU:1 now
where the time goes in v4:
time: 53.8 us; the launch traced here: 53.7 us
  starting transfers between devices  25.7 us (48%)
  Pallas kernels  14.2 us (26%)
  waiting for transfers between devices  10.1 us (19%)
  local copies, waits for them, and re-layouts  3.19 us (6%)
    ppermute x18, starting transfers between devices, flip(): lax.ppermute(value, AXES, [(source, source ^ mask) for source in range(de...  25.7 us
    ppermute x18, waiting for transfers between devices, flip(): lax.ppermute(value, AXES, [(source, source ^ mask) for source in range(de...  10.1 us
    pallas_call x1, Pallas kernels, states_of(): pl.pallas_call(functools.partial(state_kernel, width), out_shape=(side, s...  4.73 us
    pallas_call x2, Pallas kernels, inside_of(): pl.pallas_call(functools.partial(inside_kernel, width, first), out_shape=...  3.9 us
    unnamed x9, local copies, waits for them, and re-layouts  3.19 us
    pallas_call x1, Pallas kernels, mixed_of(): pl.pallas_call(functools.partial(mix_kernel, width), out_shape=jax.ShapeD...  2.51 us
    pallas_call x1, Pallas kernels, query_of(): pl.pallas_call(functools.partial(query_kernel, width), out_shape=(jax.Sha...  2.27 us
  transfers between devices with their start and end apart: 18, of which 8 were waited for; matrix products, arithmetic and copies ran while one was open for 0% of the time, Pallas kernels for 13%

profile of v4, /device:TPU:1, one launch (start us, length us, event | category | flops | bytes accessed | tf_op | source)
XLA Modules:
  0.0 53.7 jit_solution(10150587872780414062)
XLA Ops:
  0.0 4.7 %states.1 = (bf16[512,768]{1,0:T(8,128)(2,1)S(1)}, bf16[512,768]{1,0:T(8,128)(2,1)S(1)}, bf16[512,1536]{1,0:T(8,128)(2,1)S(1)}, bf16[1536,768]{1,0:T(8,128)(2,1)...) custom-call(bf16[512,1536]{1,0:T(8,128)(2,1)} %tok_hbm.1, ...), custom_call_target="tpu_custom_call" | custom-call | tf_op jit(solution)/shard_map/states/pallas_call | solution.py:127
  4.7 0.0 copy-start.1
  4.8 1.4 %copy-done.1 = bf16[1536,768]{1,0:T(8,128)(2,1)} copy-done((bf16[1536,768]{1,0:T(8,128)(2,1)}, bf16[1536,768]{1,0:T(8,128)(2,1)S(1)}, u32[]{:S(2)}) %copy-start.1) | copy-done | bytes 2359320
  6.2 4.3 %collective-permute-start = (bf16[192,128]{1,0:T(8,128)(2,1)S(1)}, bf16[192,128]{1,0:T(8,128)(2,1)S(1)}, u32[]{:S(2)}, u32[]{:S(2)}) collective-permute-start(bf16[192,128]{1,0:T(8,128)(2,1)S(1)} %get-tuple-element.37), channel_id=1, source_target_pairs={{0,18},{1,19},{2,16},{3,17},{4,22},{5,23},{6,20},{7,21},{8,26},{9,... | collective-permute-start | bytes 147464 | tf_op jit(solution)/shard_map/ppermute | solution.py:332
  10.5 0.1 collective-permute-start.1
  10.6 2.2 %collective-permute-start.2 = (bf16[192,128]{1,0:T(8,128)(2,1)S(1)}, bf16[192,128]{1,0:T(8,128)(2,1)S(1)}, u32[]{:S(2)}, u32[]{:S(2)}) collective-permute-start(bf16[192,128]{1,0:T(8,128)(2,1)S(1)} %get-tuple-element.39), channel_id=1, source_target_pairs={{0,19},{1,18},{2,17},{3,16},{4,23},{5,22},{6,21},{7,20},{8,27},{9,... | collective-permute-start | bytes 147464 | tf_op jit(solution)/shard_map/ppermute | solution.py:332
  12.8 0.0 collective-permute-start.3
  12.8 0.1 copy.7.levels
  12.9 1.7 %copy-done.2 = bf16[1536,768]{1,0:T(8,128)(2,1)S(1)} copy-done((bf16[1536,768]{1,0:T(8,128)(2,1)S(1)}, bf16[1536,768]{1,0:T(8,128)(2,1)}, u32[]{:S(2)}) %copy-start.2) | copy-done | bytes 2359320
  14.6 2.3 %query.1 = (bf16[512,768]{1,0:T(8,128)(2,1)S(1)}, f32[3,192,128]{2,1,0:T(8,128)S(1)}) custom-call(bf16[512,1536]{1,0:T(8,128)(2,1)S(1)} %get-tuple-element.41.tok, bf16[1536,768]{1,0:T(8,128)(2,1)S(1)} %copy-done.2, f32[9,6]{1,0:T(8,128)S(1)} %copy.7.levels), custom_call_target="tpu_custom_call" | custom-call | tf_op jit(solution)/shard_map/query/pallas_call | solution.py:170
  16.9 0.0 collective-permute-done.refs_2_
  16.9 0.0 collective-permute-done.1.refs_1_
  16.9 0.0 collective-permute-done.2.refs_3_
  16.9 0.0 collective-permute-done.3.refs_0_
  17.0 0.6 %collective-permute-start.7 = (bf16[192,128]{1,0:T(8,128)(2,1)S(1)}, bf16[192,128]{1,0:T(8,128)(2,1)S(1)}, u32[]{:S(2)}, u32[]{:S(2)}) collective-permute-start(bf16[192,128]{1,0:T(8,128)(2,1)S(1)} %add_convert_fusion.1.after), channel_id=1, source_target_pairs={{0,16},{1,17},{2,18},{3,19},{4,20},{5,21},{6,22},{7,23},{8,24},{9,... | collective-permute-start | bytes 147464 | tf_op jit(solution)/shard_map/ppermute | solution.py:332
  17.5 1.6 %collective-permute-start.6 = (bf16[192,128]{1,0:T(8,128)(2,1)S(1)}, bf16[192,128]{1,0:T(8,128)(2,1)S(1)}, u32[]{:S(2)}, u32[]{:S(2)}) collective-permute-start(bf16[192,128]{1,0:T(8,128)(2,1)S(1)} %add_convert_fusion.1.after), channel_id=1, source_target_pairs={{0,28},{1,29},{2,30},{3,31},{4,24},{5,25},{6,26},{7,27},{8,20},{9,... | collective-permute-start | bytes 147464 | tf_op jit(solution)/shard_map/ppermute | solution.py:332
  19.1 0.2 collective-permute-start.5
  19.3 2.3 %collective-permute-start.4 = (bf16[192,128]{1,0:T(8,128)(2,1)S(1)}, bf16[192,128]{1,0:T(8,128)(2,1)S(1)}, u32[]{:S(2)}, u32[]{:S(2)}) collective-permute-start(bf16[192,128]{1,0:T(8,128)(2,1)S(1)} %add_convert_fusion.1.after), channel_id=1, source_target_pairs={{0,24},{1,25},{2,26},{3,27},{4,28},{5,29},{6,30},{7,31},{8,16},{9,... | collective-permute-start | bytes 147464 | tf_op jit(solution)/shard_map/ppermute | solution.py:332
  21.7 1.9 %inside.2.low_ref = f32[512,384]{1,0:T(8,128)S(1)} custom-call(bf16[512,768]{1,0:T(8,128)(2,1)S(1)} %get-tuple-element.45.q_ref, bf16[512,768]{1,0:T(8,128)(2,1)S(1)} %get-tuple-element.50.k_ref, bf16[512,768]{1,0:T(8,128)(2,1)S(1)} %get-tuple-element.51.v_ref, f32[9,6]{1,0:T(8,128)S(1)} %copy.7.levels, bf16[192,128]{1,0:T(8,128)(2,1)S(1)} %add_convert_fusion.1.after), custom_call_target="tpu_custom_call" | custom-call | tf_op jit(solution)/shard_map/inside/pallas_call | solution.py:212
  23.6 0.0 collective-permute-done.7
  23.6 0.0 collective-permute-done.6
  23.6 0.0 collective-permute-done.5
  23.7 1.1 %collective-permute-done.4 = bf16[192,128]{1,0:T(8,128)(2,1)S(1)} collective-permute-done((bf16[192,128]{1,0:T(8,128)(2,1)S(1)}, bf16[192,128]{1,0:T(8,128)(2,1)S(1)}, u32[]{:S(2)}, u32[]{:S(2)}) %collective-permute-start.4) | collective-permute-done | bytes 49184 | tf_op jit(solution)/shard_map/ppermute | solution.py:332
  24.8 0.5 collective-permute-start.8
  25.3 0.9 %collective-permute-done.8 = bf16[192,128]{1,0:T(8,128)(2,1)S(1)} collective-permute-done((bf16[192,128]{1,0:T(8,128)(2,1)S(1)}, bf16[192,128]{1,0:T(8,128)(2,1)S(1)}, u32[]{:S(2)}, u32[]{:S(2)}) %collective-permute-start.8) | collective-permute-done | bytes 49184 | tf_op jit(solution)/shard_map/ppermute | solution.py:332
  26.2 0.1 fusion.1
  26.2 0.4 collective-permute-start.12
  26.7 1.2 %collective-permute-start.11 = (bf16[192,128]{1,0:T(8,128)(2,1)S(1)}, bf16[192,128]{1,0:T(8,128)(2,1)S(1)}, u32[]{:S(2)}, u32[]{:S(2)}) collective-permute-start(bf16[192,128]{1,0:T(8,128)(2,1)S(1)} %get-tuple-element.74.after), channel_id=1, source_target_pairs={{0,48},{1,49},{2,50},{3,51},{4,52},{5,53},{6,54},{7,55},{8,56},{9,... | collective-permute-start | bytes 147464 | tf_op jit(solution)/shard_map/ppermute | solution.py:332
  27.9 3.1 %collective-permute-start.10 = (bf16[192,128]{1,0:T(8,128)(2,1)S(1)}, bf16[192,128]{1,0:T(8,128)(2,1)S(1)}, u32[]{:S(2)}, u32[]{:S(2)}) collective-permute-start(bf16[192,128]{1,0:T(8,128)(2,1)S(1)} %get-tuple-element.74.after), channel_id=1, source_target_pairs={{0,80},{1,81},{2,82},{3,83},{4,84},{5,85},{6,86},{7,87},{8,88},{9,... | collective-permute-start | bytes 147464 | tf_op jit(solution)/shard_map/ppermute | solution.py:332
  31.0 0.0 collective-permute-start.9
  31.0 1.9 %inside.3.high_ref = f32[512,384]{1,0:T(8,128)S(1)} custom-call(bf16[512,768]{1,0:T(8,128)(2,1)S(1)} %get-tuple-element.45.q_ref, bf16[512,768]{1,0:T(8,128)(2,1)S(1)} %get-tuple-element.50.k_ref, bf16[512,768]{1,0:T(8,128)(2,1)S(1)} %get-tuple-element.51.v_ref, f32[9,6]{1,0:T(8,128)S(1)} %copy.7.levels, bf16[192,128]{1,0:T(8,128)(2,1)S(1)} %get-tuple-element.74.after), custom_call_target="tpu_custom_call" | custom-call | tf_op jit(solution)/shard_map/inside/pallas_call | solution.py:212
  33.0 0.0 collective-permute-done.12.refs_4_
  33.0 0.0 collective-permute-done.11.refs_6_
  33.0 1.3 %collective-permute-done.10.refs_7_ = bf16[192,128]{1,0:T(8,128)(2,1)S(1)} collective-permute-done((bf16[192,128]{1,0:T(8,128)(2,1)S(1)}, bf16[192,128]{1,0:T(8,128)(2,1)S(1)}, u32[]{:S(2)}, u32[]{:S(2)}) %collective-permute-start.10) | collective-permute-done | bytes 49184 | tf_op jit(solution)/shard_map/ppermute | solution.py:332
  34.3 2.2 %collective-permute-done.9.refs_8_ = bf16[192,128]{1,0:T(8,128)(2,1)S(1)} collective-permute-done((bf16[192,128]{1,0:T(8,128)(2,1)S(1)}, bf16[192,128]{1,0:T(8,128)(2,1)S(1)}, u32[]{:S(2)}, u32[]{:S(2)}) %collective-permute-start.9) | collective-permute-done | bytes 49184 | tf_op jit(solution)/shard_map/ppermute | solution.py:332
  36.4 0.1 add_convert_fusion
  36.5 4.1 %collective-permute-start.13 = (bf16[192,128]{1,0:T(8,128)(2,1)S(1)}, bf16[192,128]{1,0:T(8,128)(2,1)S(1)}, u32[]{:S(2)}, u32[]{:S(2)}) collective-permute-start(bf16[192,128]{1,0:T(8,128)(2,1)S(1)} %add_convert_fusion), channel_id=1, source_target_pairs={{0,208},{1,209},{2,210},{3,211},{4,212},{5,213},{6,214},{7,215},{8... | collective-permute-start | bytes 147464 | tf_op jit(solution)/shard_map/ppermute | solution.py:332
  40.6 0.8 %gather.1 = f32[4,192,128]{2,1,0:T(8,128)S(1)} custom-call(f32[9,6]{1,0:T(8,128)S(1)} %copy.7.levels, bf16[192,128]{1,0:T(8,128)(2,1)S(1)} %collective-permute-done.3.refs_0_, bf16[192,128]{1,0:T(8,128)(2,1)S(1)} %collective-permute-done.1.refs_1_, bf16[192,128]{1,0:T(8,128)(2,1)S(1)} %collective-permute-done.refs_2_, ...), custom_call_target="tpu_custom_call" | custom-call | tf_op jit(solution)/shard_map/gather/pallas_call | solution.py:255
  41.4 1.5 %collective-permute-done.13 = bf16[192,128]{1,0:T(8,128)(2,1)S(1)} collective-permute-done((bf16[192,128]{1,0:T(8,128)(2,1)S(1)}, bf16[192,128]{1,0:T(8,128)(2,1)S(1)}, u32[]{:S(2)}, u32[]{:S(2)}) %collective-permute-start.13) | collective-permute-done | bytes 49184 | tf_op jit(solution)/shard_map/ppermute | solution.py:332
  42.9 0.8 %collective-permute-start.17 = (bf16[192,128]{1,0:T(8,128)(2,1)S(1)}, bf16[192,128]{1,0:T(8,128)(2,1)S(1)}, u32[]{:S(2)}, u32[]{:S(2)}) collective-permute-start(bf16[192,128]{1,0:T(8,128)(2,1)S(1)} %get-tuple-element.69), channel_id=1, source_target_pairs={{0,16},{1,17},{2,18},{3,19},{4,20},{5,21},{6,22},{7,23},{8,24},{9,... | collective-permute-start | bytes 147464 | tf_op jit(solution)/shard_map/ppermute | solution.py:332
  43.8 1.9 %collective-permute-start.16 = (bf16[192,128]{1,0:T(8,128)(2,1)S(1)}, bf16[192,128]{1,0:T(8,128)(2,1)S(1)}, u32[]{:S(2)}, u32[]{:S(2)}) collective-permute-start(bf16[192,128]{1,0:T(8,128)(2,1)S(1)} %get-tuple-element.70), channel_id=1, source_target_pairs={{0,19},{1,18},{2,17},{3,16},{4,23},{5,22},{6,21},{7,20},{8,27},{9,... | collective-permute-start | bytes 147464 | tf_op jit(solution)/shard_map/ppermute | solution.py:332
  45.7 0.2 collective-permute-start.15
  45.8 2.0 %collective-permute-start.14 = (bf16[192,128]{1,0:T(8,128)(2,1)S(1)}, bf16[192,128]{1,0:T(8,128)(2,1)S(1)}, u32[]{:S(2)}, u32[]{:S(2)}) collective-permute-start(bf16[192,128]{1,0:T(8,128)(2,1)S(1)} %get-tuple-element.72), channel_id=1, source_target_pairs={{0,18},{1,19},{2,16},{3,17},{4,22},{5,23},{6,20},{7,21},{8,26},{9,... | collective-permute-start | bytes 147464 | tf_op jit(solution)/shard_map/ppermute | solution.py:332
  47.9 0.0 collective-permute-done.17.own
  47.9 0.6 %collective-permute-done.16.three = bf16[192,128]{1,0:T(8,128)(2,1)S(1)} collective-permute-done((bf16[192,128]{1,0:T(8,128)(2,1)S(1)}, bf16[192,128]{1,0:T(8,128)(2,1)S(1)}, u32[]{:S(2)}, u32[]{:S(2)}) %collective-permute-start.16) | collective-permute-done | bytes 49184 | tf_op jit(solution)/shard_map/ppermute | solution.py:332
  48.5 1.5 %collective-permute-done.15.one = bf16[192,128]{1,0:T(8,128)(2,1)S(1)} collective-permute-done((bf16[192,128]{1,0:T(8,128)(2,1)S(1)}, bf16[192,128]{1,0:T(8,128)(2,1)S(1)}, u32[]{:S(2)}, u32[]{:S(2)}) %collective-permute-start.15) | collective-permute-done | bytes 49184 | tf_op jit(solution)/shard_map/ppermute | solution.py:332
  50.0 1.0 %collective-permute-done.14.two = bf16[192,128]{1,0:T(8,128)(2,1)S(1)} collective-permute-done((bf16[192,128]{1,0:T(8,128)(2,1)S(1)}, bf16[192,128]{1,0:T(8,128)(2,1)S(1)}, u32[]{:S(2)}, u32[]{:S(2)}) %collective-permute-start.14) | collective-permute-done | bytes 49184 | tf_op jit(solution)/shard_map/ppermute | solution.py:332
  51.0 2.5 %mix.1 = bf16[512,1536]{1,0:T(8,128)(2,1)} custom-call(bf16[512,768]{1,0:T(8,128)(2,1)S(1)} %get-tuple-element.45.q_ref, f32[512,384]{1,0:T(8,128)S(1)} %inside.2.low_ref, f32[512,384]{1,0:T(8,128)S(1)} %inside.3.high_ref, bf16[192,128]{1,0:T(8,128)(2,1)S(1)} %collective-permute-done.17.own, bf16[192,128]{1,0:T(8,128)(2,1)S(1)} %collective-permute-done.15.one, ...), custom_call_target="tpu_custom_call" | custom-call | tf_op jit(solution)/shard_map/mix/pallas_call | solution.py:310
  (8 shorter events, 0.1 us)
Async XLA Ops:
  0.0 12.8 %copy-start.3 = (f32[9,6]{0,1:T(8,128)S(1)}, f32[9,6]{0,1:T(8,128)}, u32[]{:S(2)}) copy-start(f32[9,6]{0,1:T(8,128)} %param.11) | copy-start | bytes 652
  4.7 1.4 %copy-start.1 = (bf16[1536,768]{1,0:T(8,128)(2,1)}, bf16[1536,768]{1,0:T(8,128)(2,1)S(1)}, u32[]{:S(2)}) copy-start(bf16[1536,768]{1,0:T(8,128)(2,1)S(1)} %get-tuple-element.42.wq) | copy-start | bytes 7077892
  6.2 10.7 %collective-permute-start = (bf16[192,128]{1,0:T(8,128)(2,1)S(1)}, bf16[192,128]{1,0:T(8,128)(2,1)S(1)}, u32[]{:S(2)}, u32[]{:S(2)}) collective-permute-start(bf16[192,128]{1,0:T(8,128)(2,1)S(1)} %get-tuple-element.37), channel_id=1, source_target_pairs={{0,18},{1,19},{2,16},{3,17},{4,22},{5,23},{6,20},{7,21},{8,26},{9,... | collective-permute-start | bytes 147464 | tf_op jit(solution)/shard_map/ppermute | solution.py:332
  10.5 6.4 %collective-permute-start.1 = (bf16[192,128]{1,0:T(8,128)(2,1)S(1)}, bf16[192,128]{1,0:T(8,128)(2,1)S(1)}, u32[]{:S(2)}, u32[]{:S(2)}) collective-permute-start(bf16[192,128]{1,0:T(8,128)(2,1)S(1)} %get-tuple-element.38), channel_id=1, source_target_pairs={{0,17},{1,16},{2,19},{3,18},{4,21},{5,20},{6,23},{7,22},{8,25},{9,... | collective-permute-start | bytes 147464 | tf_op jit(solution)/shard_map/ppermute | solution.py:332
  10.6 6.3 %collective-permute-start.2 = (bf16[192,128]{1,0:T(8,128)(2,1)S(1)}, bf16[192,128]{1,0:T(8,128)(2,1)S(1)}, u32[]{:S(2)}, u32[]{:S(2)}) collective-permute-start(bf16[192,128]{1,0:T(8,128)(2,1)S(1)} %get-tuple-element.39), channel_id=1, source_target_pairs={{0,19},{1,18},{2,17},{3,16},{4,23},{5,22},{6,21},{7,20},{8,27},{9,... | collective-permute-start | bytes 147464 | tf_op jit(solution)/shard_map/ppermute | solution.py:332
  12.8 4.1 %collective-permute-start.3 = (bf16[192,128]{1,0:T(8,128)(2,1)S(1)}, bf16[192,128]{1,0:T(8,128)(2,1)S(1)}, u32[]{:S(2)}, u32[]{:S(2)}) collective-permute-start(bf16[192,128]{1,0:T(8,128)(2,1)S(1)} %get-tuple-element.40), channel_id=1, source_target_pairs={{0,16},{1,17},{2,18},{3,19},{4,20},{5,21},{6,22},{7,23},{8,24},{9,... | collective-permute-start | bytes 147464 | tf_op jit(solution)/shard_map/ppermute | solution.py:332
  12.9 1.7 %copy-start.2 = (bf16[1536,768]{1,0:T(8,128)(2,1)S(1)}, bf16[1536,768]{1,0:T(8,128)(2,1)}, u32[]{:S(2)}) copy-start(bf16[1536,768]{1,0:T(8,128)(2,1)} %copy-done.1) | copy-start | bytes 7077892
  17.0 6.7 %collective-permute-start.7 = (bf16[192,128]{1,0:T(8,128)(2,1)S(1)}, bf16[192,128]{1,0:T(8,128)(2,1)S(1)}, u32[]{:S(2)}, u32[]{:S(2)}) collective-permute-start(bf16[192,128]{1,0:T(8,128)(2,1)S(1)} %add_convert_fusion.1.after), channel_id=1, source_target_pairs={{0,16},{1,17},{2,18},{3,19},{4,20},{5,21},{6,22},{7,23},{8,24},{9,... | collective-permute-start | bytes 147464 | tf_op jit(solution)/shard_map/ppermute | solution.py:332
  17.5 6.1 %collective-permute-start.6 = (bf16[192,128]{1,0:T(8,128)(2,1)S(1)}, bf16[192,128]{1,0:T(8,128)(2,1)S(1)}, u32[]{:S(2)}, u32[]{:S(2)}) collective-permute-start(bf16[192,128]{1,0:T(8,128)(2,1)S(1)} %add_convert_fusion.1.after), channel_id=1, source_target_pairs={{0,28},{1,29},{2,30},{3,31},{4,24},{5,25},{6,26},{7,27},{8,20},{9,... | collective-permute-start | bytes 147464 | tf_op jit(solution)/shard_map/ppermute | solution.py:332
  19.1 4.5 %collective-permute-start.5 = (bf16[192,128]{1,0:T(8,128)(2,1)S(1)}, bf16[192,128]{1,0:T(8,128)(2,1)S(1)}, u32[]{:S(2)}, u32[]{:S(2)}) collective-permute-start(bf16[192,128]{1,0:T(8,128)(2,1)S(1)} %add_convert_fusion.1.after), channel_id=1, source_target_pairs={{0,20},{1,21},{2,22},{3,23},{4,16},{5,17},{6,18},{7,19},{8,28},{9,... | collective-permute-start | bytes 147464 | tf_op jit(solution)/shard_map/ppermute | solution.py:332
  19.3 5.4 %collective-permute-start.4 = (bf16[192,128]{1,0:T(8,128)(2,1)S(1)}, bf16[192,128]{1,0:T(8,128)(2,1)S(1)}, u32[]{:S(2)}, u32[]{:S(2)}) collective-permute-start(bf16[192,128]{1,0:T(8,128)(2,1)S(1)} %add_convert_fusion.1.after), channel_id=1, source_target_pairs={{0,24},{1,25},{2,26},{3,27},{4,28},{5,29},{6,30},{7,31},{8,16},{9,... | collective-permute-start | bytes 147464 | tf_op jit(solution)/shard_map/ppermute | solution.py:332
  24.8 1.4 %collective-permute-start.8 = (bf16[192,128]{1,0:T(8,128)(2,1)S(1)}, bf16[192,128]{1,0:T(8,128)(2,1)S(1)}, u32[]{:S(2)}, u32[]{:S(2)}) collective-permute-start(bf16[192,128]{1,0:T(8,128)(2,1)S(1)} %fusion.8.refs_5_), channel_id=1, source_target_pairs={{0,16},{1,17},{2,18},{3,19},{4,20},{5,21},{6,22},{7,23},{8,24},{9,... | collective-permute-start | bytes 147464 | tf_op jit(solution)/shard_map/ppermute | solution.py:332
  26.2 6.7 %collective-permute-start.12 = (bf16[192,128]{1,0:T(8,128)(2,1)S(1)}, bf16[192,128]{1,0:T(8,128)(2,1)S(1)}, u32[]{:S(2)}, u32[]{:S(2)}) collective-permute-start(bf16[192,128]{1,0:T(8,128)(2,1)S(1)} %get-tuple-element.73), channel_id=1, source_target_pairs={{0,16},{1,17},{2,18},{3,19},{4,20},{5,21},{6,22},{7,23},{8,24},{9,... | collective-permute-start | bytes 147464 | tf_op jit(solution)/shard_map/ppermute | solution.py:332
  26.7 24.3 %copy-start = (bf16[768,1536]{1,0:T(8,128)(2,1)S(1)}, bf16[768,1536]{1,0:T(8,128)(2,1)}, u32[]{:S(2)}) copy-start(bf16[768,1536]{1,0:T(8,128)(2,1)} %wo.1) | copy-start | bytes 7077892
  26.7 6.3 %collective-permute-start.11 = (bf16[192,128]{1,0:T(8,128)(2,1)S(1)}, bf16[192,128]{1,0:T(8,128)(2,1)S(1)}, u32[]{:S(2)}, u32[]{:S(2)}) collective-permute-start(bf16[192,128]{1,0:T(8,128)(2,1)S(1)} %get-tuple-element.74.after), channel_id=1, source_target_pairs={{0,48},{1,49},{2,50},{3,51},{4,52},{5,53},{6,54},{7,55},{8,56},{9,... | collective-permute-start | bytes 147464 | tf_op jit(solution)/shard_map/ppermute | solution.py:332
  27.9 6.4 %collective-permute-start.10 = (bf16[192,128]{1,0:T(8,128)(2,1)S(1)}, bf16[192,128]{1,0:T(8,128)(2,1)S(1)}, u32[]{:S(2)}, u32[]{:S(2)}) collective-permute-start(bf16[192,128]{1,0:T(8,128)(2,1)S(1)} %get-tuple-element.74.after), channel_id=1, source_target_pairs={{0,80},{1,81},{2,82},{3,83},{4,84},{5,85},{6,86},{7,87},{8,88},{9,... | collective-permute-start | bytes 147464 | tf_op jit(solution)/shard_map/ppermute | solution.py:332
  31.0 5.4 %collective-permute-start.9 = (bf16[192,128]{1,0:T(8,128)(2,1)S(1)}, bf16[192,128]{1,0:T(8,128)(2,1)S(1)}, u32[]{:S(2)}, u32[]{:S(2)}) collective-permute-start(bf16[192,128]{1,0:T(8,128)(2,1)S(1)} %get-tuple-element.74.after), channel_id=1, source_target_pairs={{0,112},{1,113},{2,114},{3,115},{4,116},{5,117},{6,118},{7,119},{8... | collective-permute-start | bytes 147464 | tf_op jit(solution)/shard_map/ppermute | solution.py:332
  36.5 6.4 %collective-permute-start.13 = (bf16[192,128]{1,0:T(8,128)(2,1)S(1)}, bf16[192,128]{1,0:T(8,128)(2,1)S(1)}, u32[]{:S(2)}, u32[]{:S(2)}) collective-permute-start(bf16[192,128]{1,0:T(8,128)(2,1)S(1)} %add_convert_fusion), channel_id=1, source_target_pairs={{0,208},{1,209},{2,210},{3,211},{4,212},{5,213},{6,214},{7,215},{8... | collective-permute-start | bytes 147464 | tf_op jit(solution)/shard_map/ppermute | solution.py:332
  42.9 5.0 %collective-permute-start.17 = (bf16[192,128]{1,0:T(8,128)(2,1)S(1)}, bf16[192,128]{1,0:T(8,128)(2,1)S(1)}, u32[]{:S(2)}, u32[]{:S(2)}) collective-permute-start(bf16[192,128]{1,0:T(8,128)(2,1)S(1)} %get-tuple-element.69), channel_id=1, source_target_pairs={{0,16},{1,17},{2,18},{3,19},{4,20},{5,21},{6,22},{7,23},{8,24},{9,... | collective-permute-start | bytes 147464 | tf_op jit(solution)/shard_map/ppermute | solution.py:332
  43.8 4.7 %collective-permute-start.16 = (bf16[192,128]{1,0:T(8,128)(2,1)S(1)}, bf16[192,128]{1,0:T(8,128)(2,1)S(1)}, u32[]{:S(2)}, u32[]{:S(2)}) collective-permute-start(bf16[192,128]{1,0:T(8,128)(2,1)S(1)} %get-tuple-element.70), channel_id=1, source_target_pairs={{0,19},{1,18},{2,17},{3,16},{4,23},{5,22},{6,21},{7,20},{8,27},{9,... | collective-permute-start | bytes 147464 | tf_op jit(solution)/shard_map/ppermute | solution.py:332
  45.7 4.3 %collective-permute-start.15 = (bf16[192,128]{1,0:T(8,128)(2,1)S(1)}, bf16[192,128]{1,0:T(8,128)(2,1)S(1)}, u32[]{:S(2)}, u32[]{:S(2)}) collective-permute-start(bf16[192,128]{1,0:T(8,128)(2,1)S(1)} %get-tuple-element.71), channel_id=1, source_target_pairs={{0,17},{1,16},{2,19},{3,18},{4,21},{5,20},{6,23},{7,22},{8,25},{9,... | collective-permute-start | bytes 147464 | tf_op jit(solution)/shard_map/ppermute | solution.py:332
  45.8 5.1 %collective-permute-start.14 = (bf16[192,128]{1,0:T(8,128)(2,1)S(1)}, bf16[192,128]{1,0:T(8,128)(2,1)S(1)}, u32[]{:S(2)}, u32[]{:S(2)}) collective-permute-start(bf16[192,128]{1,0:T(8,128)(2,1)S(1)} %get-tuple-element.72), channel_id=1, source_target_pairs={{0,18},{1,19},{2,16},{3,17},{4,22},{5,23},{6,20},{7,21},{8,26},{9,... | collective-permute-start | bytes 147464 | tf_op jit(solution)/shard_map/ppermute | solution.py:332

commit v5 on v4

--- a/solution.py
+++ b/solution.py
@@ -150,34 +150,22 @@
     return ((index >> level) & 1).astype(F32)
 
 
-def query_kernel(width, tok, wq, levels, q_ref, factors):
+def query_kernel(width, tok, wq, q_ref):
     pair = 2 * width
     for j in range(wq.shape[1] // pair):
         columns = slice(j * pair, (j + 1) * pair)
         q_ref[:, columns] = unit_pair(dot(tok[...], wq[:, columns]), width)
-    x, z = position()[1], position()[3]
-    heads = levels.shape[1]
-    part = factors.shape[1] // heads
-    for head in range(heads):
-        rows = slice(head * part, (head + 1) * part)
-        for slot, (level, present) in enumerate(((2, bit(x, 0)), (3, bit(x, 1)), (7, bit(z, 2)))):
-            value = levels[level + 1, head] * (present * 2.0 ** (-0.5 * level))
-            factors[slot, rows, :] = jnp.full((part, factors.shape[2]), value, F32)
-
-
-def query_of(tok, wq, level_weights, width):
-    rows, inner = tok.shape[0], wq.shape[1]
+
+
+def query_of(tok, wq, width):
     return pl.pallas_call(
         functools.partial(query_kernel, width),
-        out_shape=(
-            jax.ShapeDtypeStruct((rows, inner), BF16),
-            jax.ShapeDtypeStruct((3, inner // QUARTERS, width), F32),
-        ),
-        in_specs=[VMEM, VMEM, SMEM],
-        out_specs=[VMEM, VMEM],
+        out_shape=jax.ShapeDtypeStruct((tok.shape[0], wq.shape[1]), BF16),
+        in_specs=[VMEM, VMEM],
+        out_specs=VMEM,
         compiler_params=pltpu.CompilerParams(vmem_limit_bytes=12 << 20),
         name="query",
-    )(tok, wq, level_weights)
+    )(tok, wq)
 
 
 def inside_kernel(width, first, q_ref, k_ref, v_ref, levels, after, inside_ref):
@@ -221,8 +209,8 @@
 
 def gather_kernel(levels, *refs):
     near = refs[:4]
-    crossed, mine, z1, z2, z3, local_ref = refs[4:]
-    y, _, core, z = position()
+    crossed, mine, z1, z2, z3, local_ref, last_ref = refs[4:]
+    y, x, core, z = position()
     heads = levels.shape[1]
     part = mine.shape[0] // heads
     for head in range(heads):
@@ -235,7 +223,8 @@
             return ref[rows, :].astype(F32)
 
         far = (
-            read(crossed)
+            factor(2, bit(x, 0)) * crossed[0, rows, :].astype(F32)
+            + factor(3, bit(x, 1)) * crossed[1, rows, :].astype(F32)
             + factor(4, bit(core ^ 1, 0)) * read(mine)
             + factor(5, bit(z, 0)) * read(z1)
             + factor(6, bit(z, 1)) * (read(z2) + read(z3))
@@ -248,15 +237,16 @@
                 + factor(0, bit(target, 0)) * sides[distance ^ 1]
                 + factor(1, bit(target, 1)) * (sides[distance ^ 2] + sides[distance ^ 3])
             )
+        last_ref[rows, :] = jnp.full((part, last_ref.shape[1]), factor(7, bit(z, 2)), F32)
 
 
 def gather_of(level_weights, near, others):
     shape = near[0].shape
     return pl.pallas_call(
         gather_kernel,
-        out_shape=jax.ShapeDtypeStruct((4, *shape), F32),
+        out_shape=(jax.ShapeDtypeStruct((4, *shape), F32), jax.ShapeDtypeStruct(shape, F32)),
         in_specs=[SMEM] + [VMEM] * 9,
-        out_specs=VMEM,
+        out_specs=[VMEM, VMEM],
         compiler_params=pltpu.CompilerParams(vmem_limit_bytes=4 << 20),
         name="gather",
     )(level_weights, *near, *others)
@@ -349,8 +339,8 @@
         flip(sent[3], CORE | 3 * Y),
         flip(sent[0], CORE),
     )
-    query, factors = query_of(tok, wq, level_weights, width)
-    n2, n1, n3, n0, query, factors = lax.optimization_barrier((n2, n1, n3, n0, query, factors))
+    query = query_of(tok, wq, width)
+    n2, n1, n3, n0, query = lax.optimization_barrier((n2, n1, n3, n0, query))
     near = (n0, n1, n2, n3)
     going = plus(n0.astype(F32), near[1:]).astype(BF16)
 
@@ -360,20 +350,21 @@
     x2, x1, x3, own, low = lax.optimization_barrier((x2, x1, x3, own, low))
     total = plus(own.astype(F32), (x1, x2, x3))
     mine = total.astype(BF16)
-    crossing = (factors[0] * x1.astype(F32) + factors[1] * plus(x2.astype(F32), (x3,))).astype(BF16)
+    crossing = jnp.stack([x1.astype(F32), plus(x2.astype(F32), (x3,))]).astype(BF16)
 
     total = plus(total, (flip(mine, CORE),))
     going = total.astype(BF16)
-    z3, z2, z1 = (flip(going, CORE | distance * Z) for distance in (3, 2, 1))
+    z1, z3, z2 = (flip(going, CORE | distance * Z) for distance in (1, 3, 2))
+    high = inside_of(query, keys, values, level_weights, going, half, half, width)
+    z1, z3, z2, high = lax.optimization_barrier((z1, z3, z2, high))
+    going = plus(total, (z3, z2, z1)).astype(BF16)
+
+    going, crossing = lax.optimization_barrier((going, crossing))
     crossed = flip(crossing, CORE)
-    high = inside_of(query, keys, values, level_weights, going, half, half, width)
-    z3, z2, z1, crossed, high = lax.optimization_barrier((z3, z2, z1, crossed, high))
-    total = plus(total, (z1, z2, z3))
-
-    past = flip(total.astype(BF16), CORE | 6 * Z)
-    gathered = gather_of(level_weights, near, (crossed, mine, z1, z2, z3))
-    past, gathered = lax.optimization_barrier((past, gathered))
-    last = factors[2] * past.astype(F32)
+    past = flip(going, CORE | 6 * Z)
+    gathered, factor = gather_of(level_weights, near, (crossed, mine, z1, z2, z3))
+    past, gathered, factor = lax.optimization_barrier((past, gathered, factor))
+    last = factor * past.astype(F32)
     back = [(gathered[distance] + last).astype(BF16) for distance in range(4)]
     p2, p1, p3, p0 = lax.optimization_barrier(
         (

time: 53.8 us -> 49.6 us (0.922)
  the two profiles are of different devices: /device:TPU:1 before, /device:TPU:32 now
where the time goes in v5:
time: 49.6 us; the launch traced here: 49.2 us
  starting transfers between devices  21.9 us (44%)
  Pallas kernels  13.5 us (27%)
  waiting for transfers between devices  13.2 us (27%)
    ppermute x18, starting transfers between devices, flip(): lax.ppermute(value, AXES, [(source, source ^ mask) for source in range(de...  21.9 us
    ppermute x18, waiting for transfers between devices, flip(): lax.ppermute(value, AXES, [(source, source ^ mask) for source in range(de...  13.2 us
    pallas_call x1, Pallas kernels, states_of(): pl.pallas_call(functools.partial(state_kernel, width), out_shape=(side, s...  4.72 us
    pallas_call x2, Pallas kernels, inside_of(): pl.pallas_call(functools.partial(inside_kernel, width, first), out_shape=...  3.9 us
    pallas_call x1, Pallas kernels, mixed_of(): pl.pallas_call(functools.partial(mix_kernel, width), out_shape=jax.ShapeD...  2.52 us
    pallas_call x1, Pallas kernels, query_of(): pl.pallas_call(functools.partial(query_kernel, width), out_shape=jax.Shap...  1.6 us
  transfers between devices with their start and end apart: 18, of which 9 were waited for; matrix products, arithmetic and copies ran while one was open for 0% of the time, Pallas kernels for 13%

profile of v5, /device:TPU:32, one launch (start us, length us, event | category | flops | bytes accessed | tf_op | source)
XLA Modules:
  0.0 49.2 jit_solution(12912784573142919597)
XLA Ops:
  0.0 4.7 %states.1 = (bf16[512,768]{1,0:T(8,128)(2,1)S(1)}, bf16[512,768]{1,0:T(8,128)(2,1)S(1)}, bf16[512,1536]{1,0:T(8,128)(2,1)S(1)}, bf16[1536,768]{1,0:T(8,128)(2,1)...) custom-call(bf16[512,1536]{1,0:T(8,128)(2,1)} %tok_hbm.1, ...), custom_call_target="tpu_custom_call" | custom-call | tf_op jit(solution)/shard_map/states/pallas_call | solution.py:127
  4.7 2.7 %collective-permute-start = (bf16[192,128]{1,0:T(8,128)(2,1)S(1)}, bf16[192,128]{1,0:T(8,128)(2,1)S(1)}, u32[]{:S(2)}, u32[]{:S(2)}) collective-permute-start(bf16[192,128]{1,0:T(8,128)(2,1)S(1)} %get-tuple-element.38), channel_id=1, source_target_pairs={{0,18},{1,19},{2,16},{3,17},{4,22},{5,23},{6,20},{7,21},{8,26},{9,... | collective-permute-start | bytes 147464 | tf_op jit(solution)/shard_map/ppermute | solution.py:322
  7.4 1.0 %collective-permute-start.1 = (bf16[192,128]{1,0:T(8,128)(2,1)S(1)}, bf16[192,128]{1,0:T(8,128)(2,1)S(1)}, u32[]{:S(2)}, u32[]{:S(2)}) collective-permute-start(bf16[192,128]{1,0:T(8,128)(2,1)S(1)} %get-tuple-element.39), channel_id=1, source_target_pairs={{0,17},{1,16},{2,19},{3,18},{4,21},{5,20},{6,23},{7,22},{8,25},{9,... | collective-permute-start | bytes 147464 | tf_op jit(solution)/shard_map/ppermute | solution.py:322
  8.4 0.4 collective-permute-start.2
  8.8 0.0 collective-permute-start.3
  8.8 0.0 copy-start.1
  8.8 1.6 %query.1.q_ref = bf16[512,768]{1,0:T(8,128)(2,1)S(1)} custom-call(bf16[512,1536]{1,0:T(8,128)(2,1)S(1)} %get-tuple-element.42.tok, bf16[1536,768]{1,0:T(8,128)(2,1)S(1)} %get-tuple-element.43.wq), custom_call_target="tpu_custom_call" | custom-call | tf_op jit(solution)/shard_map/query/pallas_call | solution.py:161
  10.4 0.0 collective-permute-done.refs_2_
  10.4 0.8 %collective-permute-done.1.refs_1_ = bf16[192,128]{1,0:T(8,128)(2,1)S(1)} collective-permute-done((bf16[192,128]{1,0:T(8,128)(2,1)S(1)}, bf16[192,128]{1,0:T(8,128)(2,1)S(1)}, u32[]{:S(2)}, u32[]{:S(2)}) %collective-permute-start.1) | collective-permute-done | bytes 49184 | tf_op jit(solution)/shard_map/ppermute | solution.py:322
  11.2 2.4 %collective-permute-done.2.refs_3_ = bf16[192,128]{1,0:T(8,128)(2,1)S(1)} collective-permute-done((bf16[192,128]{1,0:T(8,128)(2,1)S(1)}, bf16[192,128]{1,0:T(8,128)(2,1)S(1)}, u32[]{:S(2)}, u32[]{:S(2)}) %collective-permute-start.2) | collective-permute-done | bytes 49184 | tf_op jit(solution)/shard_map/ppermute | solution.py:322
  13.6 0.0 collective-permute-done.3.refs_0_
  13.7 2.8 %collective-permute-start.4 = (bf16[192,128]{1,0:T(8,128)(2,1)S(1)}, bf16[192,128]{1,0:T(8,128)(2,1)S(1)}, u32[]{:S(2)}, u32[]{:S(2)}) collective-permute-start(bf16[192,128]{1,0:T(8,128)(2,1)S(1)} %add_convert_fusion.1.after), channel_id=1, source_target_pairs={{0,24},{1,25},{2,26},{3,27},{4,28},{5,29},{6,30},{7,31},{8,16},{9,... | collective-permute-start | bytes 147464 | tf_op jit(solution)/shard_map/ppermute | solution.py:322
  16.5 0.6 %collective-permute-start.5 = (bf16[192,128]{1,0:T(8,128)(2,1)S(1)}, bf16[192,128]{1,0:T(8,128)(2,1)S(1)}, u32[]{:S(2)}, u32[]{:S(2)}) collective-permute-start(bf16[192,128]{1,0:T(8,128)(2,1)S(1)} %add_convert_fusion.1.after), channel_id=1, source_target_pairs={{0,20},{1,21},{2,22},{3,23},{4,16},{5,17},{6,18},{7,19},{8,28},{9,... | collective-permute-start | bytes 147464 | tf_op jit(solution)/shard_map/ppermute | solution.py:322
  17.1 0.6 %collective-permute-start.6 = (bf16[192,128]{1,0:T(8,128)(2,1)S(1)}, bf16[192,128]{1,0:T(8,128)(2,1)S(1)}, u32[]{:S(2)}, u32[]{:S(2)}) collective-permute-start(bf16[192,128]{1,0:T(8,128)(2,1)S(1)} %add_convert_fusion.1.after), channel_id=1, source_target_pairs={{0,28},{1,29},{2,30},{3,31},{4,24},{5,25},{6,26},{7,27},{8,20},{9,... | collective-permute-start | bytes 147464 | tf_op jit(solution)/shard_map/ppermute | solution.py:322
  17.7 0.1 collective-permute-start.7
  17.8 0.0 copy-done.1
  17.8 0.1 copy.7.levels
  17.9 1.9 %inside.2.low_ref = f32[512,384]{1,0:T(8,128)S(1)} custom-call(bf16[512,768]{1,0:T(8,128)(2,1)S(1)} %query.1.q_ref, bf16[512,768]{1,0:T(8,128)(2,1)S(1)} %get-tuple-element.49.k_ref, bf16[512,768]{1,0:T(8,128)(2,1)S(1)} %get-tuple-element.50.v_ref, f32[9,6]{1,0:T(8,128)S(1)} %copy.7.levels, bf16[192,128]{1,0:T(8,128)(2,1)S(1)} %add_convert_fusion.1.after), custom_call_target="tpu_custom_call" | custom-call | tf_op jit(solution)/shard_map/inside/pallas_call | solution.py:200
  19.8 0.0 collective-permute-done.4
  19.8 0.2 collective-permute-done.5
  20.0 2.1 %collective-permute-done.6 = bf16[192,128]{1,0:T(8,128)(2,1)S(1)} collective-permute-done((bf16[192,128]{1,0:T(8,128)(2,1)S(1)}, bf16[192,128]{1,0:T(8,128)(2,1)S(1)}, u32[]{:S(2)}, u32[]{:S(2)}) %collective-permute-start.6) | collective-permute-done | bytes 49184 | tf_op jit(solution)/shard_map/ppermute | solution.py:322
  22.1 0.0 collective-permute-done.7
  22.2 0.2 collective-permute-start.8
  22.4 1.1 %collective-permute-done.8 = bf16[192,128]{1,0:T(8,128)(2,1)S(1)} collective-permute-done((bf16[192,128]{1,0:T(8,128)(2,1)S(1)}, bf16[192,128]{1,0:T(8,128)(2,1)S(1)}, u32[]{:S(2)}, u32[]{:S(2)}) %collective-permute-start.8) | collective-permute-done | bytes 49184 | tf_op jit(solution)/shard_map/ppermute | solution.py:322
  23.5 1.8 %collective-permute-start.10 = (bf16[192,128]{1,0:T(8,128)(2,1)S(1)}, bf16[192,128]{1,0:T(8,128)(2,1)S(1)}, u32[]{:S(2)}, u32[]{:S(2)}) collective-permute-start(bf16[192,128]{1,0:T(8,128)(2,1)S(1)} %get-tuple-element.76.after), channel_id=1, source_target_pairs={{0,112},{1,113},{2,114},{3,115},{4,116},{5,117},{6,118},{7,119},{8... | collective-permute-start | bytes 147464 | tf_op jit(solution)/shard_map/ppermute | solution.py:322
  25.3 1.4 %collective-permute-start.11 = (bf16[192,128]{1,0:T(8,128)(2,1)S(1)}, bf16[192,128]{1,0:T(8,128)(2,1)S(1)}, u32[]{:S(2)}, u32[]{:S(2)}) collective-permute-start(bf16[192,128]{1,0:T(8,128)(2,1)S(1)} %get-tuple-element.76.after), channel_id=1, source_target_pairs={{0,80},{1,81},{2,82},{3,83},{4,84},{5,85},{6,86},{7,87},{8,88},{9,... | collective-permute-start | bytes 147464 | tf_op jit(solution)/shard_map/ppermute | solution.py:322
  26.7 1.3 %collective-permute-start.9 = (bf16[192,128]{1,0:T(8,128)(2,1)S(1)}, bf16[192,128]{1,0:T(8,128)(2,1)S(1)}, u32[]{:S(2)}, u32[]{:S(2)}) collective-permute-start(bf16[192,128]{1,0:T(8,128)(2,1)S(1)} %get-tuple-element.76.after), channel_id=1, source_target_pairs={{0,48},{1,49},{2,50},{3,51},{4,52},{5,53},{6,54},{7,55},{8,56},{9,... | collective-permute-start | bytes 147464 | tf_op jit(solution)/shard_map/ppermute | solution.py:322
  28.1 0.0 copy-start
  28.1 2.0 %inside.3.high_ref = f32[512,384]{1,0:T(8,128)S(1)} custom-call(bf16[512,768]{1,0:T(8,128)(2,1)S(1)} %query.1.q_ref, bf16[512,768]{1,0:T(8,128)(2,1)S(1)} %get-tuple-element.49.k_ref, bf16[512,768]{1,0:T(8,128)(2,1)S(1)} %get-tuple-element.50.v_ref, f32[9,6]{1,0:T(8,128)S(1)} %copy.7.levels, bf16[192,128]{1,0:T(8,128)(2,1)S(1)} %get-tuple-element.76.after), custom_call_target="tpu_custom_call" | custom-call | tf_op jit(solution)/shard_map/inside/pallas_call | solution.py:200
  30.1 0.0 collective-permute-done.10.refs_8_
  30.1 0.0 collective-permute-done.11.refs_7_
  30.1 2.1 %collective-permute-done.9.refs_6_ = bf16[192,128]{1,0:T(8,128)(2,1)S(1)} collective-permute-done((bf16[192,128]{1,0:T(8,128)(2,1)S(1)}, bf16[192,128]{1,0:T(8,128)(2,1)S(1)}, u32[]{:S(2)}, u32[]{:S(2)}) %collective-permute-start.9) | collective-permute-done | bytes 49184 | tf_op jit(solution)/shard_map/ppermute | solution.py:322
  32.2 0.1 add_convert_fusion
  32.2 0.2 collective-permute-start.13
  32.5 4.7 %collective-permute-start.12 = (bf16[192,128]{1,0:T(8,128)(2,1)S(1)}, bf16[192,128]{1,0:T(8,128)(2,1)S(1)}, u32[]{:S(2)}, u32[]{:S(2)}) collective-permute-start(bf16[192,128]{1,0:T(8,128)(2,1)S(1)} %add_convert_fusion), channel_id=1, source_target_pairs={{0,208},{1,209},{2,210},{3,211},{4,212},{5,213},{6,214},{7,215},{8... | collective-permute-start | bytes 147464 | tf_op jit(solution)/shard_map/ppermute | solution.py:322
  37.2 0.0 collective-permute-done.13.refs_4_
  37.2 0.8 %gather.1 = (f32[4,192,128]{2,1,0:T(8,128)S(1)}, f32[192,128]{1,0:T(8,128)S(1)}) custom-call(f32[9,6]{1,0:T(8,128)S(1)} %copy.7.levels, bf16[192,128]{1,0:T(8,128)(2,1)S(1)} %collective-permute-done.3.refs_0_, bf16[192,128]{1,0:T(8,128)(2,1)S(1)} %collective-permute-done.1.refs_1_, bf16[192,128]{1,0:T(8,128)(2,1)S(1)} %collective-permute-done.refs_2_, ...), custom_call_target="tpu_custom_call" | custom-call | tf_op jit(solution)/shard_map/gather/pallas_call | solution.py:245
  38.0 1.8 %collective-permute-done.12 = bf16[192,128]{1,0:T(8,128)(2,1)S(1)} collective-permute-done((bf16[192,128]{1,0:T(8,128)(2,1)S(1)}, bf16[192,128]{1,0:T(8,128)(2,1)S(1)}, u32[]{:S(2)}, u32[]{:S(2)}) %collective-permute-start.12) | collective-permute-done | bytes 49184 | tf_op jit(solution)/shard_map/ppermute | solution.py:322
  39.9 0.8 %collective-permute-start.14 = (bf16[192,128]{1,0:T(8,128)(2,1)S(1)}, bf16[192,128]{1,0:T(8,128)(2,1)S(1)}, u32[]{:S(2)}, u32[]{:S(2)}) collective-permute-start(bf16[192,128]{1,0:T(8,128)(2,1)S(1)} %get-tuple-element.74), channel_id=1, source_target_pairs={{0,18},{1,19},{2,16},{3,17},{4,22},{5,23},{6,20},{7,21},{8,26},{9,... | collective-permute-start | bytes 147464 | tf_op jit(solution)/shard_map/ppermute | solution.py:322
  40.7 0.5 %collective-permute-start.15 = (bf16[192,128]{1,0:T(8,128)(2,1)S(1)}, bf16[192,128]{1,0:T(8,128)(2,1)S(1)}, u32[]{:S(2)}, u32[]{:S(2)}) collective-permute-start(bf16[192,128]{1,0:T(8,128)(2,1)S(1)} %get-tuple-element.73), channel_id=1, source_target_pairs={{0,17},{1,16},{2,19},{3,18},{4,21},{5,20},{6,23},{7,22},{8,25},{9,... | collective-permute-start | bytes 147464 | tf_op jit(solution)/shard_map/ppermute | solution.py:322
  41.2 2.3 %collective-permute-start.16 = (bf16[192,128]{1,0:T(8,128)(2,1)S(1)}, bf16[192,128]{1,0:T(8,128)(2,1)S(1)}, u32[]{:S(2)}, u32[]{:S(2)}) collective-permute-start(bf16[192,128]{1,0:T(8,128)(2,1)S(1)} %get-tuple-element.72), channel_id=1, source_target_pairs={{0,19},{1,18},{2,17},{3,16},{4,23},{5,22},{6,21},{7,20},{8,27},{9,... | collective-permute-start | bytes 147464 | tf_op jit(solution)/shard_map/ppermute | solution.py:322
  43.5 0.4 collective-permute-start.17
  43.9 1.3 %collective-permute-done.14.two = bf16[192,128]{1,0:T(8,128)(2,1)S(1)} collective-permute-done((bf16[192,128]{1,0:T(8,128)(2,1)S(1)}, bf16[192,128]{1,0:T(8,128)(2,1)S(1)}, u32[]{:S(2)}, u32[]{:S(2)}) %collective-permute-start.14) | collective-permute-done | bytes 49184 | tf_op jit(solution)/shard_map/ppermute | solution.py:322
  45.2 0.0 collective-permute-done.15.one
  45.2 1.3 %collective-permute-done.16.three = bf16[192,128]{1,0:T(8,128)(2,1)S(1)} collective-permute-done((bf16[192,128]{1,0:T(8,128)(2,1)S(1)}, bf16[192,128]{1,0:T(8,128)(2,1)S(1)}, u32[]{:S(2)}, u32[]{:S(2)}) %collective-permute-start.16) | collective-permute-done | bytes 49184 | tf_op jit(solution)/shard_map/ppermute | solution.py:322
  46.5 0.0 collective-permute-done.17.own
  46.5 0.0 copy-done
  46.5 2.5 %mix.1 = bf16[512,1536]{1,0:T(8,128)(2,1)} custom-call(bf16[512,768]{1,0:T(8,128)(2,1)S(1)} %query.1.q_ref, f32[512,384]{1,0:T(8,128)S(1)} %inside.2.low_ref, f32[512,384]{1,0:T(8,128)S(1)} %inside.3.high_ref, bf16[192,128]{1,0:T(8,128)(2,1)S(1)} %collective-permute-done.17.own, bf16[192,128]{1,0:T(8,128)(2,1)S(1)} %collective-permute-done.15.one, ...), custom_call_target="tpu_custom_call" | custom-call | tf_op jit(solution)/shard_map/mix/pallas_call | solution.py:300
  (5 shorter events, 0.2 us)
Async XLA Ops:
  4.7 5.7 %collective-permute-start = (bf16[192,128]{1,0:T(8,128)(2,1)S(1)}, bf16[192,128]{1,0:T(8,128)(2,1)S(1)}, u32[]{:S(2)}, u32[]{:S(2)}) collective-permute-start(bf16[192,128]{1,0:T(8,128)(2,1)S(1)} %get-tuple-element.38), channel_id=1, source_target_pairs={{0,18},{1,19},{2,16},{3,17},{4,22},{5,23},{6,20},{7,21},{8,26},{9,... | collective-permute-start | bytes 147464 | tf_op jit(solution)/shard_map/ppermute | solution.py:322
  7.4 3.8 %collective-permute-start.1 = (bf16[192,128]{1,0:T(8,128)(2,1)S(1)}, bf16[192,128]{1,0:T(8,128)(2,1)S(1)}, u32[]{:S(2)}, u32[]{:S(2)}) collective-permute-start(bf16[192,128]{1,0:T(8,128)(2,1)S(1)} %get-tuple-element.39), channel_id=1, source_target_pairs={{0,17},{1,16},{2,19},{3,18},{4,21},{5,20},{6,23},{7,22},{8,25},{9,... | collective-permute-start | bytes 147464 | tf_op jit(solution)/shard_map/ppermute | solution.py:322
  8.4 5.2 %collective-permute-start.2 = (bf16[192,128]{1,0:T(8,128)(2,1)S(1)}, bf16[192,128]{1,0:T(8,128)(2,1)S(1)}, u32[]{:S(2)}, u32[]{:S(2)}) collective-permute-start(bf16[192,128]{1,0:T(8,128)(2,1)S(1)} %get-tuple-element.40), channel_id=1, source_target_pairs={{0,19},{1,18},{2,17},{3,16},{4,23},{5,22},{6,21},{7,20},{8,27},{9,... | collective-permute-start | bytes 147464 | tf_op jit(solution)/shard_map/ppermute | solution.py:322
  8.8 4.9 %collective-permute-start.3 = (bf16[192,128]{1,0:T(8,128)(2,1)S(1)}, bf16[192,128]{1,0:T(8,128)(2,1)S(1)}, u32[]{:S(2)}, u32[]{:S(2)}) collective-permute-start(bf16[192,128]{1,0:T(8,128)(2,1)S(1)} %get-tuple-element.41), channel_id=1, source_target_pairs={{0,16},{1,17},{2,18},{3,19},{4,20},{5,21},{6,22},{7,23},{8,24},{9,... | collective-permute-start | bytes 147464 | tf_op jit(solution)/shard_map/ppermute | solution.py:322
  8.8 9.0 %copy-start.1 = (f32[9,6]{0,1:T(8,128)S(1)}, f32[9,6]{0,1:T(8,128)}, u32[]{:S(2)}) copy-start(f32[9,6]{0,1:T(8,128)} %param.11) | copy-start | bytes 652
  13.7 6.1 %collective-permute-start.4 = (bf16[192,128]{1,0:T(8,128)(2,1)S(1)}, bf16[192,128]{1,0:T(8,128)(2,1)S(1)}, u32[]{:S(2)}, u32[]{:S(2)}) collective-permute-start(bf16[192,128]{1,0:T(8,128)(2,1)S(1)} %add_convert_fusion.1.after), channel_id=1, source_target_pairs={{0,24},{1,25},{2,26},{3,27},{4,28},{5,29},{6,30},{7,31},{8,16},{9,... | collective-permute-start | bytes 147464 | tf_op jit(solution)/shard_map/ppermute | solution.py:322
  16.5 3.5 %collective-permute-start.5 = (bf16[192,128]{1,0:T(8,128)(2,1)S(1)}, bf16[192,128]{1,0:T(8,128)(2,1)S(1)}, u32[]{:S(2)}, u32[]{:S(2)}) collective-permute-start(bf16[192,128]{1,0:T(8,128)(2,1)S(1)} %add_convert_fusion.1.after), channel_id=1, source_target_pairs={{0,20},{1,21},{2,22},{3,23},{4,16},{5,17},{6,18},{7,19},{8,28},{9,... | collective-permute-start | bytes 147464 | tf_op jit(solution)/shard_map/ppermute | solution.py:322
  17.1 5.0 %collective-permute-start.6 = (bf16[192,128]{1,0:T(8,128)(2,1)S(1)}, bf16[192,128]{1,0:T(8,128)(2,1)S(1)}, u32[]{:S(2)}, u32[]{:S(2)}) collective-permute-start(bf16[192,128]{1,0:T(8,128)(2,1)S(1)} %add_convert_fusion.1.after), channel_id=1, source_target_pairs={{0,28},{1,29},{2,30},{3,31},{4,24},{5,25},{6,26},{7,27},{8,20},{9,... | collective-permute-start | bytes 147464 | tf_op jit(solution)/shard_map/ppermute | solution.py:322
  17.7 4.4 %collective-permute-start.7 = (bf16[192,128]{1,0:T(8,128)(2,1)S(1)}, bf16[192,128]{1,0:T(8,128)(2,1)S(1)}, u32[]{:S(2)}, u32[]{:S(2)}) collective-permute-start(bf16[192,128]{1,0:T(8,128)(2,1)S(1)} %add_convert_fusion.1.after), channel_id=1, source_target_pairs={{0,16},{1,17},{2,18},{3,19},{4,20},{5,21},{6,22},{7,23},{8,24},{9,... | collective-permute-start | bytes 147464 | tf_op jit(solution)/shard_map/ppermute | solution.py:322
  22.2 1.3 %collective-permute-start.8 = (bf16[192,128]{1,0:T(8,128)(2,1)S(1)}, bf16[192,128]{1,0:T(8,128)(2,1)S(1)}, u32[]{:S(2)}, u32[]{:S(2)}) collective-permute-start(bf16[192,128]{1,0:T(8,128)(2,1)S(1)} %fusion.7.refs_5_), channel_id=1, source_target_pairs={{0,16},{1,17},{2,18},{3,19},{4,20},{5,21},{6,22},{7,23},{8,24},{9,... | collective-permute-start | bytes 147464 | tf_op jit(solution)/shard_map/ppermute | solution.py:322
  23.5 6.5 %collective-permute-start.10 = (bf16[192,128]{1,0:T(8,128)(2,1)S(1)}, bf16[192,128]{1,0:T(8,128)(2,1)S(1)}, u32[]{:S(2)}, u32[]{:S(2)}) collective-permute-start(bf16[192,128]{1,0:T(8,128)(2,1)S(1)} %get-tuple-element.76.after), channel_id=1, source_target_pairs={{0,112},{1,113},{2,114},{3,115},{4,116},{5,117},{6,118},{7,119},{8... | collective-permute-start | bytes 147464 | tf_op jit(solution)/shard_map/ppermute | solution.py:322
  25.3 4.8 %collective-permute-start.11 = (bf16[192,128]{1,0:T(8,128)(2,1)S(1)}, bf16[192,128]{1,0:T(8,128)(2,1)S(1)}, u32[]{:S(2)}, u32[]{:S(2)}) collective-permute-start(bf16[192,128]{1,0:T(8,128)(2,1)S(1)} %get-tuple-element.76.after), channel_id=1, source_target_pairs={{0,80},{1,81},{2,82},{3,83},{4,84},{5,85},{6,86},{7,87},{8,88},{9,... | collective-permute-start | bytes 147464 | tf_op jit(solution)/shard_map/ppermute | solution.py:322
  26.7 5.4 %collective-permute-start.9 = (bf16[192,128]{1,0:T(8,128)(2,1)S(1)}, bf16[192,128]{1,0:T(8,128)(2,1)S(1)}, u32[]{:S(2)}, u32[]{:S(2)}) collective-permute-start(bf16[192,128]{1,0:T(8,128)(2,1)S(1)} %get-tuple-element.76.after), channel_id=1, source_target_pairs={{0,48},{1,49},{2,50},{3,51},{4,52},{5,53},{6,54},{7,55},{8,56},{9,... | collective-permute-start | bytes 147464 | tf_op jit(solution)/shard_map/ppermute | solution.py:322
  28.1 18.5 %copy-start = (bf16[768,1536]{1,0:T(8,128)(2,1)S(1)}, bf16[768,1536]{1,0:T(8,128)(2,1)}, u32[]{:S(2)}) copy-start(bf16[768,1536]{1,0:T(8,128)(2,1)} %wo.1) | copy-start | bytes 7077892
  32.2 4.9 %collective-permute-start.13 = (bf16[2,192,128]{2,1,0:T(8,128)(2,1)S(1)}, bf16[2,192,128]{2,1,0:T(8,128)(2,1)S(1)}, u32[]{:S(2)}, u32[]{:S(2)}) collective-permute-start(bf16[2,192,128]{2,1,0:T(8,128)(2,1)S(1)} %pad_maximum_fusion), channel_id=1, source_target_pairs={{0,16},{1,17},{2,18},{3,19},{4,20},{5,21},{6,22},{7,23},{8,24},{9,... | collective-permute-start | bytes 294920 | tf_op jit(solution)/shard_map/ppermute | solution.py:322
  32.5 7.4 %collective-permute-start.12 = (bf16[192,128]{1,0:T(8,128)(2,1)S(1)}, bf16[192,128]{1,0:T(8,128)(2,1)S(1)}, u32[]{:S(2)}, u32[]{:S(2)}) collective-permute-start(bf16[192,128]{1,0:T(8,128)(2,1)S(1)} %add_convert_fusion), channel_id=1, source_target_pairs={{0,208},{1,209},{2,210},{3,211},{4,212},{5,213},{6,214},{7,215},{8... | collective-permute-start | bytes 147464 | tf_op jit(solution)/shard_map/ppermute | solution.py:322
  39.9 5.3 %collective-permute-start.14 = (bf16[192,128]{1,0:T(8,128)(2,1)S(1)}, bf16[192,128]{1,0:T(8,128)(2,1)S(1)}, u32[]{:S(2)}, u32[]{:S(2)}) collective-permute-start(bf16[192,128]{1,0:T(8,128)(2,1)S(1)} %get-tuple-element.74), channel_id=1, source_target_pairs={{0,18},{1,19},{2,16},{3,17},{4,22},{5,23},{6,20},{7,21},{8,26},{9,... | collective-permute-start | bytes 147464 | tf_op jit(solution)/shard_map/ppermute | solution.py:322
  40.7 4.6 %collective-permute-start.15 = (bf16[192,128]{1,0:T(8,128)(2,1)S(1)}, bf16[192,128]{1,0:T(8,128)(2,1)S(1)}, u32[]{:S(2)}, u32[]{:S(2)}) collective-permute-start(bf16[192,128]{1,0:T(8,128)(2,1)S(1)} %get-tuple-element.73), channel_id=1, source_target_pairs={{0,17},{1,16},{2,19},{3,18},{4,21},{5,20},{6,23},{7,22},{8,25},{9,... | collective-permute-start | bytes 147464 | tf_op jit(solution)/shard_map/ppermute | solution.py:322
  41.2 5.3 %collective-permute-start.16 = (bf16[192,128]{1,0:T(8,128)(2,1)S(1)}, bf16[192,128]{1,0:T(8,128)(2,1)S(1)}, u32[]{:S(2)}, u32[]{:S(2)}) collective-permute-start(bf16[192,128]{1,0:T(8,128)(2,1)S(1)} %get-tuple-element.72), channel_id=1, source_target_pairs={{0,19},{1,18},{2,17},{3,16},{4,23},{5,22},{6,21},{7,20},{8,27},{9,... | collective-permute-start | bytes 147464 | tf_op jit(solution)/shard_map/ppermute | solution.py:322
  43.5 3.0 %collective-permute-start.17 = (bf16[192,128]{1,0:T(8,128)(2,1)S(1)}, bf16[192,128]{1,0:T(8,128)(2,1)S(1)}, u32[]{:S(2)}, u32[]{:S(2)}) collective-permute-start(bf16[192,128]{1,0:T(8,128)(2,1)S(1)} %get-tuple-element.71), channel_id=1, source_target_pairs={{0,16},{1,17},{2,18},{3,19},{4,20},{5,21},{6,22},{7,23},{8,24},{9,... | collective-permute-start | bytes 147464 | tf_op jit(solution)/shard_map/ppermute | solution.py:322

commit v6 on v5

--- a/solution.py
+++ b/solution.py
@@ -333,21 +333,21 @@
     width = w_query.shape[1] // heads
     half = heads // 2
     keys, values, tok, wq, *sent = states_of(tokens, w_key, w_value, w_query, heads, width)
-    n2, n1, n3, n0 = (
+    n2, n3, n1, n0 = (
         flip(sent[2], CORE | 2 * Y),
+        flip(sent[3], CORE | 3 * Y),
         flip(sent[1], CORE | Y),
-        flip(sent[3], CORE | 3 * Y),
         flip(sent[0], CORE),
     )
     query = query_of(tok, wq, width)
-    n2, n1, n3, n0, query = lax.optimization_barrier((n2, n1, n3, n0, query))
+    n2, n3, n1, n0, query = lax.optimization_barrier((n2, n3, n1, n0, query))
     near = (n0, n1, n2, n3)
     going = plus(n0.astype(F32), near[1:]).astype(BF16)
 
-    x2, x1, x3 = (flip(going, CORE | distance * X) for distance in (2, 1, 3))
+    x2, x3, x1 = (flip(going, CORE | distance * X) for distance in (2, 3, 1))
     own = flip(going, CORE)
     low = inside_of(query, keys, values, level_weights, going, 0, half, width)
-    x2, x1, x3, own, low = lax.optimization_barrier((x2, x1, x3, own, low))
+    x2, x3, x1, own, low = lax.optimization_barrier((x2, x3, x1, own, low))
     total = plus(own.astype(F32), (x1, x2, x3))
     mine = total.astype(BF16)
     crossing = jnp.stack([x1.astype(F32), plus(x2.astype(F32), (x3,))]).astype(BF16)
@@ -356,21 +356,21 @@
     going = total.astype(BF16)
     z1, z3, z2 = (flip(going, CORE | distance * Z) for distance in (1, 3, 2))
     high = inside_of(query, keys, values, level_weights, going, half, half, width)
-    z1, z3, z2, high = lax.optimization_barrier((z1, z3, z2, high))
+    crossed = flip(crossing, CORE)
+    crossed, z3, z2, z1, high = lax.optimization_barrier((crossed, z3, z2, z1, high))
     going = plus(total, (z3, z2, z1)).astype(BF16)
 
     going, crossing = lax.optimization_barrier((going, crossing))
-    crossed = flip(crossing, CORE)
     past = flip(going, CORE | 6 * Z)
     gathered, factor = gather_of(level_weights, near, (crossed, mine, z1, z2, z3))
     past, gathered, factor = lax.optimization_barrier((past, gathered, factor))
     last = factor * past.astype(F32)
     back = [(gathered[distance] + last).astype(BF16) for distance in range(4)]
-    p2, p1, p3, p0 = lax.optimization_barrier(
+    p2, p3, p1, p0 = lax.optimization_barrier(
         (
             flip(back[2], CORE | 2 * Y),
+            flip(back[3], CORE | 3 * Y),
             flip(back[1], CORE | Y),
-            flip(back[3], CORE | 3 * Y),
             flip(back[0], CORE),
         )
     )

time: 49.6 us -> 48.2 us (0.972)
  waiting for transfers between devices: 13.2 us -> 12.3 us
  starting transfers between devices: 21.9 us -> 21.3 us
    ppermute x18, waiting for transfers between devices: 13.2 us -> 12.3 us  [flip(): lax.ppermute(value, AXES, [(source, source ^ mask) for source in range(de...]
    ppermute x18, starting transfers between devices: 21.9 us -> 21.3 us  [flip(): lax.ppermute(value, AXES, [(source, source ^ mask) for source in range(de...]
where the time goes in v6:
time: 48.2 us; the launch traced here: 47.8 us
  starting transfers between devices  21.3 us (44%)
  Pallas kernels  13.6 us (28%)
  waiting for transfers between devices  12.3 us (26%)
    ppermute x18, starting transfers between devices, flip(): lax.ppermute(value, AXES, [(source, source ^ mask) for source in range(de...  21.3 us
    ppermute x18, waiting for transfers between devices, flip(): lax.ppermute(value, AXES, [(source, source ^ mask) for source in range(de...  12.3 us
    pallas_call x1, Pallas kernels, states_of(): pl.pallas_call(functools.partial(state_kernel, width), out_shape=(side, s...  4.72 us
    pallas_call x2, Pallas kernels, inside_of(): pl.pallas_call(functools.partial(inside_kernel, width, first), out_shape=...  3.9 us
    pallas_call x1, Pallas kernels, mixed_of(): pl.pallas_call(functools.partial(mix_kernel, width), out_shape=jax.ShapeD...  2.53 us
    pallas_call x1, Pallas kernels, query_of(): pl.pallas_call(functools.partial(query_kernel, width), out_shape=jax.Shap...  1.6 us
  transfers between devices with their start and end apart: 18, of which 9 were waited for; matrix products, arithmetic and copies ran while one was open for 0% of the time, Pallas kernels for 13%

profile of v6, /device:TPU:32, one launch (start us, length us, event | category | flops | bytes accessed | tf_op | source)
XLA Modules:
  0.0 47.8 jit_solution(16337765944435669280)
XLA Ops:
  0.0 4.7 %states.1 = (bf16[512,768]{1,0:T(8,128)(2,1)S(1)}, bf16[512,768]{1,0:T(8,128)(2,1)S(1)}, bf16[512,1536]{1,0:T(8,128)(2,1)S(1)}, bf16[1536,768]{1,0:T(8,128)(2,1)...) custom-call(bf16[512,1536]{1,0:T(8,128)(2,1)} %tok_hbm.1, ...), custom_call_target="tpu_custom_call" | custom-call | tf_op jit(solution)/shard_map/states/pallas_call | solution.py:127
  4.7 2.7 %collective-permute-start = (bf16[192,128]{1,0:T(8,128)(2,1)S(1)}, bf16[192,128]{1,0:T(8,128)(2,1)S(1)}, u32[]{:S(2)}, u32[]{:S(2)}) collective-permute-start(bf16[192,128]{1,0:T(8,128)(2,1)S(1)} %get-tuple-element.38), channel_id=1, source_target_pairs={{0,18},{1,19},{2,16},{3,17},{4,22},{5,23},{6,20},{7,21},{8,26},{9,... | collective-permute-start | bytes 147464 | tf_op jit(solution)/shard_map/ppermute | solution.py:322
  7.4 1.3 %collective-permute-start.1 = (bf16[192,128]{1,0:T(8,128)(2,1)S(1)}, bf16[192,128]{1,0:T(8,128)(2,1)S(1)}, u32[]{:S(2)}, u32[]{:S(2)}) collective-permute-start(bf16[192,128]{1,0:T(8,128)(2,1)S(1)} %get-tuple-element.39), channel_id=1, source_target_pairs={{0,19},{1,18},{2,17},{3,16},{4,23},{5,22},{6,21},{7,20},{8,27},{9,... | collective-permute-start | bytes 147464 | tf_op jit(solution)/shard_map/ppermute | solution.py:322
  8.8 0.0 collective-permute-start.2
  8.8 0.0 collective-permute-start.3
  8.8 0.0 copy-start.1
  8.8 1.6 %query.1.q_ref = bf16[512,768]{1,0:T(8,128)(2,1)S(1)} custom-call(bf16[512,1536]{1,0:T(8,128)(2,1)S(1)} %get-tuple-element.42.tok, bf16[1536,768]{1,0:T(8,128)(2,1)S(1)} %get-tuple-element.43.wq), custom_call_target="tpu_custom_call" | custom-call | tf_op jit(solution)/shard_map/query/pallas_call | solution.py:161
  10.4 0.0 collective-permute-done.refs_2_
  10.4 1.8 %collective-permute-done.1.refs_3_ = bf16[192,128]{1,0:T(8,128)(2,1)S(1)} collective-permute-done((bf16[192,128]{1,0:T(8,128)(2,1)S(1)}, bf16[192,128]{1,0:T(8,128)(2,1)S(1)}, u32[]{:S(2)}, u32[]{:S(2)}) %collective-permute-start.1) | collective-permute-done | bytes 49184 | tf_op jit(solution)/shard_map/ppermute | solution.py:322
  12.2 0.6 %collective-permute-done.2.refs_1_ = bf16[192,128]{1,0:T(8,128)(2,1)S(1)} collective-permute-done((bf16[192,128]{1,0:T(8,128)(2,1)S(1)}, bf16[192,128]{1,0:T(8,128)(2,1)S(1)}, u32[]{:S(2)}, u32[]{:S(2)}) %collective-permute-start.2) | collective-permute-done | bytes 49184 | tf_op jit(solution)/shard_map/ppermute | solution.py:322
  12.8 0.0 collective-permute-done.3.refs_0_
  12.9 2.8 %collective-permute-start.4 = (bf16[192,128]{1,0:T(8,128)(2,1)S(1)}, bf16[192,128]{1,0:T(8,128)(2,1)S(1)}, u32[]{:S(2)}, u32[]{:S(2)}) collective-permute-start(bf16[192,128]{1,0:T(8,128)(2,1)S(1)} %add_convert_fusion.1.after), channel_id=1, source_target_pairs={{0,24},{1,25},{2,26},{3,27},{4,28},{5,29},{6,30},{7,31},{8,16},{9,... | collective-permute-start | bytes 147464 | tf_op jit(solution)/shard_map/ppermute | solution.py:322
  15.7 1.2 %collective-permute-start.5 = (bf16[192,128]{1,0:T(8,128)(2,1)S(1)}, bf16[192,128]{1,0:T(8,128)(2,1)S(1)}, u32[]{:S(2)}, u32[]{:S(2)}) collective-permute-start(bf16[192,128]{1,0:T(8,128)(2,1)S(1)} %add_convert_fusion.1.after), channel_id=1, source_target_pairs={{0,28},{1,29},{2,30},{3,31},{4,24},{5,25},{6,26},{7,27},{8,20},{9,... | collective-permute-start | bytes 147464 | tf_op jit(solution)/shard_map/ppermute | solution.py:322
  16.8 0.0 collective-permute-start.6
  16.9 0.1 collective-permute-start.7
  16.9 0.0 copy-done.1
  16.9 0.1 copy.7.levels
  17.0 1.9 %inside.2.low_ref = f32[512,384]{1,0:T(8,128)S(1)} custom-call(bf16[512,768]{1,0:T(8,128)(2,1)S(1)} %query.1.q_ref, bf16[512,768]{1,0:T(8,128)(2,1)S(1)} %get-tuple-element.49.k_ref, bf16[512,768]{1,0:T(8,128)(2,1)S(1)} %get-tuple-element.50.v_ref, f32[9,6]{1,0:T(8,128)S(1)} %copy.7.levels, bf16[192,128]{1,0:T(8,128)(2,1)S(1)} %add_convert_fusion.1.after), custom_call_target="tpu_custom_call" | custom-call | tf_op jit(solution)/shard_map/inside/pallas_call | solution.py:200
  19.0 0.0 collective-permute-done.4
  19.0 1.4 %collective-permute-done.5 = bf16[192,128]{1,0:T(8,128)(2,1)S(1)} collective-permute-done((bf16[192,128]{1,0:T(8,128)(2,1)S(1)}, bf16[192,128]{1,0:T(8,128)(2,1)S(1)}, u32[]{:S(2)}, u32[]{:S(2)}) %collective-permute-start.5) | collective-permute-done | bytes 49184 | tf_op jit(solution)/shard_map/ppermute | solution.py:322
  20.4 0.2 collective-permute-done.6
  20.6 0.0 collective-permute-done.7
  20.7 0.3 collective-permute-start.9
  21.0 1.0 %collective-permute-done.9 = bf16[192,128]{1,0:T(8,128)(2,1)S(1)} collective-permute-done((bf16[192,128]{1,0:T(8,128)(2,1)S(1)}, bf16[192,128]{1,0:T(8,128)(2,1)S(1)}, u32[]{:S(2)}, u32[]{:S(2)}) %collective-permute-start.9) | collective-permute-done | bytes 49184 | tf_op jit(solution)/shard_map/ppermute | solution.py:322
  22.0 0.3 collective-permute-start.8
  22.3 0.0 copy-start
  22.3 1.8 %collective-permute-start.10 = (bf16[192,128]{1,0:T(8,128)(2,1)S(1)}, bf16[192,128]{1,0:T(8,128)(2,1)S(1)}, u32[]{:S(2)}, u32[]{:S(2)}) collective-permute-start(bf16[192,128]{1,0:T(8,128)(2,1)S(1)} %get-tuple-element.75.after), channel_id=1, source_target_pairs={{0,112},{1,113},{2,114},{3,115},{4,116},{5,117},{6,118},{7,119},{8... | collective-permute-start | bytes 147464 | tf_op jit(solution)/shard_map/ppermute | solution.py:322
  24.2 1.4 %collective-permute-start.11 = (bf16[192,128]{1,0:T(8,128)(2,1)S(1)}, bf16[192,128]{1,0:T(8,128)(2,1)S(1)}, u32[]{:S(2)}, u32[]{:S(2)}) collective-permute-start(bf16[192,128]{1,0:T(8,128)(2,1)S(1)} %get-tuple-element.75.after), channel_id=1, source_target_pairs={{0,80},{1,81},{2,82},{3,83},{4,84},{5,85},{6,86},{7,87},{8,88},{9,... | collective-permute-start | bytes 147464 | tf_op jit(solution)/shard_map/ppermute | solution.py:322
  25.5 1.3 %collective-permute-start.12 = (bf16[192,128]{1,0:T(8,128)(2,1)S(1)}, bf16[192,128]{1,0:T(8,128)(2,1)S(1)}, u32[]{:S(2)}, u32[]{:S(2)}) collective-permute-start(bf16[192,128]{1,0:T(8,128)(2,1)S(1)} %get-tuple-element.75.after), channel_id=1, source_target_pairs={{0,48},{1,49},{2,50},{3,51},{4,52},{5,53},{6,54},{7,55},{8,56},{9,... | collective-permute-start | bytes 147464 | tf_op jit(solution)/shard_map/ppermute | solution.py:322
  26.8 1.9 %inside.3.high_ref = f32[512,384]{1,0:T(8,128)S(1)} custom-call(bf16[512,768]{1,0:T(8,128)(2,1)S(1)} %query.1.q_ref, bf16[512,768]{1,0:T(8,128)(2,1)S(1)} %get-tuple-element.49.k_ref, bf16[512,768]{1,0:T(8,128)(2,1)S(1)} %get-tuple-element.50.v_ref, f32[9,6]{1,0:T(8,128)S(1)} %copy.7.levels, bf16[192,128]{1,0:T(8,128)(2,1)S(1)} %get-tuple-element.75.after), custom_call_target="tpu_custom_call" | custom-call | tf_op jit(solution)/shard_map/inside/pallas_call | solution.py:200
  28.8 0.0 collective-permute-done.10.refs_8_
  28.8 0.0 collective-permute-done.11.refs_7_
  28.8 2.0 %collective-permute-done.12.refs_6_ = bf16[192,128]{1,0:T(8,128)(2,1)S(1)} collective-permute-done((bf16[192,128]{1,0:T(8,128)(2,1)S(1)}, bf16[192,128]{1,0:T(8,128)(2,1)S(1)}, u32[]{:S(2)}, u32[]{:S(2)}) %collective-permute-start.12) | collective-permute-done | bytes 49184 | tf_op jit(solution)/shard_map/ppermute | solution.py:322
  30.8 0.0 collective-permute-done.8.refs_4_
  30.8 0.1 add_convert_fusion
  30.9 4.6 %collective-permute-start.13 = (bf16[192,128]{1,0:T(8,128)(2,1)S(1)}, bf16[192,128]{1,0:T(8,128)(2,1)S(1)}, u32[]{:S(2)}, u32[]{:S(2)}) collective-permute-start(bf16[192,128]{1,0:T(8,128)(2,1)S(1)} %add_convert_fusion), channel_id=1, source_target_pairs={{0,208},{1,209},{2,210},{3,211},{4,212},{5,213},{6,214},{7,215},{8... | collective-permute-start | bytes 147464 | tf_op jit(solution)/shard_map/ppermute | solution.py:322
  35.5 0.8 %gather.1 = (f32[4,192,128]{2,1,0:T(8,128)S(1)}, f32[192,128]{1,0:T(8,128)S(1)}) custom-call(f32[9,6]{1,0:T(8,128)S(1)} %copy.7.levels, bf16[192,128]{1,0:T(8,128)(2,1)S(1)} %collective-permute-done.3.refs_0_, bf16[192,128]{1,0:T(8,128)(2,1)S(1)} %collective-permute-done.2.refs_1_, bf16[192,128]{1,0:T(8,128)(2,1)S(1)} %collective-permute-done.refs_2_, ...), custom_call_target="tpu_custom_call" | custom-call | tf_op jit(solution)/shard_map/gather/pallas_call | solution.py:245
  36.4 2.1 %collective-permute-done.13 = bf16[192,128]{1,0:T(8,128)(2,1)S(1)} collective-permute-done((bf16[192,128]{1,0:T(8,128)(2,1)S(1)}, bf16[192,128]{1,0:T(8,128)(2,1)S(1)}, u32[]{:S(2)}, u32[]{:S(2)}) %collective-permute-start.13) | collective-permute-done | bytes 49184 | tf_op jit(solution)/shard_map/ppermute | solution.py:322
  38.5 1.0 %collective-permute-start.14 = (bf16[192,128]{1,0:T(8,128)(2,1)S(1)}, bf16[192,128]{1,0:T(8,128)(2,1)S(1)}, u32[]{:S(2)}, u32[]{:S(2)}) collective-permute-start(bf16[192,128]{1,0:T(8,128)(2,1)S(1)} %get-tuple-element.74), channel_id=1, source_target_pairs={{0,18},{1,19},{2,16},{3,17},{4,22},{5,23},{6,20},{7,21},{8,26},{9,... | collective-permute-start | bytes 147464 | tf_op jit(solution)/shard_map/ppermute | solution.py:322
  39.5 1.6 %collective-permute-start.15 = (bf16[192,128]{1,0:T(8,128)(2,1)S(1)}, bf16[192,128]{1,0:T(8,128)(2,1)S(1)}, u32[]{:S(2)}, u32[]{:S(2)}) collective-permute-start(bf16[192,128]{1,0:T(8,128)(2,1)S(1)} %get-tuple-element.73), channel_id=1, source_target_pairs={{0,19},{1,18},{2,17},{3,16},{4,23},{5,22},{6,21},{7,20},{8,27},{9,... | collective-permute-start | bytes 147464 | tf_op jit(solution)/shard_map/ppermute | solution.py:322
  41.1 0.4 collective-permute-start.16
  41.5 0.4 collective-permute-start.17
  42.0 1.9 %collective-permute-done.14.two = bf16[192,128]{1,0:T(8,128)(2,1)S(1)} collective-permute-done((bf16[192,128]{1,0:T(8,128)(2,1)S(1)}, bf16[192,128]{1,0:T(8,128)(2,1)S(1)}, u32[]{:S(2)}, u32[]{:S(2)}) %collective-permute-start.14) | collective-permute-done | bytes 49184 | tf_op jit(solution)/shard_map/ppermute | solution.py:322
  43.9 1.2 %collective-permute-done.15.three = bf16[192,128]{1,0:T(8,128)(2,1)S(1)} collective-permute-done((bf16[192,128]{1,0:T(8,128)(2,1)S(1)}, bf16[192,128]{1,0:T(8,128)(2,1)S(1)}, u32[]{:S(2)}, u32[]{:S(2)}) %collective-permute-start.15) | collective-permute-done | bytes 49184 | tf_op jit(solution)/shard_map/ppermute | solution.py:322
  45.1 0.0 collective-permute-done.16.one
  45.1 0.0 collective-permute-done.17.own
  45.1 0.0 copy-done
  45.1 2.5 %mix.1 = bf16[512,1536]{1,0:T(8,128)(2,1)} custom-call(bf16[512,768]{1,0:T(8,128)(2,1)S(1)} %query.1.q_ref, f32[512,384]{1,0:T(8,128)S(1)} %inside.2.low_ref, f32[512,384]{1,0:T(8,128)S(1)} %inside.3.high_ref, bf16[192,128]{1,0:T(8,128)(2,1)S(1)} %collective-permute-done.17.own, bf16[192,128]{1,0:T(8,128)(2,1)S(1)} %collective-permute-done.16.one, ...), custom_call_target="tpu_custom_call" | custom-call | tf_op jit(solution)/shard_map/mix/pallas_call | solution.py:300
  (5 shorter events, 0.2 us)
Async XLA Ops:
  4.7 5.7 %collective-permute-start = (bf16[192,128]{1,0:T(8,128)(2,1)S(1)}, bf16[192,128]{1,0:T(8,128)(2,1)S(1)}, u32[]{:S(2)}, u32[]{:S(2)}) collective-permute-start(bf16[192,128]{1,0:T(8,128)(2,1)S(1)} %get-tuple-element.38), channel_id=1, source_target_pairs={{0,18},{1,19},{2,16},{3,17},{4,22},{5,23},{6,20},{7,21},{8,26},{9,... | collective-permute-start | bytes 147464 | tf_op jit(solution)/shard_map/ppermute | solution.py:322
  7.4 4.7 %collective-permute-start.1 = (bf16[192,128]{1,0:T(8,128)(2,1)S(1)}, bf16[192,128]{1,0:T(8,128)(2,1)S(1)}, u32[]{:S(2)}, u32[]{:S(2)}) collective-permute-start(bf16[192,128]{1,0:T(8,128)(2,1)S(1)} %get-tuple-element.39), channel_id=1, source_target_pairs={{0,19},{1,18},{2,17},{3,16},{4,23},{5,22},{6,21},{7,20},{8,27},{9,... | collective-permute-start | bytes 147464 | tf_op jit(solution)/shard_map/ppermute | solution.py:322
  8.8 4.0 %collective-permute-start.2 = (bf16[192,128]{1,0:T(8,128)(2,1)S(1)}, bf16[192,128]{1,0:T(8,128)(2,1)S(1)}, u32[]{:S(2)}, u32[]{:S(2)}) collective-permute-start(bf16[192,128]{1,0:T(8,128)(2,1)S(1)} %get-tuple-element.40), channel_id=1, source_target_pairs={{0,17},{1,16},{2,19},{3,18},{4,21},{5,20},{6,23},{7,22},{8,25},{9,... | collective-permute-start | bytes 147464 | tf_op jit(solution)/shard_map/ppermute | solution.py:322
  8.8 4.0 %collective-permute-start.3 = (bf16[192,128]{1,0:T(8,128)(2,1)S(1)}, bf16[192,128]{1,0:T(8,128)(2,1)S(1)}, u32[]{:S(2)}, u32[]{:S(2)}) collective-permute-start(bf16[192,128]{1,0:T(8,128)(2,1)S(1)} %get-tuple-element.41), channel_id=1, source_target_pairs={{0,16},{1,17},{2,18},{3,19},{4,20},{5,21},{6,22},{7,23},{8,24},{9,... | collective-permute-start | bytes 147464 | tf_op jit(solution)/shard_map/ppermute | solution.py:322
  8.8 8.1 %copy-start.1 = (f32[9,6]{0,1:T(8,128)S(1)}, f32[9,6]{0,1:T(8,128)}, u32[]{:S(2)}) copy-start(f32[9,6]{0,1:T(8,128)} %param.11) | copy-start | bytes 652
  12.9 6.1 %collective-permute-start.4 = (bf16[192,128]{1,0:T(8,128)(2,1)S(1)}, bf16[192,128]{1,0:T(8,128)(2,1)S(1)}, u32[]{:S(2)}, u32[]{:S(2)}) collective-permute-start(bf16[192,128]{1,0:T(8,128)(2,1)S(1)} %add_convert_fusion.1.after), channel_id=1, source_target_pairs={{0,24},{1,25},{2,26},{3,27},{4,28},{5,29},{6,30},{7,31},{8,16},{9,... | collective-permute-start | bytes 147464 | tf_op jit(solution)/shard_map/ppermute | solution.py:322
  15.7 4.7 %collective-permute-start.5 = (bf16[192,128]{1,0:T(8,128)(2,1)S(1)}, bf16[192,128]{1,0:T(8,128)(2,1)S(1)}, u32[]{:S(2)}, u32[]{:S(2)}) collective-permute-start(bf16[192,128]{1,0:T(8,128)(2,1)S(1)} %add_convert_fusion.1.after), channel_id=1, source_target_pairs={{0,28},{1,29},{2,30},{3,31},{4,24},{5,25},{6,26},{7,27},{8,20},{9,... | collective-permute-start | bytes 147464 | tf_op jit(solution)/shard_map/ppermute | solution.py:322
  16.8 3.8 %collective-permute-start.6 = (bf16[192,128]{1,0:T(8,128)(2,1)S(1)}, bf16[192,128]{1,0:T(8,128)(2,1)S(1)}, u32[]{:S(2)}, u32[]{:S(2)}) collective-permute-start(bf16[192,128]{1,0:T(8,128)(2,1)S(1)} %add_convert_fusion.1.after), channel_id=1, source_target_pairs={{0,20},{1,21},{2,22},{3,23},{4,16},{5,17},{6,18},{7,19},{8,28},{9,... | collective-permute-start | bytes 147464 | tf_op jit(solution)/shard_map/ppermute | solution.py:322
  16.9 3.8 %collective-permute-start.7 = (bf16[192,128]{1,0:T(8,128)(2,1)S(1)}, bf16[192,128]{1,0:T(8,128)(2,1)S(1)}, u32[]{:S(2)}, u32[]{:S(2)}) collective-permute-start(bf16[192,128]{1,0:T(8,128)(2,1)S(1)} %add_convert_fusion.1.after), channel_id=1, source_target_pairs={{0,16},{1,17},{2,18},{3,19},{4,20},{5,21},{6,22},{7,23},{8,24},{9,... | collective-permute-start | bytes 147464 | tf_op jit(solution)/shard_map/ppermute | solution.py:322
  20.7 1.3 %collective-permute-start.9 = (bf16[192,128]{1,0:T(8,128)(2,1)S(1)}, bf16[192,128]{1,0:T(8,128)(2,1)S(1)}, u32[]{:S(2)}, u32[]{:S(2)}) collective-permute-start(bf16[192,128]{1,0:T(8,128)(2,1)S(1)} %fusion.7.refs_5_), channel_id=1, source_target_pairs={{0,16},{1,17},{2,18},{3,19},{4,20},{5,21},{6,22},{7,23},{8,24},{9,... | collective-permute-start | bytes 147464 | tf_op jit(solution)/shard_map/ppermute | solution.py:322
  22.0 8.8 %collective-permute-start.8 = (bf16[2,192,128]{2,1,0:T(8,128)(2,1)S(1)}, bf16[2,192,128]{2,1,0:T(8,128)(2,1)S(1)}, u32[]{:S(2)}, u32[]{:S(2)}) collective-permute-start(bf16[2,192,128]{2,1,0:T(8,128)(2,1)S(1)} %pad_maximum_fusion), channel_id=1, source_target_pairs={{0,16},{1,17},{2,18},{3,19},{4,20},{5,21},{6,22},{7,23},{8,24},{9,... | collective-permute-start | bytes 294920 | tf_op jit(solution)/shard_map/ppermute | solution.py:322
  22.3 22.7 %copy-start = (bf16[768,1536]{1,0:T(8,128)(2,1)S(1)}, bf16[768,1536]{1,0:T(8,128)(2,1)}, u32[]{:S(2)}) copy-start(bf16[768,1536]{1,0:T(8,128)(2,1)} %wo.1) | copy-start | bytes 7077892
  22.3 6.4 %collective-permute-start.10 = (bf16[192,128]{1,0:T(8,128)(2,1)S(1)}, bf16[192,128]{1,0:T(8,128)(2,1)S(1)}, u32[]{:S(2)}, u32[]{:S(2)}) collective-permute-start(bf16[192,128]{1,0:T(8,128)(2,1)S(1)} %get-tuple-element.75.after), channel_id=1, source_target_pairs={{0,112},{1,113},{2,114},{3,115},{4,116},{5,117},{6,118},{7,119},{8... | collective-permute-start | bytes 147464 | tf_op jit(solution)/shard_map/ppermute | solution.py:322
  24.2 4.6 %collective-permute-start.11 = (bf16[192,128]{1,0:T(8,128)(2,1)S(1)}, bf16[192,128]{1,0:T(8,128)(2,1)S(1)}, u32[]{:S(2)}, u32[]{:S(2)}) collective-permute-start(bf16[192,128]{1,0:T(8,128)(2,1)S(1)} %get-tuple-element.75.after), channel_id=1, source_target_pairs={{0,80},{1,81},{2,82},{3,83},{4,84},{5,85},{6,86},{7,87},{8,88},{9,... | collective-permute-start | bytes 147464 | tf_op jit(solution)/shard_map/ppermute | solution.py:322
  25.5 5.3 %collective-permute-start.12 = (bf16[192,128]{1,0:T(8,128)(2,1)S(1)}, bf16[192,128]{1,0:T(8,128)(2,1)S(1)}, u32[]{:S(2)}, u32[]{:S(2)}) collective-permute-start(bf16[192,128]{1,0:T(8,128)(2,1)S(1)} %get-tuple-element.75.after), channel_id=1, source_target_pairs={{0,48},{1,49},{2,50},{3,51},{4,52},{5,53},{6,54},{7,55},{8,56},{9,... | collective-permute-start | bytes 147464 | tf_op jit(solution)/shard_map/ppermute | solution.py:322
  30.9 7.6 %collective-permute-start.13 = (bf16[192,128]{1,0:T(8,128)(2,1)S(1)}, bf16[192,128]{1,0:T(8,128)(2,1)S(1)}, u32[]{:S(2)}, u32[]{:S(2)}) collective-permute-start(bf16[192,128]{1,0:T(8,128)(2,1)S(1)} %add_convert_fusion), channel_id=1, source_target_pairs={{0,208},{1,209},{2,210},{3,211},{4,212},{5,213},{6,214},{7,215},{8... | collective-permute-start | bytes 147464 | tf_op jit(solution)/shard_map/ppermute | solution.py:322
  38.5 5.3 %collective-permute-start.14 = (bf16[192,128]{1,0:T(8,128)(2,1)S(1)}, bf16[192,128]{1,0:T(8,128)(2,1)S(1)}, u32[]{:S(2)}, u32[]{:S(2)}) collective-permute-start(bf16[192,128]{1,0:T(8,128)(2,1)S(1)} %get-tuple-element.74), channel_id=1, source_target_pairs={{0,18},{1,19},{2,16},{3,17},{4,22},{5,23},{6,20},{7,21},{8,26},{9,... | collective-permute-start | bytes 147464 | tf_op jit(solution)/shard_map/ppermute | solution.py:322
  39.5 5.5 %collective-permute-start.15 = (bf16[192,128]{1,0:T(8,128)(2,1)S(1)}, bf16[192,128]{1,0:T(8,128)(2,1)S(1)}, u32[]{:S(2)}, u32[]{:S(2)}) collective-permute-start(bf16[192,128]{1,0:T(8,128)(2,1)S(1)} %get-tuple-element.73), channel_id=1, source_target_pairs={{0,19},{1,18},{2,17},{3,16},{4,23},{5,22},{6,21},{7,20},{8,27},{9,... | collective-permute-start | bytes 147464 | tf_op jit(solution)/shard_map/ppermute | solution.py:322
  41.1 3.9 %collective-permute-start.16 = (bf16[192,128]{1,0:T(8,128)(2,1)S(1)}, bf16[192,128]{1,0:T(8,128)(2,1)S(1)}, u32[]{:S(2)}, u32[]{:S(2)}) collective-permute-start(bf16[192,128]{1,0:T(8,128)(2,1)S(1)} %get-tuple-element.72), channel_id=1, source_target_pairs={{0,17},{1,16},{2,19},{3,18},{4,21},{5,20},{6,23},{7,22},{8,25},{9,... | collective-permute-start | bytes 147464 | tf_op jit(solution)/shard_map/ppermute | solution.py:322
  41.5 3.5 %collective-permute-start.17 = (bf16[192,128]{1,0:T(8,128)(2,1)S(1)}, bf16[192,128]{1,0:T(8,128)(2,1)S(1)}, u32[]{:S(2)}, u32[]{:S(2)}) collective-permute-start(bf16[192,128]{1,0:T(8,128)(2,1)S(1)} %get-tuple-element.71), channel_id=1, source_target_pairs={{0,16},{1,17},{2,18},{3,19},{4,20},{5,21},{6,22},{7,23},{8,24},{9,... | collective-permute-start | bytes 147464 | tf_op jit(solution)/shard_map/ppermute | solution.py:322

commit v7 on v6

--- a/solution.py
+++ b/solution.py
@@ -263,33 +263,53 @@
         slices[y ^ distance] = source[...]
     half = inner // 2
     zero = jnp.zeros((width, width), BF16)
-    for j in range(inner // pair):
+    pairs = inner // pair
+
+    def states(j):
         halves = []
-        insides = []
         for side in range(2):
             head = 2 * j + side
             state = jnp.concatenate(
                 [slices[q, head * part : (head + 1) * part, :] for q in range(QUARTERS)], 0
             )
             halves.append(jnp.concatenate([zero, state] if side else [state, zero], 1))
-            start = head * width
-            insides.append(
-                low_ref[:, start : start + width]
-                if start < half
-                else high_ref[:, start - half : start - half + width]
-            )
-        columns = slice(j * pair, (j + 1) * pair)
-        earlier = dot(q_ref[:, columns], jnp.concatenate(halves, 0))
-        attended[:, columns] = (jnp.concatenate(insides, 1) + earlier).astype(BF16)
-    steps = sems.shape[0]
+        return jnp.concatenate(halves, 0)
+
+    def inside(here, start):
+        ref, start = (low_ref, start) if start < half else (high_ref, start - half)
+        return ref[here, start : start + width]
+
+    blocks = 2
+    height = rows // blocks
+    steps = sems.shape[0] // blocks
     block = out.shape[1] // steps
     copies = []
-    for i in range(steps):
-        columns = pl.ds(i * block, block)
-        out[:, columns] = dot(attended[...], wo[:, columns]).astype(BF16)
-        copy = pltpu.make_async_copy(out.at[:, columns], out_hbm.at[:, columns], sems.at[i])
-        copy.start()
-        copies.append(copy)
+
+    def attend(i):
+        here = slice(i * height, (i + 1) * height)
+        for j in range(pairs):
+            columns = slice(j * pair, (j + 1) * pair)
+            within = jnp.concatenate(
+                [inside(here, j * pair), inside(here, j * pair + width)], 1
+            )
+            attended[here, columns] = (within + dot(q_ref[here, columns], states(j))).astype(BF16)
+
+    def project(i):
+        here = pl.ds(i * height, height)
+        for step in range(steps):
+            columns = pl.ds(step * block, block)
+            out[here, columns] = dot(attended[here, :], wo[:, columns]).astype(BF16)
+            copy = pltpu.make_async_copy(
+                out.at[here, columns], out_hbm.at[here, columns], sems.at[len(copies)]
+            )
+            copy.start()
+            copies.append(copy)
+
+    attend(0)
+    for i in range(blocks):
+        if i + 1 < blocks:
+            attend(i + 1)
+        project(i)
     for copy in copies:
         copy.wait()
 
@@ -356,8 +376,9 @@
     going = total.astype(BF16)
     z1, z3, z2 = (flip(going, CORE | distance * Z) for distance in (1, 3, 2))
     high = inside_of(query, keys, values, level_weights, going, half, half, width)
+    crossing, high = lax.optimization_barrier((crossing, high))
     crossed = flip(crossing, CORE)
-    crossed, z3, z2, z1, high = lax.optimization_barrier((crossed, z3, z2, z1, high))
+    z1, z3, z2, high = lax.optimization_barrier((z1, z3, z2, high))
     going = plus(total, (z3, z2, z1)).astype(BF16)
 
     going, crossing = lax.optimization_barrier((going, crossing))

time: 48.2 us -> 47.3 us (0.981)
  waiting for transfers between devices: 12.3 us -> 11.8 us
    ppermute x18, waiting for transfers between devices: 12.3 us -> 11.8 us  [flip(): lax.ppermute(value, AXES, [(source, source ^ mask) for source in range(de...]
  transfers between devices with their start and end apart: 18 -> 18, of which waited for: 9 -> 10; matrix products, arithmetic and copies ran while one was open for 0% -> 0% of each run, Pallas kernels for 13% -> 13%
where the time goes in v7:
time: 47.3 us; the launch traced here: 47 us
  starting transfers between devices  21.2 us (45%)
  Pallas kernels  13.4 us (28%)
  waiting for transfers between devices  11.8 us (25%)
    ppermute x18, starting transfers between devices, flip(): lax.ppermute(value, AXES, [(source, source ^ mask) for source in range(de...  21.2 us
    ppermute x18, waiting for transfers between devices, flip(): lax.ppermute(value, AXES, [(source, source ^ mask) for source in range(de...  11.8 us
    pallas_call x1, Pallas kernels, states_of(): pl.pallas_call(functools.partial(state_kernel, width), out_shape=(side, s...  4.72 us
    pallas_call x2, Pallas kernels, inside_of(): pl.pallas_call(functools.partial(inside_kernel, width, first), out_shape=...  3.9 us
    pallas_call x1, Pallas kernels, mixed_of(): pl.pallas_call(functools.partial(mix_kernel, width), out_shape=jax.ShapeD...  2.37 us
    pallas_call x1, Pallas kernels, query_of(): pl.pallas_call(functools.partial(query_kernel, width), out_shape=jax.Shap...  1.6 us
  transfers between devices with their start and end apart: 18, of which 10 were waited for; matrix products, arithmetic and copies ran while one was open for 0% of the time, Pallas kernels for 13%

profile of v7, /device:TPU:32, one launch (start us, length us, event | category | flops | bytes accessed | tf_op | source)
XLA Modules:
  0.0 47.0 jit_solution(13711101427227833089)
XLA Ops:
  0.0 4.7 %states.1 = (bf16[512,768]{1,0:T(8,128)(2,1)S(1)}, bf16[512,768]{1,0:T(8,128)(2,1)S(1)}, bf16[512,1536]{1,0:T(8,128)(2,1)S(1)}, bf16[1536,768]{1,0:T(8,128)(2,1)...) custom-call(bf16[512,1536]{1,0:T(8,128)(2,1)} %tok_hbm.1, ...), custom_call_target="tpu_custom_call" | custom-call | tf_op jit(solution)/shard_map/states/pallas_call | solution.py:127
  4.7 2.7 %collective-permute-start = (bf16[192,128]{1,0:T(8,128)(2,1)S(1)}, bf16[192,128]{1,0:T(8,128)(2,1)S(1)}, u32[]{:S(2)}, u32[]{:S(2)}) collective-permute-start(bf16[192,128]{1,0:T(8,128)(2,1)S(1)} %get-tuple-element.39), channel_id=1, source_target_pairs={{0,18},{1,19},{2,16},{3,17},{4,22},{5,23},{6,20},{7,21},{8,26},{9,... | collective-permute-start | bytes 147464 | tf_op jit(solution)/shard_map/ppermute | solution.py:342
  7.4 1.3 %collective-permute-start.1 = (bf16[192,128]{1,0:T(8,128)(2,1)S(1)}, bf16[192,128]{1,0:T(8,128)(2,1)S(1)}, u32[]{:S(2)}, u32[]{:S(2)}) collective-permute-start(bf16[192,128]{1,0:T(8,128)(2,1)S(1)} %get-tuple-element.40), channel_id=1, source_target_pairs={{0,19},{1,18},{2,17},{3,16},{4,23},{5,22},{6,21},{7,20},{8,27},{9,... | collective-permute-start | bytes 147464 | tf_op jit(solution)/shard_map/ppermute | solution.py:342
  8.8 0.0 collective-permute-start.2
  8.8 0.0 collective-permute-start.3
  8.8 0.0 copy-start.1
  8.8 1.6 %query.1.q_ref = bf16[512,768]{1,0:T(8,128)(2,1)S(1)} custom-call(bf16[512,1536]{1,0:T(8,128)(2,1)S(1)} %get-tuple-element.43.tok, bf16[1536,768]{1,0:T(8,128)(2,1)S(1)} %get-tuple-element.44.wq), custom_call_target="tpu_custom_call" | custom-call | tf_op jit(solution)/shard_map/query/pallas_call | solution.py:161
  10.4 0.0 collective-permute-done.refs_2_
  10.4 1.8 %collective-permute-done.1.refs_3_ = bf16[192,128]{1,0:T(8,128)(2,1)S(1)} collective-permute-done((bf16[192,128]{1,0:T(8,128)(2,1)S(1)}, bf16[192,128]{1,0:T(8,128)(2,1)S(1)}, u32[]{:S(2)}, u32[]{:S(2)}) %collective-permute-start.1) | collective-permute-done | bytes 49184 | tf_op jit(solution)/shard_map/ppermute | solution.py:342
  12.2 0.6 %collective-permute-done.2.refs_1_ = bf16[192,128]{1,0:T(8,128)(2,1)S(1)} collective-permute-done((bf16[192,128]{1,0:T(8,128)(2,1)S(1)}, bf16[192,128]{1,0:T(8,128)(2,1)S(1)}, u32[]{:S(2)}, u32[]{:S(2)}) %collective-permute-start.2) | collective-permute-done | bytes 49184 | tf_op jit(solution)/shard_map/ppermute | solution.py:342
  12.8 0.0 collective-permute-done.3.refs_0_
  12.9 2.8 %collective-permute-start.4 = (bf16[192,128]{1,0:T(8,128)(2,1)S(1)}, bf16[192,128]{1,0:T(8,128)(2,1)S(1)}, u32[]{:S(2)}, u32[]{:S(2)}) collective-permute-start(bf16[192,128]{1,0:T(8,128)(2,1)S(1)} %add_convert_fusion.1.after), channel_id=1, source_target_pairs={{0,24},{1,25},{2,26},{3,27},{4,28},{5,29},{6,30},{7,31},{8,16},{9,... | collective-permute-start | bytes 147464 | tf_op jit(solution)/shard_map/ppermute | solution.py:342
  15.7 1.2 %collective-permute-start.5 = (bf16[192,128]{1,0:T(8,128)(2,1)S(1)}, bf16[192,128]{1,0:T(8,128)(2,1)S(1)}, u32[]{:S(2)}, u32[]{:S(2)}) collective-permute-start(bf16[192,128]{1,0:T(8,128)(2,1)S(1)} %add_convert_fusion.1.after), channel_id=1, source_target_pairs={{0,28},{1,29},{2,30},{3,31},{4,24},{5,25},{6,26},{7,27},{8,20},{9,... | collective-permute-start | bytes 147464 | tf_op jit(solution)/shard_map/ppermute | solution.py:342
  16.8 0.0 collective-permute-start.6
  16.9 0.1 collective-permute-start.7
  16.9 0.0 copy-done.1
  16.9 0.1 copy.7.levels
  17.0 1.9 %inside.2.low_ref = f32[512,384]{1,0:T(8,128)S(1)} custom-call(bf16[512,768]{1,0:T(8,128)(2,1)S(1)} %query.1.q_ref, bf16[512,768]{1,0:T(8,128)(2,1)S(1)} %get-tuple-element.50.k_ref, bf16[512,768]{1,0:T(8,128)(2,1)S(1)} %get-tuple-element.51.v_ref, f32[9,6]{1,0:T(8,128)S(1)} %copy.7.levels, bf16[192,128]{1,0:T(8,128)(2,1)S(1)} %add_convert_fusion.1.after), custom_call_target="tpu_custom_call" | custom-call | tf_op jit(solution)/shard_map/inside/pallas_call | solution.py:200
  19.0 0.0 collective-permute-done.4
  19.0 1.4 %collective-permute-done.5 = bf16[192,128]{1,0:T(8,128)(2,1)S(1)} collective-permute-done((bf16[192,128]{1,0:T(8,128)(2,1)S(1)}, bf16[192,128]{1,0:T(8,128)(2,1)S(1)}, u32[]{:S(2)}, u32[]{:S(2)}) %collective-permute-start.5) | collective-permute-done | bytes 49184 | tf_op jit(solution)/shard_map/ppermute | solution.py:342
  20.4 0.2 collective-permute-done.6
  20.6 0.0 collective-permute-done.7
  20.7 0.3 collective-permute-start.8
  21.0 1.0 %collective-permute-done.8 = bf16[192,128]{1,0:T(8,128)(2,1)S(1)} collective-permute-done((bf16[192,128]{1,0:T(8,128)(2,1)S(1)}, bf16[192,128]{1,0:T(8,128)(2,1)S(1)}, u32[]{:S(2)}, u32[]{:S(2)}) %collective-permute-start.8) | collective-permute-done | bytes 49184 | tf_op jit(solution)/shard_map/ppermute | solution.py:342
  22.0 1.8 %collective-permute-start.10 = (bf16[192,128]{1,0:T(8,128)(2,1)S(1)}, bf16[192,128]{1,0:T(8,128)(2,1)S(1)}, u32[]{:S(2)}, u32[]{:S(2)}) collective-permute-start(bf16[192,128]{1,0:T(8,128)(2,1)S(1)} %get-tuple-element.78.after), channel_id=1, source_target_pairs={{0,112},{1,113},{2,114},{3,115},{4,116},{5,117},{6,118},{7,119},{8... | collective-permute-start | bytes 147464 | tf_op jit(solution)/shard_map/ppermute | solution.py:342
  23.8 1.4 %collective-permute-start.11 = (bf16[192,128]{1,0:T(8,128)(2,1)S(1)}, bf16[192,128]{1,0:T(8,128)(2,1)S(1)}, u32[]{:S(2)}, u32[]{:S(2)}) collective-permute-start(bf16[192,128]{1,0:T(8,128)(2,1)S(1)} %get-tuple-element.78.after), channel_id=1, source_target_pairs={{0,80},{1,81},{2,82},{3,83},{4,84},{5,85},{6,86},{7,87},{8,88},{9,... | collective-permute-start | bytes 147464 | tf_op jit(solution)/shard_map/ppermute | solution.py:342
  25.3 1.3 %collective-permute-start.9 = (bf16[192,128]{1,0:T(8,128)(2,1)S(1)}, bf16[192,128]{1,0:T(8,128)(2,1)S(1)}, u32[]{:S(2)}, u32[]{:S(2)}) collective-permute-start(bf16[192,128]{1,0:T(8,128)(2,1)S(1)} %get-tuple-element.78.after), channel_id=1, source_target_pairs={{0,48},{1,49},{2,50},{3,51},{4,52},{5,53},{6,54},{7,55},{8,56},{9,... | collective-permute-start | bytes 147464 | tf_op jit(solution)/shard_map/ppermute | solution.py:342
  26.6 0.0 copy-start
  26.6 2.0 %inside.3.high_ref = f32[512,384]{1,0:T(8,128)S(1)} custom-call(bf16[512,768]{1,0:T(8,128)(2,1)S(1)} %query.1.q_ref, bf16[512,768]{1,0:T(8,128)(2,1)S(1)} %get-tuple-element.50.k_ref, bf16[512,768]{1,0:T(8,128)(2,1)S(1)} %get-tuple-element.51.v_ref, f32[9,6]{1,0:T(8,128)S(1)} %copy.7.levels, bf16[192,128]{1,0:T(8,128)(2,1)S(1)} %get-tuple-element.78.after), custom_call_target="tpu_custom_call" | custom-call | tf_op jit(solution)/shard_map/inside/pallas_call | solution.py:200
  28.6 0.3 collective-permute-start.13
  28.8 0.0 collective-permute-done.10.refs_8_
  28.9 0.0 collective-permute-done.11.refs_7_
  28.9 1.9 %collective-permute-done.9.refs_6_ = bf16[192,128]{1,0:T(8,128)(2,1)S(1)} collective-permute-done((bf16[192,128]{1,0:T(8,128)(2,1)S(1)}, bf16[192,128]{1,0:T(8,128)(2,1)S(1)}, u32[]{:S(2)}, u32[]{:S(2)}) %collective-permute-start.9) | collective-permute-done | bytes 49184 | tf_op jit(solution)/shard_map/ppermute | solution.py:342
  30.7 0.1 add_convert_fusion
  30.8 4.5 %collective-permute-start.12 = (bf16[192,128]{1,0:T(8,128)(2,1)S(1)}, bf16[192,128]{1,0:T(8,128)(2,1)S(1)}, u32[]{:S(2)}, u32[]{:S(2)}) collective-permute-start(bf16[192,128]{1,0:T(8,128)(2,1)S(1)} %add_convert_fusion), channel_id=1, source_target_pairs={{0,208},{1,209},{2,210},{3,211},{4,212},{5,213},{6,214},{7,215},{8... | collective-permute-start | bytes 147464 | tf_op jit(solution)/shard_map/ppermute | solution.py:342
  35.3 0.0 collective-permute-done.13.refs_4_
  35.3 0.8 %gather.1 = (f32[4,192,128]{2,1,0:T(8,128)S(1)}, f32[192,128]{1,0:T(8,128)S(1)}) custom-call(f32[9,6]{1,0:T(8,128)S(1)} %copy.7.levels, bf16[192,128]{1,0:T(8,128)(2,1)S(1)} %collective-permute-done.3.refs_0_, bf16[192,128]{1,0:T(8,128)(2,1)S(1)} %collective-permute-done.2.refs_1_, bf16[192,128]{1,0:T(8,128)(2,1)S(1)} %collective-permute-done.refs_2_, ...), custom_call_target="tpu_custom_call" | custom-call | tf_op jit(solution)/shard_map/gather/pallas_call | solution.py:245
  36.1 1.9 %collective-permute-done.12 = bf16[192,128]{1,0:T(8,128)(2,1)S(1)} collective-permute-done((bf16[192,128]{1,0:T(8,128)(2,1)S(1)}, bf16[192,128]{1,0:T(8,128)(2,1)S(1)}, u32[]{:S(2)}, u32[]{:S(2)}) %collective-permute-start.12) | collective-permute-done | bytes 49184 | tf_op jit(solution)/shard_map/ppermute | solution.py:342
  38.0 1.3 %collective-permute-start.14 = (bf16[192,128]{1,0:T(8,128)(2,1)S(1)}, bf16[192,128]{1,0:T(8,128)(2,1)S(1)}, u32[]{:S(2)}, u32[]{:S(2)}) collective-permute-start(bf16[192,128]{1,0:T(8,128)(2,1)S(1)} %get-tuple-element.76), channel_id=1, source_target_pairs={{0,18},{1,19},{2,16},{3,17},{4,22},{5,23},{6,20},{7,21},{8,26},{9,... | collective-permute-start | bytes 147464 | tf_op jit(solution)/shard_map/ppermute | solution.py:342
  39.3 1.3 %collective-permute-start.15 = (bf16[192,128]{1,0:T(8,128)(2,1)S(1)}, bf16[192,128]{1,0:T(8,128)(2,1)S(1)}, u32[]{:S(2)}, u32[]{:S(2)}) collective-permute-start(bf16[192,128]{1,0:T(8,128)(2,1)S(1)} %get-tuple-element.75), channel_id=1, source_target_pairs={{0,19},{1,18},{2,17},{3,16},{4,23},{5,22},{6,21},{7,20},{8,27},{9,... | collective-permute-start | bytes 147464 | tf_op jit(solution)/shard_map/ppermute | solution.py:342
  40.7 0.4 collective-permute-start.16
  41.1 0.4 collective-permute-start.17
  41.5 1.9 %collective-permute-done.14.two = bf16[192,128]{1,0:T(8,128)(2,1)S(1)} collective-permute-done((bf16[192,128]{1,0:T(8,128)(2,1)S(1)}, bf16[192,128]{1,0:T(8,128)(2,1)S(1)}, u32[]{:S(2)}, u32[]{:S(2)}) %collective-permute-start.14) | collective-permute-done | bytes 49184 | tf_op jit(solution)/shard_map/ppermute | solution.py:342
  43.4 0.9 %collective-permute-done.15.three = bf16[192,128]{1,0:T(8,128)(2,1)S(1)} collective-permute-done((bf16[192,128]{1,0:T(8,128)(2,1)S(1)}, bf16[192,128]{1,0:T(8,128)(2,1)S(1)}, u32[]{:S(2)}, u32[]{:S(2)}) %collective-permute-start.15) | collective-permute-done | bytes 49184 | tf_op jit(solution)/shard_map/ppermute | solution.py:342
  44.3 0.1 collective-permute-done.16.one
  44.4 0.0 collective-permute-done.17.own
  44.4 0.0 copy-done
  44.4 2.4 %mix.1 = bf16[512,1536]{1,0:T(8,128)(2,1)} custom-call(bf16[512,768]{1,0:T(8,128)(2,1)S(1)} %query.1.q_ref, f32[512,384]{1,0:T(8,128)S(1)} %inside.2.low_ref, f32[512,384]{1,0:T(8,128)S(1)} %inside.3.high_ref, bf16[192,128]{1,0:T(8,128)(2,1)S(1)} %collective-permute-done.17.own, bf16[192,128]{1,0:T(8,128)(2,1)S(1)} %collective-permute-done.16.one, ...), custom_call_target="tpu_custom_call" | custom-call | tf_op jit(solution)/shard_map/mix/pallas_call | solution.py:320
  (5 shorter events, 0.2 us)
Async XLA Ops:
  4.7 5.7 %collective-permute-start = (bf16[192,128]{1,0:T(8,128)(2,1)S(1)}, bf16[192,128]{1,0:T(8,128)(2,1)S(1)}, u32[]{:S(2)}, u32[]{:S(2)}) collective-permute-start(bf16[192,128]{1,0:T(8,128)(2,1)S(1)} %get-tuple-element.39), channel_id=1, source_target_pairs={{0,18},{1,19},{2,16},{3,17},{4,22},{5,23},{6,20},{7,21},{8,26},{9,... | collective-permute-start | bytes 147464 | tf_op jit(solution)/shard_map/ppermute | solution.py:342
  7.4 4.7 %collective-permute-start.1 = (bf16[192,128]{1,0:T(8,128)(2,1)S(1)}, bf16[192,128]{1,0:T(8,128)(2,1)S(1)}, u32[]{:S(2)}, u32[]{:S(2)}) collective-permute-start(bf16[192,128]{1,0:T(8,128)(2,1)S(1)} %get-tuple-element.40), channel_id=1, source_target_pairs={{0,19},{1,18},{2,17},{3,16},{4,23},{5,22},{6,21},{7,20},{8,27},{9,... | collective-permute-start | bytes 147464 | tf_op jit(solution)/shard_map/ppermute | solution.py:342
  8.8 4.0 %collective-permute-start.2 = (bf16[192,128]{1,0:T(8,128)(2,1)S(1)}, bf16[192,128]{1,0:T(8,128)(2,1)S(1)}, u32[]{:S(2)}, u32[]{:S(2)}) collective-permute-start(bf16[192,128]{1,0:T(8,128)(2,1)S(1)} %get-tuple-element.41), channel_id=1, source_target_pairs={{0,17},{1,16},{2,19},{3,18},{4,21},{5,20},{6,23},{7,22},{8,25},{9,... | collective-permute-start | bytes 147464 | tf_op jit(solution)/shard_map/ppermute | solution.py:342
  8.8 4.0 %collective-permute-start.3 = (bf16[192,128]{1,0:T(8,128)(2,1)S(1)}, bf16[192,128]{1,0:T(8,128)(2,1)S(1)}, u32[]{:S(2)}, u32[]{:S(2)}) collective-permute-start(bf16[192,128]{1,0:T(8,128)(2,1)S(1)} %get-tuple-element.42), channel_id=1, source_target_pairs={{0,16},{1,17},{2,18},{3,19},{4,20},{5,21},{6,22},{7,23},{8,24},{9,... | collective-permute-start | bytes 147464 | tf_op jit(solution)/shard_map/ppermute | solution.py:342
  8.8 8.1 %copy-start.1 = (f32[9,6]{0,1:T(8,128)S(1)}, f32[9,6]{0,1:T(8,128)}, u32[]{:S(2)}) copy-start(f32[9,6]{0,1:T(8,128)} %param.11) | copy-start | bytes 652
  12.9 6.1 %collective-permute-start.4 = (bf16[192,128]{1,0:T(8,128)(2,1)S(1)}, bf16[192,128]{1,0:T(8,128)(2,1)S(1)}, u32[]{:S(2)}, u32[]{:S(2)}) collective-permute-start(bf16[192,128]{1,0:T(8,128)(2,1)S(1)} %add_convert_fusion.1.after), channel_id=1, source_target_pairs={{0,24},{1,25},{2,26},{3,27},{4,28},{5,29},{6,30},{7,31},{8,16},{9,... | collective-permute-start | bytes 147464 | tf_op jit(solution)/shard_map/ppermute | solution.py:342
  15.7 4.7 %collective-permute-start.5 = (bf16[192,128]{1,0:T(8,128)(2,1)S(1)}, bf16[192,128]{1,0:T(8,128)(2,1)S(1)}, u32[]{:S(2)}, u32[]{:S(2)}) collective-permute-start(bf16[192,128]{1,0:T(8,128)(2,1)S(1)} %add_convert_fusion.1.after), channel_id=1, source_target_pairs={{0,28},{1,29},{2,30},{3,31},{4,24},{5,25},{6,26},{7,27},{8,20},{9,... | collective-permute-start | bytes 147464 | tf_op jit(solution)/shard_map/ppermute | solution.py:342
  16.8 3.8 %collective-permute-start.6 = (bf16[192,128]{1,0:T(8,128)(2,1)S(1)}, bf16[192,128]{1,0:T(8,128)(2,1)S(1)}, u32[]{:S(2)}, u32[]{:S(2)}) collective-permute-start(bf16[192,128]{1,0:T(8,128)(2,1)S(1)} %add_convert_fusion.1.after), channel_id=1, source_target_pairs={{0,20},{1,21},{2,22},{3,23},{4,16},{5,17},{6,18},{7,19},{8,28},{9,... | collective-permute-start | bytes 147464 | tf_op jit(solution)/shard_map/ppermute | solution.py:342
  16.9 3.8 %collective-permute-start.7 = (bf16[192,128]{1,0:T(8,128)(2,1)S(1)}, bf16[192,128]{1,0:T(8,128)(2,1)S(1)}, u32[]{:S(2)}, u32[]{:S(2)}) collective-permute-start(bf16[192,128]{1,0:T(8,128)(2,1)S(1)} %add_convert_fusion.1.after), channel_id=1, source_target_pairs={{0,16},{1,17},{2,18},{3,19},{4,20},{5,21},{6,22},{7,23},{8,24},{9,... | collective-permute-start | bytes 147464 | tf_op jit(solution)/shard_map/ppermute | solution.py:342
  20.7 1.3 %collective-permute-start.8 = (bf16[192,128]{1,0:T(8,128)(2,1)S(1)}, bf16[192,128]{1,0:T(8,128)(2,1)S(1)}, u32[]{:S(2)}, u32[]{:S(2)}) collective-permute-start(bf16[192,128]{1,0:T(8,128)(2,1)S(1)} %fusion.7.refs_5_), channel_id=1, source_target_pairs={{0,16},{1,17},{2,18},{3,19},{4,20},{5,21},{6,22},{7,23},{8,24},{9,... | collective-permute-start | bytes 147464 | tf_op jit(solution)/shard_map/ppermute | solution.py:342
  22.0 6.8 %collective-permute-start.10 = (bf16[192,128]{1,0:T(8,128)(2,1)S(1)}, bf16[192,128]{1,0:T(8,128)(2,1)S(1)}, u32[]{:S(2)}, u32[]{:S(2)}) collective-permute-start(bf16[192,128]{1,0:T(8,128)(2,1)S(1)} %get-tuple-element.78.after), channel_id=1, source_target_pairs={{0,112},{1,113},{2,114},{3,115},{4,116},{5,117},{6,118},{7,119},{8... | collective-permute-start | bytes 147464 | tf_op jit(solution)/shard_map/ppermute | solution.py:342
  23.8 5.0 %collective-permute-start.11 = (bf16[192,128]{1,0:T(8,128)(2,1)S(1)}, bf16[192,128]{1,0:T(8,128)(2,1)S(1)}, u32[]{:S(2)}, u32[]{:S(2)}) collective-permute-start(bf16[192,128]{1,0:T(8,128)(2,1)S(1)} %get-tuple-element.78.after), channel_id=1, source_target_pairs={{0,80},{1,81},{2,82},{3,83},{4,84},{5,85},{6,86},{7,87},{8,88},{9,... | collective-permute-start | bytes 147464 | tf_op jit(solution)/shard_map/ppermute | solution.py:342
  25.3 5.4 %collective-permute-start.9 = (bf16[192,128]{1,0:T(8,128)(2,1)S(1)}, bf16[192,128]{1,0:T(8,128)(2,1)S(1)}, u32[]{:S(2)}, u32[]{:S(2)}) collective-permute-start(bf16[192,128]{1,0:T(8,128)(2,1)S(1)} %get-tuple-element.78.after), channel_id=1, source_target_pairs={{0,48},{1,49},{2,50},{3,51},{4,52},{5,53},{6,54},{7,55},{8,56},{9,... | collective-permute-start | bytes 147464 | tf_op jit(solution)/shard_map/ppermute | solution.py:342
  26.6 17.8 %copy-start = (bf16[768,1536]{1,0:T(8,128)(2,1)S(1)}, bf16[768,1536]{1,0:T(8,128)(2,1)}, u32[]{:S(2)}) copy-start(bf16[768,1536]{1,0:T(8,128)(2,1)} %wo.1) | copy-start | bytes 7077892
  28.6 6.7 %collective-permute-start.13 = (bf16[2,192,128]{2,1,0:T(8,128)(2,1)S(1)}, bf16[2,192,128]{2,1,0:T(8,128)(2,1)S(1)}, u32[]{:S(2)}, u32[]{:S(2)}) collective-permute-start(bf16[2,192,128]{2,1,0:T(8,128)(2,1)S(1)} %pad_maximum_fusion), channel_id=1, source_target_pairs={{0,16},{1,17},{2,18},{3,19},{4,20},{5,21},{6,22},{7,23},{8,24},{9,... | collective-permute-start | bytes 294920 | tf_op jit(solution)/shard_map/ppermute | solution.py:342
  30.8 7.2 %collective-permute-start.12 = (bf16[192,128]{1,0:T(8,128)(2,1)S(1)}, bf16[192,128]{1,0:T(8,128)(2,1)S(1)}, u32[]{:S(2)}, u32[]{:S(2)}) collective-permute-start(bf16[192,128]{1,0:T(8,128)(2,1)S(1)} %add_convert_fusion), channel_id=1, source_target_pairs={{0,208},{1,209},{2,210},{3,211},{4,212},{5,213},{6,214},{7,215},{8... | collective-permute-start | bytes 147464 | tf_op jit(solution)/shard_map/ppermute | solution.py:342
  38.0 5.3 %collective-permute-start.14 = (bf16[192,128]{1,0:T(8,128)(2,1)S(1)}, bf16[192,128]{1,0:T(8,128)(2,1)S(1)}, u32[]{:S(2)}, u32[]{:S(2)}) collective-permute-start(bf16[192,128]{1,0:T(8,128)(2,1)S(1)} %get-tuple-element.76), channel_id=1, source_target_pairs={{0,18},{1,19},{2,16},{3,17},{4,22},{5,23},{6,20},{7,21},{8,26},{9,... | collective-permute-start | bytes 147464 | tf_op jit(solution)/shard_map/ppermute | solution.py:342
  39.3 5.0 %collective-permute-start.15 = (bf16[192,128]{1,0:T(8,128)(2,1)S(1)}, bf16[192,128]{1,0:T(8,128)(2,1)S(1)}, u32[]{:S(2)}, u32[]{:S(2)}) collective-permute-start(bf16[192,128]{1,0:T(8,128)(2,1)S(1)} %get-tuple-element.75), channel_id=1, source_target_pairs={{0,19},{1,18},{2,17},{3,16},{4,23},{5,22},{6,21},{7,20},{8,27},{9,... | collective-permute-start | bytes 147464 | tf_op jit(solution)/shard_map/ppermute | solution.py:342
  40.7 3.8 %collective-permute-start.16 = (bf16[192,128]{1,0:T(8,128)(2,1)S(1)}, bf16[192,128]{1,0:T(8,128)(2,1)S(1)}, u32[]{:S(2)}, u32[]{:S(2)}) collective-permute-start(bf16[192,128]{1,0:T(8,128)(2,1)S(1)} %get-tuple-element.74), channel_id=1, source_target_pairs={{0,17},{1,16},{2,19},{3,18},{4,21},{5,20},{6,23},{7,22},{8,25},{9,... | collective-permute-start | bytes 147464 | tf_op jit(solution)/shard_map/ppermute | solution.py:342
  41.1 3.4 %collective-permute-start.17 = (bf16[192,128]{1,0:T(8,128)(2,1)S(1)}, bf16[192,128]{1,0:T(8,128)(2,1)S(1)}, u32[]{:S(2)}, u32[]{:S(2)}) collective-permute-start(bf16[192,128]{1,0:T(8,128)(2,1)S(1)} %get-tuple-element.73), channel_id=1, source_target_pairs={{0,16},{1,17},{2,18},{3,19},{4,20},{5,21},{6,22},{7,23},{8,24},{9,... | collective-permute-start | bytes 147464 | tf_op jit(solution)/shard_map/ppermute | solution.py:342

commit v8 on v7

--- a/solution.py
+++ b/solution.py
@@ -209,7 +209,7 @@
 
 def gather_kernel(levels, *refs):
     near = refs[:4]
-    crossed, mine, z1, z2, z3, local_ref, last_ref = refs[4:]
+    x1, x2, x3, mine, z1, z2, z3, local_ref, last_ref = refs[4:]
     y, x, core, z = position()
     heads = levels.shape[1]
     part = mine.shape[0] // heads
@@ -223,8 +223,8 @@
             return ref[rows, :].astype(F32)
 
         far = (
-            factor(2, bit(x, 0)) * crossed[0, rows, :].astype(F32)
-            + factor(3, bit(x, 1)) * crossed[1, rows, :].astype(F32)
+            factor(2, bit(x, 0)) * x1[1, rows, :].astype(F32)
+            + factor(3, bit(x, 1)) * (read(x2) + x3[1, rows, :].astype(F32))
             + factor(4, bit(core ^ 1, 0)) * read(mine)
             + factor(5, bit(z, 0)) * read(z1)
             + factor(6, bit(z, 1)) * (read(z2) + read(z3))
@@ -245,7 +245,7 @@
     return pl.pallas_call(
         gather_kernel,
         out_shape=(jax.ShapeDtypeStruct((4, *shape), F32), jax.ShapeDtypeStruct(shape, F32)),
-        in_specs=[SMEM] + [VMEM] * 9,
+        in_specs=[SMEM] + [VMEM] * 11,
         out_specs=[VMEM, VMEM],
         compiler_params=pltpu.CompilerParams(vmem_limit_bytes=4 << 20),
         name="gather",
@@ -362,28 +362,27 @@
     query = query_of(tok, wq, width)
     n2, n3, n1, n0, query = lax.optimization_barrier((n2, n3, n1, n0, query))
     near = (n0, n1, n2, n3)
-    going = plus(n0.astype(F32), near[1:]).astype(BF16)
-
-    x2, x3, x1 = (flip(going, CORE | distance * X) for distance in (2, 3, 1))
+    total = plus(n0.astype(F32), near[1:])
+    going = total.astype(BF16)
+
     own = flip(going, CORE)
-    low = inside_of(query, keys, values, level_weights, going, 0, half, width)
-    x2, x3, x1, own, low = lax.optimization_barrier((x2, x3, x1, own, low))
-    total = plus(own.astype(F32), (x1, x2, x3))
-    mine = total.astype(BF16)
-    crossing = jnp.stack([x1.astype(F32), plus(x2.astype(F32), (x3,))]).astype(BF16)
-
-    total = plus(total, (flip(mine, CORE),))
+    x2 = flip(going, CORE | 2 * X)
+    both = jnp.stack([going, own])
+    x3, x1 = flip(both, CORE | 3 * X), flip(both, CORE | X)
+    other2 = flip(x2, CORE)
+    low = inside_of(query, keys, values, level_weights, x2, 0, half, width)
+    other2, x3, x1, low = lax.optimization_barrier((other2, x3, x1, low))
+    mine = plus(own.astype(F32), (x1[0], x2, x3[0]))
+    total = plus(total + mine, (x1[1], other2, x3[1]))
+    mine = mine.astype(BF16)
     going = total.astype(BF16)
     z1, z3, z2 = (flip(going, CORE | distance * Z) for distance in (1, 3, 2))
     high = inside_of(query, keys, values, level_weights, going, half, half, width)
-    crossing, high = lax.optimization_barrier((crossing, high))
-    crossed = flip(crossing, CORE)
     z1, z3, z2, high = lax.optimization_barrier((z1, z3, z2, high))
     going = plus(total, (z3, z2, z1)).astype(BF16)
 
-    going, crossing = lax.optimization_barrier((going, crossing))
     past = flip(going, CORE | 6 * Z)
-    gathered, factor = gather_of(level_weights, near, (crossed, mine, z1, z2, z3))
+    gathered, factor = gather_of(level_weights, near, (x1, other2, x3, mine, z1, z2, z3))
     past, gathered, factor = lax.optimization_barrier((past, gathered, factor))
     last = factor * past.astype(F32)
     back = [(gathered[distance] + last).astype(BF16) for distance in range(4)]

time: 47.3 us -> 47.4 us (level)
    ppermute x18 -> x17, waiting for transfers between devices: 11.8 us -> 12 us  [flip(): lax.ppermute(value, AXES, [(source, source ^ mask) for source in range(de...]
    ppermute x18 -> x17, starting transfers between devices: 21.2 us -> 21.1 us  [flip(): lax.ppermute(value, AXES, [(source, source ^ mask) for source in range(de...]
  transfers between devices with their start and end apart: 18 -> 17, of which waited for: 10 -> 8; matrix products, arithmetic and copies ran while one was open for 0% -> 0% of each run, Pallas kernels for 13% -> 13%
where the time goes in v8:
time: 47.4 us; the launch traced here: 47.1 us
  starting transfers between devices  21.1 us (45%)
  Pallas kernels  13.4 us (28%)
  waiting for transfers between devices  12 us (25%)
    ppermute x17, starting transfers between devices, flip(): lax.ppermute(value, AXES, [(source, source ^ mask) for source in range(de...  21.1 us
    ppermute x17, waiting for transfers between devices, flip(): lax.ppermute(value, AXES, [(source, source ^ mask) for source in range(de...  12 us
    pallas_call x1, Pallas kernels, states_of(): pl.pallas_call(functools.partial(state_kernel, width), out_shape=(side, s...  4.72 us
    pallas_call x2, Pallas kernels, inside_of(): pl.pallas_call(functools.partial(inside_kernel, width, first), out_shape=...  3.9 us
    pallas_call x1, Pallas kernels, mixed_of(): pl.pallas_call(functools.partial(mix_kernel, width), out_shape=jax.ShapeD...  2.37 us
    pallas_call x1, Pallas kernels, query_of(): pl.pallas_call(functools.partial(query_kernel, width), out_shape=jax.Shap...  1.6 us
  transfers between devices with their start and end apart: 17, of which 8 were waited for; matrix products, arithmetic and copies ran while one was open for 0% of the time, Pallas kernels for 13%

profile of v8, /device:TPU:32, one launch (start us, length us, event | category | flops | bytes accessed | tf_op | source)
XLA Modules:
  0.0 47.1 jit_solution(11861612593053002343)
XLA Ops:
  0.0 4.7 %states.1 = (bf16[512,768]{1,0:T(8,128)(2,1)S(1)}, bf16[512,768]{1,0:T(8,128)(2,1)S(1)}, bf16[512,1536]{1,0:T(8,128)(2,1)S(1)}, bf16[1536,768]{1,0:T(8,128)(2,1)...) custom-call(bf16[512,1536]{1,0:T(8,128)(2,1)} %tok_hbm.1, ...), custom_call_target="tpu_custom_call" | custom-call | tf_op jit(solution)/shard_map/states/pallas_call | solution.py:127
  4.7 2.7 %collective-permute-start = (bf16[192,128]{1,0:T(8,128)(2,1)S(1)}, bf16[192,128]{1,0:T(8,128)(2,1)S(1)}, u32[]{:S(2)}, u32[]{:S(2)}) collective-permute-start(bf16[192,128]{1,0:T(8,128)(2,1)S(1)} %get-tuple-element.35), channel_id=1, source_target_pairs={{0,18},{1,19},{2,16},{3,17},{4,22},{5,23},{6,20},{7,21},{8,26},{9,... | collective-permute-start | bytes 147464 | tf_op jit(solution)/shard_map/ppermute | solution.py:342
  7.4 1.3 %collective-permute-start.1 = (bf16[192,128]{1,0:T(8,128)(2,1)S(1)}, bf16[192,128]{1,0:T(8,128)(2,1)S(1)}, u32[]{:S(2)}, u32[]{:S(2)}) collective-permute-start(bf16[192,128]{1,0:T(8,128)(2,1)S(1)} %get-tuple-element.36), channel_id=1, source_target_pairs={{0,19},{1,18},{2,17},{3,16},{4,23},{5,22},{6,21},{7,20},{8,27},{9,... | collective-permute-start | bytes 147464 | tf_op jit(solution)/shard_map/ppermute | solution.py:342
  8.8 0.0 collective-permute-start.2
  8.8 0.0 collective-permute-start.3
  8.8 0.0 copy-start.1
  8.8 1.6 %query.1.q_ref = bf16[512,768]{1,0:T(8,128)(2,1)S(1)} custom-call(bf16[512,1536]{1,0:T(8,128)(2,1)S(1)} %get-tuple-element.39.tok, bf16[1536,768]{1,0:T(8,128)(2,1)S(1)} %get-tuple-element.40.wq), custom_call_target="tpu_custom_call" | custom-call | tf_op jit(solution)/shard_map/query/pallas_call | solution.py:161
  10.4 0.0 collective-permute-done.refs_2_
  10.4 1.8 %collective-permute-done.1.refs_3_ = bf16[192,128]{1,0:T(8,128)(2,1)S(1)} collective-permute-done((bf16[192,128]{1,0:T(8,128)(2,1)S(1)}, bf16[192,128]{1,0:T(8,128)(2,1)S(1)}, u32[]{:S(2)}, u32[]{:S(2)}) %collective-permute-start.1) | collective-permute-done | bytes 49184 | tf_op jit(solution)/shard_map/ppermute | solution.py:342
  12.2 0.6 %collective-permute-done.2.refs_1_ = bf16[192,128]{1,0:T(8,128)(2,1)S(1)} collective-permute-done((bf16[192,128]{1,0:T(8,128)(2,1)S(1)}, bf16[192,128]{1,0:T(8,128)(2,1)S(1)}, u32[]{:S(2)}, u32[]{:S(2)}) %collective-permute-start.2) | collective-permute-done | bytes 49184 | tf_op jit(solution)/shard_map/ppermute | solution.py:342
  12.8 0.0 collective-permute-done.3.refs_0_
  12.9 0.2 collective-permute-start.6
  13.1 3.0 %collective-permute-start.4 = (bf16[192,128]{1,0:T(8,128)(2,1)S(1)}, bf16[192,128]{1,0:T(8,128)(2,1)S(1)}, u32[]{:S(2)}, u32[]{:S(2)}) collective-permute-start(bf16[192,128]{1,0:T(8,128)(2,1)S(1)} %fusion.6), channel_id=1, source_target_pairs={{0,24},{1,25},{2,26},{3,27},{4,28},{5,29},{6,30},{7,31},{8,16},{9,... | collective-permute-start | bytes 147464 | tf_op jit(solution)/shard_map/ppermute | solution.py:342
  16.1 0.0 collective-permute-done.6
  16.1 1.0 %collective-permute-start.7 = (bf16[2,192,128]{2,1,0:T(8,128)(2,1)S(1)}, bf16[2,192,128]{2,1,0:T(8,128)(2,1)S(1)}, u32[]{:S(2)}, u32[]{:S(2)}) collective-permute-start(bf16[2,192,128]{2,1,0:T(8,128)(2,1)S(1)} %pad_maximum_fusion), channel_id=1, source_target_pairs={{0,28},{1,29},{2,30},{3,31},{4,24},{5,25},{6,26},{7,27},{8,20},{9,... | collective-permute-start | bytes 294920 | tf_op jit(solution)/shard_map/ppermute | solution.py:342
  17.1 0.0 collective-permute-start.8
  17.1 1.0 %collective-permute-done.4.after = bf16[192,128]{1,0:T(8,128)(2,1)S(1)} collective-permute-done((bf16[192,128]{1,0:T(8,128)(2,1)S(1)}, bf16[192,128]{1,0:T(8,128)(2,1)S(1)}, u32[]{:S(2)}, u32[]{:S(2)}) %collective-permute-start.4) | collective-permute-done | bytes 49184 | tf_op jit(solution)/shard_map/ppermute | solution.py:342
  18.1 0.4 collective-permute-start.5
  18.5 0.0 copy-done.1
  18.5 0.1 copy.7.levels
  18.6 1.9 %inside.2.low_ref = f32[512,384]{1,0:T(8,128)S(1)} custom-call(bf16[512,768]{1,0:T(8,128)(2,1)S(1)} %query.1.q_ref, bf16[512,768]{1,0:T(8,128)(2,1)S(1)} %get-tuple-element.46.k_ref, bf16[512,768]{1,0:T(8,128)(2,1)S(1)} %get-tuple-element.47.v_ref, f32[9,6]{1,0:T(8,128)S(1)} %copy.7.levels, bf16[192,128]{1,0:T(8,128)(2,1)S(1)} %collective-permute-done.4.after), custom_call_target="tpu_custom_call" | custom-call | tf_op jit(solution)/shard_map/inside/pallas_call | solution.py:200
  20.5 0.0 collective-permute-done.5.refs_5_
  20.5 1.6 %collective-permute-done.7.refs_6_ = bf16[2,192,128]{2,1,0:T(8,128)(2,1)S(1)} collective-permute-done((bf16[2,192,128]{2,1,0:T(8,128)(2,1)S(1)}, bf16[2,192,128]{2,1,0:T(8,128)(2,1)S(1)}, u32[]{:S(2)}, u32[]{:S(2)}) %collective-permute-start.7) | collective-permute-done | bytes 98336 | tf_op jit(solution)/shard_map/ppermute | solution.py:342
  22.2 0.0 collective-permute-done.8.refs_4_
  22.2 0.1 fusion.8
  22.2 0.0 copy-start
  22.2 1.8 %collective-permute-start.10 = (bf16[192,128]{1,0:T(8,128)(2,1)S(1)}, bf16[192,128]{1,0:T(8,128)(2,1)S(1)}, u32[]{:S(2)}, u32[]{:S(2)}) collective-permute-start(bf16[192,128]{1,0:T(8,128)(2,1)S(1)} %get-tuple-element.65.after), channel_id=1, source_target_pairs={{0,112},{1,113},{2,114},{3,115},{4,116},{5,117},{6,118},{7,119},{8... | collective-permute-start | bytes 147464 | tf_op jit(solution)/shard_map/ppermute | solution.py:342
  24.0 1.4 %collective-permute-start.11 = (bf16[192,128]{1,0:T(8,128)(2,1)S(1)}, bf16[192,128]{1,0:T(8,128)(2,1)S(1)}, u32[]{:S(2)}, u32[]{:S(2)}) collective-permute-start(bf16[192,128]{1,0:T(8,128)(2,1)S(1)} %get-tuple-element.65.after), channel_id=1, source_target_pairs={{0,80},{1,81},{2,82},{3,83},{4,84},{5,85},{6,86},{7,87},{8,88},{9,... | collective-permute-start | bytes 147464 | tf_op jit(solution)/shard_map/ppermute | solution.py:342
  25.5 1.3 %collective-permute-start.9 = (bf16[192,128]{1,0:T(8,128)(2,1)S(1)}, bf16[192,128]{1,0:T(8,128)(2,1)S(1)}, u32[]{:S(2)}, u32[]{:S(2)}) collective-permute-start(bf16[192,128]{1,0:T(8,128)(2,1)S(1)} %get-tuple-element.65.after), channel_id=1, source_target_pairs={{0,48},{1,49},{2,50},{3,51},{4,52},{5,53},{6,54},{7,55},{8,56},{9,... | collective-permute-start | bytes 147464 | tf_op jit(solution)/shard_map/ppermute | solution.py:342
  26.8 1.9 %inside.3.high_ref = f32[512,384]{1,0:T(8,128)S(1)} custom-call(bf16[512,768]{1,0:T(8,128)(2,1)S(1)} %query.1.q_ref, bf16[512,768]{1,0:T(8,128)(2,1)S(1)} %get-tuple-element.46.k_ref, bf16[512,768]{1,0:T(8,128)(2,1)S(1)} %get-tuple-element.47.v_ref, f32[9,6]{1,0:T(8,128)S(1)} %copy.7.levels, bf16[192,128]{1,0:T(8,128)(2,1)S(1)} %get-tuple-element.65.after), custom_call_target="tpu_custom_call" | custom-call | tf_op jit(solution)/shard_map/inside/pallas_call | solution.py:200
  28.7 0.0 collective-permute-done.10.refs_10_
  28.8 0.0 collective-permute-done.11.refs_9_
  28.8 2.1 %collective-permute-done.9.refs_8_ = bf16[192,128]{1,0:T(8,128)(2,1)S(1)} collective-permute-done((bf16[192,128]{1,0:T(8,128)(2,1)S(1)}, bf16[192,128]{1,0:T(8,128)(2,1)S(1)}, u32[]{:S(2)}, u32[]{:S(2)}) %collective-permute-start.9) | collective-permute-done | bytes 49184 | tf_op jit(solution)/shard_map/ppermute | solution.py:342
  30.9 4.5 %collective-permute-start.12 = (bf16[192,128]{1,0:T(8,128)(2,1)S(1)}, bf16[192,128]{1,0:T(8,128)(2,1)S(1)}, u32[]{:S(2)}, u32[]{:S(2)}) collective-permute-start(bf16[192,128]{1,0:T(8,128)(2,1)S(1)} %add_convert_fusion), channel_id=1, source_target_pairs={{0,208},{1,209},{2,210},{3,211},{4,212},{5,213},{6,214},{7,215},{8... | collective-permute-start | bytes 147464 | tf_op jit(solution)/shard_map/ppermute | solution.py:342
  35.5 0.8 %gather.1 = (f32[4,192,128]{2,1,0:T(8,128)S(1)}, f32[192,128]{1,0:T(8,128)S(1)}) custom-call(f32[9,6]{1,0:T(8,128)S(1)} %copy.7.levels, bf16[192,128]{1,0:T(8,128)(2,1)S(1)} %collective-permute-done.3.refs_0_, bf16[192,128]{1,0:T(8,128)(2,1)S(1)} %collective-permute-done.2.refs_1_, bf16[192,128]{1,0:T(8,128)(2,1)S(1)} %collective-permute-done.refs_2_, ...), custom_call_target="tpu_custom_call" | custom-call | tf_op jit(solution)/shard_map/gather/pallas_call | solution.py:245
  36.3 1.8 %collective-permute-done.12 = bf16[192,128]{1,0:T(8,128)(2,1)S(1)} collective-permute-done((bf16[192,128]{1,0:T(8,128)(2,1)S(1)}, bf16[192,128]{1,0:T(8,128)(2,1)S(1)}, u32[]{:S(2)}, u32[]{:S(2)}) %collective-permute-start.12) | collective-permute-done | bytes 49184 | tf_op jit(solution)/shard_map/ppermute | solution.py:342
  38.1 1.2 %collective-permute-start.13 = (bf16[192,128]{1,0:T(8,128)(2,1)S(1)}, bf16[192,128]{1,0:T(8,128)(2,1)S(1)}, u32[]{:S(2)}, u32[]{:S(2)}) collective-permute-start(bf16[192,128]{1,0:T(8,128)(2,1)S(1)} %get-tuple-element.70), channel_id=1, source_target_pairs={{0,18},{1,19},{2,16},{3,17},{4,22},{5,23},{6,20},{7,21},{8,26},{9,... | collective-permute-start | bytes 147464 | tf_op jit(solution)/shard_map/ppermute | solution.py:342
  39.3 1.4 %collective-permute-start.14 = (bf16[192,128]{1,0:T(8,128)(2,1)S(1)}, bf16[192,128]{1,0:T(8,128)(2,1)S(1)}, u32[]{:S(2)}, u32[]{:S(2)}) collective-permute-start(bf16[192,128]{1,0:T(8,128)(2,1)S(1)} %get-tuple-element.69), channel_id=1, source_target_pairs={{0,19},{1,18},{2,17},{3,16},{4,23},{5,22},{6,21},{7,20},{8,27},{9,... | collective-permute-start | bytes 147464 | tf_op jit(solution)/shard_map/ppermute | solution.py:342
  40.7 0.4 collective-permute-start.15
  41.1 0.4 collective-permute-start.16
  41.6 1.9 %collective-permute-done.13.two = bf16[192,128]{1,0:T(8,128)(2,1)S(1)} collective-permute-done((bf16[192,128]{1,0:T(8,128)(2,1)S(1)}, bf16[192,128]{1,0:T(8,128)(2,1)S(1)}, u32[]{:S(2)}, u32[]{:S(2)}) %collective-permute-start.13) | collective-permute-done | bytes 49184 | tf_op jit(solution)/shard_map/ppermute | solution.py:342
  43.5 1.0 %collective-permute-done.14.three = bf16[192,128]{1,0:T(8,128)(2,1)S(1)} collective-permute-done((bf16[192,128]{1,0:T(8,128)(2,1)S(1)}, bf16[192,128]{1,0:T(8,128)(2,1)S(1)}, u32[]{:S(2)}, u32[]{:S(2)}) %collective-permute-start.14) | collective-permute-done | bytes 49184 | tf_op jit(solution)/shard_map/ppermute | solution.py:342
  44.5 0.0 collective-permute-done.15.one
  44.5 0.0 collective-permute-done.16.own
  44.5 0.0 copy-done
  44.5 2.4 %mix.1 = bf16[512,1536]{1,0:T(8,128)(2,1)} custom-call(bf16[512,768]{1,0:T(8,128)(2,1)S(1)} %query.1.q_ref, f32[512,384]{1,0:T(8,128)S(1)} %inside.2.low_ref, f32[512,384]{1,0:T(8,128)S(1)} %inside.3.high_ref, bf16[192,128]{1,0:T(8,128)(2,1)S(1)} %collective-permute-done.16.own, bf16[192,128]{1,0:T(8,128)(2,1)S(1)} %collective-permute-done.15.one, ...), custom_call_target="tpu_custom_call" | custom-call | tf_op jit(solution)/shard_map/mix/pallas_call | solution.py:320
  (4 shorter events, 0.1 us)
Async XLA Ops:
  4.7 5.7 %collective-permute-start = (bf16[192,128]{1,0:T(8,128)(2,1)S(1)}, bf16[192,128]{1,0:T(8,128)(2,1)S(1)}, u32[]{:S(2)}, u32[]{:S(2)}) collective-permute-start(bf16[192,128]{1,0:T(8,128)(2,1)S(1)} %get-tuple-element.35), channel_id=1, source_target_pairs={{0,18},{1,19},{2,16},{3,17},{4,22},{5,23},{6,20},{7,21},{8,26},{9,... | collective-permute-start | bytes 147464 | tf_op jit(solution)/shard_map/ppermute | solution.py:342
  7.4 4.7 %collective-permute-start.1 = (bf16[192,128]{1,0:T(8,128)(2,1)S(1)}, bf16[192,128]{1,0:T(8,128)(2,1)S(1)}, u32[]{:S(2)}, u32[]{:S(2)}) collective-permute-start(bf16[192,128]{1,0:T(8,128)(2,1)S(1)} %get-tuple-element.36), channel_id=1, source_target_pairs={{0,19},{1,18},{2,17},{3,16},{4,23},{5,22},{6,21},{7,20},{8,27},{9,... | collective-permute-start | bytes 147464 | tf_op jit(solution)/shard_map/ppermute | solution.py:342
  8.8 4.0 %collective-permute-start.2 = (bf16[192,128]{1,0:T(8,128)(2,1)S(1)}, bf16[192,128]{1,0:T(8,128)(2,1)S(1)}, u32[]{:S(2)}, u32[]{:S(2)}) collective-permute-start(bf16[192,128]{1,0:T(8,128)(2,1)S(1)} %get-tuple-element.37), channel_id=1, source_target_pairs={{0,17},{1,16},{2,19},{3,18},{4,21},{5,20},{6,23},{7,22},{8,25},{9,... | collective-permute-start | bytes 147464 | tf_op jit(solution)/shard_map/ppermute | solution.py:342
  8.8 4.0 %collective-permute-start.3 = (bf16[192,128]{1,0:T(8,128)(2,1)S(1)}, bf16[192,128]{1,0:T(8,128)(2,1)S(1)}, u32[]{:S(2)}, u32[]{:S(2)}) collective-permute-start(bf16[192,128]{1,0:T(8,128)(2,1)S(1)} %get-tuple-element.38), channel_id=1, source_target_pairs={{0,16},{1,17},{2,18},{3,19},{4,20},{5,21},{6,22},{7,23},{8,24},{9,... | collective-permute-start | bytes 147464 | tf_op jit(solution)/shard_map/ppermute | solution.py:342
  8.8 9.7 %copy-start.1 = (f32[9,6]{0,1:T(8,128)S(1)}, f32[9,6]{0,1:T(8,128)}, u32[]{:S(2)}) copy-start(f32[9,6]{0,1:T(8,128)} %param.11) | copy-start | bytes 652
  12.9 3.2 %collective-permute-start.6 = (bf16[192,128]{1,0:T(8,128)(2,1)S(1)}, bf16[192,128]{1,0:T(8,128)(2,1)S(1)}, u32[]{:S(2)}, u32[]{:S(2)}) collective-permute-start(bf16[192,128]{1,0:T(8,128)(2,1)S(1)} %fusion.6), channel_id=1, source_target_pairs={{0,16},{1,17},{2,18},{3,19},{4,20},{5,21},{6,22},{7,23},{8,24},{9,... | collective-permute-start | bytes 147464 | tf_op jit(solution)/shard_map/ppermute | solution.py:342
  13.1 5.1 %collective-permute-start.4 = (bf16[192,128]{1,0:T(8,128)(2,1)S(1)}, bf16[192,128]{1,0:T(8,128)(2,1)S(1)}, u32[]{:S(2)}, u32[]{:S(2)}) collective-permute-start(bf16[192,128]{1,0:T(8,128)(2,1)S(1)} %fusion.6), channel_id=1, source_target_pairs={{0,24},{1,25},{2,26},{3,27},{4,28},{5,29},{6,30},{7,31},{8,16},{9,... | collective-permute-start | bytes 147464 | tf_op jit(solution)/shard_map/ppermute | solution.py:342
  16.1 6.1 %collective-permute-start.7 = (bf16[2,192,128]{2,1,0:T(8,128)(2,1)S(1)}, bf16[2,192,128]{2,1,0:T(8,128)(2,1)S(1)}, u32[]{:S(2)}, u32[]{:S(2)}) collective-permute-start(bf16[2,192,128]{2,1,0:T(8,128)(2,1)S(1)} %pad_maximum_fusion), channel_id=1, source_target_pairs={{0,28},{1,29},{2,30},{3,31},{4,24},{5,25},{6,26},{7,27},{8,20},{9,... | collective-permute-start | bytes 294920 | tf_op jit(solution)/shard_map/ppermute | solution.py:342
  17.1 5.1 %collective-permute-start.8 = (bf16[2,192,128]{2,1,0:T(8,128)(2,1)S(1)}, bf16[2,192,128]{2,1,0:T(8,128)(2,1)S(1)}, u32[]{:S(2)}, u32[]{:S(2)}) collective-permute-start(bf16[2,192,128]{2,1,0:T(8,128)(2,1)S(1)} %pad_maximum_fusion), channel_id=1, source_target_pairs={{0,20},{1,21},{2,22},{3,23},{4,16},{5,17},{6,18},{7,19},{8,28},{9,... | collective-permute-start | bytes 294920 | tf_op jit(solution)/shard_map/ppermute | solution.py:342
  18.1 2.4 %collective-permute-start.5 = (bf16[192,128]{1,0:T(8,128)(2,1)S(1)}, bf16[192,128]{1,0:T(8,128)(2,1)S(1)}, u32[]{:S(2)}, u32[]{:S(2)}) collective-permute-start(bf16[192,128]{1,0:T(8,128)(2,1)S(1)} %collective-permute-done.4.after), channel_id=1, source_target_pairs={{0,16},{1,17},{2,18},{3,19},{4,20},{5,21},{6,22},{7,23},{8,24},{9,... | collective-permute-start | bytes 147464 | tf_op jit(solution)/shard_map/ppermute | solution.py:342
  22.2 22.3 %copy-start = (bf16[768,1536]{1,0:T(8,128)(2,1)S(1)}, bf16[768,1536]{1,0:T(8,128)(2,1)}, u32[]{:S(2)}) copy-start(bf16[768,1536]{1,0:T(8,128)(2,1)} %wo.1) | copy-start | bytes 7077892
  22.2 6.5 %collective-permute-start.10 = (bf16[192,128]{1,0:T(8,128)(2,1)S(1)}, bf16[192,128]{1,0:T(8,128)(2,1)S(1)}, u32[]{:S(2)}, u32[]{:S(2)}) collective-permute-start(bf16[192,128]{1,0:T(8,128)(2,1)S(1)} %get-tuple-element.65.after), channel_id=1, source_target_pairs={{0,112},{1,113},{2,114},{3,115},{4,116},{5,117},{6,118},{7,119},{8... | collective-permute-start | bytes 147464 | tf_op jit(solution)/shard_map/ppermute | solution.py:342
  24.0 4.7 %collective-permute-start.11 = (bf16[192,128]{1,0:T(8,128)(2,1)S(1)}, bf16[192,128]{1,0:T(8,128)(2,1)S(1)}, u32[]{:S(2)}, u32[]{:S(2)}) collective-permute-start(bf16[192,128]{1,0:T(8,128)(2,1)S(1)} %get-tuple-element.65.after), channel_id=1, source_target_pairs={{0,80},{1,81},{2,82},{3,83},{4,84},{5,85},{6,86},{7,87},{8,88},{9,... | collective-permute-start | bytes 147464 | tf_op jit(solution)/shard_map/ppermute | solution.py:342
  25.5 5.4 %collective-permute-start.9 = (bf16[192,128]{1,0:T(8,128)(2,1)S(1)}, bf16[192,128]{1,0:T(8,128)(2,1)S(1)}, u32[]{:S(2)}, u32[]{:S(2)}) collective-permute-start(bf16[192,128]{1,0:T(8,128)(2,1)S(1)} %get-tuple-element.65.after), channel_id=1, source_target_pairs={{0,48},{1,49},{2,50},{3,51},{4,52},{5,53},{6,54},{7,55},{8,56},{9,... | collective-permute-start | bytes 147464 | tf_op jit(solution)/shard_map/ppermute | solution.py:342
  30.9 7.1 %collective-permute-start.12 = (bf16[192,128]{1,0:T(8,128)(2,1)S(1)}, bf16[192,128]{1,0:T(8,128)(2,1)S(1)}, u32[]{:S(2)}, u32[]{:S(2)}) collective-permute-start(bf16[192,128]{1,0:T(8,128)(2,1)S(1)} %add_convert_fusion), channel_id=1, source_target_pairs={{0,208},{1,209},{2,210},{3,211},{4,212},{5,213},{6,214},{7,215},{8... | collective-permute-start | bytes 147464 | tf_op jit(solution)/shard_map/ppermute | solution.py:342
  38.1 5.3 %collective-permute-start.13 = (bf16[192,128]{1,0:T(8,128)(2,1)S(1)}, bf16[192,128]{1,0:T(8,128)(2,1)S(1)}, u32[]{:S(2)}, u32[]{:S(2)}) collective-permute-start(bf16[192,128]{1,0:T(8,128)(2,1)S(1)} %get-tuple-element.70), channel_id=1, source_target_pairs={{0,18},{1,19},{2,16},{3,17},{4,22},{5,23},{6,20},{7,21},{8,26},{9,... | collective-permute-start | bytes 147464 | tf_op jit(solution)/shard_map/ppermute | solution.py:342
  39.3 5.2 %collective-permute-start.14 = (bf16[192,128]{1,0:T(8,128)(2,1)S(1)}, bf16[192,128]{1,0:T(8,128)(2,1)S(1)}, u32[]{:S(2)}, u32[]{:S(2)}) collective-permute-start(bf16[192,128]{1,0:T(8,128)(2,1)S(1)} %get-tuple-element.69), channel_id=1, source_target_pairs={{0,19},{1,18},{2,17},{3,16},{4,23},{5,22},{6,21},{7,20},{8,27},{9,... | collective-permute-start | bytes 147464 | tf_op jit(solution)/shard_map/ppermute | solution.py:342
  40.7 3.8 %collective-permute-start.15 = (bf16[192,128]{1,0:T(8,128)(2,1)S(1)}, bf16[192,128]{1,0:T(8,128)(2,1)S(1)}, u32[]{:S(2)}, u32[]{:S(2)}) collective-permute-start(bf16[192,128]{1,0:T(8,128)(2,1)S(1)} %get-tuple-element.68), channel_id=1, source_target_pairs={{0,17},{1,16},{2,19},{3,18},{4,21},{5,20},{6,23},{7,22},{8,25},{9,... | collective-permute-start | bytes 147464 | tf_op jit(solution)/shard_map/ppermute | solution.py:342
  41.1 3.4 %collective-permute-start.16 = (bf16[192,128]{1,0:T(8,128)(2,1)S(1)}, bf16[192,128]{1,0:T(8,128)(2,1)S(1)}, u32[]{:S(2)}, u32[]{:S(2)}) collective-permute-start(bf16[192,128]{1,0:T(8,128)(2,1)S(1)} %get-tuple-element.67), channel_id=1, source_target_pairs={{0,16},{1,17},{2,18},{3,19},{4,20},{5,21},{6,22},{7,23},{8,24},{9,... | collective-permute-start | bytes 147464 | tf_op jit(solution)/shard_map/ppermute | solution.py:342

commit v9 on v8

--- a/solution.py
+++ b/solution.py
@@ -370,8 +370,7 @@
     both = jnp.stack([going, own])
     x3, x1 = flip(both, CORE | 3 * X), flip(both, CORE | X)
     other2 = flip(x2, CORE)
-    low = inside_of(query, keys, values, level_weights, x2, 0, half, width)
-    other2, x3, x1, low = lax.optimization_barrier((other2, x3, x1, low))
+    other2, x3, x1 = lax.optimization_barrier((other2, x3, x1))
     mine = plus(own.astype(F32), (x1[0], x2, x3[0]))
     total = plus(total + mine, (x1[1], other2, x3[1]))
     mine = mine.astype(BF16)
@@ -386,14 +385,14 @@
     past, gathered, factor = lax.optimization_barrier((past, gathered, factor))
     last = factor * past.astype(F32)
     back = [(gathered[distance] + last).astype(BF16) for distance in range(4)]
-    p2, p3, p1, p0 = lax.optimization_barrier(
-        (
-            flip(back[2], CORE | 2 * Y),
-            flip(back[3], CORE | 3 * Y),
-            flip(back[1], CORE | Y),
-            flip(back[0], CORE),
-        )
+    p2, p3, p1, p0 = (
+        flip(back[2], CORE | 2 * Y),
+        flip(back[3], CORE | 3 * Y),
+        flip(back[1], CORE | Y),
+        flip(back[0], CORE),
     )
+    low = inside_of(query, keys, values, level_weights, back[0], 0, half, width)
+    p2, p3, p1, p0, low = lax.optimization_barrier((p2, p3, p1, p0, low))
     return mixed_of(query, (low, high), (p0, p1, p2, p3), w_output, width)
 
 

time: 47.4 us -> 47.6 us (level)
  no operation moved by 1% of the time
where the time goes in v9:
time: 47.6 us; the launch traced here: 47.3 us
  starting transfers between devices  21.3 us (45%)
  Pallas kernels  13.4 us (28%)
  waiting for transfers between devices  12 us (25%)
    ppermute x17, starting transfers between devices, flip(): lax.ppermute(value, AXES, [(source, source ^ mask) for source in range(de...  21.3 us
    ppermute x17, waiting for transfers between devices, flip(): lax.ppermute(value, AXES, [(source, source ^ mask) for source in range(de...  12 us
    pallas_call x1, Pallas kernels, states_of(): pl.pallas_call(functools.partial(state_kernel, width), out_shape=(side, s...  4.72 us
    pallas_call x2, Pallas kernels, inside_of(): pl.pallas_call(functools.partial(inside_kernel, width, first), out_shape=...  3.9 us
    pallas_call x1, Pallas kernels, mixed_of(): pl.pallas_call(functools.partial(mix_kernel, width), out_shape=jax.ShapeD...  2.37 us
    pallas_call x1, Pallas kernels, query_of(): pl.pallas_call(functools.partial(query_kernel, width), out_shape=jax.Shap...  1.6 us
  transfers between devices with their start and end apart: 17, of which 8 were waited for; matrix products, arithmetic and copies ran while one was open for 0% of the time, Pallas kernels for 13%

profile of v9, /device:TPU:32, one launch (start us, length us, event | category | flops | bytes accessed | tf_op | source)
XLA Modules:
  0.0 47.3 jit_solution(16585395633503979250)
XLA Ops:
  0.0 4.7 %states.1 = (bf16[512,768]{1,0:T(8,128)(2,1)S(1)}, bf16[512,768]{1,0:T(8,128)(2,1)S(1)}, bf16[512,1536]{1,0:T(8,128)(2,1)S(1)}, bf16[1536,768]{1,0:T(8,128)(2,1)...) custom-call(bf16[512,1536]{1,0:T(8,128)(2,1)} %tok_hbm.1, ...), custom_call_target="tpu_custom_call" | custom-call | tf_op jit(solution)/shard_map/states/pallas_call | solution.py:127
  4.7 2.7 %collective-permute-start = (bf16[192,128]{1,0:T(8,128)(2,1)S(1)}, bf16[192,128]{1,0:T(8,128)(2,1)S(1)}, u32[]{:S(2)}, u32[]{:S(2)}) collective-permute-start(bf16[192,128]{1,0:T(8,128)(2,1)S(1)} %get-tuple-element.35), channel_id=1, source_target_pairs={{0,18},{1,19},{2,16},{3,17},{4,22},{5,23},{6,20},{7,21},{8,26},{9,... | collective-permute-start | bytes 147464 | tf_op jit(solution)/shard_map/ppermute | solution.py:342
  7.4 1.3 %collective-permute-start.1 = (bf16[192,128]{1,0:T(8,128)(2,1)S(1)}, bf16[192,128]{1,0:T(8,128)(2,1)S(1)}, u32[]{:S(2)}, u32[]{:S(2)}) collective-permute-start(bf16[192,128]{1,0:T(8,128)(2,1)S(1)} %get-tuple-element.36), channel_id=1, source_target_pairs={{0,19},{1,18},{2,17},{3,16},{4,23},{5,22},{6,21},{7,20},{8,27},{9,... | collective-permute-start | bytes 147464 | tf_op jit(solution)/shard_map/ppermute | solution.py:342
  8.8 0.0 collective-permute-start.2
  8.8 0.0 collective-permute-start.3
  8.8 0.0 copy-start.1
  8.8 1.6 %query.1.q_ref = bf16[512,768]{1,0:T(8,128)(2,1)S(1)} custom-call(bf16[512,1536]{1,0:T(8,128)(2,1)S(1)} %get-tuple-element.39.tok, bf16[1536,768]{1,0:T(8,128)(2,1)S(1)} %get-tuple-element.40.wq), custom_call_target="tpu_custom_call" | custom-call | tf_op jit(solution)/shard_map/query/pallas_call | solution.py:161
  10.4 0.0 collective-permute-done.refs_2_
  10.4 1.8 %collective-permute-done.1.refs_3_ = bf16[192,128]{1,0:T(8,128)(2,1)S(1)} collective-permute-done((bf16[192,128]{1,0:T(8,128)(2,1)S(1)}, bf16[192,128]{1,0:T(8,128)(2,1)S(1)}, u32[]{:S(2)}, u32[]{:S(2)}) %collective-permute-start.1) | collective-permute-done | bytes 49184 | tf_op jit(solution)/shard_map/ppermute | solution.py:342
  12.2 0.6 %collective-permute-done.2.refs_1_ = bf16[192,128]{1,0:T(8,128)(2,1)S(1)} collective-permute-done((bf16[192,128]{1,0:T(8,128)(2,1)S(1)}, bf16[192,128]{1,0:T(8,128)(2,1)S(1)}, u32[]{:S(2)}, u32[]{:S(2)}) %collective-permute-start.2) | collective-permute-done | bytes 49184 | tf_op jit(solution)/shard_map/ppermute | solution.py:342
  12.8 0.0 collective-permute-done.3.refs_0_
  12.9 0.2 collective-permute-start.4
  13.1 3.0 %collective-permute-start.5 = (bf16[192,128]{1,0:T(8,128)(2,1)S(1)}, bf16[192,128]{1,0:T(8,128)(2,1)S(1)}, u32[]{:S(2)}, u32[]{:S(2)}) collective-permute-start(bf16[192,128]{1,0:T(8,128)(2,1)S(1)} %fusion.6), channel_id=1, source_target_pairs={{0,24},{1,25},{2,26},{3,27},{4,28},{5,29},{6,30},{7,31},{8,16},{9,... | collective-permute-start | bytes 147464 | tf_op jit(solution)/shard_map/ppermute | solution.py:342
  16.1 0.0 collective-permute-done.4
  16.1 1.0 %collective-permute-start.7 = (bf16[2,192,128]{2,1,0:T(8,128)(2,1)S(1)}, bf16[2,192,128]{2,1,0:T(8,128)(2,1)S(1)}, u32[]{:S(2)}, u32[]{:S(2)}) collective-permute-start(bf16[2,192,128]{2,1,0:T(8,128)(2,1)S(1)} %pad_maximum_fusion), channel_id=1, source_target_pairs={{0,28},{1,29},{2,30},{3,31},{4,24},{5,25},{6,26},{7,27},{8,20},{9,... | collective-permute-start | bytes 294920 | tf_op jit(solution)/shard_map/ppermute | solution.py:342
  17.1 0.0 collective-permute-start.8
  17.1 1.0 %collective-permute-done.5 = bf16[192,128]{1,0:T(8,128)(2,1)S(1)} collective-permute-done((bf16[192,128]{1,0:T(8,128)(2,1)S(1)}, bf16[192,128]{1,0:T(8,128)(2,1)S(1)}, u32[]{:S(2)}, u32[]{:S(2)}) %collective-permute-start.5) | collective-permute-done | bytes 49184 | tf_op jit(solution)/shard_map/ppermute | solution.py:342
  18.1 0.4 collective-permute-start.6
  18.5 0.9 %collective-permute-done.6.refs_5_ = bf16[192,128]{1,0:T(8,128)(2,1)S(1)} collective-permute-done((bf16[192,128]{1,0:T(8,128)(2,1)S(1)}, bf16[192,128]{1,0:T(8,128)(2,1)S(1)}, u32[]{:S(2)}, u32[]{:S(2)}) %collective-permute-start.6) | collective-permute-done | bytes 49184 | tf_op jit(solution)/shard_map/ppermute | solution.py:342
  19.4 2.8 %collective-permute-done.7.refs_6_ = bf16[2,192,128]{2,1,0:T(8,128)(2,1)S(1)} collective-permute-done((bf16[2,192,128]{2,1,0:T(8,128)(2,1)S(1)}, bf16[2,192,128]{2,1,0:T(8,128)(2,1)S(1)}, u32[]{:S(2)}, u32[]{:S(2)}) %collective-permute-start.7) | collective-permute-done | bytes 98336 | tf_op jit(solution)/shard_map/ppermute | solution.py:342
  22.2 0.0 collective-permute-done.8.refs_4_
  22.2 0.1 fusion.8
  22.2 1.8 %collective-permute-start.10 = (bf16[192,128]{1,0:T(8,128)(2,1)S(1)}, bf16[192,128]{1,0:T(8,128)(2,1)S(1)}, u32[]{:S(2)}, u32[]{:S(2)}) collective-permute-start(bf16[192,128]{1,0:T(8,128)(2,1)S(1)} %get-tuple-element.65.after), channel_id=1, source_target_pairs={{0,112},{1,113},{2,114},{3,115},{4,116},{5,117},{6,118},{7,119},{8... | collective-permute-start | bytes 147464 | tf_op jit(solution)/shard_map/ppermute | solution.py:342
  24.0 1.4 %collective-permute-start.11 = (bf16[192,128]{1,0:T(8,128)(2,1)S(1)}, bf16[192,128]{1,0:T(8,128)(2,1)S(1)}, u32[]{:S(2)}, u32[]{:S(2)}) collective-permute-start(bf16[192,128]{1,0:T(8,128)(2,1)S(1)} %get-tuple-element.65.after), channel_id=1, source_target_pairs={{0,80},{1,81},{2,82},{3,83},{4,84},{5,85},{6,86},{7,87},{8,88},{9,... | collective-permute-start | bytes 147464 | tf_op jit(solution)/shard_map/ppermute | solution.py:342
  25.4 1.3 %collective-permute-start.9 = (bf16[192,128]{1,0:T(8,128)(2,1)S(1)}, bf16[192,128]{1,0:T(8,128)(2,1)S(1)}, u32[]{:S(2)}, u32[]{:S(2)}) collective-permute-start(bf16[192,128]{1,0:T(8,128)(2,1)S(1)} %get-tuple-element.65.after), channel_id=1, source_target_pairs={{0,48},{1,49},{2,50},{3,51},{4,52},{5,53},{6,54},{7,55},{8,56},{9,... | collective-permute-start | bytes 147464 | tf_op jit(solution)/shard_map/ppermute | solution.py:342
  26.8 0.0 copy-done.1
  26.8 0.1 copy.7.levels
  26.9 1.9 %inside.2.high_ref = f32[512,384]{1,0:T(8,128)S(1)} custom-call(bf16[512,768]{1,0:T(8,128)(2,1)S(1)} %query.1.q_ref, bf16[512,768]{1,0:T(8,128)(2,1)S(1)} %get-tuple-element.49.k_ref, bf16[512,768]{1,0:T(8,128)(2,1)S(1)} %get-tuple-element.50.v_ref, f32[9,6]{1,0:T(8,128)S(1)} %copy.7.levels, bf16[192,128]{1,0:T(8,128)(2,1)S(1)} %get-tuple-element.65.after), custom_call_target="tpu_custom_call" | custom-call | tf_op jit(solution)/shard_map/inside/pallas_call | solution.py:200
  28.8 0.0 collective-permute-done.10.refs_10_
  28.8 0.0 collective-permute-done.11.refs_9_
  28.9 2.0 %collective-permute-done.9.refs_8_ = bf16[192,128]{1,0:T(8,128)(2,1)S(1)} collective-permute-done((bf16[192,128]{1,0:T(8,128)(2,1)S(1)}, bf16[192,128]{1,0:T(8,128)(2,1)S(1)}, u32[]{:S(2)}, u32[]{:S(2)}) %collective-permute-start.9) | collective-permute-done | bytes 49184 | tf_op jit(solution)/shard_map/ppermute | solution.py:342
  30.9 0.0 copy-start
  30.9 4.5 %collective-permute-start.12 = (bf16[192,128]{1,0:T(8,128)(2,1)S(1)}, bf16[192,128]{1,0:T(8,128)(2,1)S(1)}, u32[]{:S(2)}, u32[]{:S(2)}) collective-permute-start(bf16[192,128]{1,0:T(8,128)(2,1)S(1)} %add_convert_fusion), channel_id=1, source_target_pairs={{0,208},{1,209},{2,210},{3,211},{4,212},{5,213},{6,214},{7,215},{8... | collective-permute-start | bytes 147464 | tf_op jit(solution)/shard_map/ppermute | solution.py:342
  35.5 0.8 %gather.1 = (f32[4,192,128]{2,1,0:T(8,128)S(1)}, f32[192,128]{1,0:T(8,128)S(1)}) custom-call(f32[9,6]{1,0:T(8,128)S(1)} %copy.7.levels, bf16[192,128]{1,0:T(8,128)(2,1)S(1)} %collective-permute-done.3.refs_0_, bf16[192,128]{1,0:T(8,128)(2,1)S(1)} %collective-permute-done.2.refs_1_, bf16[192,128]{1,0:T(8,128)(2,1)S(1)} %collective-permute-done.refs_2_, ...), custom_call_target="tpu_custom_call" | custom-call | tf_op jit(solution)/shard_map/gather/pallas_call | solution.py:245
  36.3 1.8 %collective-permute-done.12 = bf16[192,128]{1,0:T(8,128)(2,1)S(1)} collective-permute-done((bf16[192,128]{1,0:T(8,128)(2,1)S(1)}, bf16[192,128]{1,0:T(8,128)(2,1)S(1)}, u32[]{:S(2)}, u32[]{:S(2)}) %collective-permute-start.12) | collective-permute-done | bytes 49184 | tf_op jit(solution)/shard_map/ppermute | solution.py:342
  38.1 1.4 %collective-permute-start.13 = (bf16[192,128]{1,0:T(8,128)(2,1)S(1)}, bf16[192,128]{1,0:T(8,128)(2,1)S(1)}, u32[]{:S(2)}, u32[]{:S(2)}) collective-permute-start(bf16[192,128]{1,0:T(8,128)(2,1)S(1)} %get-tuple-element.70), channel_id=1, source_target_pairs={{0,18},{1,19},{2,16},{3,17},{4,22},{5,23},{6,20},{7,21},{8,26},{9,... | collective-permute-start | bytes 147464 | tf_op jit(solution)/shard_map/ppermute | solution.py:342
  39.5 1.4 %collective-permute-start.14 = (bf16[192,128]{1,0:T(8,128)(2,1)S(1)}, bf16[192,128]{1,0:T(8,128)(2,1)S(1)}, u32[]{:S(2)}, u32[]{:S(2)}) collective-permute-start(bf16[192,128]{1,0:T(8,128)(2,1)S(1)} %get-tuple-element.69), channel_id=1, source_target_pairs={{0,19},{1,18},{2,17},{3,16},{4,23},{5,22},{6,21},{7,20},{8,27},{9,... | collective-permute-start | bytes 147464 | tf_op jit(solution)/shard_map/ppermute | solution.py:342
  40.9 0.4 collective-permute-start.15
  41.3 0.4 collective-permute-start.16
  41.8 1.9 %inside.3.low_ref = f32[512,384]{1,0:T(8,128)S(1)} custom-call(bf16[512,768]{1,0:T(8,128)(2,1)S(1)} %query.1.q_ref, bf16[512,768]{1,0:T(8,128)(2,1)S(1)} %get-tuple-element.49.k_ref, bf16[512,768]{1,0:T(8,128)(2,1)S(1)} %get-tuple-element.50.v_ref, f32[9,6]{1,0:T(8,128)S(1)} %copy.7.levels, bf16[192,128]{1,0:T(8,128)(2,1)S(1)} %get-tuple-element.67.after), custom_call_target="tpu_custom_call" | custom-call | tf_op jit(solution)/shard_map/inside/pallas_call | solution.py:200
  43.7 0.0 collective-permute-done.13.two
  43.7 1.0 %collective-permute-done.14.three = bf16[192,128]{1,0:T(8,128)(2,1)S(1)} collective-permute-done((bf16[192,128]{1,0:T(8,128)(2,1)S(1)}, bf16[192,128]{1,0:T(8,128)(2,1)S(1)}, u32[]{:S(2)}, u32[]{:S(2)}) %collective-permute-start.14) | collective-permute-done | bytes 49184 | tf_op jit(solution)/shard_map/ppermute | solution.py:342
  44.7 0.0 collective-permute-done.15.one
  44.7 0.0 collective-permute-done.16.own
  44.7 0.0 copy-done
  44.7 2.4 %mix.1 = bf16[512,1536]{1,0:T(8,128)(2,1)} custom-call(bf16[512,768]{1,0:T(8,128)(2,1)S(1)} %query.1.q_ref, f32[512,384]{1,0:T(8,128)S(1)} %inside.3.low_ref, f32[512,384]{1,0:T(8,128)S(1)} %inside.2.high_ref, bf16[192,128]{1,0:T(8,128)(2,1)S(1)} %collective-permute-done.16.own, bf16[192,128]{1,0:T(8,128)(2,1)S(1)} %collective-permute-done.15.one, ...), custom_call_target="tpu_custom_call" | custom-call | tf_op jit(solution)/shard_map/mix/pallas_call | solution.py:320
  (4 shorter events, 0.1 us)
Async XLA Ops:
  4.7 5.7 %collective-permute-start = (bf16[192,128]{1,0:T(8,128)(2,1)S(1)}, bf16[192,128]{1,0:T(8,128)(2,1)S(1)}, u32[]{:S(2)}, u32[]{:S(2)}) collective-permute-start(bf16[192,128]{1,0:T(8,128)(2,1)S(1)} %get-tuple-element.35), channel_id=1, source_target_pairs={{0,18},{1,19},{2,16},{3,17},{4,22},{5,23},{6,20},{7,21},{8,26},{9,... | collective-permute-start | bytes 147464 | tf_op jit(solution)/shard_map/ppermute | solution.py:342
  7.4 4.7 %collective-permute-start.1 = (bf16[192,128]{1,0:T(8,128)(2,1)S(1)}, bf16[192,128]{1,0:T(8,128)(2,1)S(1)}, u32[]{:S(2)}, u32[]{:S(2)}) collective-permute-start(bf16[192,128]{1,0:T(8,128)(2,1)S(1)} %get-tuple-element.36), channel_id=1, source_target_pairs={{0,19},{1,18},{2,17},{3,16},{4,23},{5,22},{6,21},{7,20},{8,27},{9,... | collective-permute-start | bytes 147464 | tf_op jit(solution)/shard_map/ppermute | solution.py:342
  8.8 4.0 %collective-permute-start.2 = (bf16[192,128]{1,0:T(8,128)(2,1)S(1)}, bf16[192,128]{1,0:T(8,128)(2,1)S(1)}, u32[]{:S(2)}, u32[]{:S(2)}) collective-permute-start(bf16[192,128]{1,0:T(8,128)(2,1)S(1)} %get-tuple-element.37), channel_id=1, source_target_pairs={{0,17},{1,16},{2,19},{3,18},{4,21},{5,20},{6,23},{7,22},{8,25},{9,... | collective-permute-start | bytes 147464 | tf_op jit(solution)/shard_map/ppermute | solution.py:342
  8.8 4.0 %collective-permute-start.3 = (bf16[192,128]{1,0:T(8,128)(2,1)S(1)}, bf16[192,128]{1,0:T(8,128)(2,1)S(1)}, u32[]{:S(2)}, u32[]{:S(2)}) collective-permute-start(bf16[192,128]{1,0:T(8,128)(2,1)S(1)} %get-tuple-element.38), channel_id=1, source_target_pairs={{0,16},{1,17},{2,18},{3,19},{4,20},{5,21},{6,22},{7,23},{8,24},{9,... | collective-permute-start | bytes 147464 | tf_op jit(solution)/shard_map/ppermute | solution.py:342
  8.8 18.0 %copy-start.1 = (f32[9,6]{0,1:T(8,128)S(1)}, f32[9,6]{0,1:T(8,128)}, u32[]{:S(2)}) copy-start(f32[9,6]{0,1:T(8,128)} %param.11) | copy-start | bytes 652
  12.9 3.2 %collective-permute-start.4 = (bf16[192,128]{1,0:T(8,128)(2,1)S(1)}, bf16[192,128]{1,0:T(8,128)(2,1)S(1)}, u32[]{:S(2)}, u32[]{:S(2)}) collective-permute-start(bf16[192,128]{1,0:T(8,128)(2,1)S(1)} %fusion.6), channel_id=1, source_target_pairs={{0,16},{1,17},{2,18},{3,19},{4,20},{5,21},{6,22},{7,23},{8,24},{9,... | collective-permute-start | bytes 147464 | tf_op jit(solution)/shard_map/ppermute | solution.py:342
  13.1 5.1 %collective-permute-start.5 = (bf16[192,128]{1,0:T(8,128)(2,1)S(1)}, bf16[192,128]{1,0:T(8,128)(2,1)S(1)}, u32[]{:S(2)}, u32[]{:S(2)}) collective-permute-start(bf16[192,128]{1,0:T(8,128)(2,1)S(1)} %fusion.6), channel_id=1, source_target_pairs={{0,24},{1,25},{2,26},{3,27},{4,28},{5,29},{6,30},{7,31},{8,16},{9,... | collective-permute-start | bytes 147464 | tf_op jit(solution)/shard_map/ppermute | solution.py:342
  16.1 6.1 %collective-permute-start.7 = (bf16[2,192,128]{2,1,0:T(8,128)(2,1)S(1)}, bf16[2,192,128]{2,1,0:T(8,128)(2,1)S(1)}, u32[]{:S(2)}, u32[]{:S(2)}) collective-permute-start(bf16[2,192,128]{2,1,0:T(8,128)(2,1)S(1)} %pad_maximum_fusion), channel_id=1, source_target_pairs={{0,28},{1,29},{2,30},{3,31},{4,24},{5,25},{6,26},{7,27},{8,20},{9,... | collective-permute-start | bytes 294920 | tf_op jit(solution)/shard_map/ppermute | solution.py:342
  17.1 5.1 %collective-permute-start.8 = (bf16[2,192,128]{2,1,0:T(8,128)(2,1)S(1)}, bf16[2,192,128]{2,1,0:T(8,128)(2,1)S(1)}, u32[]{:S(2)}, u32[]{:S(2)}) collective-permute-start(bf16[2,192,128]{2,1,0:T(8,128)(2,1)S(1)} %pad_maximum_fusion), channel_id=1, source_target_pairs={{0,20},{1,21},{2,22},{3,23},{4,16},{5,17},{6,18},{7,19},{8,28},{9,... | collective-permute-start | bytes 294920 | tf_op jit(solution)/shard_map/ppermute | solution.py:342
  18.1 1.2 %collective-permute-start.6 = (bf16[192,128]{1,0:T(8,128)(2,1)S(1)}, bf16[192,128]{1,0:T(8,128)(2,1)S(1)}, u32[]{:S(2)}, u32[]{:S(2)}) collective-permute-start(bf16[192,128]{1,0:T(8,128)(2,1)S(1)} %collective-permute-done.5), channel_id=1, source_target_pairs={{0,16},{1,17},{2,18},{3,19},{4,20},{5,21},{6,22},{7,23},{8,24},{9,... | collective-permute-start | bytes 147464 | tf_op jit(solution)/shard_map/ppermute | solution.py:342
  22.2 6.6 %collective-permute-start.10 = (bf16[192,128]{1,0:T(8,128)(2,1)S(1)}, bf16[192,128]{1,0:T(8,128)(2,1)S(1)}, u32[]{:S(2)}, u32[]{:S(2)}) collective-permute-start(bf16[192,128]{1,0:T(8,128)(2,1)S(1)} %get-tuple-element.65.after), channel_id=1, source_target_pairs={{0,112},{1,113},{2,114},{3,115},{4,116},{5,117},{6,118},{7,119},{8... | collective-permute-start | bytes 147464 | tf_op jit(solution)/shard_map/ppermute | solution.py:342
  24.0 4.8 %collective-permute-start.11 = (bf16[192,128]{1,0:T(8,128)(2,1)S(1)}, bf16[192,128]{1,0:T(8,128)(2,1)S(1)}, u32[]{:S(2)}, u32[]{:S(2)}) collective-permute-start(bf16[192,128]{1,0:T(8,128)(2,1)S(1)} %get-tuple-element.65.after), channel_id=1, source_target_pairs={{0,80},{1,81},{2,82},{3,83},{4,84},{5,85},{6,86},{7,87},{8,88},{9,... | collective-permute-start | bytes 147464 | tf_op jit(solution)/shard_map/ppermute | solution.py:342
  25.4 5.4 %collective-permute-start.9 = (bf16[192,128]{1,0:T(8,128)(2,1)S(1)}, bf16[192,128]{1,0:T(8,128)(2,1)S(1)}, u32[]{:S(2)}, u32[]{:S(2)}) collective-permute-start(bf16[192,128]{1,0:T(8,128)(2,1)S(1)} %get-tuple-element.65.after), channel_id=1, source_target_pairs={{0,48},{1,49},{2,50},{3,51},{4,52},{5,53},{6,54},{7,55},{8,56},{9,... | collective-permute-start | bytes 147464 | tf_op jit(solution)/shard_map/ppermute | solution.py:342
  30.9 13.8 %copy-start = (bf16[768,1536]{1,0:T(8,128)(2,1)S(1)}, bf16[768,1536]{1,0:T(8,128)(2,1)}, u32[]{:S(2)}) copy-start(bf16[768,1536]{1,0:T(8,128)(2,1)} %wo.1) | copy-start | bytes 7077892
  30.9 7.1 %collective-permute-start.12 = (bf16[192,128]{1,0:T(8,128)(2,1)S(1)}, bf16[192,128]{1,0:T(8,128)(2,1)S(1)}, u32[]{:S(2)}, u32[]{:S(2)}) collective-permute-start(bf16[192,128]{1,0:T(8,128)(2,1)S(1)} %add_convert_fusion), channel_id=1, source_target_pairs={{0,208},{1,209},{2,210},{3,211},{4,212},{5,213},{6,214},{7,215},{8... | collective-permute-start | bytes 147464 | tf_op jit(solution)/shard_map/ppermute | solution.py:342
  38.1 5.6 %collective-permute-start.13 = (bf16[192,128]{1,0:T(8,128)(2,1)S(1)}, bf16[192,128]{1,0:T(8,128)(2,1)S(1)}, u32[]{:S(2)}, u32[]{:S(2)}) collective-permute-start(bf16[192,128]{1,0:T(8,128)(2,1)S(1)} %get-tuple-element.70), channel_id=1, source_target_pairs={{0,18},{1,19},{2,16},{3,17},{4,22},{5,23},{6,20},{7,21},{8,26},{9,... | collective-permute-start | bytes 147464 | tf_op jit(solution)/shard_map/ppermute | solution.py:342
  39.5 5.2 %collective-permute-start.14 = (bf16[192,128]{1,0:T(8,128)(2,1)S(1)}, bf16[192,128]{1,0:T(8,128)(2,1)S(1)}, u32[]{:S(2)}, u32[]{:S(2)}) collective-permute-start(bf16[192,128]{1,0:T(8,128)(2,1)S(1)} %get-tuple-element.69), channel_id=1, source_target_pairs={{0,19},{1,18},{2,17},{3,16},{4,23},{5,22},{6,21},{7,20},{8,27},{9,... | collective-permute-start | bytes 147464 | tf_op jit(solution)/shard_map/ppermute | solution.py:342
  40.9 3.8 %collective-permute-start.15 = (bf16[192,128]{1,0:T(8,128)(2,1)S(1)}, bf16[192,128]{1,0:T(8,128)(2,1)S(1)}, u32[]{:S(2)}, u32[]{:S(2)}) collective-permute-start(bf16[192,128]{1,0:T(8,128)(2,1)S(1)} %get-tuple-element.68), channel_id=1, source_target_pairs={{0,17},{1,16},{2,19},{3,18},{4,21},{5,20},{6,23},{7,22},{8,25},{9,... | collective-permute-start | bytes 147464 | tf_op jit(solution)/shard_map/ppermute | solution.py:342
  41.3 3.4 %collective-permute-start.16 = (bf16[192,128]{1,0:T(8,128)(2,1)S(1)}, bf16[192,128]{1,0:T(8,128)(2,1)S(1)}, u32[]{:S(2)}, u32[]{:S(2)}) collective-permute-start(bf16[192,128]{1,0:T(8,128)(2,1)S(1)} %get-tuple-element.67.after), channel_id=1, source_target_pairs={{0,16},{1,17},{2,18},{3,19},{4,20},{5,21},{6,22},{7,23},{8,24},{9,... | collective-permute-start | bytes 147464 | tf_op jit(solution)/shard_map/ppermute | solution.py:342

commit v10 on v8

--- a/solution.py
+++ b/solution.py
@@ -224,7 +224,7 @@
 
         far = (
             factor(2, bit(x, 0)) * x1[1, rows, :].astype(F32)
-            + factor(3, bit(x, 1)) * (read(x2) + x3[1, rows, :].astype(F32))
+            + factor(3, bit(x, 1)) * (x2[1, rows, :].astype(F32) + read(x3))
             + factor(4, bit(core ^ 1, 0)) * read(mine)
             + factor(5, bit(z, 0)) * read(z1)
             + factor(6, bit(z, 1)) * (read(z2) + read(z3))
@@ -353,27 +353,27 @@
     width = w_query.shape[1] // heads
     half = heads // 2
     keys, values, tok, wq, *sent = states_of(tokens, w_key, w_value, w_query, heads, width)
-    n2, n3, n1, n0 = (
+    n3, n2, n1, n0 = (
+        flip(sent[3], CORE | 3 * Y),
         flip(sent[2], CORE | 2 * Y),
-        flip(sent[3], CORE | 3 * Y),
         flip(sent[1], CORE | Y),
         flip(sent[0], CORE),
     )
     query = query_of(tok, wq, width)
-    n2, n3, n1, n0, query = lax.optimization_barrier((n2, n3, n1, n0, query))
+    n3, n2, n1, n0, query = lax.optimization_barrier((n3, n2, n1, n0, query))
     near = (n0, n1, n2, n3)
     total = plus(n0.astype(F32), near[1:])
     going = total.astype(BF16)
 
     own = flip(going, CORE)
-    x2 = flip(going, CORE | 2 * X)
+    x3 = flip(going, CORE | 3 * X)
     both = jnp.stack([going, own])
-    x3, x1 = flip(both, CORE | 3 * X), flip(both, CORE | X)
-    other2 = flip(x2, CORE)
-    low = inside_of(query, keys, values, level_weights, x2, 0, half, width)
-    other2, x3, x1, low = lax.optimization_barrier((other2, x3, x1, low))
-    mine = plus(own.astype(F32), (x1[0], x2, x3[0]))
-    total = plus(total + mine, (x1[1], other2, x3[1]))
+    x2, x1 = flip(both, CORE | 2 * X), flip(both, CORE | X)
+    other3 = flip(x3, CORE)
+    low = inside_of(query, keys, values, level_weights, x3, 0, half, width)
+    other3, x2, x1, low = lax.optimization_barrier((other3, x2, x1, low))
+    mine = plus(own.astype(F32), (x1[0], x2[0], x3))
+    total = plus(total + mine, (x1[1], x2[1], other3))
     mine = mine.astype(BF16)
     going = total.astype(BF16)
     z1, z3, z2 = (flip(going, CORE | distance * Z) for distance in (1, 3, 2))
@@ -382,14 +382,14 @@
     going = plus(total, (z3, z2, z1)).astype(BF16)
 
     past = flip(going, CORE | 6 * Z)
-    gathered, factor = gather_of(level_weights, near, (x1, other2, x3, mine, z1, z2, z3))
+    gathered, factor = gather_of(level_weights, near, (x1, x2, other3, mine, z1, z2, z3))
     past, gathered, factor = lax.optimization_barrier((past, gathered, factor))
     last = factor * past.astype(F32)
     back = [(gathered[distance] + last).astype(BF16) for distance in range(4)]
-    p2, p3, p1, p0 = lax.optimization_barrier(
+    p3, p2, p1, p0 = lax.optimization_barrier(
         (
+            flip(back[3], CORE | 3 * Y),
             flip(back[2], CORE | 2 * Y),
-            flip(back[3], CORE | 3 * Y),
             flip(back[1], CORE | Y),
             flip(back[0], CORE),
         )

time: 47.4 us -> 48.9 us (1.032); the launches traced: 47.1 us -> 48 us
  starting transfers between devices: 21.1 us -> 22.8 us
  waiting for transfers between devices: 12 us -> 11.3 us
    ppermute x17, starting transfers between devices: 21.1 us -> 22.8 us  [flip(): lax.ppermute(value, AXES, [(source, source ^ mask) for source in range(de...]
    ppermute x17, waiting for transfers between devices: 12 us -> 11.3 us  [flip(): lax.ppermute(value, AXES, [(source, source ^ mask) for source in range(de...]
  transfers between devices with their start and end apart: 17 -> 17, of which waited for: 8 -> 10; matrix products, arithmetic and copies ran while one was open for 0% -> 0% of each run, Pallas kernels for 13% -> 13%
where the time goes in v10:
time: 48.9 us; the launch traced here: 48 us
  starting transfers between devices  22.8 us (47%)
  Pallas kernels  13.4 us (27%)
  waiting for transfers between devices  11.3 us (23%)
    ppermute x17, starting transfers between devices, flip(): lax.ppermute(value, AXES, [(source, source ^ mask) for source in range(de...  22.8 us
    ppermute x17, waiting for transfers between devices, flip(): lax.ppermute(value, AXES, [(source, source ^ mask) for source in range(de...  11.3 us
    pallas_call x1, Pallas kernels, states_of(): pl.pallas_call(functools.partial(state_kernel, width), out_shape=(side, s...  4.72 us
    pallas_call x2, Pallas kernels, inside_of(): pl.pallas_call(functools.partial(inside_kernel, width, first), out_shape=...  3.89 us
    pallas_call x1, Pallas kernels, mixed_of(): pl.pallas_call(functools.partial(mix_kernel, width), out_shape=jax.ShapeD...  2.37 us
    pallas_call x1, Pallas kernels, query_of(): pl.pallas_call(functools.partial(query_kernel, width), out_shape=jax.Shap...  1.6 us
  transfers between devices with their start and end apart: 17, of which 10 were waited for; matrix products, arithmetic and copies ran while one was open for 0% of the time, Pallas kernels for 13%

profile of v10, /device:TPU:32, one launch (start us, length us, event | category | flops | bytes accessed | tf_op | source)
XLA Modules:
  0.0 48.0 jit_solution(12718029381255791113)
XLA Ops:
  0.0 4.7 %states.1 = (bf16[512,768]{1,0:T(8,128)(2,1)S(1)}, bf16[512,768]{1,0:T(8,128)(2,1)S(1)}, bf16[512,1536]{1,0:T(8,128)(2,1)S(1)}, bf16[1536,768]{1,0:T(8,128)(2,1)...) custom-call(bf16[512,1536]{1,0:T(8,128)(2,1)} %tok_hbm.1, ...), custom_call_target="tpu_custom_call" | custom-call | tf_op jit(solution)/shard_map/states/pallas_call | solution.py:127
  4.7 2.5 %collective-permute-start = (bf16[192,128]{1,0:T(8,128)(2,1)S(1)}, bf16[192,128]{1,0:T(8,128)(2,1)S(1)}, u32[]{:S(2)}, u32[]{:S(2)}) collective-permute-start(bf16[192,128]{1,0:T(8,128)(2,1)S(1)} %get-tuple-element.35), channel_id=1, source_target_pairs={{0,19},{1,18},{2,17},{3,16},{4,23},{5,22},{6,21},{7,20},{8,27},{9,... | collective-permute-start | bytes 147464 | tf_op jit(solution)/shard_map/ppermute | solution.py:342
  7.3 0.9 %collective-permute-start.1 = (bf16[192,128]{1,0:T(8,128)(2,1)S(1)}, bf16[192,128]{1,0:T(8,128)(2,1)S(1)}, u32[]{:S(2)}, u32[]{:S(2)}) collective-permute-start(bf16[192,128]{1,0:T(8,128)(2,1)S(1)} %get-tuple-element.36), channel_id=1, source_target_pairs={{0,18},{1,19},{2,16},{3,17},{4,22},{5,23},{6,20},{7,21},{8,26},{9,... | collective-permute-start | bytes 147464 | tf_op jit(solution)/shard_map/ppermute | solution.py:342
  8.2 0.3 collective-permute-start.2
  8.5 0.2 collective-permute-start.3
  8.7 0.0 copy-start.1
  8.7 1.6 %query.1.q_ref = bf16[512,768]{1,0:T(8,128)(2,1)S(1)} custom-call(bf16[512,1536]{1,0:T(8,128)(2,1)S(1)} %get-tuple-element.39.tok, bf16[1536,768]{1,0:T(8,128)(2,1)S(1)} %get-tuple-element.40.wq), custom_call_target="tpu_custom_call" | custom-call | tf_op jit(solution)/shard_map/query/pallas_call | solution.py:161
  10.4 0.1 collective-permute-done.refs_3_
  10.5 1.8 %collective-permute-done.1.refs_2_ = bf16[192,128]{1,0:T(8,128)(2,1)S(1)} collective-permute-done((bf16[192,128]{1,0:T(8,128)(2,1)S(1)}, bf16[192,128]{1,0:T(8,128)(2,1)S(1)}, u32[]{:S(2)}, u32[]{:S(2)}) %collective-permute-start.1) | collective-permute-done | bytes 49184 | tf_op jit(solution)/shard_map/ppermute | solution.py:342
  12.3 0.0 collective-permute-done.2.refs_1_
  12.3 0.0 collective-permute-done.3.refs_0_
  12.3 1.1 %collective-permute-start.6 = (bf16[192,128]{1,0:T(8,128)(2,1)S(1)}, bf16[192,128]{1,0:T(8,128)(2,1)S(1)}, u32[]{:S(2)}, u32[]{:S(2)}) collective-permute-start(bf16[192,128]{1,0:T(8,128)(2,1)S(1)} %fusion.6), channel_id=1, source_target_pairs={{0,16},{1,17},{2,18},{3,19},{4,20},{5,21},{6,22},{7,23},{8,24},{9,... | collective-permute-start | bytes 147464 | tf_op jit(solution)/shard_map/ppermute | solution.py:342
  13.4 2.5 %collective-permute-start.4 = (bf16[192,128]{1,0:T(8,128)(2,1)S(1)}, bf16[192,128]{1,0:T(8,128)(2,1)S(1)}, u32[]{:S(2)}, u32[]{:S(2)}) collective-permute-start(bf16[192,128]{1,0:T(8,128)(2,1)S(1)} %fusion.6), channel_id=1, source_target_pairs={{0,28},{1,29},{2,30},{3,31},{4,24},{5,25},{6,26},{7,27},{8,20},{9,... | collective-permute-start | bytes 147464 | tf_op jit(solution)/shard_map/ppermute | solution.py:342
  15.9 0.0 collective-permute-done.6
  15.9 1.5 %collective-permute-start.7 = (bf16[2,192,128]{2,1,0:T(8,128)(2,1)S(1)}, bf16[2,192,128]{2,1,0:T(8,128)(2,1)S(1)}, u32[]{:S(2)}, u32[]{:S(2)}) collective-permute-start(bf16[2,192,128]{2,1,0:T(8,128)(2,1)S(1)} %pad_maximum_fusion), channel_id=1, source_target_pairs={{0,24},{1,25},{2,26},{3,27},{4,28},{5,29},{6,30},{7,31},{8,16},{9,... | collective-permute-start | bytes 294920 | tf_op jit(solution)/shard_map/ppermute | solution.py:342
  17.4 0.4 collective-permute-start.8
  17.8 0.7 %collective-permute-done.4.after = bf16[192,128]{1,0:T(8,128)(2,1)S(1)} collective-permute-done((bf16[192,128]{1,0:T(8,128)(2,1)S(1)}, bf16[192,128]{1,0:T(8,128)(2,1)S(1)}, u32[]{:S(2)}, u32[]{:S(2)}) %collective-permute-start.4) | collective-permute-done | bytes 49184 | tf_op jit(solution)/shard_map/ppermute | solution.py:342
  18.4 0.1 collective-permute-start.5
  18.5 0.0 copy-done.1
  18.5 0.1 copy.7.levels
  18.6 1.9 %inside.2.low_ref = f32[512,384]{1,0:T(8,128)S(1)} custom-call(bf16[512,768]{1,0:T(8,128)(2,1)S(1)} %query.1.q_ref, bf16[512,768]{1,0:T(8,128)(2,1)S(1)} %get-tuple-element.46.k_ref, bf16[512,768]{1,0:T(8,128)(2,1)S(1)} %get-tuple-element.47.v_ref, f32[9,6]{1,0:T(8,128)S(1)} %copy.7.levels, bf16[192,128]{1,0:T(8,128)(2,1)S(1)} %collective-permute-done.4.after), custom_call_target="tpu_custom_call" | custom-call | tf_op jit(solution)/shard_map/inside/pallas_call | solution.py:200
  20.6 0.0 collective-permute-done.5.refs_6_
  20.6 1.5 %collective-permute-done.7.refs_5_ = bf16[2,192,128]{2,1,0:T(8,128)(2,1)S(1)} collective-permute-done((bf16[2,192,128]{2,1,0:T(8,128)(2,1)S(1)}, bf16[2,192,128]{2,1,0:T(8,128)(2,1)S(1)}, u32[]{:S(2)}, u32[]{:S(2)}) %collective-permute-start.7) | collective-permute-done | bytes 98336 | tf_op jit(solution)/shard_map/ppermute | solution.py:342
  22.1 0.7 %collective-permute-done.8.refs_4_ = bf16[2,192,128]{2,1,0:T(8,128)(2,1)S(1)} collective-permute-done((bf16[2,192,128]{2,1,0:T(8,128)(2,1)S(1)}, bf16[2,192,128]{2,1,0:T(8,128)(2,1)S(1)}, u32[]{:S(2)}, u32[]{:S(2)}) %collective-permute-start.8) | collective-permute-done | bytes 98336 | tf_op jit(solution)/shard_map/ppermute | solution.py:342
  22.8 0.1 fusion.8
  22.8 0.0 copy-start
  22.8 1.9 %collective-permute-start.10 = (bf16[192,128]{1,0:T(8,128)(2,1)S(1)}, bf16[192,128]{1,0:T(8,128)(2,1)S(1)}, u32[]{:S(2)}, u32[]{:S(2)}) collective-permute-start(bf16[192,128]{1,0:T(8,128)(2,1)S(1)} %get-tuple-element.65.after), channel_id=1, source_target_pairs={{0,112},{1,113},{2,114},{3,115},{4,116},{5,117},{6,118},{7,119},{8... | collective-permute-start | bytes 147464 | tf_op jit(solution)/shard_map/ppermute | solution.py:342
  24.7 1.4 %collective-permute-start.11 = (bf16[192,128]{1,0:T(8,128)(2,1)S(1)}, bf16[192,128]{1,0:T(8,128)(2,1)S(1)}, u32[]{:S(2)}, u32[]{:S(2)}) collective-permute-start(bf16[192,128]{1,0:T(8,128)(2,1)S(1)} %get-tuple-element.65.after), channel_id=1, source_target_pairs={{0,80},{1,81},{2,82},{3,83},{4,84},{5,85},{6,86},{7,87},{8,88},{9,... | collective-permute-start | bytes 147464 | tf_op jit(solution)/shard_map/ppermute | solution.py:342
  26.2 1.2 %collective-permute-start.9 = (bf16[192,128]{1,0:T(8,128)(2,1)S(1)}, bf16[192,128]{1,0:T(8,128)(2,1)S(1)}, u32[]{:S(2)}, u32[]{:S(2)}) collective-permute-start(bf16[192,128]{1,0:T(8,128)(2,1)S(1)} %get-tuple-element.65.after), channel_id=1, source_target_pairs={{0,48},{1,49},{2,50},{3,51},{4,52},{5,53},{6,54},{7,55},{8,56},{9,... | collective-permute-start | bytes 147464 | tf_op jit(solution)/shard_map/ppermute | solution.py:342
  27.4 1.9 %inside.3.high_ref = f32[512,384]{1,0:T(8,128)S(1)} custom-call(bf16[512,768]{1,0:T(8,128)(2,1)S(1)} %query.1.q_ref, bf16[512,768]{1,0:T(8,128)(2,1)S(1)} %get-tuple-element.46.k_ref, bf16[512,768]{1,0:T(8,128)(2,1)S(1)} %get-tuple-element.47.v_ref, f32[9,6]{1,0:T(8,128)S(1)} %copy.7.levels, bf16[192,128]{1,0:T(8,128)(2,1)S(1)} %get-tuple-element.65.after), custom_call_target="tpu_custom_call" | custom-call | tf_op jit(solution)/shard_map/inside/pallas_call | solution.py:200
  29.3 0.0 collective-permute-done.10.refs_10_
  29.4 0.0 collective-permute-done.11.refs_9_
  29.4 2.1 %collective-permute-done.9.refs_8_ = bf16[192,128]{1,0:T(8,128)(2,1)S(1)} collective-permute-done((bf16[192,128]{1,0:T(8,128)(2,1)S(1)}, bf16[192,128]{1,0:T(8,128)(2,1)S(1)}, u32[]{:S(2)}, u32[]{:S(2)}) %collective-permute-start.9) | collective-permute-done | bytes 49184 | tf_op jit(solution)/shard_map/ppermute | solution.py:342
  31.5 4.6 %collective-permute-start.12 = (bf16[192,128]{1,0:T(8,128)(2,1)S(1)}, bf16[192,128]{1,0:T(8,128)(2,1)S(1)}, u32[]{:S(2)}, u32[]{:S(2)}) collective-permute-start(bf16[192,128]{1,0:T(8,128)(2,1)S(1)} %add_convert_fusion), channel_id=1, source_target_pairs={{0,208},{1,209},{2,210},{3,211},{4,212},{5,213},{6,214},{7,215},{8... | collective-permute-start | bytes 147464 | tf_op jit(solution)/shard_map/ppermute | solution.py:342
  36.1 0.8 %gather.1 = (f32[4,192,128]{2,1,0:T(8,128)S(1)}, f32[192,128]{1,0:T(8,128)S(1)}) custom-call(f32[9,6]{1,0:T(8,128)S(1)} %copy.7.levels, bf16[192,128]{1,0:T(8,128)(2,1)S(1)} %collective-permute-done.3.refs_0_, bf16[192,128]{1,0:T(8,128)(2,1)S(1)} %collective-permute-done.2.refs_1_, bf16[192,128]{1,0:T(8,128)(2,1)S(1)} %collective-permute-done.1.refs_2_, ...), custom_call_target="tpu_custom_call" | custom-call | tf_op jit(solution)/shard_map/gather/pallas_call | solution.py:245
  36.9 2.1 %collective-permute-done.12 = bf16[192,128]{1,0:T(8,128)(2,1)S(1)} collective-permute-done((bf16[192,128]{1,0:T(8,128)(2,1)S(1)}, bf16[192,128]{1,0:T(8,128)(2,1)S(1)}, u32[]{:S(2)}, u32[]{:S(2)}) %collective-permute-start.12) | collective-permute-done | bytes 49184 | tf_op jit(solution)/shard_map/ppermute | solution.py:342
  39.0 1.2 %collective-permute-start.13 = (bf16[192,128]{1,0:T(8,128)(2,1)S(1)}, bf16[192,128]{1,0:T(8,128)(2,1)S(1)}, u32[]{:S(2)}, u32[]{:S(2)}) collective-permute-start(bf16[192,128]{1,0:T(8,128)(2,1)S(1)} %get-tuple-element.70), channel_id=1, source_target_pairs={{0,19},{1,18},{2,17},{3,16},{4,23},{5,22},{6,21},{7,20},{8,27},{9,... | collective-permute-start | bytes 147464 | tf_op jit(solution)/shard_map/ppermute | solution.py:342
  40.2 0.7 %collective-permute-start.14 = (bf16[192,128]{1,0:T(8,128)(2,1)S(1)}, bf16[192,128]{1,0:T(8,128)(2,1)S(1)}, u32[]{:S(2)}, u32[]{:S(2)}) collective-permute-start(bf16[192,128]{1,0:T(8,128)(2,1)S(1)} %get-tuple-element.69), channel_id=1, source_target_pairs={{0,18},{1,19},{2,16},{3,17},{4,22},{5,23},{6,20},{7,21},{8,26},{9,... | collective-permute-start | bytes 147464 | tf_op jit(solution)/shard_map/ppermute | solution.py:342
  40.9 1.8 %collective-permute-start.15 = (bf16[192,128]{1,0:T(8,128)(2,1)S(1)}, bf16[192,128]{1,0:T(8,128)(2,1)S(1)}, u32[]{:S(2)}, u32[]{:S(2)}) collective-permute-start(bf16[192,128]{1,0:T(8,128)(2,1)S(1)} %get-tuple-element.68), channel_id=1, source_target_pairs={{0,17},{1,16},{2,19},{3,18},{4,21},{5,20},{6,23},{7,22},{8,25},{9,... | collective-permute-start | bytes 147464 | tf_op jit(solution)/shard_map/ppermute | solution.py:342
  42.7 0.4 collective-permute-start.16
  43.1 1.0 %collective-permute-done.13.three = bf16[192,128]{1,0:T(8,128)(2,1)S(1)} collective-permute-done((bf16[192,128]{1,0:T(8,128)(2,1)S(1)}, bf16[192,128]{1,0:T(8,128)(2,1)S(1)}, u32[]{:S(2)}, u32[]{:S(2)}) %collective-permute-start.13) | collective-permute-done | bytes 49184 | tf_op jit(solution)/shard_map/ppermute | solution.py:342
  44.1 1.2 %collective-permute-done.14.two = bf16[192,128]{1,0:T(8,128)(2,1)S(1)} collective-permute-done((bf16[192,128]{1,0:T(8,128)(2,1)S(1)}, bf16[192,128]{1,0:T(8,128)(2,1)S(1)}, u32[]{:S(2)}, u32[]{:S(2)}) %collective-permute-start.14) | collective-permute-done | bytes 49184 | tf_op jit(solution)/shard_map/ppermute | solution.py:342
  45.2 0.2 collective-permute-done.15.one
  45.5 0.0 collective-permute-done.16.own
  45.5 0.0 copy-done
  45.5 2.4 %mix.1 = bf16[512,1536]{1,0:T(8,128)(2,1)} custom-call(bf16[512,768]{1,0:T(8,128)(2,1)S(1)} %query.1.q_ref, f32[512,384]{1,0:T(8,128)S(1)} %inside.2.low_ref, f32[512,384]{1,0:T(8,128)S(1)} %inside.3.high_ref, bf16[192,128]{1,0:T(8,128)(2,1)S(1)} %collective-permute-done.16.own, bf16[192,128]{1,0:T(8,128)(2,1)S(1)} %collective-permute-done.15.one, ...), custom_call_target="tpu_custom_call" | custom-call | tf_op jit(solution)/shard_map/mix/pallas_call | solution.py:320
  (4 shorter events, 0.1 us)
Async XLA Ops:
  4.7 5.8 %collective-permute-start = (bf16[192,128]{1,0:T(8,128)(2,1)S(1)}, bf16[192,128]{1,0:T(8,128)(2,1)S(1)}, u32[]{:S(2)}, u32[]{:S(2)}) collective-permute-start(bf16[192,128]{1,0:T(8,128)(2,1)S(1)} %get-tuple-element.35), channel_id=1, source_target_pairs={{0,19},{1,18},{2,17},{3,16},{4,23},{5,22},{6,21},{7,20},{8,27},{9,... | collective-permute-start | bytes 147464 | tf_op jit(solution)/shard_map/ppermute | solution.py:342
  7.3 5.0 %collective-permute-start.1 = (bf16[192,128]{1,0:T(8,128)(2,1)S(1)}, bf16[192,128]{1,0:T(8,128)(2,1)S(1)}, u32[]{:S(2)}, u32[]{:S(2)}) collective-permute-start(bf16[192,128]{1,0:T(8,128)(2,1)S(1)} %get-tuple-element.36), channel_id=1, source_target_pairs={{0,18},{1,19},{2,16},{3,17},{4,22},{5,23},{6,20},{7,21},{8,26},{9,... | collective-permute-start | bytes 147464 | tf_op jit(solution)/shard_map/ppermute | solution.py:342
  8.2 4.1 %collective-permute-start.2 = (bf16[192,128]{1,0:T(8,128)(2,1)S(1)}, bf16[192,128]{1,0:T(8,128)(2,1)S(1)}, u32[]{:S(2)}, u32[]{:S(2)}) collective-permute-start(bf16[192,128]{1,0:T(8,128)(2,1)S(1)} %get-tuple-element.37), channel_id=1, source_target_pairs={{0,17},{1,16},{2,19},{3,18},{4,21},{5,20},{6,23},{7,22},{8,25},{9,... | collective-permute-start | bytes 147464 | tf_op jit(solution)/shard_map/ppermute | solution.py:342
  8.5 3.8 %collective-permute-start.3 = (bf16[192,128]{1,0:T(8,128)(2,1)S(1)}, bf16[192,128]{1,0:T(8,128)(2,1)S(1)}, u32[]{:S(2)}, u32[]{:S(2)}) collective-permute-start(bf16[192,128]{1,0:T(8,128)(2,1)S(1)} %get-tuple-element.38), channel_id=1, source_target_pairs={{0,16},{1,17},{2,18},{3,19},{4,20},{5,21},{6,22},{7,23},{8,24},{9,... | collective-permute-start | bytes 147464 | tf_op jit(solution)/shard_map/ppermute | solution.py:342
  8.7 9.8 %copy-start.1 = (f32[9,6]{0,1:T(8,128)S(1)}, f32[9,6]{0,1:T(8,128)}, u32[]{:S(2)}) copy-start(f32[9,6]{0,1:T(8,128)} %param.11) | copy-start | bytes 652
  12.3 3.6 %collective-permute-start.6 = (bf16[192,128]{1,0:T(8,128)(2,1)S(1)}, bf16[192,128]{1,0:T(8,128)(2,1)S(1)}, u32[]{:S(2)}, u32[]{:S(2)}) collective-permute-start(bf16[192,128]{1,0:T(8,128)(2,1)S(1)} %fusion.6), channel_id=1, source_target_pairs={{0,16},{1,17},{2,18},{3,19},{4,20},{5,21},{6,22},{7,23},{8,24},{9,... | collective-permute-start | bytes 147464 | tf_op jit(solution)/shard_map/ppermute | solution.py:342
  13.4 5.0 %collective-permute-start.4 = (bf16[192,128]{1,0:T(8,128)(2,1)S(1)}, bf16[192,128]{1,0:T(8,128)(2,1)S(1)}, u32[]{:S(2)}, u32[]{:S(2)}) collective-permute-start(bf16[192,128]{1,0:T(8,128)(2,1)S(1)} %fusion.6), channel_id=1, source_target_pairs={{0,28},{1,29},{2,30},{3,31},{4,24},{5,25},{6,26},{7,27},{8,20},{9,... | collective-permute-start | bytes 147464 | tf_op jit(solution)/shard_map/ppermute | solution.py:342
  15.9 6.1 %collective-permute-start.7 = (bf16[2,192,128]{2,1,0:T(8,128)(2,1)S(1)}, bf16[2,192,128]{2,1,0:T(8,128)(2,1)S(1)}, u32[]{:S(2)}, u32[]{:S(2)}) collective-permute-start(bf16[2,192,128]{2,1,0:T(8,128)(2,1)S(1)} %pad_maximum_fusion), channel_id=1, source_target_pairs={{0,24},{1,25},{2,26},{3,27},{4,28},{5,29},{6,30},{7,31},{8,16},{9,... | collective-permute-start | bytes 294920 | tf_op jit(solution)/shard_map/ppermute | solution.py:342
  17.4 5.3 %collective-permute-start.8 = (bf16[2,192,128]{2,1,0:T(8,128)(2,1)S(1)}, bf16[2,192,128]{2,1,0:T(8,128)(2,1)S(1)}, u32[]{:S(2)}, u32[]{:S(2)}) collective-permute-start(bf16[2,192,128]{2,1,0:T(8,128)(2,1)S(1)} %pad_maximum_fusion), channel_id=1, source_target_pairs={{0,20},{1,21},{2,22},{3,23},{4,16},{5,17},{6,18},{7,19},{8,28},{9,... | collective-permute-start | bytes 294920 | tf_op jit(solution)/shard_map/ppermute | solution.py:342
  18.4 2.2 %collective-permute-start.5 = (bf16[192,128]{1,0:T(8,128)(2,1)S(1)}, bf16[192,128]{1,0:T(8,128)(2,1)S(1)}, u32[]{:S(2)}, u32[]{:S(2)}) collective-permute-start(bf16[192,128]{1,0:T(8,128)(2,1)S(1)} %collective-permute-done.4.after), channel_id=1, source_target_pairs={{0,16},{1,17},{2,18},{3,19},{4,20},{5,21},{6,22},{7,23},{8,24},{9,... | collective-permute-start | bytes 147464 | tf_op jit(solution)/shard_map/ppermute | solution.py:342
  22.8 22.6 %copy-start = (bf16[768,1536]{1,0:T(8,128)(2,1)S(1)}, bf16[768,1536]{1,0:T(8,128)(2,1)}, u32[]{:S(2)}) copy-start(bf16[768,1536]{1,0:T(8,128)(2,1)} %wo.1) | copy-start | bytes 7077892
  22.8 6.5 %collective-permute-start.10 = (bf16[192,128]{1,0:T(8,128)(2,1)S(1)}, bf16[192,128]{1,0:T(8,128)(2,1)S(1)}, u32[]{:S(2)}, u32[]{:S(2)}) collective-permute-start(bf16[192,128]{1,0:T(8,128)(2,1)S(1)} %get-tuple-element.65.after), channel_id=1, source_target_pairs={{0,112},{1,113},{2,114},{3,115},{4,116},{5,117},{6,118},{7,119},{8... | collective-permute-start | bytes 147464 | tf_op jit(solution)/shard_map/ppermute | solution.py:342
  24.7 4.6 %collective-permute-start.11 = (bf16[192,128]{1,0:T(8,128)(2,1)S(1)}, bf16[192,128]{1,0:T(8,128)(2,1)S(1)}, u32[]{:S(2)}, u32[]{:S(2)}) collective-permute-start(bf16[192,128]{1,0:T(8,128)(2,1)S(1)} %get-tuple-element.65.after), channel_id=1, source_target_pairs={{0,80},{1,81},{2,82},{3,83},{4,84},{5,85},{6,86},{7,87},{8,88},{9,... | collective-permute-start | bytes 147464 | tf_op jit(solution)/shard_map/ppermute | solution.py:342
  26.2 5.2 %collective-permute-start.9 = (bf16[192,128]{1,0:T(8,128)(2,1)S(1)}, bf16[192,128]{1,0:T(8,128)(2,1)S(1)}, u32[]{:S(2)}, u32[]{:S(2)}) collective-permute-start(bf16[192,128]{1,0:T(8,128)(2,1)S(1)} %get-tuple-element.65.after), channel_id=1, source_target_pairs={{0,48},{1,49},{2,50},{3,51},{4,52},{5,53},{6,54},{7,55},{8,56},{9,... | collective-permute-start | bytes 147464 | tf_op jit(solution)/shard_map/ppermute | solution.py:342
  31.5 7.5 %collective-permute-start.12 = (bf16[192,128]{1,0:T(8,128)(2,1)S(1)}, bf16[192,128]{1,0:T(8,128)(2,1)S(1)}, u32[]{:S(2)}, u32[]{:S(2)}) collective-permute-start(bf16[192,128]{1,0:T(8,128)(2,1)S(1)} %add_convert_fusion), channel_id=1, source_target_pairs={{0,208},{1,209},{2,210},{3,211},{4,212},{5,213},{6,214},{7,215},{8... | collective-permute-start | bytes 147464 | tf_op jit(solution)/shard_map/ppermute | solution.py:342
  39.0 5.0 %collective-permute-start.13 = (bf16[192,128]{1,0:T(8,128)(2,1)S(1)}, bf16[192,128]{1,0:T(8,128)(2,1)S(1)}, u32[]{:S(2)}, u32[]{:S(2)}) collective-permute-start(bf16[192,128]{1,0:T(8,128)(2,1)S(1)} %get-tuple-element.70), channel_id=1, source_target_pairs={{0,19},{1,18},{2,17},{3,16},{4,23},{5,22},{6,21},{7,20},{8,27},{9,... | collective-permute-start | bytes 147464 | tf_op jit(solution)/shard_map/ppermute | solution.py:342
  40.2 5.0 %collective-permute-start.14 = (bf16[192,128]{1,0:T(8,128)(2,1)S(1)}, bf16[192,128]{1,0:T(8,128)(2,1)S(1)}, u32[]{:S(2)}, u32[]{:S(2)}) collective-permute-start(bf16[192,128]{1,0:T(8,128)(2,1)S(1)} %get-tuple-element.69), channel_id=1, source_target_pairs={{0,18},{1,19},{2,16},{3,17},{4,22},{5,23},{6,20},{7,21},{8,26},{9,... | collective-permute-start | bytes 147464 | tf_op jit(solution)/shard_map/ppermute | solution.py:342
  40.9 4.6 %collective-permute-start.15 = (bf16[192,128]{1,0:T(8,128)(2,1)S(1)}, bf16[192,128]{1,0:T(8,128)(2,1)S(1)}, u32[]{:S(2)}, u32[]{:S(2)}) collective-permute-start(bf16[192,128]{1,0:T(8,128)(2,1)S(1)} %get-tuple-element.68), channel_id=1, source_target_pairs={{0,17},{1,16},{2,19},{3,18},{4,21},{5,20},{6,23},{7,22},{8,25},{9,... | collective-permute-start | bytes 147464 | tf_op jit(solution)/shard_map/ppermute | solution.py:342
  42.7 2.8 %collective-permute-start.16 = (bf16[192,128]{1,0:T(8,128)(2,1)S(1)}, bf16[192,128]{1,0:T(8,128)(2,1)S(1)}, u32[]{:S(2)}, u32[]{:S(2)}) collective-permute-start(bf16[192,128]{1,0:T(8,128)(2,1)S(1)} %get-tuple-element.67), channel_id=1, source_target_pairs={{0,16},{1,17},{2,18},{3,19},{4,20},{5,21},{6,22},{7,23},{8,24},{9,... | collective-permute-start | bytes 147464 | tf_op jit(solution)/shard_map/ppermute | solution.py:342

commit v11 on v7

--- a/solution.py
+++ b/solution.py
@@ -209,7 +209,7 @@
 
 def gather_kernel(levels, *refs):
     near = refs[:4]
-    crossed, mine, z1, z2, z3, local_ref, last_ref = refs[4:]
+    crossed, mine, z1, z2, z3, other3, local_ref, last_ref = refs[4:]
     y, x, core, z = position()
     heads = levels.shape[1]
     part = mine.shape[0] // heads
@@ -227,7 +227,7 @@
             + factor(3, bit(x, 1)) * crossed[1, rows, :].astype(F32)
             + factor(4, bit(core ^ 1, 0)) * read(mine)
             + factor(5, bit(z, 0)) * read(z1)
-            + factor(6, bit(z, 1)) * (read(z2) + read(z3))
+            + factor(6, bit(z, 1)) * (read(z2) + read(z3) + read(other3))
         )
         sides = [read(ref) for ref in near]
         for distance in range(4):
@@ -245,7 +245,7 @@
     return pl.pallas_call(
         gather_kernel,
         out_shape=(jax.ShapeDtypeStruct((4, *shape), F32), jax.ShapeDtypeStruct(shape, F32)),
-        in_specs=[SMEM] + [VMEM] * 9,
+        in_specs=[SMEM] + [VMEM] * 10,
         out_specs=[VMEM, VMEM],
         compiler_params=pltpu.CompilerParams(vmem_limit_bytes=4 << 20),
         name="gather",
@@ -370,20 +370,22 @@
     x2, x3, x1, own, low = lax.optimization_barrier((x2, x3, x1, own, low))
     total = plus(own.astype(F32), (x1, x2, x3))
     mine = total.astype(BF16)
+
+    other = flip(mine, CORE)
+    z3 = flip(mine, CORE | 3 * Z)
+    total = plus(total, (other,))
+    going = total.astype(BF16)
+    z2, z1 = flip(going, CORE | 2 * Z), flip(going, CORE | Z)
+    other3 = flip(z3, CORE)
+    high = inside_of(query, keys, values, level_weights, going, half, half, width)
     crossing = jnp.stack([x1.astype(F32), plus(x2.astype(F32), (x3,))]).astype(BF16)
-
-    total = plus(total, (flip(mine, CORE),))
-    going = total.astype(BF16)
-    z1, z3, z2 = (flip(going, CORE | distance * Z) for distance in (1, 3, 2))
-    high = inside_of(query, keys, values, level_weights, going, half, half, width)
     crossing, high = lax.optimization_barrier((crossing, high))
     crossed = flip(crossing, CORE)
-    z1, z3, z2, high = lax.optimization_barrier((z1, z3, z2, high))
-    going = plus(total, (z3, z2, z1)).astype(BF16)
-
-    going, crossing = lax.optimization_barrier((going, crossing))
+    other3, z2, z1, high = lax.optimization_barrier((other3, z2, z1, high))
+    going = plus(total, (z3, z2, z1, other3)).astype(BF16)
+
     past = flip(going, CORE | 6 * Z)
-    gathered, factor = gather_of(level_weights, near, (crossed, mine, z1, z2, z3))
+    gathered, factor = gather_of(level_weights, near, (crossed, mine, z1, z2, z3, other3))
     past, gathered, factor = lax.optimization_barrier((past, gathered, factor))
     last = factor * past.astype(F32)
     back = [(gathered[distance] + last).astype(BF16) for distance in range(4)]

time: 47.3 us -> 46.9 us (level)
  waiting for transfers between devices: 11.8 us -> 10.1 us
  starting transfers between devices: 21.2 us -> 22.4 us
    ppermute x18 -> x19, waiting for transfers between devices: 11.8 us -> 10.1 us  [flip(): lax.ppermute(value, AXES, [(source, source ^ mask) for source in range(de...]
    ppermute x18 -> x19, starting transfers between devices: 21.2 us -> 22.4 us  [flip(): lax.ppermute(value, AXES, [(source, source ^ mask) for source in range(de...]
  transfers between devices with their start and end apart: 18 -> 19, of which waited for: 10 -> 9; matrix products, arithmetic and copies ran while one was open for 0% -> 0% of each run, Pallas kernels for 13% -> 14%
where the time goes in v11:
time: 46.9 us; the launch traced here: 46.5 us
  starting transfers between devices  22.4 us (48%)
  Pallas kernels  13.4 us (29%)
  waiting for transfers between devices  10.1 us (22%)
    ppermute x19, starting transfers between devices, flip(): lax.ppermute(value, AXES, [(source, source ^ mask) for source in range(de...  22.4 us
    ppermute x19, waiting for transfers between devices, flip(): lax.ppermute(value, AXES, [(source, source ^ mask) for source in range(de...  10.1 us
    pallas_call x1, Pallas kernels, states_of(): pl.pallas_call(functools.partial(state_kernel, width), out_shape=(side, s...  4.72 us
    pallas_call x2, Pallas kernels, inside_of(): pl.pallas_call(functools.partial(inside_kernel, width, first), out_shape=...  3.9 us
    pallas_call x1, Pallas kernels, mixed_of(): pl.pallas_call(functools.partial(mix_kernel, width), out_shape=jax.ShapeD...  2.38 us
    pallas_call x1, Pallas kernels, query_of(): pl.pallas_call(functools.partial(query_kernel, width), out_shape=jax.Shap...  1.6 us
  transfers between devices with their start and end apart: 19, of which 9 were waited for; matrix products, arithmetic and copies ran while one was open for 0% of the time, Pallas kernels for 14%

profile of v11, /device:TPU:32, one launch (start us, length us, event | category | flops | bytes accessed | tf_op | source)
XLA Modules:
  0.0 46.5 jit_solution(15933961701582473270)
XLA Ops:
  0.0 4.7 %states.1 = (bf16[512,768]{1,0:T(8,128)(2,1)S(1)}, bf16[512,768]{1,0:T(8,128)(2,1)S(1)}, bf16[512,1536]{1,0:T(8,128)(2,1)S(1)}, bf16[1536,768]{1,0:T(8,128)(2,1)...) custom-call(bf16[512,1536]{1,0:T(8,128)(2,1)} %tok_hbm.1, ...), custom_call_target="tpu_custom_call" | custom-call | tf_op jit(solution)/shard_map/states/pallas_call | solution.py:127
  4.7 2.7 %collective-permute-start = (bf16[192,128]{1,0:T(8,128)(2,1)S(1)}, bf16[192,128]{1,0:T(8,128)(2,1)S(1)}, u32[]{:S(2)}, u32[]{:S(2)}) collective-permute-start(bf16[192,128]{1,0:T(8,128)(2,1)S(1)} %get-tuple-element.38), channel_id=1, source_target_pairs={{0,18},{1,19},{2,16},{3,17},{4,22},{5,23},{6,20},{7,21},{8,26},{9,... | collective-permute-start | bytes 147464 | tf_op jit(solution)/shard_map/ppermute | solution.py:342
  7.4 1.3 %collective-permute-start.1 = (bf16[192,128]{1,0:T(8,128)(2,1)S(1)}, bf16[192,128]{1,0:T(8,128)(2,1)S(1)}, u32[]{:S(2)}, u32[]{:S(2)}) collective-permute-start(bf16[192,128]{1,0:T(8,128)(2,1)S(1)} %get-tuple-element.39), channel_id=1, source_target_pairs={{0,19},{1,18},{2,17},{3,16},{4,23},{5,22},{6,21},{7,20},{8,27},{9,... | collective-permute-start | bytes 147464 | tf_op jit(solution)/shard_map/ppermute | solution.py:342
  8.8 0.0 collective-permute-start.2
  8.8 0.0 collective-permute-start.3
  8.8 1.6 %query.1.q_ref = bf16[512,768]{1,0:T(8,128)(2,1)S(1)} custom-call(bf16[512,1536]{1,0:T(8,128)(2,1)S(1)} %get-tuple-element.42.tok, bf16[1536,768]{1,0:T(8,128)(2,1)S(1)} %get-tuple-element.43.wq), custom_call_target="tpu_custom_call" | custom-call | tf_op jit(solution)/shard_map/query/pallas_call | solution.py:161
  10.4 0.0 collective-permute-done.refs_2_
  10.4 1.8 %collective-permute-done.1.refs_3_ = bf16[192,128]{1,0:T(8,128)(2,1)S(1)} collective-permute-done((bf16[192,128]{1,0:T(8,128)(2,1)S(1)}, bf16[192,128]{1,0:T(8,128)(2,1)S(1)}, u32[]{:S(2)}, u32[]{:S(2)}) %collective-permute-start.1) | collective-permute-done | bytes 49184 | tf_op jit(solution)/shard_map/ppermute | solution.py:342
  12.2 0.6 %collective-permute-done.2.refs_1_ = bf16[192,128]{1,0:T(8,128)(2,1)S(1)} collective-permute-done((bf16[192,128]{1,0:T(8,128)(2,1)S(1)}, bf16[192,128]{1,0:T(8,128)(2,1)S(1)}, u32[]{:S(2)}, u32[]{:S(2)}) %collective-permute-start.2) | collective-permute-done | bytes 49184 | tf_op jit(solution)/shard_map/ppermute | solution.py:342
  12.8 0.0 collective-permute-done.3.refs_0_
  12.9 2.8 %collective-permute-start.4 = (bf16[192,128]{1,0:T(8,128)(2,1)S(1)}, bf16[192,128]{1,0:T(8,128)(2,1)S(1)}, u32[]{:S(2)}, u32[]{:S(2)}) collective-permute-start(bf16[192,128]{1,0:T(8,128)(2,1)S(1)} %add_convert_fusion.1.after), channel_id=1, source_target_pairs={{0,24},{1,25},{2,26},{3,27},{4,28},{5,29},{6,30},{7,31},{8,16},{9,... | collective-permute-start | bytes 147464 | tf_op jit(solution)/shard_map/ppermute | solution.py:342
  15.7 1.2 %collective-permute-start.5 = (bf16[192,128]{1,0:T(8,128)(2,1)S(1)}, bf16[192,128]{1,0:T(8,128)(2,1)S(1)}, u32[]{:S(2)}, u32[]{:S(2)}) collective-permute-start(bf16[192,128]{1,0:T(8,128)(2,1)S(1)} %add_convert_fusion.1.after), channel_id=1, source_target_pairs={{0,28},{1,29},{2,30},{3,31},{4,24},{5,25},{6,26},{7,27},{8,20},{9,... | collective-permute-start | bytes 147464 | tf_op jit(solution)/shard_map/ppermute | solution.py:342
  16.8 0.0 collective-permute-start.6
  16.9 0.1 collective-permute-start.7
  16.9 0.0 copy-done.1
  16.9 0.1 copy.7.levels
  17.0 1.9 %inside.2.low_ref = f32[512,384]{1,0:T(8,128)S(1)} custom-call(bf16[512,768]{1,0:T(8,128)(2,1)S(1)} %query.1.q_ref, bf16[512,768]{1,0:T(8,128)(2,1)S(1)} %get-tuple-element.49.k_ref, bf16[512,768]{1,0:T(8,128)(2,1)S(1)} %get-tuple-element.50.v_ref, f32[9,6]{1,0:T(8,128)S(1)} %copy.7.levels, bf16[192,128]{1,0:T(8,128)(2,1)S(1)} %add_convert_fusion.1.after), custom_call_target="tpu_custom_call" | custom-call | tf_op jit(solution)/shard_map/inside/pallas_call | solution.py:200
  19.0 0.0 collective-permute-done.4
  19.0 1.4 %collective-permute-done.5 = bf16[192,128]{1,0:T(8,128)(2,1)S(1)} collective-permute-done((bf16[192,128]{1,0:T(8,128)(2,1)S(1)}, bf16[192,128]{1,0:T(8,128)(2,1)S(1)}, u32[]{:S(2)}, u32[]{:S(2)}) %collective-permute-start.5) | collective-permute-done | bytes 49184 | tf_op jit(solution)/shard_map/ppermute | solution.py:342
  20.4 0.2 collective-permute-done.6
  20.6 0.0 collective-permute-done.7
  20.7 0.3 collective-permute-start.10
  21.0 1.8 %collective-permute-start.8 = (bf16[192,128]{1,0:T(8,128)(2,1)S(1)}, bf16[192,128]{1,0:T(8,128)(2,1)S(1)}, u32[]{:S(2)}, u32[]{:S(2)}) collective-permute-start(bf16[192,128]{1,0:T(8,128)(2,1)S(1)} %fusion.7.refs_5_), channel_id=1, source_target_pairs={{0,112},{1,113},{2,114},{3,115},{4,116},{5,117},{6,118},{7,119},{8... | collective-permute-start | bytes 147464 | tf_op jit(solution)/shard_map/ppermute | solution.py:342
  22.8 0.0 collective-permute-done.10
  22.8 2.4 %collective-permute-start.11 = (bf16[192,128]{1,0:T(8,128)(2,1)S(1)}, bf16[192,128]{1,0:T(8,128)(2,1)S(1)}, u32[]{:S(2)}, u32[]{:S(2)}) collective-permute-start(bf16[192,128]{1,0:T(8,128)(2,1)S(1)} %get-tuple-element.76.after), channel_id=1, source_target_pairs={{0,80},{1,81},{2,82},{3,83},{4,84},{5,85},{6,86},{7,87},{8,88},{9,... | collective-permute-start | bytes 147464 | tf_op jit(solution)/shard_map/ppermute | solution.py:342
  25.2 0.5 collective-permute-start.12
  25.6 0.0 collective-permute-done.8.refs_8_
  25.7 0.3 collective-permute-start.9
  26.0 0.0 copy-start
  26.0 2.0 %inside.3.high_ref = f32[512,384]{1,0:T(8,128)S(1)} custom-call(bf16[512,768]{1,0:T(8,128)(2,1)S(1)} %query.1.q_ref, bf16[512,768]{1,0:T(8,128)(2,1)S(1)} %get-tuple-element.49.k_ref, bf16[512,768]{1,0:T(8,128)(2,1)S(1)} %get-tuple-element.50.v_ref, f32[9,6]{1,0:T(8,128)S(1)} %copy.7.levels, bf16[192,128]{1,0:T(8,128)(2,1)S(1)} %get-tuple-element.76.after), custom_call_target="tpu_custom_call" | custom-call | tf_op jit(solution)/shard_map/inside/pallas_call | solution.py:200
  27.9 0.3 collective-permute-start.14
  28.2 0.6 %collective-permute-done.11.refs_7_ = bf16[192,128]{1,0:T(8,128)(2,1)S(1)} collective-permute-done((bf16[192,128]{1,0:T(8,128)(2,1)S(1)}, bf16[192,128]{1,0:T(8,128)(2,1)S(1)}, u32[]{:S(2)}, u32[]{:S(2)}) %collective-permute-start.11) | collective-permute-done | bytes 49184 | tf_op jit(solution)/shard_map/ppermute | solution.py:342
  28.8 0.6 %collective-permute-done.12.refs_6_ = bf16[192,128]{1,0:T(8,128)(2,1)S(1)} collective-permute-done((bf16[192,128]{1,0:T(8,128)(2,1)S(1)}, bf16[192,128]{1,0:T(8,128)(2,1)S(1)}, u32[]{:S(2)}, u32[]{:S(2)}) %collective-permute-start.12) | collective-permute-done | bytes 49184 | tf_op jit(solution)/shard_map/ppermute | solution.py:342
  29.4 0.0 collective-permute-done.9.refs_9_
  29.4 0.1 add_convert_fusion
  29.5 5.3 %collective-permute-start.13 = (bf16[192,128]{1,0:T(8,128)(2,1)S(1)}, bf16[192,128]{1,0:T(8,128)(2,1)S(1)}, u32[]{:S(2)}, u32[]{:S(2)}) collective-permute-start(bf16[192,128]{1,0:T(8,128)(2,1)S(1)} %add_convert_fusion), channel_id=1, source_target_pairs={{0,208},{1,209},{2,210},{3,211},{4,212},{5,213},{6,214},{7,215},{8... | collective-permute-start | bytes 147464 | tf_op jit(solution)/shard_map/ppermute | solution.py:342
  34.7 0.0 collective-permute-done.14.refs_4_
  34.7 0.8 %gather.1 = (f32[4,192,128]{2,1,0:T(8,128)S(1)}, f32[192,128]{1,0:T(8,128)S(1)}) custom-call(f32[9,6]{1,0:T(8,128)S(1)} %copy.7.levels, bf16[192,128]{1,0:T(8,128)(2,1)S(1)} %collective-permute-done.3.refs_0_, bf16[192,128]{1,0:T(8,128)(2,1)S(1)} %collective-permute-done.2.refs_1_, bf16[192,128]{1,0:T(8,128)(2,1)S(1)} %collective-permute-done.refs_2_, ...), custom_call_target="tpu_custom_call" | custom-call | tf_op jit(solution)/shard_map/gather/pallas_call | solution.py:245
  35.6 1.7 %collective-permute-done.13 = bf16[192,128]{1,0:T(8,128)(2,1)S(1)} collective-permute-done((bf16[192,128]{1,0:T(8,128)(2,1)S(1)}, bf16[192,128]{1,0:T(8,128)(2,1)S(1)}, u32[]{:S(2)}, u32[]{:S(2)}) %collective-permute-start.13) | collective-permute-done | bytes 49184 | tf_op jit(solution)/shard_map/ppermute | solution.py:342
  37.3 0.9 %collective-permute-start.15 = (bf16[192,128]{1,0:T(8,128)(2,1)S(1)}, bf16[192,128]{1,0:T(8,128)(2,1)S(1)}, u32[]{:S(2)}, u32[]{:S(2)}) collective-permute-start(bf16[192,128]{1,0:T(8,128)(2,1)S(1)} %get-tuple-element.74), channel_id=1, source_target_pairs={{0,18},{1,19},{2,16},{3,17},{4,22},{5,23},{6,20},{7,21},{8,26},{9,... | collective-permute-start | bytes 147464 | tf_op jit(solution)/shard_map/ppermute | solution.py:342
  38.2 1.7 %collective-permute-start.16 = (bf16[192,128]{1,0:T(8,128)(2,1)S(1)}, bf16[192,128]{1,0:T(8,128)(2,1)S(1)}, u32[]{:S(2)}, u32[]{:S(2)}) collective-permute-start(bf16[192,128]{1,0:T(8,128)(2,1)S(1)} %get-tuple-element.73), channel_id=1, source_target_pairs={{0,19},{1,18},{2,17},{3,16},{4,23},{5,22},{6,21},{7,20},{8,27},{9,... | collective-permute-start | bytes 147464 | tf_op jit(solution)/shard_map/ppermute | solution.py:342
  39.9 0.4 collective-permute-start.17
  40.3 0.4 collective-permute-start.18
  40.8 1.9 %collective-permute-done.15.two = bf16[192,128]{1,0:T(8,128)(2,1)S(1)} collective-permute-done((bf16[192,128]{1,0:T(8,128)(2,1)S(1)}, bf16[192,128]{1,0:T(8,128)(2,1)S(1)}, u32[]{:S(2)}, u32[]{:S(2)}) %collective-permute-start.15) | collective-permute-done | bytes 49184 | tf_op jit(solution)/shard_map/ppermute | solution.py:342
  42.7 1.3 %collective-permute-done.16.three = bf16[192,128]{1,0:T(8,128)(2,1)S(1)} collective-permute-done((bf16[192,128]{1,0:T(8,128)(2,1)S(1)}, bf16[192,128]{1,0:T(8,128)(2,1)S(1)}, u32[]{:S(2)}, u32[]{:S(2)}) %collective-permute-start.16) | collective-permute-done | bytes 49184 | tf_op jit(solution)/shard_map/ppermute | solution.py:342
  44.0 0.0 collective-permute-done.17.one
  44.0 0.0 collective-permute-done.18.own
  44.0 2.4 %mix.1 = bf16[512,1536]{1,0:T(8,128)(2,1)} custom-call(bf16[512,768]{1,0:T(8,128)(2,1)S(1)} %query.1.q_ref, f32[512,384]{1,0:T(8,128)S(1)} %inside.2.low_ref, f32[512,384]{1,0:T(8,128)S(1)} %inside.3.high_ref, bf16[192,128]{1,0:T(8,128)(2,1)S(1)} %collective-permute-done.18.own, bf16[192,128]{1,0:T(8,128)(2,1)S(1)} %collective-permute-done.17.one, ...), custom_call_target="tpu_custom_call" | custom-call | tf_op jit(solution)/shard_map/mix/pallas_call | solution.py:320
  (7 shorter events, 0.2 us)
Async XLA Ops:
  4.7 5.7 %collective-permute-start = (bf16[192,128]{1,0:T(8,128)(2,1)S(1)}, bf16[192,128]{1,0:T(8,128)(2,1)S(1)}, u32[]{:S(2)}, u32[]{:S(2)}) collective-permute-start(bf16[192,128]{1,0:T(8,128)(2,1)S(1)} %get-tuple-element.38), channel_id=1, source_target_pairs={{0,18},{1,19},{2,16},{3,17},{4,22},{5,23},{6,20},{7,21},{8,26},{9,... | collective-permute-start | bytes 147464 | tf_op jit(solution)/shard_map/ppermute | solution.py:342
  7.4 4.7 %collective-permute-start.1 = (bf16[192,128]{1,0:T(8,128)(2,1)S(1)}, bf16[192,128]{1,0:T(8,128)(2,1)S(1)}, u32[]{:S(2)}, u32[]{:S(2)}) collective-permute-start(bf16[192,128]{1,0:T(8,128)(2,1)S(1)} %get-tuple-element.39), channel_id=1, source_target_pairs={{0,19},{1,18},{2,17},{3,16},{4,23},{5,22},{6,21},{7,20},{8,27},{9,... | collective-permute-start | bytes 147464 | tf_op jit(solution)/shard_map/ppermute | solution.py:342
  8.8 4.0 %collective-permute-start.2 = (bf16[192,128]{1,0:T(8,128)(2,1)S(1)}, bf16[192,128]{1,0:T(8,128)(2,1)S(1)}, u32[]{:S(2)}, u32[]{:S(2)}) collective-permute-start(bf16[192,128]{1,0:T(8,128)(2,1)S(1)} %get-tuple-element.40), channel_id=1, source_target_pairs={{0,17},{1,16},{2,19},{3,18},{4,21},{5,20},{6,23},{7,22},{8,25},{9,... | collective-permute-start | bytes 147464 | tf_op jit(solution)/shard_map/ppermute | solution.py:342
  8.8 4.0 %collective-permute-start.3 = (bf16[192,128]{1,0:T(8,128)(2,1)S(1)}, bf16[192,128]{1,0:T(8,128)(2,1)S(1)}, u32[]{:S(2)}, u32[]{:S(2)}) collective-permute-start(bf16[192,128]{1,0:T(8,128)(2,1)S(1)} %get-tuple-element.41), channel_id=1, source_target_pairs={{0,16},{1,17},{2,18},{3,19},{4,20},{5,21},{6,22},{7,23},{8,24},{9,... | collective-permute-start | bytes 147464 | tf_op jit(solution)/shard_map/ppermute | solution.py:342
  8.8 8.1 %copy-start.1 = (f32[9,6]{0,1:T(8,128)S(1)}, f32[9,6]{0,1:T(8,128)}, u32[]{:S(2)}) copy-start(f32[9,6]{0,1:T(8,128)} %param.11) | copy-start | bytes 652
  12.9 6.1 %collective-permute-start.4 = (bf16[192,128]{1,0:T(8,128)(2,1)S(1)}, bf16[192,128]{1,0:T(8,128)(2,1)S(1)}, u32[]{:S(2)}, u32[]{:S(2)}) collective-permute-start(bf16[192,128]{1,0:T(8,128)(2,1)S(1)} %add_convert_fusion.1.after), channel_id=1, source_target_pairs={{0,24},{1,25},{2,26},{3,27},{4,28},{5,29},{6,30},{7,31},{8,16},{9,... | collective-permute-start | bytes 147464 | tf_op jit(solution)/shard_map/ppermute | solution.py:342
  15.7 4.7 %collective-permute-start.5 = (bf16[192,128]{1,0:T(8,128)(2,1)S(1)}, bf16[192,128]{1,0:T(8,128)(2,1)S(1)}, u32[]{:S(2)}, u32[]{:S(2)}) collective-permute-start(bf16[192,128]{1,0:T(8,128)(2,1)S(1)} %add_convert_fusion.1.after), channel_id=1, source_target_pairs={{0,28},{1,29},{2,30},{3,31},{4,24},{5,25},{6,26},{7,27},{8,20},{9,... | collective-permute-start | bytes 147464 | tf_op jit(solution)/shard_map/ppermute | solution.py:342
  16.8 3.8 %collective-permute-start.6 = (bf16[192,128]{1,0:T(8,128)(2,1)S(1)}, bf16[192,128]{1,0:T(8,128)(2,1)S(1)}, u32[]{:S(2)}, u32[]{:S(2)}) collective-permute-start(bf16[192,128]{1,0:T(8,128)(2,1)S(1)} %add_convert_fusion.1.after), channel_id=1, source_target_pairs={{0,20},{1,21},{2,22},{3,23},{4,16},{5,17},{6,18},{7,19},{8,28},{9,... | collective-permute-start | bytes 147464 | tf_op jit(solution)/shard_map/ppermute | solution.py:342
  16.9 3.8 %collective-permute-start.7 = (bf16[192,128]{1,0:T(8,128)(2,1)S(1)}, bf16[192,128]{1,0:T(8,128)(2,1)S(1)}, u32[]{:S(2)}, u32[]{:S(2)}) collective-permute-start(bf16[192,128]{1,0:T(8,128)(2,1)S(1)} %add_convert_fusion.1.after), channel_id=1, source_target_pairs={{0,16},{1,17},{2,18},{3,19},{4,20},{5,21},{6,22},{7,23},{8,24},{9,... | collective-permute-start | bytes 147464 | tf_op jit(solution)/shard_map/ppermute | solution.py:342
  20.7 2.1 %collective-permute-start.10 = (bf16[192,128]{1,0:T(8,128)(2,1)S(1)}, bf16[192,128]{1,0:T(8,128)(2,1)S(1)}, u32[]{:S(2)}, u32[]{:S(2)}) collective-permute-start(bf16[192,128]{1,0:T(8,128)(2,1)S(1)} %fusion.7.refs_5_), channel_id=1, source_target_pairs={{0,16},{1,17},{2,18},{3,19},{4,20},{5,21},{6,22},{7,23},{8,24},{9,... | collective-permute-start | bytes 147464 | tf_op jit(solution)/shard_map/ppermute | solution.py:342
  21.0 4.7 %collective-permute-start.8 = (bf16[192,128]{1,0:T(8,128)(2,1)S(1)}, bf16[192,128]{1,0:T(8,128)(2,1)S(1)}, u32[]{:S(2)}, u32[]{:S(2)}) collective-permute-start(bf16[192,128]{1,0:T(8,128)(2,1)S(1)} %fusion.7.refs_5_), channel_id=1, source_target_pairs={{0,112},{1,113},{2,114},{3,115},{4,116},{5,117},{6,118},{7,119},{8... | collective-permute-start | bytes 147464 | tf_op jit(solution)/shard_map/ppermute | solution.py:342
  22.8 6.0 %collective-permute-start.11 = (bf16[192,128]{1,0:T(8,128)(2,1)S(1)}, bf16[192,128]{1,0:T(8,128)(2,1)S(1)}, u32[]{:S(2)}, u32[]{:S(2)}) collective-permute-start(bf16[192,128]{1,0:T(8,128)(2,1)S(1)} %get-tuple-element.76.after), channel_id=1, source_target_pairs={{0,80},{1,81},{2,82},{3,83},{4,84},{5,85},{6,86},{7,87},{8,88},{9,... | collective-permute-start | bytes 147464 | tf_op jit(solution)/shard_map/ppermute | solution.py:342
  25.2 4.2 %collective-permute-start.12 = (bf16[192,128]{1,0:T(8,128)(2,1)S(1)}, bf16[192,128]{1,0:T(8,128)(2,1)S(1)}, u32[]{:S(2)}, u32[]{:S(2)}) collective-permute-start(bf16[192,128]{1,0:T(8,128)(2,1)S(1)} %get-tuple-element.76.after), channel_id=1, source_target_pairs={{0,48},{1,49},{2,50},{3,51},{4,52},{5,53},{6,54},{7,55},{8,56},{9,... | collective-permute-start | bytes 147464 | tf_op jit(solution)/shard_map/ppermute | solution.py:342
  25.7 3.7 %collective-permute-start.9 = (bf16[192,128]{1,0:T(8,128)(2,1)S(1)}, bf16[192,128]{1,0:T(8,128)(2,1)S(1)}, u32[]{:S(2)}, u32[]{:S(2)}) collective-permute-start(bf16[192,128]{1,0:T(8,128)(2,1)S(1)} %collective-permute-done.8.refs_8_), channel_id=1, source_target_pairs={{0,16},{1,17},{2,18},{3,19},{4,20},{5,21},{6,22},{7,23},{8,24},{9,... | collective-permute-start | bytes 147464 | tf_op jit(solution)/shard_map/ppermute | solution.py:342
  26.0 18.0 %copy-start = (bf16[768,1536]{1,0:T(8,128)(2,1)S(1)}, bf16[768,1536]{1,0:T(8,128)(2,1)}, u32[]{:S(2)}) copy-start(bf16[768,1536]{1,0:T(8,128)(2,1)} %wo.1) | copy-start | bytes 7077892
  27.9 6.8 %collective-permute-start.14 = (bf16[2,192,128]{2,1,0:T(8,128)(2,1)S(1)}, bf16[2,192,128]{2,1,0:T(8,128)(2,1)S(1)}, u32[]{:S(2)}, u32[]{:S(2)}) collective-permute-start(bf16[2,192,128]{2,1,0:T(8,128)(2,1)S(1)} %pad_maximum_fusion), channel_id=1, source_target_pairs={{0,16},{1,17},{2,18},{3,19},{4,20},{5,21},{6,22},{7,23},{8,24},{9,... | collective-permute-start | bytes 294920 | tf_op jit(solution)/shard_map/ppermute | solution.py:342
  29.5 7.8 %collective-permute-start.13 = (bf16[192,128]{1,0:T(8,128)(2,1)S(1)}, bf16[192,128]{1,0:T(8,128)(2,1)S(1)}, u32[]{:S(2)}, u32[]{:S(2)}) collective-permute-start(bf16[192,128]{1,0:T(8,128)(2,1)S(1)} %add_convert_fusion), channel_id=1, source_target_pairs={{0,208},{1,209},{2,210},{3,211},{4,212},{5,213},{6,214},{7,215},{8... | collective-permute-start | bytes 147464 | tf_op jit(solution)/shard_map/ppermute | solution.py:342
  37.3 5.4 %collective-permute-start.15 = (bf16[192,128]{1,0:T(8,128)(2,1)S(1)}, bf16[192,128]{1,0:T(8,128)(2,1)S(1)}, u32[]{:S(2)}, u32[]{:S(2)}) collective-permute-start(bf16[192,128]{1,0:T(8,128)(2,1)S(1)} %get-tuple-element.74), channel_id=1, source_target_pairs={{0,18},{1,19},{2,16},{3,17},{4,22},{5,23},{6,20},{7,21},{8,26},{9,... | collective-permute-start | bytes 147464 | tf_op jit(solution)/shard_map/ppermute | solution.py:342
  38.2 5.7 %collective-permute-start.16 = (bf16[192,128]{1,0:T(8,128)(2,1)S(1)}, bf16[192,128]{1,0:T(8,128)(2,1)S(1)}, u32[]{:S(2)}, u32[]{:S(2)}) collective-permute-start(bf16[192,128]{1,0:T(8,128)(2,1)S(1)} %get-tuple-element.73), channel_id=1, source_target_pairs={{0,19},{1,18},{2,17},{3,16},{4,23},{5,22},{6,21},{7,20},{8,27},{9,... | collective-permute-start | bytes 147464 | tf_op jit(solution)/shard_map/ppermute | solution.py:342
  39.9 4.0 %collective-permute-start.17 = (bf16[192,128]{1,0:T(8,128)(2,1)S(1)}, bf16[192,128]{1,0:T(8,128)(2,1)S(1)}, u32[]{:S(2)}, u32[]{:S(2)}) collective-permute-start(bf16[192,128]{1,0:T(8,128)(2,1)S(1)} %get-tuple-element.72), channel_id=1, source_target_pairs={{0,17},{1,16},{2,19},{3,18},{4,21},{5,20},{6,23},{7,22},{8,25},{9,... | collective-permute-start | bytes 147464 | tf_op jit(solution)/shard_map/ppermute | solution.py:342
  40.3 3.6 %collective-permute-start.18 = (bf16[192,128]{1,0:T(8,128)(2,1)S(1)}, bf16[192,128]{1,0:T(8,128)(2,1)S(1)}, u32[]{:S(2)}, u32[]{:S(2)}) collective-permute-start(bf16[192,128]{1,0:T(8,128)(2,1)S(1)} %get-tuple-element.71), channel_id=1, source_target_pairs={{0,16},{1,17},{2,18},{3,19},{4,20},{5,21},{6,22},{7,23},{8,24},{9,... | collective-permute-start | bytes 147464 | tf_op jit(solution)/shard_map/ppermute | solution.py:342

commit v12 on v11

--- a/solution.py
+++ b/solution.py
@@ -253,15 +253,16 @@
 
 
 def mix_kernel(
-    width, q_ref, low_ref, high_ref, own, one, two, three, wo, out_hbm, slices, attended, out, sems
+    width, q_ref, *refs
 ):
+    insides = refs[:3]
+    own, one, two, three, wo, out_hbm, slices, attended, out, sems = refs[3:]
     rows, inner = q_ref.shape
     part = width // QUARTERS
     pair = 2 * width
     y = lax.axis_index("grp") % QUARTERS
     for distance, source in enumerate((own, one, two, three)):
         slices[y ^ distance] = source[...]
-    half = inner // 2
     zero = jnp.zeros((width, width), BF16)
     pairs = inner // pair
 
@@ -275,10 +276,6 @@
             halves.append(jnp.concatenate([zero, state] if side else [state, zero], 1))
         return jnp.concatenate(halves, 0)
 
-    def inside(here, start):
-        ref, start = (low_ref, start) if start < half else (high_ref, start - half)
-        return ref[here, start : start + width]
-
     blocks = 2
     height = rows // blocks
     steps = sems.shape[0] // blocks
@@ -289,10 +286,9 @@
         here = slice(i * height, (i + 1) * height)
         for j in range(pairs):
             columns = slice(j * pair, (j + 1) * pair)
-            within = jnp.concatenate(
-                [inside(here, j * pair), inside(here, j * pair + width)], 1
-            )
-            attended[here, columns] = (within + dot(q_ref[here, columns], states(j))).astype(BF16)
+            attended[here, columns] = (
+                insides[j][here, :] + dot(q_ref[here, columns], states(j))
+            ).astype(BF16)
 
     def project(i):
         here = pl.ds(i * height, height)
@@ -320,7 +316,7 @@
     return pl.pallas_call(
         functools.partial(mix_kernel, width),
         out_shape=jax.ShapeDtypeStruct((rows, wide), BF16),
-        in_specs=[VMEM] * 8,
+        in_specs=[VMEM] * 9,
         out_specs=HBM,
         scratch_shapes=[
             pltpu.VMEM((QUARTERS, inner // QUARTERS, width), BF16),
@@ -351,7 +347,6 @@
 def per_device(tokens, w_query, w_key, w_value, w_output, level_weights):
     heads = level_weights.shape[1]
     width = w_query.shape[1] // heads
-    half = heads // 2
     keys, values, tok, wq, *sent = states_of(tokens, w_key, w_value, w_query, heads, width)
     n2, n3, n1, n0 = (
         flip(sent[2], CORE | 2 * Y),
@@ -366,8 +361,8 @@
 
     x2, x3, x1 = (flip(going, CORE | distance * X) for distance in (2, 3, 1))
     own = flip(going, CORE)
-    low = inside_of(query, keys, values, level_weights, going, 0, half, width)
-    x2, x3, x1, own, low = lax.optimization_barrier((x2, x3, x1, own, low))
+    inside0 = inside_of(query, keys, values, level_weights, going, 0, 2, width)
+    x2, x3, x1, own, inside0 = lax.optimization_barrier((x2, x3, x1, own, inside0))
     total = plus(own.astype(F32), (x1, x2, x3))
     mine = total.astype(BF16)
 
@@ -377,11 +372,11 @@
     going = total.astype(BF16)
     z2, z1 = flip(going, CORE | 2 * Z), flip(going, CORE | Z)
     other3 = flip(z3, CORE)
-    high = inside_of(query, keys, values, level_weights, going, half, half, width)
+    inside1 = inside_of(query, keys, values, level_weights, going, 2, 2, width)
     crossing = jnp.stack([x1.astype(F32), plus(x2.astype(F32), (x3,))]).astype(BF16)
-    crossing, high = lax.optimization_barrier((crossing, high))
+    crossing, inside1 = lax.optimization_barrier((crossing, inside1))
     crossed = flip(crossing, CORE)
-    other3, z2, z1, high = lax.optimization_barrier((other3, z2, z1, high))
+    other3, z2, z1, inside1 = lax.optimization_barrier((other3, z2, z1, inside1))
     going = plus(total, (z3, z2, z1, other3)).astype(BF16)
 
     past = flip(going, CORE | 6 * Z)
@@ -389,15 +384,15 @@
     past, gathered, factor = lax.optimization_barrier((past, gathered, factor))
     last = factor * past.astype(F32)
     back = [(gathered[distance] + last).astype(BF16) for distance in range(4)]
-    p2, p3, p1, p0 = lax.optimization_barrier(
-        (
-            flip(back[2], CORE | 2 * Y),
-            flip(back[3], CORE | 3 * Y),
-            flip(back[1], CORE | Y),
-            flip(back[0], CORE),
-        )
+    p2, p3, p1, p0 = (
+        flip(back[2], CORE | 2 * Y),
+        flip(back[3], CORE | 3 * Y),
+        flip(back[1], CORE | Y),
+        flip(back[0], CORE),
     )
-    return mixed_of(query, (low, high), (p0, p1, p2, p3), w_output, width)
+    inside2 = inside_of(query, keys, values, level_weights, back[0], 4, 2, width)
+    p2, p3, p1, p0, inside2 = lax.optimization_barrier((p2, p3, p1, p0, inside2))
+    return mixed_of(query, (inside0, inside1, inside2), (p0, p1, p2, p3), w_output, width)
 
 
 def solution(mesh):

time: 46.9 us -> 46.8 us (level)
  Pallas kernels: 13.4 us -> 14.2 us
  waiting for transfers between devices: 10.1 us -> 9.63 us
    pallas_call x2 -> x3, Pallas kernels: 3.9 us -> 4.64 us  [inside_of(): pl.pallas_call(functools.partial(inside_kernel, width, first), out_shape=...]
  transfers between devices with their start and end apart: 19 -> 19, of which waited for: 9 -> 9; matrix products, arithmetic and copies ran while one was open for 0% -> 0% of each run, Pallas kernels for 14% -> 15%
where the time goes in v12:
time: 46.8 us; the launch traced here: 46.4 us
  starting transfers between devices  22 us (47%)
  Pallas kernels  14.2 us (30%)
  waiting for transfers between devices  9.63 us (21%)
    ppermute x19, starting transfers between devices, flip(): lax.ppermute(value, AXES, [(source, source ^ mask) for source in range(de...  22 us
    ppermute x19, waiting for transfers between devices, flip(): lax.ppermute(value, AXES, [(source, source ^ mask) for source in range(de...  9.63 us
    pallas_call x1, Pallas kernels, states_of(): pl.pallas_call(functools.partial(state_kernel, width), out_shape=(side, s...  4.72 us
    pallas_call x3, Pallas kernels, inside_of(): pl.pallas_call(functools.partial(inside_kernel, width, first), out_shape=...  4.64 us
    pallas_call x1, Pallas kernels, mixed_of(): pl.pallas_call(functools.partial(mix_kernel, width), out_shape=jax.ShapeD...  2.38 us
    pallas_call x1, Pallas kernels, query_of(): pl.pallas_call(functools.partial(query_kernel, width), out_shape=jax.Shap...  1.6 us
  transfers between devices with their start and end apart: 19, of which 9 were waited for; matrix products, arithmetic and copies ran while one was open for 0% of the time, Pallas kernels for 15%

profile of v12, /device:TPU:32, one launch (start us, length us, event | category | flops | bytes accessed | tf_op | source)
XLA Modules:
  0.0 46.4 jit_solution(17834616521676889591)
XLA Ops:
  0.0 4.7 %states.1 = (bf16[512,768]{1,0:T(8,128)(2,1)S(1)}, bf16[512,768]{1,0:T(8,128)(2,1)S(1)}, bf16[512,1536]{1,0:T(8,128)(2,1)S(1)}, bf16[1536,768]{1,0:T(8,128)(2,1)...) custom-call(bf16[512,1536]{1,0:T(8,128)(2,1)} %tok_hbm.1, ...), custom_call_target="tpu_custom_call" | custom-call | tf_op jit(solution)/shard_map/states/pallas_call | solution.py:127
  4.7 2.7 %collective-permute-start = (bf16[192,128]{1,0:T(8,128)(2,1)S(1)}, bf16[192,128]{1,0:T(8,128)(2,1)S(1)}, u32[]{:S(2)}, u32[]{:S(2)}) collective-permute-start(bf16[192,128]{1,0:T(8,128)(2,1)S(1)} %get-tuple-element.39), channel_id=1, source_target_pairs={{0,18},{1,19},{2,16},{3,17},{4,22},{5,23},{6,20},{7,21},{8,26},{9,... | collective-permute-start | bytes 147464 | tf_op jit(solution)/shard_map/ppermute | solution.py:338
  7.4 1.3 %collective-permute-start.1 = (bf16[192,128]{1,0:T(8,128)(2,1)S(1)}, bf16[192,128]{1,0:T(8,128)(2,1)S(1)}, u32[]{:S(2)}, u32[]{:S(2)}) collective-permute-start(bf16[192,128]{1,0:T(8,128)(2,1)S(1)} %get-tuple-element.40), channel_id=1, source_target_pairs={{0,19},{1,18},{2,17},{3,16},{4,23},{5,22},{6,21},{7,20},{8,27},{9,... | collective-permute-start | bytes 147464 | tf_op jit(solution)/shard_map/ppermute | solution.py:338
  8.8 0.0 collective-permute-start.2
  8.8 0.0 collective-permute-start.3
  8.8 1.6 %query.1.q_ref = bf16[512,768]{1,0:T(8,128)(2,1)S(1)} custom-call(bf16[512,1536]{1,0:T(8,128)(2,1)S(1)} %get-tuple-element.43.tok, bf16[1536,768]{1,0:T(8,128)(2,1)S(1)} %get-tuple-element.44.wq), custom_call_target="tpu_custom_call" | custom-call | tf_op jit(solution)/shard_map/query/pallas_call | solution.py:161
  10.4 0.0 collective-permute-done.refs_2_
  10.4 1.8 %collective-permute-done.1.refs_3_ = bf16[192,128]{1,0:T(8,128)(2,1)S(1)} collective-permute-done((bf16[192,128]{1,0:T(8,128)(2,1)S(1)}, bf16[192,128]{1,0:T(8,128)(2,1)S(1)}, u32[]{:S(2)}, u32[]{:S(2)}) %collective-permute-start.1) | collective-permute-done | bytes 49184 | tf_op jit(solution)/shard_map/ppermute | solution.py:338
  12.2 0.6 %collective-permute-done.2.refs_1_ = bf16[192,128]{1,0:T(8,128)(2,1)S(1)} collective-permute-done((bf16[192,128]{1,0:T(8,128)(2,1)S(1)}, bf16[192,128]{1,0:T(8,128)(2,1)S(1)}, u32[]{:S(2)}, u32[]{:S(2)}) %collective-permute-start.2) | collective-permute-done | bytes 49184 | tf_op jit(solution)/shard_map/ppermute | solution.py:338
  12.8 0.0 collective-permute-done.3.refs_0_
  12.9 2.8 %collective-permute-start.4 = (bf16[192,128]{1,0:T(8,128)(2,1)S(1)}, bf16[192,128]{1,0:T(8,128)(2,1)S(1)}, u32[]{:S(2)}, u32[]{:S(2)}) collective-permute-start(bf16[192,128]{1,0:T(8,128)(2,1)S(1)} %add_convert_fusion.1.after), channel_id=1, source_target_pairs={{0,24},{1,25},{2,26},{3,27},{4,28},{5,29},{6,30},{7,31},{8,16},{9,... | collective-permute-start | bytes 147464 | tf_op jit(solution)/shard_map/ppermute | solution.py:338
  15.7 1.2 %collective-permute-start.5 = (bf16[192,128]{1,0:T(8,128)(2,1)S(1)}, bf16[192,128]{1,0:T(8,128)(2,1)S(1)}, u32[]{:S(2)}, u32[]{:S(2)}) collective-permute-start(bf16[192,128]{1,0:T(8,128)(2,1)S(1)} %add_convert_fusion.1.after), channel_id=1, source_target_pairs={{0,28},{1,29},{2,30},{3,31},{4,24},{5,25},{6,26},{7,27},{8,20},{9,... | collective-permute-start | bytes 147464 | tf_op jit(solution)/shard_map/ppermute | solution.py:338
  16.8 0.0 collective-permute-start.6
  16.9 0.1 collective-permute-start.7
  16.9 0.1 copy.7.levels
  17.0 1.5 %inside.3.refs_0_ = f32[512,256]{1,0:T(8,128)S(1)} custom-call(bf16[512,768]{1,0:T(8,128)(2,1)S(1)} %query.1.q_ref, bf16[512,768]{1,0:T(8,128)(2,1)S(1)} %get-tuple-element.50.k_ref, bf16[512,768]{1,0:T(8,128)(2,1)S(1)} %get-tuple-element.51.v_ref, f32[9,6]{1,0:T(8,128)S(1)} %copy.7.levels, bf16[192,128]{1,0:T(8,128)(2,1)S(1)} %add_convert_fusion.1.after), custom_call_target="tpu_custom_call" | custom-call | tf_op jit(solution)/shard_map/inside/pallas_call | solution.py:200
  18.6 0.0 collective-permute-done.4
  18.6 1.8 %collective-permute-done.5 = bf16[192,128]{1,0:T(8,128)(2,1)S(1)} collective-permute-done((bf16[192,128]{1,0:T(8,128)(2,1)S(1)}, bf16[192,128]{1,0:T(8,128)(2,1)S(1)}, u32[]{:S(2)}, u32[]{:S(2)}) %collective-permute-start.5) | collective-permute-done | bytes 49184 | tf_op jit(solution)/shard_map/ppermute | solution.py:338
  20.4 0.2 collective-permute-done.6
  20.6 0.0 collective-permute-done.7
  20.7 0.3 collective-permute-start.10
  21.0 1.8 %collective-permute-start.8 = (bf16[192,128]{1,0:T(8,128)(2,1)S(1)}, bf16[192,128]{1,0:T(8,128)(2,1)S(1)}, u32[]{:S(2)}, u32[]{:S(2)}) collective-permute-start(bf16[192,128]{1,0:T(8,128)(2,1)S(1)} %fusion.7.refs_5_), channel_id=1, source_target_pairs={{0,112},{1,113},{2,114},{3,115},{4,116},{5,117},{6,118},{7,119},{8... | collective-permute-start | bytes 147464 | tf_op jit(solution)/shard_map/ppermute | solution.py:338
  22.8 0.0 collective-permute-done.10
  22.8 2.4 %collective-permute-start.11 = (bf16[192,128]{1,0:T(8,128)(2,1)S(1)}, bf16[192,128]{1,0:T(8,128)(2,1)S(1)}, u32[]{:S(2)}, u32[]{:S(2)}) collective-permute-start(bf16[192,128]{1,0:T(8,128)(2,1)S(1)} %get-tuple-element.78.after), channel_id=1, source_target_pairs={{0,80},{1,81},{2,82},{3,83},{4,84},{5,85},{6,86},{7,87},{8,88},{9,... | collective-permute-start | bytes 147464 | tf_op jit(solution)/shard_map/ppermute | solution.py:338
  25.2 0.5 collective-permute-start.12
  25.6 0.0 collective-permute-done.8.refs_8_
  25.7 0.3 collective-permute-start.9
  26.0 1.5 %inside.4.refs_1_ = f32[512,256]{1,0:T(8,128)S(1)} custom-call(bf16[512,768]{1,0:T(8,128)(2,1)S(1)} %query.1.q_ref, bf16[512,768]{1,0:T(8,128)(2,1)S(1)} %get-tuple-element.50.k_ref, bf16[512,768]{1,0:T(8,128)(2,1)S(1)} %get-tuple-element.51.v_ref, f32[9,6]{1,0:T(8,128)S(1)} %copy.7.levels, bf16[192,128]{1,0:T(8,128)(2,1)S(1)} %get-tuple-element.78.after), custom_call_target="tpu_custom_call" | custom-call | tf_op jit(solution)/shard_map/inside/pallas_call | solution.py:200
  27.5 0.0 copy-start
  27.5 0.3 collective-permute-start.14
  27.8 1.0 %collective-permute-done.11.refs_7_ = bf16[192,128]{1,0:T(8,128)(2,1)S(1)} collective-permute-done((bf16[192,128]{1,0:T(8,128)(2,1)S(1)}, bf16[192,128]{1,0:T(8,128)(2,1)S(1)}, u32[]{:S(2)}, u32[]{:S(2)}) %collective-permute-start.11) | collective-permute-done | bytes 49184 | tf_op jit(solution)/shard_map/ppermute | solution.py:338
  28.8 0.6 %collective-permute-done.12.refs_6_ = bf16[192,128]{1,0:T(8,128)(2,1)S(1)} collective-permute-done((bf16[192,128]{1,0:T(8,128)(2,1)S(1)}, bf16[192,128]{1,0:T(8,128)(2,1)S(1)}, u32[]{:S(2)}, u32[]{:S(2)}) %collective-permute-start.12) | collective-permute-done | bytes 49184 | tf_op jit(solution)/shard_map/ppermute | solution.py:338
  29.4 0.0 collective-permute-done.9.refs_9_
  29.4 0.1 add_convert_fusion
  29.5 4.9 %collective-permute-start.13 = (bf16[192,128]{1,0:T(8,128)(2,1)S(1)}, bf16[192,128]{1,0:T(8,128)(2,1)S(1)}, u32[]{:S(2)}, u32[]{:S(2)}) collective-permute-start(bf16[192,128]{1,0:T(8,128)(2,1)S(1)} %add_convert_fusion), channel_id=1, source_target_pairs={{0,208},{1,209},{2,210},{3,211},{4,212},{5,213},{6,214},{7,215},{8... | collective-permute-start | bytes 147464 | tf_op jit(solution)/shard_map/ppermute | solution.py:338
  34.3 0.0 collective-permute-done.14.refs_4_
  34.3 0.8 %gather.1 = (f32[4,192,128]{2,1,0:T(8,128)S(1)}, f32[192,128]{1,0:T(8,128)S(1)}) custom-call(f32[9,6]{1,0:T(8,128)S(1)} %copy.7.levels, bf16[192,128]{1,0:T(8,128)(2,1)S(1)} %collective-permute-done.3.refs_0_, bf16[192,128]{1,0:T(8,128)(2,1)S(1)} %collective-permute-done.2.refs_1_, bf16[192,128]{1,0:T(8,128)(2,1)S(1)} %collective-permute-done.refs_2_, ...), custom_call_target="tpu_custom_call" | custom-call | tf_op jit(solution)/shard_map/gather/pallas_call | solution.py:245
  35.2 2.1 %collective-permute-done.13 = bf16[192,128]{1,0:T(8,128)(2,1)S(1)} collective-permute-done((bf16[192,128]{1,0:T(8,128)(2,1)S(1)}, bf16[192,128]{1,0:T(8,128)(2,1)S(1)}, u32[]{:S(2)}, u32[]{:S(2)}) %collective-permute-start.13) | collective-permute-done | bytes 49184 | tf_op jit(solution)/shard_map/ppermute | solution.py:338
  37.3 1.0 %collective-permute-start.15 = (bf16[192,128]{1,0:T(8,128)(2,1)S(1)}, bf16[192,128]{1,0:T(8,128)(2,1)S(1)}, u32[]{:S(2)}, u32[]{:S(2)}) collective-permute-start(bf16[192,128]{1,0:T(8,128)(2,1)S(1)} %get-tuple-element.76), channel_id=1, source_target_pairs={{0,18},{1,19},{2,16},{3,17},{4,22},{5,23},{6,20},{7,21},{8,26},{9,... | collective-permute-start | bytes 147464 | tf_op jit(solution)/shard_map/ppermute | solution.py:338
  38.3 1.6 %collective-permute-start.16 = (bf16[192,128]{1,0:T(8,128)(2,1)S(1)}, bf16[192,128]{1,0:T(8,128)(2,1)S(1)}, u32[]{:S(2)}, u32[]{:S(2)}) collective-permute-start(bf16[192,128]{1,0:T(8,128)(2,1)S(1)} %get-tuple-element.75), channel_id=1, source_target_pairs={{0,19},{1,18},{2,17},{3,16},{4,23},{5,22},{6,21},{7,20},{8,27},{9,... | collective-permute-start | bytes 147464 | tf_op jit(solution)/shard_map/ppermute | solution.py:338
  39.9 0.4 collective-permute-start.17
  40.3 0.4 collective-permute-start.18
  40.8 1.5 %inside.5.refs_2_ = f32[512,256]{1,0:T(8,128)S(1)} custom-call(bf16[512,768]{1,0:T(8,128)(2,1)S(1)} %query.1.q_ref, bf16[512,768]{1,0:T(8,128)(2,1)S(1)} %get-tuple-element.50.k_ref, bf16[512,768]{1,0:T(8,128)(2,1)S(1)} %get-tuple-element.51.v_ref, f32[9,6]{1,0:T(8,128)S(1)} %copy.7.levels, bf16[192,128]{1,0:T(8,128)(2,1)S(1)} %get-tuple-element.73.after), custom_call_target="tpu_custom_call" | custom-call | tf_op jit(solution)/shard_map/inside/pallas_call | solution.py:200
  42.3 0.4 collective-permute-done.15.refs_5_
  42.7 1.2 %collective-permute-done.16.refs_6_ = bf16[192,128]{1,0:T(8,128)(2,1)S(1)} collective-permute-done((bf16[192,128]{1,0:T(8,128)(2,1)S(1)}, bf16[192,128]{1,0:T(8,128)(2,1)S(1)}, u32[]{:S(2)}, u32[]{:S(2)}) %collective-permute-start.16) | collective-permute-done | bytes 49184 | tf_op jit(solution)/shard_map/ppermute | solution.py:338
  43.8 0.0 collective-permute-done.17.refs_4_
  43.8 0.0 collective-permute-done.18.refs_3_
  43.8 2.4 %mix.1 = bf16[512,1536]{1,0:T(8,128)(2,1)} custom-call(bf16[512,768]{1,0:T(8,128)(2,1)S(1)} %query.1.q_ref, f32[512,256]{1,0:T(8,128)S(1)} %inside.3.refs_0_, f32[512,256]{1,0:T(8,128)S(1)} %inside.4.refs_1_, f32[512,256]{1,0:T(8,128)S(1)} %inside.5.refs_2_, bf16[192,128]{1,0:T(8,128)(2,1)S(1)} %collective-permute-done.18.refs_3_, ...), custom_call_target="tpu_custom_call" | custom-call | tf_op jit(solution)/shard_map/mix/pallas_call | solution.py:316
  (8 shorter events, 0.2 us)
Async XLA Ops:
  4.7 5.7 %collective-permute-start = (bf16[192,128]{1,0:T(8,128)(2,1)S(1)}, bf16[192,128]{1,0:T(8,128)(2,1)S(1)}, u32[]{:S(2)}, u32[]{:S(2)}) collective-permute-start(bf16[192,128]{1,0:T(8,128)(2,1)S(1)} %get-tuple-element.39), channel_id=1, source_target_pairs={{0,18},{1,19},{2,16},{3,17},{4,22},{5,23},{6,20},{7,21},{8,26},{9,... | collective-permute-start | bytes 147464 | tf_op jit(solution)/shard_map/ppermute | solution.py:338
  7.4 4.7 %collective-permute-start.1 = (bf16[192,128]{1,0:T(8,128)(2,1)S(1)}, bf16[192,128]{1,0:T(8,128)(2,1)S(1)}, u32[]{:S(2)}, u32[]{:S(2)}) collective-permute-start(bf16[192,128]{1,0:T(8,128)(2,1)S(1)} %get-tuple-element.40), channel_id=1, source_target_pairs={{0,19},{1,18},{2,17},{3,16},{4,23},{5,22},{6,21},{7,20},{8,27},{9,... | collective-permute-start | bytes 147464 | tf_op jit(solution)/shard_map/ppermute | solution.py:338
  8.8 4.0 %collective-permute-start.2 = (bf16[192,128]{1,0:T(8,128)(2,1)S(1)}, bf16[192,128]{1,0:T(8,128)(2,1)S(1)}, u32[]{:S(2)}, u32[]{:S(2)}) collective-permute-start(bf16[192,128]{1,0:T(8,128)(2,1)S(1)} %get-tuple-element.41), channel_id=1, source_target_pairs={{0,17},{1,16},{2,19},{3,18},{4,21},{5,20},{6,23},{7,22},{8,25},{9,... | collective-permute-start | bytes 147464 | tf_op jit(solution)/shard_map/ppermute | solution.py:338
  8.8 4.0 %collective-permute-start.3 = (bf16[192,128]{1,0:T(8,128)(2,1)S(1)}, bf16[192,128]{1,0:T(8,128)(2,1)S(1)}, u32[]{:S(2)}, u32[]{:S(2)}) collective-permute-start(bf16[192,128]{1,0:T(8,128)(2,1)S(1)} %get-tuple-element.42), channel_id=1, source_target_pairs={{0,16},{1,17},{2,18},{3,19},{4,20},{5,21},{6,22},{7,23},{8,24},{9,... | collective-permute-start | bytes 147464 | tf_op jit(solution)/shard_map/ppermute | solution.py:338
  8.8 8.1 %copy-start.1 = (f32[9,6]{0,1:T(8,128)S(1)}, f32[9,6]{0,1:T(8,128)}, u32[]{:S(2)}) copy-start(f32[9,6]{0,1:T(8,128)} %param.11) | copy-start | bytes 652
  12.9 5.7 %collective-permute-start.4 = (bf16[192,128]{1,0:T(8,128)(2,1)S(1)}, bf16[192,128]{1,0:T(8,128)(2,1)S(1)}, u32[]{:S(2)}, u32[]{:S(2)}) collective-permute-start(bf16[192,128]{1,0:T(8,128)(2,1)S(1)} %add_convert_fusion.1.after), channel_id=1, source_target_pairs={{0,24},{1,25},{2,26},{3,27},{4,28},{5,29},{6,30},{7,31},{8,16},{9,... | collective-permute-start | bytes 147464 | tf_op jit(solution)/shard_map/ppermute | solution.py:338
  15.7 4.7 %collective-permute-start.5 = (bf16[192,128]{1,0:T(8,128)(2,1)S(1)}, bf16[192,128]{1,0:T(8,128)(2,1)S(1)}, u32[]{:S(2)}, u32[]{:S(2)}) collective-permute-start(bf16[192,128]{1,0:T(8,128)(2,1)S(1)} %add_convert_fusion.1.after), channel_id=1, source_target_pairs={{0,28},{1,29},{2,30},{3,31},{4,24},{5,25},{6,26},{7,27},{8,20},{9,... | collective-permute-start | bytes 147464 | tf_op jit(solution)/shard_map/ppermute | solution.py:338
  16.8 3.8 %collective-permute-start.6 = (bf16[192,128]{1,0:T(8,128)(2,1)S(1)}, bf16[192,128]{1,0:T(8,128)(2,1)S(1)}, u32[]{:S(2)}, u32[]{:S(2)}) collective-permute-start(bf16[192,128]{1,0:T(8,128)(2,1)S(1)} %add_convert_fusion.1.after), channel_id=1, source_target_pairs={{0,20},{1,21},{2,22},{3,23},{4,16},{5,17},{6,18},{7,19},{8,28},{9,... | collective-permute-start | bytes 147464 | tf_op jit(solution)/shard_map/ppermute | solution.py:338
  16.9 3.8 %collective-permute-start.7 = (bf16[192,128]{1,0:T(8,128)(2,1)S(1)}, bf16[192,128]{1,0:T(8,128)(2,1)S(1)}, u32[]{:S(2)}, u32[]{:S(2)}) collective-permute-start(bf16[192,128]{1,0:T(8,128)(2,1)S(1)} %add_convert_fusion.1.after), channel_id=1, source_target_pairs={{0,16},{1,17},{2,18},{3,19},{4,20},{5,21},{6,22},{7,23},{8,24},{9,... | collective-permute-start | bytes 147464 | tf_op jit(solution)/shard_map/ppermute | solution.py:338
  20.7 2.1 %collective-permute-start.10 = (bf16[192,128]{1,0:T(8,128)(2,1)S(1)}, bf16[192,128]{1,0:T(8,128)(2,1)S(1)}, u32[]{:S(2)}, u32[]{:S(2)}) collective-permute-start(bf16[192,128]{1,0:T(8,128)(2,1)S(1)} %fusion.7.refs_5_), channel_id=1, source_target_pairs={{0,16},{1,17},{2,18},{3,19},{4,20},{5,21},{6,22},{7,23},{8,24},{9,... | collective-permute-start | bytes 147464 | tf_op jit(solution)/shard_map/ppermute | solution.py:338
  21.0 4.7 %collective-permute-start.8 = (bf16[192,128]{1,0:T(8,128)(2,1)S(1)}, bf16[192,128]{1,0:T(8,128)(2,1)S(1)}, u32[]{:S(2)}, u32[]{:S(2)}) collective-permute-start(bf16[192,128]{1,0:T(8,128)(2,1)S(1)} %fusion.7.refs_5_), channel_id=1, source_target_pairs={{0,112},{1,113},{2,114},{3,115},{4,116},{5,117},{6,118},{7,119},{8... | collective-permute-start | bytes 147464 | tf_op jit(solution)/shard_map/ppermute | solution.py:338
  22.8 6.0 %collective-permute-start.11 = (bf16[192,128]{1,0:T(8,128)(2,1)S(1)}, bf16[192,128]{1,0:T(8,128)(2,1)S(1)}, u32[]{:S(2)}, u32[]{:S(2)}) collective-permute-start(bf16[192,128]{1,0:T(8,128)(2,1)S(1)} %get-tuple-element.78.after), channel_id=1, source_target_pairs={{0,80},{1,81},{2,82},{3,83},{4,84},{5,85},{6,86},{7,87},{8,88},{9,... | collective-permute-start | bytes 147464 | tf_op jit(solution)/shard_map/ppermute | solution.py:338
  25.2 4.2 %collective-permute-start.12 = (bf16[192,128]{1,0:T(8,128)(2,1)S(1)}, bf16[192,128]{1,0:T(8,128)(2,1)S(1)}, u32[]{:S(2)}, u32[]{:S(2)}) collective-permute-start(bf16[192,128]{1,0:T(8,128)(2,1)S(1)} %get-tuple-element.78.after), channel_id=1, source_target_pairs={{0,48},{1,49},{2,50},{3,51},{4,52},{5,53},{6,54},{7,55},{8,56},{9,... | collective-permute-start | bytes 147464 | tf_op jit(solution)/shard_map/ppermute | solution.py:338
  25.7 3.7 %collective-permute-start.9 = (bf16[192,128]{1,0:T(8,128)(2,1)S(1)}, bf16[192,128]{1,0:T(8,128)(2,1)S(1)}, u32[]{:S(2)}, u32[]{:S(2)}) collective-permute-start(bf16[192,128]{1,0:T(8,128)(2,1)S(1)} %collective-permute-done.8.refs_8_), channel_id=1, source_target_pairs={{0,16},{1,17},{2,18},{3,19},{4,20},{5,21},{6,22},{7,23},{8,24},{9,... | collective-permute-start | bytes 147464 | tf_op jit(solution)/shard_map/ppermute | solution.py:338
  27.5 16.3 %copy-start = (bf16[768,1536]{1,0:T(8,128)(2,1)S(1)}, bf16[768,1536]{1,0:T(8,128)(2,1)}, u32[]{:S(2)}) copy-start(bf16[768,1536]{1,0:T(8,128)(2,1)} %refs_7_.1) | copy-start | bytes 7077892
  27.5 6.8 %collective-permute-start.14 = (bf16[2,192,128]{2,1,0:T(8,128)(2,1)S(1)}, bf16[2,192,128]{2,1,0:T(8,128)(2,1)S(1)}, u32[]{:S(2)}, u32[]{:S(2)}) collective-permute-start(bf16[2,192,128]{2,1,0:T(8,128)(2,1)S(1)} %pad_maximum_fusion), channel_id=1, source_target_pairs={{0,16},{1,17},{2,18},{3,19},{4,20},{5,21},{6,22},{7,23},{8,24},{9,... | collective-permute-start | bytes 294920 | tf_op jit(solution)/shard_map/ppermute | solution.py:338
  29.5 7.8 %collective-permute-start.13 = (bf16[192,128]{1,0:T(8,128)(2,1)S(1)}, bf16[192,128]{1,0:T(8,128)(2,1)S(1)}, u32[]{:S(2)}, u32[]{:S(2)}) collective-permute-start(bf16[192,128]{1,0:T(8,128)(2,1)S(1)} %add_convert_fusion), channel_id=1, source_target_pairs={{0,208},{1,209},{2,210},{3,211},{4,212},{5,213},{6,214},{7,215},{8... | collective-permute-start | bytes 147464 | tf_op jit(solution)/shard_map/ppermute | solution.py:338
  37.3 5.3 %collective-permute-start.15 = (bf16[192,128]{1,0:T(8,128)(2,1)S(1)}, bf16[192,128]{1,0:T(8,128)(2,1)S(1)}, u32[]{:S(2)}, u32[]{:S(2)}) collective-permute-start(bf16[192,128]{1,0:T(8,128)(2,1)S(1)} %get-tuple-element.76), channel_id=1, source_target_pairs={{0,18},{1,19},{2,16},{3,17},{4,22},{5,23},{6,20},{7,21},{8,26},{9,... | collective-permute-start | bytes 147464 | tf_op jit(solution)/shard_map/ppermute | solution.py:338
  38.3 5.5 %collective-permute-start.16 = (bf16[192,128]{1,0:T(8,128)(2,1)S(1)}, bf16[192,128]{1,0:T(8,128)(2,1)S(1)}, u32[]{:S(2)}, u32[]{:S(2)}) collective-permute-start(bf16[192,128]{1,0:T(8,128)(2,1)S(1)} %get-tuple-element.75), channel_id=1, source_target_pairs={{0,19},{1,18},{2,17},{3,16},{4,23},{5,22},{6,21},{7,20},{8,27},{9,... | collective-permute-start | bytes 147464 | tf_op jit(solution)/shard_map/ppermute | solution.py:338
  39.9 3.9 %collective-permute-start.17 = (bf16[192,128]{1,0:T(8,128)(2,1)S(1)}, bf16[192,128]{1,0:T(8,128)(2,1)S(1)}, u32[]{:S(2)}, u32[]{:S(2)}) collective-permute-start(bf16[192,128]{1,0:T(8,128)(2,1)S(1)} %get-tuple-element.74), channel_id=1, source_target_pairs={{0,17},{1,16},{2,19},{3,18},{4,21},{5,20},{6,23},{7,22},{8,25},{9,... | collective-permute-start | bytes 147464 | tf_op jit(solution)/shard_map/ppermute | solution.py:338
  40.3 3.5 %collective-permute-start.18 = (bf16[192,128]{1,0:T(8,128)(2,1)S(1)}, bf16[192,128]{1,0:T(8,128)(2,1)S(1)}, u32[]{:S(2)}, u32[]{:S(2)}) collective-permute-start(bf16[192,128]{1,0:T(8,128)(2,1)S(1)} %get-tuple-element.73.after), channel_id=1, source_target_pairs={{0,16},{1,17},{2,18},{3,19},{4,20},{5,21},{6,22},{7,23},{8,24},{9,... | collective-permute-start | bytes 147464 | tf_op jit(solution)/shard_map/ppermute | solution.py:338

commit v13 on v12

--- a/solution.py
+++ b/solution.py
@@ -209,7 +209,7 @@
 
 def gather_kernel(levels, *refs):
     near = refs[:4]
-    crossed, mine, z1, z2, z3, other3, local_ref, last_ref = refs[4:]
+    crossed, mine, z1, z2, z3, other2, local_ref, last_ref = refs[4:]
     y, x, core, z = position()
     heads = levels.shape[1]
     part = mine.shape[0] // heads
@@ -227,7 +227,7 @@
             + factor(3, bit(x, 1)) * crossed[1, rows, :].astype(F32)
             + factor(4, bit(core ^ 1, 0)) * read(mine)
             + factor(5, bit(z, 0)) * read(z1)
-            + factor(6, bit(z, 1)) * (read(z2) + read(z3) + read(other3))
+            + factor(6, bit(z, 1)) * (read(z2) + read(z3) + read(other2))
         )
         sides = [read(ref) for ref in near]
         for distance in range(4):
@@ -367,20 +367,20 @@
     mine = total.astype(BF16)
 
     other = flip(mine, CORE)
-    z3 = flip(mine, CORE | 3 * Z)
+    z2 = flip(mine, CORE | 2 * Z)
     total = plus(total, (other,))
     going = total.astype(BF16)
-    z2, z1 = flip(going, CORE | 2 * Z), flip(going, CORE | Z)
-    other3 = flip(z3, CORE)
+    z3, z1 = flip(going, CORE | 3 * Z), flip(going, CORE | Z)
+    other2 = flip(z2, CORE)
     inside1 = inside_of(query, keys, values, level_weights, going, 2, 2, width)
     crossing = jnp.stack([x1.astype(F32), plus(x2.astype(F32), (x3,))]).astype(BF16)
     crossing, inside1 = lax.optimization_barrier((crossing, inside1))
     crossed = flip(crossing, CORE)
-    other3, z2, z1, inside1 = lax.optimization_barrier((other3, z2, z1, inside1))
-    going = plus(total, (z3, z2, z1, other3)).astype(BF16)
+    other2, z3, z1, inside1 = lax.optimization_barrier((other2, z3, z1, inside1))
+    going = plus(total, (z2, z3, z1, other2)).astype(BF16)
 
     past = flip(going, CORE | 6 * Z)
-    gathered, factor = gather_of(level_weights, near, (crossed, mine, z1, z2, z3, other3))
+    gathered, factor = gather_of(level_weights, near, (crossed, mine, z1, z2, z3, other2))
     past, gathered, factor = lax.optimization_barrier((past, gathered, factor))
     last = factor * past.astype(F32)
     back = [(gathered[distance] + last).astype(BF16) for distance in range(4)]

time: 46.8 us -> 47.5 us (1.015)
  starting transfers between devices: 22 us -> 23.8 us
  waiting for transfers between devices: 9.63 us -> 8.58 us
    ppermute x19, starting transfers between devices: 22 us -> 23.8 us  [flip(): lax.ppermute(value, AXES, [(source, source ^ mask) for source in range(de...]
    ppermute x19, waiting for transfers between devices: 9.63 us -> 8.58 us  [flip(): lax.ppermute(value, AXES, [(source, source ^ mask) for source in range(de...]
where the time goes in v13:
time: 47.5 us; the launch traced here: 47.1 us
  starting transfers between devices  23.8 us (50%)
  Pallas kernels  14.2 us (30%)
  waiting for transfers between devices  8.58 us (18%)
    ppermute x19, starting transfers between devices, flip(): lax.ppermute(value, AXES, [(source, source ^ mask) for source in range(de...  23.8 us
    ppermute x19, waiting for transfers between devices, flip(): lax.ppermute(value, AXES, [(source, source ^ mask) for source in range(de...  8.58 us
    pallas_call x1, Pallas kernels, states_of(): pl.pallas_call(functools.partial(state_kernel, width), out_shape=(side, s...  4.72 us
    pallas_call x3, Pallas kernels, inside_of(): pl.pallas_call(functools.partial(inside_kernel, width, first), out_shape=...  4.64 us
    pallas_call x1, Pallas kernels, mixed_of(): pl.pallas_call(functools.partial(mix_kernel, width), out_shape=jax.ShapeD...  2.38 us
    pallas_call x1, Pallas kernels, query_of(): pl.pallas_call(functools.partial(query_kernel, width), out_shape=jax.Shap...  1.6 us
  transfers between devices with their start and end apart: 19, of which 9 were waited for; matrix products, arithmetic and copies ran while one was open for 0% of the time, Pallas kernels for 15%

profile of v13, /device:TPU:32, one launch (start us, length us, event | category | flops | bytes accessed | tf_op | source)
XLA Modules:
  0.0 47.1 jit_solution(7704124168103625586)
XLA Ops:
  0.0 4.7 %states.1 = (bf16[512,768]{1,0:T(8,128)(2,1)S(1)}, bf16[512,768]{1,0:T(8,128)(2,1)S(1)}, bf16[512,1536]{1,0:T(8,128)(2,1)S(1)}, bf16[1536,768]{1,0:T(8,128)(2,1)...) custom-call(bf16[512,1536]{1,0:T(8,128)(2,1)} %tok_hbm.1, ...), custom_call_target="tpu_custom_call" | custom-call | tf_op jit(solution)/shard_map/states/pallas_call | solution.py:127
  4.7 2.7 %collective-permute-start = (bf16[192,128]{1,0:T(8,128)(2,1)S(1)}, bf16[192,128]{1,0:T(8,128)(2,1)S(1)}, u32[]{:S(2)}, u32[]{:S(2)}) collective-permute-start(bf16[192,128]{1,0:T(8,128)(2,1)S(1)} %get-tuple-element.39), channel_id=1, source_target_pairs={{0,18},{1,19},{2,16},{3,17},{4,22},{5,23},{6,20},{7,21},{8,26},{9,... | collective-permute-start | bytes 147464 | tf_op jit(solution)/shard_map/ppermute | solution.py:338
  7.4 1.3 %collective-permute-start.1 = (bf16[192,128]{1,0:T(8,128)(2,1)S(1)}, bf16[192,128]{1,0:T(8,128)(2,1)S(1)}, u32[]{:S(2)}, u32[]{:S(2)}) collective-permute-start(bf16[192,128]{1,0:T(8,128)(2,1)S(1)} %get-tuple-element.40), channel_id=1, source_target_pairs={{0,19},{1,18},{2,17},{3,16},{4,23},{5,22},{6,21},{7,20},{8,27},{9,... | collective-permute-start | bytes 147464 | tf_op jit(solution)/shard_map/ppermute | solution.py:338
  8.8 0.0 collective-permute-start.2
  8.8 0.0 collective-permute-start.3
  8.8 1.6 %query.1.q_ref = bf16[512,768]{1,0:T(8,128)(2,1)S(1)} custom-call(bf16[512,1536]{1,0:T(8,128)(2,1)S(1)} %get-tuple-element.43.tok, bf16[1536,768]{1,0:T(8,128)(2,1)S(1)} %get-tuple-element.44.wq), custom_call_target="tpu_custom_call" | custom-call | tf_op jit(solution)/shard_map/query/pallas_call | solution.py:161
  10.4 0.0 collective-permute-done.refs_2_
  10.4 1.8 %collective-permute-done.1.refs_3_ = bf16[192,128]{1,0:T(8,128)(2,1)S(1)} collective-permute-done((bf16[192,128]{1,0:T(8,128)(2,1)S(1)}, bf16[192,128]{1,0:T(8,128)(2,1)S(1)}, u32[]{:S(2)}, u32[]{:S(2)}) %collective-permute-start.1) | collective-permute-done | bytes 49184 | tf_op jit(solution)/shard_map/ppermute | solution.py:338
  12.2 0.6 %collective-permute-done.2.refs_1_ = bf16[192,128]{1,0:T(8,128)(2,1)S(1)} collective-permute-done((bf16[192,128]{1,0:T(8,128)(2,1)S(1)}, bf16[192,128]{1,0:T(8,128)(2,1)S(1)}, u32[]{:S(2)}, u32[]{:S(2)}) %collective-permute-start.2) | collective-permute-done | bytes 49184 | tf_op jit(solution)/shard_map/ppermute | solution.py:338
  12.8 0.0 collective-permute-done.3.refs_0_
  12.9 2.8 %collective-permute-start.4 = (bf16[192,128]{1,0:T(8,128)(2,1)S(1)}, bf16[192,128]{1,0:T(8,128)(2,1)S(1)}, u32[]{:S(2)}, u32[]{:S(2)}) collective-permute-start(bf16[192,128]{1,0:T(8,128)(2,1)S(1)} %add_convert_fusion.1.after), channel_id=1, source_target_pairs={{0,24},{1,25},{2,26},{3,27},{4,28},{5,29},{6,30},{7,31},{8,16},{9,... | collective-permute-start | bytes 147464 | tf_op jit(solution)/shard_map/ppermute | solution.py:338
  15.7 1.2 %collective-permute-start.5 = (bf16[192,128]{1,0:T(8,128)(2,1)S(1)}, bf16[192,128]{1,0:T(8,128)(2,1)S(1)}, u32[]{:S(2)}, u32[]{:S(2)}) collective-permute-start(bf16[192,128]{1,0:T(8,128)(2,1)S(1)} %add_convert_fusion.1.after), channel_id=1, source_target_pairs={{0,28},{1,29},{2,30},{3,31},{4,24},{5,25},{6,26},{7,27},{8,20},{9,... | collective-permute-start | bytes 147464 | tf_op jit(solution)/shard_map/ppermute | solution.py:338
  16.8 0.0 collective-permute-start.6
  16.9 0.1 collective-permute-start.7
  16.9 0.1 copy.7.levels
  17.0 1.5 %inside.3.refs_0_ = f32[512,256]{1,0:T(8,128)S(1)} custom-call(bf16[512,768]{1,0:T(8,128)(2,1)S(1)} %query.1.q_ref, bf16[512,768]{1,0:T(8,128)(2,1)S(1)} %get-tuple-element.50.k_ref, bf16[512,768]{1,0:T(8,128)(2,1)S(1)} %get-tuple-element.51.v_ref, f32[9,6]{1,0:T(8,128)S(1)} %copy.7.levels, bf16[192,128]{1,0:T(8,128)(2,1)S(1)} %add_convert_fusion.1.after), custom_call_target="tpu_custom_call" | custom-call | tf_op jit(solution)/shard_map/inside/pallas_call | solution.py:200
  18.6 0.0 collective-permute-done.4
  18.6 1.8 %collective-permute-done.5 = bf16[192,128]{1,0:T(8,128)(2,1)S(1)} collective-permute-done((bf16[192,128]{1,0:T(8,128)(2,1)S(1)}, bf16[192,128]{1,0:T(8,128)(2,1)S(1)}, u32[]{:S(2)}, u32[]{:S(2)}) %collective-permute-start.5) | collective-permute-done | bytes 49184 | tf_op jit(solution)/shard_map/ppermute | solution.py:338
  20.4 0.2 collective-permute-done.6
  20.6 0.0 collective-permute-done.7
  20.7 0.3 collective-permute-start.10
  21.0 3.2 %collective-permute-start.8 = (bf16[192,128]{1,0:T(8,128)(2,1)S(1)}, bf16[192,128]{1,0:T(8,128)(2,1)S(1)}, u32[]{:S(2)}, u32[]{:S(2)}) collective-permute-start(bf16[192,128]{1,0:T(8,128)(2,1)S(1)} %fusion.7.refs_5_), channel_id=1, source_target_pairs={{0,80},{1,81},{2,82},{3,83},{4,84},{5,85},{6,86},{7,87},{8,88},{9,... | collective-permute-start | bytes 147464 | tf_op jit(solution)/shard_map/ppermute | solution.py:338
  24.1 0.0 collective-permute-done.10
  24.2 0.1 collective-permute-start.11
  24.3 2.3 %collective-permute-start.12 = (bf16[192,128]{1,0:T(8,128)(2,1)S(1)}, bf16[192,128]{1,0:T(8,128)(2,1)S(1)}, u32[]{:S(2)}, u32[]{:S(2)}) collective-permute-start(bf16[192,128]{1,0:T(8,128)(2,1)S(1)} %get-tuple-element.78.after), channel_id=1, source_target_pairs={{0,48},{1,49},{2,50},{3,51},{4,52},{5,53},{6,54},{7,55},{8,56},{9,... | collective-permute-start | bytes 147464 | tf_op jit(solution)/shard_map/ppermute | solution.py:338
  26.6 0.0 collective-permute-done.8.refs_7_
  26.6 0.2 collective-permute-start.9
  26.8 1.5 %inside.4.refs_1_ = f32[512,256]{1,0:T(8,128)S(1)} custom-call(bf16[512,768]{1,0:T(8,128)(2,1)S(1)} %query.1.q_ref, bf16[512,768]{1,0:T(8,128)(2,1)S(1)} %get-tuple-element.50.k_ref, bf16[512,768]{1,0:T(8,128)(2,1)S(1)} %get-tuple-element.51.v_ref, f32[9,6]{1,0:T(8,128)S(1)} %copy.7.levels, bf16[192,128]{1,0:T(8,128)(2,1)S(1)} %get-tuple-element.78.after), custom_call_target="tpu_custom_call" | custom-call | tf_op jit(solution)/shard_map/inside/pallas_call | solution.py:200
  28.3 0.0 copy-start
  28.4 0.4 collective-permute-start.14
  28.8 0.3 collective-permute-done.11.refs_8_
  29.1 0.5 %collective-permute-done.12.refs_6_ = bf16[192,128]{1,0:T(8,128)(2,1)S(1)} collective-permute-done((bf16[192,128]{1,0:T(8,128)(2,1)S(1)}, bf16[192,128]{1,0:T(8,128)(2,1)S(1)}, u32[]{:S(2)}, u32[]{:S(2)}) %collective-permute-start.12) | collective-permute-done | bytes 49184 | tf_op jit(solution)/shard_map/ppermute | solution.py:338
  29.6 0.0 collective-permute-done.9.refs_9_
  29.6 0.1 add_convert_fusion
  29.7 5.8 %collective-permute-start.13 = (bf16[192,128]{1,0:T(8,128)(2,1)S(1)}, bf16[192,128]{1,0:T(8,128)(2,1)S(1)}, u32[]{:S(2)}, u32[]{:S(2)}) collective-permute-start(bf16[192,128]{1,0:T(8,128)(2,1)S(1)} %add_convert_fusion), channel_id=1, source_target_pairs={{0,208},{1,209},{2,210},{3,211},{4,212},{5,213},{6,214},{7,215},{8... | collective-permute-start | bytes 147464 | tf_op jit(solution)/shard_map/ppermute | solution.py:338
  35.5 0.0 collective-permute-done.14.refs_4_
  35.5 0.8 %gather.1 = (f32[4,192,128]{2,1,0:T(8,128)S(1)}, f32[192,128]{1,0:T(8,128)S(1)}) custom-call(f32[9,6]{1,0:T(8,128)S(1)} %copy.7.levels, bf16[192,128]{1,0:T(8,128)(2,1)S(1)} %collective-permute-done.3.refs_0_, bf16[192,128]{1,0:T(8,128)(2,1)S(1)} %collective-permute-done.2.refs_1_, bf16[192,128]{1,0:T(8,128)(2,1)S(1)} %collective-permute-done.refs_2_, ...), custom_call_target="tpu_custom_call" | custom-call | tf_op jit(solution)/shard_map/gather/pallas_call | solution.py:245
  36.3 1.8 %collective-permute-done.13 = bf16[192,128]{1,0:T(8,128)(2,1)S(1)} collective-permute-done((bf16[192,128]{1,0:T(8,128)(2,1)S(1)}, bf16[192,128]{1,0:T(8,128)(2,1)S(1)}, u32[]{:S(2)}, u32[]{:S(2)}) %collective-permute-start.13) | collective-permute-done | bytes 49184 | tf_op jit(solution)/shard_map/ppermute | solution.py:338
  38.2 1.1 %collective-permute-start.15 = (bf16[192,128]{1,0:T(8,128)(2,1)S(1)}, bf16[192,128]{1,0:T(8,128)(2,1)S(1)}, u32[]{:S(2)}, u32[]{:S(2)}) collective-permute-start(bf16[192,128]{1,0:T(8,128)(2,1)S(1)} %get-tuple-element.76), channel_id=1, source_target_pairs={{0,18},{1,19},{2,16},{3,17},{4,22},{5,23},{6,20},{7,21},{8,26},{9,... | collective-permute-start | bytes 147464 | tf_op jit(solution)/shard_map/ppermute | solution.py:338
  39.3 1.5 %collective-permute-start.16 = (bf16[192,128]{1,0:T(8,128)(2,1)S(1)}, bf16[192,128]{1,0:T(8,128)(2,1)S(1)}, u32[]{:S(2)}, u32[]{:S(2)}) collective-permute-start(bf16[192,128]{1,0:T(8,128)(2,1)S(1)} %get-tuple-element.75), channel_id=1, source_target_pairs={{0,19},{1,18},{2,17},{3,16},{4,23},{5,22},{6,21},{7,20},{8,27},{9,... | collective-permute-start | bytes 147464 | tf_op jit(solution)/shard_map/ppermute | solution.py:338
  40.8 0.4 collective-permute-start.17
  41.2 0.4 collective-permute-start.18
  41.6 1.5 %inside.5.refs_2_ = f32[512,256]{1,0:T(8,128)S(1)} custom-call(bf16[512,768]{1,0:T(8,128)(2,1)S(1)} %query.1.q_ref, bf16[512,768]{1,0:T(8,128)(2,1)S(1)} %get-tuple-element.50.k_ref, bf16[512,768]{1,0:T(8,128)(2,1)S(1)} %get-tuple-element.51.v_ref, f32[9,6]{1,0:T(8,128)S(1)} %copy.7.levels, bf16[192,128]{1,0:T(8,128)(2,1)S(1)} %get-tuple-element.73.after), custom_call_target="tpu_custom_call" | custom-call | tf_op jit(solution)/shard_map/inside/pallas_call | solution.py:200
  43.2 0.3 collective-permute-done.15.refs_5_
  43.5 1.1 %collective-permute-done.16.refs_6_ = bf16[192,128]{1,0:T(8,128)(2,1)S(1)} collective-permute-done((bf16[192,128]{1,0:T(8,128)(2,1)S(1)}, bf16[192,128]{1,0:T(8,128)(2,1)S(1)}, u32[]{:S(2)}, u32[]{:S(2)}) %collective-permute-start.16) | collective-permute-done | bytes 49184 | tf_op jit(solution)/shard_map/ppermute | solution.py:338
  44.6 0.0 collective-permute-done.17.refs_4_
  44.6 0.0 collective-permute-done.18.refs_3_
  44.6 2.4 %mix.1 = bf16[512,1536]{1,0:T(8,128)(2,1)} custom-call(bf16[512,768]{1,0:T(8,128)(2,1)S(1)} %query.1.q_ref, f32[512,256]{1,0:T(8,128)S(1)} %inside.3.refs_0_, f32[512,256]{1,0:T(8,128)S(1)} %inside.4.refs_1_, f32[512,256]{1,0:T(8,128)S(1)} %inside.5.refs_2_, bf16[192,128]{1,0:T(8,128)(2,1)S(1)} %collective-permute-done.18.refs_3_, ...), custom_call_target="tpu_custom_call" | custom-call | tf_op jit(solution)/shard_map/mix/pallas_call | solution.py:316
  (8 shorter events, 0.2 us)
Async XLA Ops:
  4.7 5.7 %collective-permute-start = (bf16[192,128]{1,0:T(8,128)(2,1)S(1)}, bf16[192,128]{1,0:T(8,128)(2,1)S(1)}, u32[]{:S(2)}, u32[]{:S(2)}) collective-permute-start(bf16[192,128]{1,0:T(8,128)(2,1)S(1)} %get-tuple-element.39), channel_id=1, source_target_pairs={{0,18},{1,19},{2,16},{3,17},{4,22},{5,23},{6,20},{7,21},{8,26},{9,... | collective-permute-start | bytes 147464 | tf_op jit(solution)/shard_map/ppermute | solution.py:338
  7.4 4.7 %collective-permute-start.1 = (bf16[192,128]{1,0:T(8,128)(2,1)S(1)}, bf16[192,128]{1,0:T(8,128)(2,1)S(1)}, u32[]{:S(2)}, u32[]{:S(2)}) collective-permute-start(bf16[192,128]{1,0:T(8,128)(2,1)S(1)} %get-tuple-element.40), channel_id=1, source_target_pairs={{0,19},{1,18},{2,17},{3,16},{4,23},{5,22},{6,21},{7,20},{8,27},{9,... | collective-permute-start | bytes 147464 | tf_op jit(solution)/shard_map/ppermute | solution.py:338
  8.8 4.0 %collective-permute-start.2 = (bf16[192,128]{1,0:T(8,128)(2,1)S(1)}, bf16[192,128]{1,0:T(8,128)(2,1)S(1)}, u32[]{:S(2)}, u32[]{:S(2)}) collective-permute-start(bf16[192,128]{1,0:T(8,128)(2,1)S(1)} %get-tuple-element.41), channel_id=1, source_target_pairs={{0,17},{1,16},{2,19},{3,18},{4,21},{5,20},{6,23},{7,22},{8,25},{9,... | collective-permute-start | bytes 147464 | tf_op jit(solution)/shard_map/ppermute | solution.py:338
  8.8 4.0 %collective-permute-start.3 = (bf16[192,128]{1,0:T(8,128)(2,1)S(1)}, bf16[192,128]{1,0:T(8,128)(2,1)S(1)}, u32[]{:S(2)}, u32[]{:S(2)}) collective-permute-start(bf16[192,128]{1,0:T(8,128)(2,1)S(1)} %get-tuple-element.42), channel_id=1, source_target_pairs={{0,16},{1,17},{2,18},{3,19},{4,20},{5,21},{6,22},{7,23},{8,24},{9,... | collective-permute-start | bytes 147464 | tf_op jit(solution)/shard_map/ppermute | solution.py:338
  8.8 8.1 %copy-start.1 = (f32[9,6]{0,1:T(8,128)S(1)}, f32[9,6]{0,1:T(8,128)}, u32[]{:S(2)}) copy-start(f32[9,6]{0,1:T(8,128)} %param.11) | copy-start | bytes 652
  12.9 5.7 %collective-permute-start.4 = (bf16[192,128]{1,0:T(8,128)(2,1)S(1)}, bf16[192,128]{1,0:T(8,128)(2,1)S(1)}, u32[]{:S(2)}, u32[]{:S(2)}) collective-permute-start(bf16[192,128]{1,0:T(8,128)(2,1)S(1)} %add_convert_fusion.1.after), channel_id=1, source_target_pairs={{0,24},{1,25},{2,26},{3,27},{4,28},{5,29},{6,30},{7,31},{8,16},{9,... | collective-permute-start | bytes 147464 | tf_op jit(solution)/shard_map/ppermute | solution.py:338
  15.7 4.7 %collective-permute-start.5 = (bf16[192,128]{1,0:T(8,128)(2,1)S(1)}, bf16[192,128]{1,0:T(8,128)(2,1)S(1)}, u32[]{:S(2)}, u32[]{:S(2)}) collective-permute-start(bf16[192,128]{1,0:T(8,128)(2,1)S(1)} %add_convert_fusion.1.after), channel_id=1, source_target_pairs={{0,28},{1,29},{2,30},{3,31},{4,24},{5,25},{6,26},{7,27},{8,20},{9,... | collective-permute-start | bytes 147464 | tf_op jit(solution)/shard_map/ppermute | solution.py:338
  16.8 3.8 %collective-permute-start.6 = (bf16[192,128]{1,0:T(8,128)(2,1)S(1)}, bf16[192,128]{1,0:T(8,128)(2,1)S(1)}, u32[]{:S(2)}, u32[]{:S(2)}) collective-permute-start(bf16[192,128]{1,0:T(8,128)(2,1)S(1)} %add_convert_fusion.1.after), channel_id=1, source_target_pairs={{0,20},{1,21},{2,22},{3,23},{4,16},{5,17},{6,18},{7,19},{8,28},{9,... | collective-permute-start | bytes 147464 | tf_op jit(solution)/shard_map/ppermute | solution.py:338
  16.9 3.8 %collective-permute-start.7 = (bf16[192,128]{1,0:T(8,128)(2,1)S(1)}, bf16[192,128]{1,0:T(8,128)(2,1)S(1)}, u32[]{:S(2)}, u32[]{:S(2)}) collective-permute-start(bf16[192,128]{1,0:T(8,128)(2,1)S(1)} %add_convert_fusion.1.after), channel_id=1, source_target_pairs={{0,16},{1,17},{2,18},{3,19},{4,20},{5,21},{6,22},{7,23},{8,24},{9,... | collective-permute-start | bytes 147464 | tf_op jit(solution)/shard_map/ppermute | solution.py:338
  20.7 3.5 %collective-permute-start.10 = (bf16[192,128]{1,0:T(8,128)(2,1)S(1)}, bf16[192,128]{1,0:T(8,128)(2,1)S(1)}, u32[]{:S(2)}, u32[]{:S(2)}) collective-permute-start(bf16[192,128]{1,0:T(8,128)(2,1)S(1)} %fusion.7.refs_5_), channel_id=1, source_target_pairs={{0,16},{1,17},{2,18},{3,19},{4,20},{5,21},{6,22},{7,23},{8,24},{9,... | collective-permute-start | bytes 147464 | tf_op jit(solution)/shard_map/ppermute | solution.py:338
  21.0 5.6 %collective-permute-start.8 = (bf16[192,128]{1,0:T(8,128)(2,1)S(1)}, bf16[192,128]{1,0:T(8,128)(2,1)S(1)}, u32[]{:S(2)}, u32[]{:S(2)}) collective-permute-start(bf16[192,128]{1,0:T(8,128)(2,1)S(1)} %fusion.7.refs_5_), channel_id=1, source_target_pairs={{0,80},{1,81},{2,82},{3,83},{4,84},{5,85},{6,86},{7,87},{8,88},{9,... | collective-permute-start | bytes 147464 | tf_op jit(solution)/shard_map/ppermute | solution.py:338
  24.2 4.9 %collective-permute-start.11 = (bf16[192,128]{1,0:T(8,128)(2,1)S(1)}, bf16[192,128]{1,0:T(8,128)(2,1)S(1)}, u32[]{:S(2)}, u32[]{:S(2)}) collective-permute-start(bf16[192,128]{1,0:T(8,128)(2,1)S(1)} %get-tuple-element.78.after), channel_id=1, source_target_pairs={{0,112},{1,113},{2,114},{3,115},{4,116},{5,117},{6,118},{7,119},{8... | collective-permute-start | bytes 147464 | tf_op jit(solution)/shard_map/ppermute | solution.py:338
  24.3 5.3 %collective-permute-start.12 = (bf16[192,128]{1,0:T(8,128)(2,1)S(1)}, bf16[192,128]{1,0:T(8,128)(2,1)S(1)}, u32[]{:S(2)}, u32[]{:S(2)}) collective-permute-start(bf16[192,128]{1,0:T(8,128)(2,1)S(1)} %get-tuple-element.78.after), channel_id=1, source_target_pairs={{0,48},{1,49},{2,50},{3,51},{4,52},{5,53},{6,54},{7,55},{8,56},{9,... | collective-permute-start | bytes 147464 | tf_op jit(solution)/shard_map/ppermute | solution.py:338
  26.6 3.1 %collective-permute-start.9 = (bf16[192,128]{1,0:T(8,128)(2,1)S(1)}, bf16[192,128]{1,0:T(8,128)(2,1)S(1)}, u32[]{:S(2)}, u32[]{:S(2)}) collective-permute-start(bf16[192,128]{1,0:T(8,128)(2,1)S(1)} %collective-permute-done.8.refs_7_), channel_id=1, source_target_pairs={{0,16},{1,17},{2,18},{3,19},{4,20},{5,21},{6,22},{7,23},{8,24},{9,... | collective-permute-start | bytes 147464 | tf_op jit(solution)/shard_map/ppermute | solution.py:338
  28.3 16.2 %copy-start = (bf16[768,1536]{1,0:T(8,128)(2,1)S(1)}, bf16[768,1536]{1,0:T(8,128)(2,1)}, u32[]{:S(2)}) copy-start(bf16[768,1536]{1,0:T(8,128)(2,1)} %refs_7_.1) | copy-start | bytes 7077892
  28.4 7.1 %collective-permute-start.14 = (bf16[2,192,128]{2,1,0:T(8,128)(2,1)S(1)}, bf16[2,192,128]{2,1,0:T(8,128)(2,1)S(1)}, u32[]{:S(2)}, u32[]{:S(2)}) collective-permute-start(bf16[2,192,128]{2,1,0:T(8,128)(2,1)S(1)} %pad_maximum_fusion), channel_id=1, source_target_pairs={{0,16},{1,17},{2,18},{3,19},{4,20},{5,21},{6,22},{7,23},{8,24},{9,... | collective-permute-start | bytes 294920 | tf_op jit(solution)/shard_map/ppermute | solution.py:338
  29.7 8.4 %collective-permute-start.13 = (bf16[192,128]{1,0:T(8,128)(2,1)S(1)}, bf16[192,128]{1,0:T(8,128)(2,1)S(1)}, u32[]{:S(2)}, u32[]{:S(2)}) collective-permute-start(bf16[192,128]{1,0:T(8,128)(2,1)S(1)} %add_convert_fusion), channel_id=1, source_target_pairs={{0,208},{1,209},{2,210},{3,211},{4,212},{5,213},{6,214},{7,215},{8... | collective-permute-start | bytes 147464 | tf_op jit(solution)/shard_map/ppermute | solution.py:338
  38.2 5.3 %collective-permute-start.15 = (bf16[192,128]{1,0:T(8,128)(2,1)S(1)}, bf16[192,128]{1,0:T(8,128)(2,1)S(1)}, u32[]{:S(2)}, u32[]{:S(2)}) collective-permute-start(bf16[192,128]{1,0:T(8,128)(2,1)S(1)} %get-tuple-element.76), channel_id=1, source_target_pairs={{0,18},{1,19},{2,16},{3,17},{4,22},{5,23},{6,20},{7,21},{8,26},{9,... | collective-permute-start | bytes 147464 | tf_op jit(solution)/shard_map/ppermute | solution.py:338
  39.3 5.3 %collective-permute-start.16 = (bf16[192,128]{1,0:T(8,128)(2,1)S(1)}, bf16[192,128]{1,0:T(8,128)(2,1)S(1)}, u32[]{:S(2)}, u32[]{:S(2)}) collective-permute-start(bf16[192,128]{1,0:T(8,128)(2,1)S(1)} %get-tuple-element.75), channel_id=1, source_target_pairs={{0,19},{1,18},{2,17},{3,16},{4,23},{5,22},{6,21},{7,20},{8,27},{9,... | collective-permute-start | bytes 147464 | tf_op jit(solution)/shard_map/ppermute | solution.py:338
  40.8 3.8 %collective-permute-start.17 = (bf16[192,128]{1,0:T(8,128)(2,1)S(1)}, bf16[192,128]{1,0:T(8,128)(2,1)S(1)}, u32[]{:S(2)}, u32[]{:S(2)}) collective-permute-start(bf16[192,128]{1,0:T(8,128)(2,1)S(1)} %get-tuple-element.74), channel_id=1, source_target_pairs={{0,17},{1,16},{2,19},{3,18},{4,21},{5,20},{6,23},{7,22},{8,25},{9,... | collective-permute-start | bytes 147464 | tf_op jit(solution)/shard_map/ppermute | solution.py:338
  41.2 3.4 %collective-permute-start.18 = (bf16[192,128]{1,0:T(8,128)(2,1)S(1)}, bf16[192,128]{1,0:T(8,128)(2,1)S(1)}, u32[]{:S(2)}, u32[]{:S(2)}) collective-permute-start(bf16[192,128]{1,0:T(8,128)(2,1)S(1)} %get-tuple-element.73.after), channel_id=1, source_target_pairs={{0,16},{1,17},{2,18},{3,19},{4,20},{5,21},{6,22},{7,23},{8,24},{9,... | collective-permute-start | bytes 147464 | tf_op jit(solution)/shard_map/ppermute | solution.py:338
